TPU v7x, 32 devices: a whole 2x2x4 slice. The times are simulated.
32 devices in a mesh: row: 8 (over z, y), col: 4 (over x, core).
Axes of the slice: x: 2, y: 2, z: 4, core: 2. Of those that a mesh axis runs over, the one named last changes fastest.
Arguments:
- coupling: bfloat16 [32, 16, 12, 128, 128], P('row', 'col'), may hold values from -1 to 1
- neighbours: int32 [32, 16, 12], P('row', 'col'), may hold values from 0 to 24, as said below
- prolong: bfloat16 [32, 16, 128, 128], P('row', 'col'), may hold values from -0.5 to 0.5
- aggregate: int32 [32, 16], P('row', 'col'), may hold values from 0 to 63, as said below
Outputs:
- coarse: bfloat16 [8, 4, 2, 9, 2, 128, 128], P('row', None, None, None, None, 'col')
Inputs may be any that keep to these rules, and one draw needn't show every extreme that they name: `neighbours`: slot 0 of every node holds the code of offset (0, 0); the other 11 slots of a node hold distinct codes of nonzero offsets. `aggregate`: each aligned 4 x 4 square of the grid, square (sx, sy), holds exactly two aggregates, numbered 2 (sx 4 + sy) and 2 (sx 4 + sy) + 1, which split the square into two halves of equal size either across its first or across its second dimension.
All inputs are finite; a program needn't handle non-finite values.
Results may differ from a plain program's by a relative error of at most 0.0049.
Values may be sent and summed in bfloat16 or wider, within the bound.
No kernel may reach another device: no remote copies, remote signals or barrier semaphores. Data moves between devices by JAX's collectives and lax.ppermute only.
A program may use at most 128 MiB of HBM per device.

v0:
```python
import jax
import jax.numpy as jnp
from jax import lax
from jax.sharding import PartitionSpec as P

BS = 128
KA = 12
REACH = 2
SIDE = 4


def padded(cells, sides, width):
    for axis, dim in sides:
        count = lax.axis_size(axis)
        ends = count - 1
        head = lax.slice_in_dim(cells, 0, width, axis=dim)
        tail = lax.slice_in_dim(cells, cells.shape[dim] - width, cells.shape[dim], axis=dim)
        cells = jnp.concatenate(
            [
                lax.ppermute(tail, axis, [(i, (i + 1) % count) for i in range(ends)]),
                cells,
                lax.ppermute(head, axis, [((i + 1) % count, i) for i in range(ends)]),
            ],
            axis=dim,
        )
    return cells


def local(coupling, neighbours, prolong, aggregate):
    tile_rows = prolong.shape[0]
    tile_cols = prolong.shape[1]
    window = 2 * REACH + 1
    col_count = lax.axis_size("col")
    half_bit = (aggregate % 2).astype(jnp.bfloat16)
    extended, half_ext = (
        padded(prolong, (("row", 0), ("col", 1)), REACH),
        padded(half_bit, (("row", 0), ("col", 1)), REACH),
    )
    step_x = neighbours // window - REACH
    step_y = neighbours % window - REACH
    reach_x = jnp.arange(tile_rows, dtype=jnp.int32)[:, None, None] + step_x
    reach_y = jnp.arange(tile_cols, dtype=jnp.int32)[None, :, None] + step_y
    position = ((reach_x + REACH) * (tile_cols + 2 * REACH) + reach_y + REACH).reshape(-1)
    flat_blocks = extended.reshape(-1, BS * BS)
    picked = jnp.take(flat_blocks, position, axis=0).reshape(-1, BS, BS)
    half_far = jnp.take(half_ext.reshape(-1), position).astype(jnp.int32)
    blocks = coupling.reshape(-1, BS, BS)
    product = jnp.einsum("nab,nbc->nac", blocks, picked, preferred_element_type=jnp.float32).astype(
        jnp.bfloat16
    )
    product = product.reshape(tile_rows * tile_cols, KA, BS, BS)
    own_blocks = prolong.reshape(tile_rows * tile_cols, BS, BS)
    contribution = jnp.einsum(
        "nba,nkbc->nkac", own_blocks, product, preferred_element_type=jnp.float32
    )
    contribution = contribution.reshape(-1, BS, BS)
    home_y = (jnp.arange(tile_cols, dtype=jnp.int32) // SIDE)[None, :, None]
    shift_x = jnp.floor_divide(reach_x, SIDE)
    shift_y = jnp.floor_divide(reach_y, SIDE) - home_y
    half_near = (aggregate % 2)[:, :, None]
    segment = (home_y * 2 + half_near) * 18 + ((shift_x + 1) * 3 + shift_y + 1) * 2
    segment = segment.reshape(-1) + half_far
    squares = tile_cols // SIDE
    seg_count = squares * 36
    onehot = (jnp.arange(seg_count, dtype=jnp.int32)[:, None] == segment[None, :]).astype(
        jnp.float32
    )
    summed = jnp.einsum(
        "sm,mac->asc",
        onehot,
        contribution,
        precision=lax.Precision.HIGH,
        preferred_element_type=jnp.float32,
    )
    rows_part = BS // col_count
    outgoing = summed.astype(jnp.bfloat16).reshape(col_count, rows_part, seg_count, BS)
    received = lax.all_to_all(outgoing, "col", split_axis=0, concat_axis=0, tiled=True)
    arranged = received.reshape(col_count, rows_part, squares, 36, BS).transpose(0, 2, 3, 1, 4)
    return arranged.reshape(1, col_count * squares, 2, 9, 2, rows_part, BS)


def solution(mesh):
    return jax.shard_map(
        local,
        mesh=mesh,
        in_specs=(
            P("row", "col", None, None, None),
            P("row", "col", None),
            P("row", "col", None, None),
            P("row", "col"),
        ),
        out_specs=P("row", None, None, None, None, "col", None),
        check_vma=False,
    )
```

profile of v0, /device:TPU:5, one launch (start us, length us, event | category | flops | bytes accessed | tf_op | source)
XLA Modules:
  0.0 124.2 jit_solution(10683739562029927614)
XLA Ops:
  0.0 0.7 fusion.26
  0.7 3.1 %collective-permute-start.4 = (bf16[2,4]{1,0:T(2,128)(2,1)S(1)}, bf16[2,4]{1,0:T(2,128)(2,1)S(1)}, u32[]{:S(2)}, u32[]{:S(2)}) collective-permute-start(bf16[2,4]{1,0:T(2,128)(2,1)S(1)} %get-tuple-element.17), channel_id=1, source_target_pairs={{0,4},{4,8},{8,12},{12,16},{16,20},{20,24},{24,28},{1,5},{5,9},{9,... | collective-permute-start | bytes 56 | tf_op jit(solution)/shard_map/ppermute | solution.py:20
  3.9 2.1 %collective-permute-start.5 = (bf16[2,4]{1,0:T(2,128)(2,1)S(1)}, bf16[2,4]{1,0:T(2,128)(2,1)S(1)}, u32[]{:S(2)}, u32[]{:S(2)}) collective-permute-start(bf16[2,4]{1,0:T(2,128)(2,1)S(1)} %get-tuple-element.18), channel_id=1, source_target_pairs={{4,0},{8,4},{12,8},{16,12},{20,16},{24,20},{28,24},{5,1},{9,5},{13... | collective-permute-start | bytes 56 | tf_op jit(solution)/shard_map/ppermute | solution.py:22
  6.0 1.1 fusion.28
  7.1 1.9 %collective-permute-start.1 = (bf16[2,4,128,128]{3,2,1,0:T(8,128)(2,1)S(1)}, bf16[2,4,128,128]{3,2,1,0:T(8,128)(2,1)S(1)}, u32[]{:S(2)}, u32[]{:S(2)}) collective-permute-start(bf16[2,4,128,128]{3,2,1,0:T(8,128)(2,1)S(1)} %get-tuple-element.9), channel_id=1, source_target_pairs={{4,0},{8,4},{12,8},{16,12},{20,16},{24,20},{28,24},{5,1},{9,5},{13... | collective-permute-start | bytes 786440 | tf_op jit(solution)/shard_map/ppermute | solution.py:22
  9.0 4.3 %collective-permute-start = (bf16[2,4,128,128]{3,2,1,0:T(8,128)(2,1)S(1)}, bf16[2,4,128,128]{3,2,1,0:T(8,128)(2,1)S(1)}, u32[]{:S(2)}, u32[]{:S(2)}) collective-permute-start(bf16[2,4,128,128]{3,2,1,0:T(8,128)(2,1)S(1)} %get-tuple-element.10), channel_id=1, source_target_pairs={{0,4},{4,8},{8,12},{12,16},{16,20},{20,24},{24,28},{1,5},{5,9},{9,... | collective-permute-start | bytes 786440 | tf_op jit(solution)/shard_map/ppermute | solution.py:20
  13.3 0.8 fusion.23
  14.1 0.1 reshape.124
  14.2 0.1 reshape.122
  14.2 0.1 reshape.129
  14.4 0.0 collective-permute-done.4
  14.4 0.0 collective-permute-done.5
  14.4 9.3 %collective-permute-done = bf16[2,4,128,128]{3,2,1,0:T(8,128)(2,1)S(1)} collective-permute-done((bf16[2,4,128,128]{3,2,1,0:T(8,128)(2,1)S(1)}, bf16[2,4,128,128]{3,2,1,0:T(8,128)(2,1)S(1)}, u32[]{:S(2)}, u32[]{:S(2)}) %collective-permute-start) | collective-permute-done | bytes 262176 | tf_op jit(solution)/shard_map/ppermute | solution.py:20
  23.7 1.1 constant_dynamic-update-slice_fusion.1
  24.9 0.0 collective-permute-done.1
  24.9 0.1 fusion.27
  25.0 3.5 %collective-permute-start.2 = (bf16[8,2,128,128]{3,2,1,0:T(8,128)(2,1)S(1)}, bf16[8,2,128,128]{3,2,1,0:T(8,128)(2,1)S(1)}, u32[]{:S(2)}, u32[]{:S(2)}) collective-permute-start(bf16[8,2,128,128]{3,2,1,0:T(8,128)(2,1)S(1)} %get-tuple-element.7), channel_id=1, source_target_pairs={{0,1},{1,2},{2,3},{4,5},{5,6},{6,7},{8,9},{9,10},{10,11},{12,13},{... | collective-permute-start | bytes 1572872 | tf_op jit(solution)/shard_map/ppermute | solution.py:20
  28.5 1.9 %collective-permute-start.3 = (bf16[8,2,128,128]{3,2,1,0:T(8,128)(2,1)S(1)}, bf16[8,2,128,128]{3,2,1,0:T(8,128)(2,1)S(1)}, u32[]{:S(2)}, u32[]{:S(2)}) collective-permute-start(bf16[8,2,128,128]{3,2,1,0:T(8,128)(2,1)S(1)} %get-tuple-element.8), channel_id=1, source_target_pairs={{1,0},{2,1},{3,2},{5,4},{6,5},{7,6},{9,8},{10,9},{11,10},{13,12},{... | collective-permute-start | bytes 1572872 | tf_op jit(solution)/shard_map/ppermute | solution.py:22
  30.5 0.1 fusion.29
  30.5 3.6 %collective-permute-start.6 = (bf16[8,2]{1,0:T(8,128)(2,1)S(1)}, bf16[8,2]{1,0:T(8,128)(2,1)S(1)}, u32[]{:S(2)}, u32[]{:S(2)}) collective-permute-start(bf16[8,2]{1,0:T(8,128)(2,1)S(1)} %get-tuple-element.13), channel_id=1, source_target_pairs={{0,1},{1,2},{2,3},{4,5},{5,6},{6,7},{8,9},{9,10},{10,11},{12,13},{... | collective-permute-start | bytes 104 | tf_op jit(solution)/shard_map/ppermute | solution.py:20
  34.2 1.9 %collective-permute-start.7 = (bf16[8,2]{1,0:T(8,128)(2,1)S(1)}, bf16[8,2]{1,0:T(8,128)(2,1)S(1)}, u32[]{:S(2)}, u32[]{:S(2)}) collective-permute-start(bf16[8,2]{1,0:T(8,128)(2,1)S(1)} %get-tuple-element.14), channel_id=1, source_target_pairs={{1,0},{2,1},{3,2},{5,4},{6,5},{7,6},{9,8},{10,9},{11,10},{13,12},{... | collective-permute-start | bytes 104 | tf_op jit(solution)/shard_map/ppermute | solution.py:22
  36.1 0.0 collective-permute-done.6
  36.1 3.0 %collective-permute-done.7 = bf16[8,2]{1,0:T(8,128)(2,1)S(1)} collective-permute-done((bf16[8,2]{1,0:T(8,128)(2,1)S(1)}, bf16[8,2]{1,0:T(8,128)(2,1)S(1)}, u32[]{:S(2)}, u32[]{:S(2)}) %collective-permute-start.7) | collective-permute-done | bytes 64 | tf_op jit(solution)/shard_map/ppermute | solution.py:22
  39.1 0.1 pad_maximum_fusion.1
  39.1 0.1 reshape.130
  39.2 1.6 %gather_fusion.1 = bf16[192]{0:T(256)(128)(2,1)S(1)} fusion(bf16[64]{0:T(256)(128)(2,1)S(1)} %reshape.130, s32[1024]{0:T(1024)S(1)} %pad_clamp_fusion), kind=kCustom, calls=%fused_computation.1 | custom fusion | bytes 1536 | tf_op jit(solution)/shard_map/jit(_take)/gather | solution.py:46
  40.8 0.0 collective-permute-done.2
  40.8 0.0 collective-permute-done.3
  40.9 0.2 maximum_bitcast_fusion
  41.1 1.4 %copy.18 = bf16[8,8,128,128]{3,1,2,0:T(8,128)(2,1)S(1)} copy(bf16[8,8,128,128]{3,2,1,0:T(8,128)(2,1)S(1)} %maximum_bitcast_fusion) | data formatting | bytes 4194304
  42.5 7.1 %gather_fusion = bf16[192,16384]{1,0:T(8,128)(2,1)} fusion(bf16[64,16384]{1,0:T(8,128)(2,1)S(1)} %bitcast.36, s32[1024]{0:T(1024)S(1)} %pad_clamp_fusion), kind=kCustom, calls=%fused_computation | custom fusion | bytes 12583680 | tf_op jit(solution)/shard_map/jit(_take)/gather | solution.py:45
  49.6 7.3 %copy.16 = bf16[24,8,128,128]{3,2,1,0:T(8,128)(2,1)} copy(bf16[24,8,128,128]{3,1,2,0:T(8,128)(2,1)} %bitcast.40) | data formatting | bytes 12582912
  57.0 8.6 %copy.11 = bf16[192,128,128]{1,2,0:T(8,128)(2,1)} copy(bf16[192,128,128]{2,1,0:T(8,128)(2,1)} %bitcast.39) | data formatting | bytes 12582912 | tf_op jit(solution)/shard_map/jit(_take)/gather | solution.py:45
  65.6 0.0 copy-start
  65.6 11.8 %fusion.3 = bf16[192,128,128]{2,1,0:T(8,128)(2,1)} fusion(bf16[192,128,128]{2,1,0:T(8,128)(2,1)} %bitcast.42, bf16[192,128,128]{1,2,0:T(8,128)(2,1)} %copy.11, pred[192]{0:T(512)(128)(4,1)S(1)} %get-tuple-element.6), kind=kOutput, calls=%fused_computation.5 | convolution fusion | flops 811597824 | bytes 18874560 | tf_op jit(solution)/shard_map/nab,nbc->nac/dot_general | solution.py:48
  77.4 0.0 copy-done
  77.4 9.1 %fusion.31 = f32[16,12,128,128]{3,2,1,0:T(8,128)} fusion(bf16[16,12,128,128]{2,3,1,0:T(8,128)(2,1)} %bitcast.38, bf16[16,128,128,1]{2,1,3,0:T(8,128)(2,1)S(1)} %bitcast.41), kind=kOutput, calls=%fused_computation.69 | convolution fusion | flops 805306368 | bytes 19398656 | tf_op jit(solution)/shard_map/nba,nkbc->nkac/dot_general | solution.py:53
  86.5 12.7 %copy.12 = f32[192,128,128]{2,0,1:T(8,128)} copy(f32[192,128,128]{1,2,0:T(8,128)} %bitcast.37) | data formatting | bytes 25165824 | tf_op jit(solution)/shard_map/reshape | solution.py:56
  99.2 7.4 %convolution_convert_fusion = bf16[128,128,36]{1,2,0:T(8,128)(2,1)S(1)} fusion(f32[192,128,128]{2,0,1:T(8,128)} %copy.12, s32[192]{0:T(256)S(1)} %get-tuple-element.5), kind=kOutput, calls=%fused_computation.9 | convolution fusion | flops 680073984 | bytes 13763328 | tf_op jit(solution)/shard_map/sm,mac->asc/dot_general | solution.py:68
  106.6 0.2 copy.13
  106.8 16.4 %all_to_all.5 = bf16[4,32,36,128]{3,1,2,0:T(8,128)(2,1)S(1)} all-to-all(bf16[4,32,36,128]{3,1,2,0:T(8,128)(2,1)S(1)} %copy.13), channel_id=1, replica_groups=mesh['row'=8,'col'=4] {'col'}, dimensions={0} | all-to-all | bytes 2359296 | tf_op jit(solution)/shard_map/all_to_all | solution.py:77
  123.2 1.0 copy.22
  (9 shorter events, 0.1 us)
Async XLA Ops:
  0.7 13.7 %collective-permute-start.4 = (bf16[2,4]{1,0:T(2,128)(2,1)S(1)}, bf16[2,4]{1,0:T(2,128)(2,1)S(1)}, u32[]{:S(2)}, u32[]{:S(2)}) collective-permute-start(bf16[2,4]{1,0:T(2,128)(2,1)S(1)} %get-tuple-element.17), channel_id=1, source_target_pairs={{0,4},{4,8},{8,12},{12,16},{16,20},{20,24},{24,28},{1,5},{5,9},{9,... | collective-permute-start | bytes 56 | tf_op jit(solution)/shard_map/ppermute | solution.py:20
  3.9 10.5 %collective-permute-start.5 = (bf16[2,4]{1,0:T(2,128)(2,1)S(1)}, bf16[2,4]{1,0:T(2,128)(2,1)S(1)}, u32[]{:S(2)}, u32[]{:S(2)}) collective-permute-start(bf16[2,4]{1,0:T(2,128)(2,1)S(1)} %get-tuple-element.18), channel_id=1, source_target_pairs={{4,0},{8,4},{12,8},{16,12},{20,16},{24,20},{28,24},{5,1},{9,5},{13... | collective-permute-start | bytes 56 | tf_op jit(solution)/shard_map/ppermute | solution.py:22
  7.1 17.8 %collective-permute-start.1 = (bf16[2,4,128,128]{3,2,1,0:T(8,128)(2,1)S(1)}, bf16[2,4,128,128]{3,2,1,0:T(8,128)(2,1)S(1)}, u32[]{:S(2)}, u32[]{:S(2)}) collective-permute-start(bf16[2,4,128,128]{3,2,1,0:T(8,128)(2,1)S(1)} %get-tuple-element.9), channel_id=1, source_target_pairs={{4,0},{8,4},{12,8},{16,12},{20,16},{24,20},{28,24},{5,1},{9,5},{13... | collective-permute-start | bytes 786440 | tf_op jit(solution)/shard_map/ppermute | solution.py:22
  9.0 14.7 %collective-permute-start = (bf16[2,4,128,128]{3,2,1,0:T(8,128)(2,1)S(1)}, bf16[2,4,128,128]{3,2,1,0:T(8,128)(2,1)S(1)}, u32[]{:S(2)}, u32[]{:S(2)}) collective-permute-start(bf16[2,4,128,128]{3,2,1,0:T(8,128)(2,1)S(1)} %get-tuple-element.10), channel_id=1, source_target_pairs={{0,4},{4,8},{8,12},{12,16},{16,20},{20,24},{24,28},{1,5},{5,9},{9,... | collective-permute-start | bytes 786440 | tf_op jit(solution)/shard_map/ppermute | solution.py:20
  25.0 15.8 %collective-permute-start.2 = (bf16[8,2,128,128]{3,2,1,0:T(8,128)(2,1)S(1)}, bf16[8,2,128,128]{3,2,1,0:T(8,128)(2,1)S(1)}, u32[]{:S(2)}, u32[]{:S(2)}) collective-permute-start(bf16[8,2,128,128]{3,2,1,0:T(8,128)(2,1)S(1)} %get-tuple-element.7), channel_id=1, source_target_pairs={{0,1},{1,2},{2,3},{4,5},{5,6},{6,7},{8,9},{9,10},{10,11},{12,13},{... | collective-permute-start | bytes 1572872 | tf_op jit(solution)/shard_map/ppermute | solution.py:20
  28.5 12.3 %collective-permute-start.3 = (bf16[8,2,128,128]{3,2,1,0:T(8,128)(2,1)S(1)}, bf16[8,2,128,128]{3,2,1,0:T(8,128)(2,1)S(1)}, u32[]{:S(2)}, u32[]{:S(2)}) collective-permute-start(bf16[8,2,128,128]{3,2,1,0:T(8,128)(2,1)S(1)} %get-tuple-element.8), channel_id=1, source_target_pairs={{1,0},{2,1},{3,2},{5,4},{6,5},{7,6},{9,8},{10,9},{11,10},{13,12},{... | collective-permute-start | bytes 1572872 | tf_op jit(solution)/shard_map/ppermute | solution.py:22
  30.5 5.6 %collective-permute-start.6 = (bf16[8,2]{1,0:T(8,128)(2,1)S(1)}, bf16[8,2]{1,0:T(8,128)(2,1)S(1)}, u32[]{:S(2)}, u32[]{:S(2)}) collective-permute-start(bf16[8,2]{1,0:T(8,128)(2,1)S(1)} %get-tuple-element.13), channel_id=1, source_target_pairs={{0,1},{1,2},{2,3},{4,5},{5,6},{6,7},{8,9},{9,10},{10,11},{12,13},{... | collective-permute-start | bytes 104 | tf_op jit(solution)/shard_map/ppermute | solution.py:20
  34.2 4.9 %collective-permute-start.7 = (bf16[8,2]{1,0:T(8,128)(2,1)S(1)}, bf16[8,2]{1,0:T(8,128)(2,1)S(1)}, u32[]{:S(2)}, u32[]{:S(2)}) collective-permute-start(bf16[8,2]{1,0:T(8,128)(2,1)S(1)} %get-tuple-element.14), channel_id=1, source_target_pairs={{1,0},{2,1},{3,2},{5,4},{6,5},{7,6},{9,8},{10,9},{11,10},{13,12},{... | collective-permute-start | bytes 104 | tf_op jit(solution)/shard_map/ppermute | solution.py:22
  65.6 11.8 %copy-start = (bf16[4,4,128,128]{3,2,1,0:T(8,128)(2,1)S(1)}, bf16[4,4,128,128]{3,2,1,0:T(8,128)(2,1)}, u32[]{:S(2)}) copy-start(bf16[4,4,128,128]{3,2,1,0:T(8,128)(2,1)} %param.6) | copy-start | bytes 1572868
where the time goes:
time: 126 us; the launch traced here: 124 us
  local copies, waits for them, and re-layouts  42.8 us (34%)
  matrix products  28.3 us (22%)
  starting transfers between devices  22.4 us (18%)
  blocking collectives  16.4 us (13%)
  waiting for transfers between devices  12.3 us (10%)
  other arithmetic  1.81 us (1%)
    all_to_all x1, blocking collectives, local(): lax.all_to_all(outgoing, 'col', split_axis=0, concat_axis=0, tiled=True)  16.4 us
    gather x2, local copies, waits for them, and re-layouts, local(): picked = jnp.take(flat_blocks, position, axis=0).reshape(-1, BS, BS)  15.8 us
    ppermute x4, starting transfers between devices, padded(): lax.ppermute(tail, axis, [(i, (i + 1) % count) for i in range(ends)])  14.5 us
    reshape x1, local copies, waits for them, and re-layouts, local(): contribution = contribution.reshape(-1, BS, BS)  12.7 us
    dot_general x1, matrix products, local(): jnp.einsum('nab,nbc->nac', blocks, picked, preferred_element_type=jnp.flo...  11.8 us
    unnamed x7, local copies, waits for them, and re-layouts  10.9 us
    ppermute x4, waiting for transfers between devices, padded(): lax.ppermute(tail, axis, [(i, (i + 1) % count) for i in range(ends)])  9.31 us
    dot_general x1, matrix products, local(): jnp.einsum('nba,nkbc->nkac', own_blocks, product, preferred_element_type=...  9.1 us
  transfers between devices with their start and end apart: 8, of which 2 were waited for; matrix products, arithmetic and copies ran while one was open for 4% of the time, Pallas kernels for 0%

commit v1 on v0

v1 whole, which is shorter than its diff:
```python
import functools

import jax
import jax.numpy as jnp
from jax import lax
from jax.experimental import pallas as pl
from jax.experimental.pallas import tpu as pltpu
from jax.sharding import PartitionSpec as P

BS = 128
KA = 12
SIDE = 4
QUAD = 4 * BS
HEAD = 16
ROWS = HEAD + QUAD
EARLY = 16
LATE = 6
ANY = pl.BlockSpec(memory_space=pl.ANY)
SMEM = pl.BlockSpec(memory_space=pltpu.SMEM)
VMEM = pl.BlockSpec(memory_space=pltpu.VMEM)
BF16 = jnp.bfloat16
F32 = jnp.float32


def flips():
    return lax.rem(lax.axis_index("row"), 2), lax.rem(lax.axis_index("col"), 2)


def turned(index, flip):
    return index + flip - 2 * index * flip


def rims_kernel(agg, prolong, row_a, row_b, col_a, col_b, sems):
    fx, fy = flips()
    copies = []
    plans = (
        (row_a, ((1, 0), (1, 1))),
        (row_b, ((0, 0), (0, 1))),
        (col_a, ((0, 1), (1, 1))),
        (col_b, ((0, 0), (1, 0))),
    )
    for out, quads in plans:
        for h, (u, v) in enumerate(quads):
            ur, vr = turned(u, fx), turned(v, fy)
            for m in range(2):
                copies.append(
                    pltpu.make_async_copy(
                        prolong.at[2 * ur + m, pl.ds(pl.multiple_of(vr * 256, 256), 256), :],
                        out.at[h, HEAD + 256 * m : HEAD + 256 * (m + 1), :],
                        sems.at[len(copies)],
                    )
                )
                copies[-1].start()
    for out, quads in plans:
        for h, (u, v) in enumerate(quads):
            ur, vr = turned(u, fx), turned(v, fy)
            bit = lax.rem(agg[2 * ur, 2 * vr], 2).astype(F32)
            out[h, 0:HEAD, :] = jnp.full((HEAD, BS), bit, F32).astype(BF16)
    for copy in copies:
        copy.wait()


def rims(agg, prolong_rows):
    shape = jax.ShapeDtypeStruct((2, ROWS, BS), BF16)
    return pl.pallas_call(
        rims_kernel,
        out_shape=(shape,) * 4,
        in_specs=[SMEM, ANY],
        out_specs=(VMEM,) * 4,
        scratch_shapes=[pltpu.SemaphoreType.DMA((16,))],
        compiler_params=pltpu.CompilerParams(vmem_limit_bytes=4 << 20),
        name="rims",
    )(agg, prolong_rows)


def step_one_kernel(codes, coupling, prolong, out, acc):
    quad, node = pl.program_id(0), pl.program_id(1)
    fx, fy = flips()
    ix, iy = node // 2, node % 2
    x, y = 2 * (quad // 2) + ix, 2 * (quad % 2) + iy

    @pl.when(node == 0)
    def _():
        acc[...] = jnp.zeros_like(acc)

    left = prolong[0, 0].T
    for k in range(0, KA, 2):
        pair = jnp.concatenate([coupling[0, 0, k], coupling[0, 0, k + 1]], axis=1)
        both = jnp.dot(left, pair, preferred_element_type=F32)
        for e in range(2):
            code = codes[x, y, k + e]
            off_x = lax.shift_right_logical(code * 13, 6)
            jx = ix + off_x
            jy = iy + code - 5 * off_x
            du, dv = lax.shift_right_logical(jx, 1), lax.shift_right_logical(jy, 1)
            du = du + fx * (2 - 2 * du)
            dv = dv + fy * (2 - 2 * dv)
            at = (du * 3 + dv) * 4 + 2 * (jx & 1) + (jy & 1)
            acc[at] += both[:, e * BS : (e + 1) * BS]

    @pl.when(node == 3)
    def _():
        for t in range(36):
            out[0, t // 4, :, (t % 4) * BS : (t % 4 + 1) * BS] = acc[t].astype(BF16)


def step_one(codes, coupling, prolong):
    def node_at(q, i):
        return 2 * (q // 2) + i // 2, 2 * (q % 2) + i % 2

    return pl.pallas_call(
        step_one_kernel,
        grid=(4, 4),
        out_shape=jax.ShapeDtypeStruct((4, 9, BS, QUAD), BF16),
        in_specs=[
            SMEM,
            pl.BlockSpec((1, 1, KA, BS, BS), lambda q, i: (*node_at(q, i), 0, 0, 0)),
            pl.BlockSpec((1, 1, BS, BS), lambda q, i: (*node_at(q, i), 0, 0)),
        ],
        out_specs=pl.BlockSpec((1, 9, BS, QUAD), lambda q, i: (q, 0, 0, 0)),
        scratch_shapes=[pltpu.VMEM((36, BS, BS), F32)],
        compiler_params=pltpu.CompilerParams(vmem_limit_bytes=16 << 20),
        cost_estimate=pl.CostEstimate(
            flops=2 * 192 * BS**3, bytes_accessed=2 * 192 * BS * BS, transcendentals=0
        ),
        name="step_one",
    )(codes, coupling, prolong)


def own_bits(agg, fx, fy):
    return {
        (u + 1, v + 1): lax.rem(agg[2 * turned(u, fx), 2 * turned(v, fy)], 2).astype(F32)
        for u in range(2)
        for v in range(2)
    }


def edge_slots(terms, halves, same_a):
    near = 1.0 - jnp.abs(halves[0] - halves[1])
    by_p = []
    for first, second in terms:
        shared = near * second
        by_p.append((first + shared, second - shared))
    base = [by_p[0][v] + same_a * by_p[1][v] for v in range(2)]
    extra = [(1.0 - same_a) * by_p[1][v] for v in range(2)]
    return base, extra


def store_pieces(slots, head, outs, count):
    rows = outs[0].shape[1]
    me = lax.axis_index("col")
    for s, out in enumerate(outs):
        start = pl.multiple_of((me ^ s) * rows, rows)
        for t in range(count):
            out[t] = slots[t, pl.ds(start, rows), :].astype(BF16)
        for t in range(out.shape[0] - count):
            out[count + t] = head[t * rows : (t + 1) * rows, :].astype(BF16)


def early_kernel(agg, r, prolong, row_a, col_a, col_b, corner_aa, corner_ab, *rest):
    outs, (slots, head) = rest[:-2], rest[-2:]
    fx, fy = flips()
    bits = own_bits(agg, fx, fy)
    split_x = 1.0 - jnp.abs(bits[1, 1] - bits[1, 2])

    def far(q):
        u, v = q
        if u == 3:
            return {0: corner_ab.at[0], 3: corner_aa.at[0]}.get(v, row_a.at[v - 1])
        return (col_a if v == 3 else col_b).at[u - 1]

    def blocks(q):
        u, v = q
        if 1 <= u <= 2 and 1 <= v <= 2:
            ur, vr = turned(u - 1, fx), turned(v - 1, fy)
            at = pl.ds(pl.multiple_of(vr * 256, 256), 256)
            return jnp.concatenate([prolong[2 * ur, at, :], prolong[2 * ur + 1, at, :]], axis=0)
        return far(q)[HEAD:, :]

    def term(p, q):
        raw = 2 * turned(p[0] - 1, fx) + turned(p[1] - 1, fy)
        near = r[raw, (q[0] - p[0] + 1) * 3 + q[1] - p[1] + 1]
        return jnp.dot(near, blocks(q), preferred_element_type=F32)

    def half(q):
        return far(q)[0:1, :].astype(F32)

    own = [(1, 1), (1, 2), (2, 1), (2, 2)]
    for i, p in enumerate(own):
        for j, q in enumerate(own):
            value = term(p, q)
            for a in range(2):
                for b in range(2):
                    ia = bits[p] if a else 1.0 - bits[p]
                    ib = bits[q] if b else 1.0 - bits[q]
                    part = (ia * ib) * value
                    if i + j == 0:
                        slots[2 * a + b] = part
                    else:
                        slots[2 * a + b] += part

    rows_a = [(2, 1), (2, 2)], [(3, 1), (3, 2)], split_x
    cols_a = [(1, 2), (2, 2)], [(1, 3), (2, 3)], 1.0 - split_x
    cols_b = [(1, 1), (2, 1)], [(1, 0), (2, 0)], 1.0 - split_x
    extras = []
    for e, (ps, qs, same_a) in enumerate((rows_a, cols_a, cols_b)):
        terms = [[term(p, q) for q in qs] for p in ps]
        base, extra = edge_slots(terms, [half(q) for q in qs], same_a)
        for v in range(2):
            slots[4 + 2 * e + v] = base[v]
            if e == 0:
                slots[12 + v] = extra[v]
                extras.append(extra[v])
            elif e == 1:
                slots[12 + v] += extra[v]
            else:
                slots[14 + v] = extra[v]
    slots[10] = term((2, 2), (3, 3))
    slots[11] = term((2, 1), (3, 0))
    for k, p in enumerate(own):
        head[k : k + 1, :] = jnp.full((1, BS), bits[p], F32)
    for k, q in enumerate(((3, 1), (3, 2), (1, 3), (2, 3), (1, 0), (2, 0), (3, 3), (3, 0))):
        head[4 + k : 5 + k, :] = half(q)
    head[12:, :] = jnp.zeros((head.shape[0] - 12, BS), F32)
    store_pieces(slots, head, outs, EARLY)


def late_kernel(agg, r, row_b, corner_ba, corner_bb, *rest):
    outs, (slots, head, near, sems) = rest[:-4], rest[-4:]
    fx, fy = flips()
    copies = []
    for v in range(2):
        raw = 2 * fx + turned(v, fy)
        copies.append(pltpu.make_async_copy(r.at[raw, 0:3], near.at[v], sems.at[v]))
        copies[-1].start()
    bits = own_bits(agg, fx, fy)
    split_x = 1.0 - jnp.abs(bits[1, 1] - bits[1, 2])

    def far(v):
        return {0: corner_bb.at[0], 3: corner_ba.at[0]}.get(v, row_b.at[v - 1])

    def term(p, v):
        return jnp.dot(near[p - 1, v - p + 1], far(v)[HEAD:, :], preferred_element_type=F32)

    def half(v):
        return far(v)[0:1, :].astype(F32)

    for k, p in enumerate([(1, 1), (1, 2), (2, 1), (2, 2)]):
        head[k : k + 1, :] = jnp.full((1, BS), bits[p], F32)
    for k, v in enumerate((1, 2, 3, 0)):
        head[4 + k : 5 + k, :] = half(v)
    head[8:, :] = jnp.zeros((head.shape[0] - 8, BS), F32)
    for copy in copies:
        copy.wait()
    terms = [[term(p, v) for v in (1, 2)] for p in (1, 2)]
    base, extra = edge_slots(terms, [half(1), half(2)], split_x)
    for v in range(2):
        slots[v] = base[v]
        slots[4 + v] = extra[v]
    slots[2] = term(2, 3)
    slots[3] = term(1, 0)
    store_pieces(slots, head, outs, LATE)


def pieces(kernel, operands, specs, count, parts, extra_scratch, cost, name):
    rows = BS // parts
    heads = -(-HEAD // rows)
    shape = jax.ShapeDtypeStruct((count + heads, rows, BS), BF16)
    return pl.pallas_call(
        kernel,
        out_shape=(shape,) * parts,
        in_specs=specs,
        out_specs=(VMEM,) * parts,
        scratch_shapes=[
            pltpu.VMEM((count, BS, BS), F32),
            pltpu.VMEM((heads * rows, BS), F32),
        ]
        + extra_scratch,
        compiler_params=pltpu.CompilerParams(vmem_limit_bytes=24 << 20),
        cost_estimate=pl.CostEstimate(flops=cost, bytes_accessed=1 << 20, transcendentals=0),
        name=name,
    )(*operands)


def early_unpack_kernel(parts, *refs):
    ins, out, buf, sems = refs[:parts], refs[parts], refs[parts + 1], refs[parts + 2]
    me = lax.axis_index("col")
    fx, _ = flips()
    copies = []
    for s, ref in enumerate(ins):
        square = me ^ s
        fy = lax.rem(square, 2)
        one = functools.partial(bit_row, ref, EARLY)
        split_y = jnp.abs(one(0) - one(1))
        spread(buf, (s, 0, 1), center=[ref[t].astype(F32) for t in range(4)])
        spread_edge(buf, (s, 3, 1), ref, one, (2, 3), (4, 5), (4, 5), (12, 13), split_y)
        spread_edge(buf, (s, 0, turn3(2, fy)), ref, one, (1, 3), (6, 7), (6, 7), (12, 13), 1.0 - split_y)
        spread_edge(buf, (s, 0, turn3(0, fy)), ref, one, (0, 2), (8, 9), (8, 9), (14, 15), 1.0 - split_y)
        spread_corner(buf, (s, 3, turn3(2, fy)), ref[10].astype(F32), one(3), one(10))
        spread_corner(buf, (s, 3, turn3(0, fy)), ref[11].astype(F32), one(2), one(11))
        for a in range(2):
            for g, at in ((0, 3), (3, 6 - 6 * fx)):
                copies.append(
                    pltpu.make_async_copy(
                        buf.at[s, a, g : g + 3], out.at[square, a, pl.ds(at, 3)], sems.at[len(copies)]
                    )
                )
                copies[-1].start()
    for copy in copies:
        copy.wait()


def late_unpack_kernel(parts, *refs):
    ins, out, buf, sems = refs[:parts], refs[parts + 1], refs[parts + 2], refs[parts + 3]
    me = lax.axis_index("col")
    fx, _ = flips()
    copies = []
    for s, ref in enumerate(ins):
        square = me ^ s
        fy = lax.rem(square, 2)
        one = functools.partial(bit_row, ref, LATE)
        split_y = jnp.abs(one(0) - one(1))
        spread_edge(buf, (s, 0, 1), ref, one, (0, 1), (4, 5), (0, 1), (4, 5), split_y)
        spread_corner(buf, (s, 0, turn3(2, fy)), ref[2].astype(F32), one(1), one(6))
        spread_corner(buf, (s, 0, turn3(0, fy)), ref[3].astype(F32), one(0), one(7))
        for a in range(2):
            copies.append(
                pltpu.make_async_copy(
                    buf.at[s, a], out.at[square, a, pl.ds(6 * fx, 3)], sems.at[len(copies)]
                )
            )
            copies[-1].start()
    for copy in copies:
        copy.wait()


def turn3(index, flip):
    return index + flip * (2 - 2 * index)


def bit_row(ref, count, k):
    rows = ref.shape[1]
    return ref[count + k // rows, k % rows : k % rows + 1, :].astype(F32)


def spread(buf, at, center):
    s, group, column = at
    for a in range(2):
        for b in range(2):
            buf[s, a, group + column, b] = center[2 * a + b].astype(BF16)


def spread_edge(buf, at, ref, one, ps, qs, base, extra, used):
    a_bits = [one(p) for p in ps]
    b_bits = [one(q) for q in qs]
    values = [ref[t].astype(F32) for t in base]
    more = [ref[t].astype(F32) for t in extra]
    center = [None] * 4
    for b in range(2):
        picks = [bit if b else 1.0 - bit for bit in b_bits]
        first = picks[0] * values[0] + picks[1] * values[1]
        second = (used * picks[0]) * more[0] + (used * picks[1]) * more[1]
        for a in range(2):
            ia = [bit if a else 1.0 - bit for bit in a_bits]
            center[2 * a + b] = ia[0] * first + ia[1] * second
    spread(buf, at, center)


def spread_corner(buf, at, value, a_bit, b_bit):
    center = []
    for a in range(2):
        for b in range(2):
            center.append(((a_bit if a else 1.0 - a_bit) * (b_bit if b else 1.0 - b_bit)) * value)
    spread(buf, at, center)


def unpack_early(messages):
    parts = len(messages)
    rows = messages[0].shape[1]
    return pl.pallas_call(
        functools.partial(early_unpack_kernel, parts),
        out_shape=jax.ShapeDtypeStruct((parts, 2, 9, 2, rows, BS), BF16),
        in_specs=[VMEM] * parts,
        out_specs=ANY,
        scratch_shapes=[
            pltpu.VMEM((parts, 2, 6, 2, rows, BS), BF16),
            pltpu.SemaphoreType.DMA((4 * parts,)),
        ],
        compiler_params=pltpu.CompilerParams(vmem_limit_bytes=16 << 20),
        name="unpack_early",
    )(*messages)


def unpack_late(messages, coarse):
    parts = len(messages)
    rows = messages[0].shape[1]
    return pl.pallas_call(
        functools.partial(late_unpack_kernel, parts),
        out_shape=jax.ShapeDtypeStruct(coarse.shape, BF16),
        in_specs=[VMEM] * parts + [ANY],
        out_specs=ANY,
        scratch_shapes=[
            pltpu.VMEM((parts, 2, 3, 2, rows, BS), BF16),
            pltpu.SemaphoreType.DMA((2 * parts,)),
        ],
        input_output_aliases={parts: 0},
        compiler_params=pltpu.CompilerParams(vmem_limit_bytes=16 << 20),
        name="unpack_late",
    )(*messages, coarse)


def swap(value, axis, side):
    count = lax.axis_size(axis)
    first = range(side, count - 1, 2)
    return lax.ppermute(value, axis, [(i, i + 1) for i in first] + [(i + 1, i) for i in first])


def scatter_rows(outs):
    count = len(outs)
    return [outs[0]] + [
        lax.ppermute(outs[s], "col", [(i, i ^ s) for i in range(count)]) for s in range(1, count)
    ]


def local(coupling, neighbours, prolong, aggregate):
    parts = lax.axis_size("col")
    prolong_rows = prolong.reshape(SIDE, SIDE * BS, BS)
    to_row_a, to_row_b, to_col_a, to_col_b = rims(aggregate, prolong_rows)
    row_a = swap(to_row_a, "row", 0)
    col_a = swap(to_col_a, "col", 0)
    col_b = swap(to_col_b, "col", 1)
    row_b = swap(to_row_b, "row", 1)
    r = step_one(neighbours, coupling, prolong)
    corner_aa = swap(row_a[1:2], "col", 0)
    corner_ab = swap(row_a[0:1], "col", 1)
    corner_ba = swap(row_b[1:2], "col", 0)
    corner_bb = swap(row_b[0:1], "col", 1)
    early = pieces(
        early_kernel,
        (aggregate, r, prolong_rows, row_a, col_a, col_b, corner_aa, corner_ab),
        [SMEM] + [VMEM] * 7,
        EARLY,
        parts,
        [],
        2 * 30 * BS * BS * QUAD,
        "early_terms",
    )
    late = pieces(
        late_kernel,
        (aggregate, r, row_b, corner_ba, corner_bb),
        [SMEM, ANY] + [VMEM] * 3,
        LATE,
        parts,
        [pltpu.VMEM((2, 3, BS, QUAD), BF16), pltpu.SemaphoreType.DMA((2,))],
        2 * 6 * BS * BS * QUAD,
        "late_terms",
    )
    coarse = unpack_early(scatter_rows(early))
    coarse = unpack_late(scatter_rows(late), coarse)
    return coarse[None]


def solution(mesh):
    return jax.shard_map(
        local,
        mesh=mesh,
        in_specs=(
            P("row", "col", None, None, None),
            P("row", "col", None),
            P("row", "col", None, None),
            P("row", "col"),
        ),
        out_specs=P("row", None, None, None, None, "col", None),
        check_vma=False,
    )
```

time: 126 us -> 45.5 us (0.36); the launches traced: 124 us -> 45.1 us
  local copies, waits for them, and re-layouts: 42.8 us -> 6.29 us
  matrix products: 28.3 us -> 0 us
  blocking collectives: 16.4 us -> 0 us
  Pallas kernels: 0 us -> 15.1 us
  waiting for transfers between devices: 12.3 us -> 4.7 us
  starting transfers between devices: 22.4 us -> 18.9 us
  other arithmetic: 1.81 us -> 0 us
    dot_general x3 -> x0, matrix products: 28.3 us -> none  [the longest x1 11.8 us: local(): jnp.einsum('nab,nbc->nac', blocks, picked, preferred_element_type=jnp.flo...]
    gather x3 -> x0, local copies, waits for them, and re-layouts: 17.4 us -> none  [the longest x2 15.8 us: local(): picked = jnp.take(flat_blocks, position, axis=0).reshape(-1, BS, BS)]
    all_to_all x1 -> x0, blocking collectives: 16.4 us -> none  [local(): lax.all_to_all(outgoing, 'col', split_axis=0, concat_axis=0, tiled=True)]
    pallas_call x0 -> x6, Pallas kernels: none -> 15.1 us  [the longest x1 7.67 us: step_one(): pl.pallas_call(step_one_kernel, grid=(4, 4), out_shape=jax.ShapeDtypeStru...]
    reshape x6 -> x0, local copies, waits for them, and re-layouts: 13.2 us -> none  [the longest x1 12.7 us: local(): contribution = contribution.reshape(-1, BS, BS)]
    ppermute x8 -> x14, waiting for transfers between devices: 12.3 us -> 4.7 us  [the longest x6 4.07 us: scatter_rows(): lax.ppermute(outs[s], 'col', [(i, i ^ s) for i in range(count)])]
    unnamed x7 -> x14, local copies, waits for them, and re-layouts: 10.9 us -> 6.25 us
    ppermute x8 -> x14, starting transfers between devices: 22.4 us -> 18.9 us  [the longest x8 14.5 us: swap(): lax.ppermute(value, axis, [(i, i + 1) for i in first] + [(i + 1, i) for i...]
  transfers between devices with their start and end apart: 8 -> 14, of which waited for: 2 -> 3; matrix products, arithmetic and copies ran while one was open for 4% -> 0% of each run, Pallas kernels for 0% -> 27%
where the time goes in v1:
time: 45.5 us; the launch traced here: 45.1 us
  starting transfers between devices  18.9 us (42%)
  Pallas kernels  15.1 us (33%)
  local copies, waits for them, and re-layouts  6.29 us (14%)
  waiting for transfers between devices  4.7 us (10%)
    ppermute x8, starting transfers between devices, swap(): lax.ppermute(value, axis, [(i, i + 1) for i in first] + [(i + 1, i) for i...  14.5 us
    pallas_call x1, Pallas kernels, step_one(): pl.pallas_call(step_one_kernel, grid=(4, 4), out_shape=jax.ShapeDtypeStru...  7.67 us
    unnamed x14, local copies, waits for them, and re-layouts  6.25 us
    ppermute x6, starting transfers between devices, scatter_rows(): lax.ppermute(outs[s], 'col', [(i, i ^ s) for i in range(count)])  4.4 us
    ppermute x6, waiting for transfers between devices, scatter_rows(): lax.ppermute(outs[s], 'col', [(i, i ^ s) for i in range(count)])  4.07 us
    pallas_call x2, Pallas kernels, pieces(): pl.pallas_call(kernel, out_shape=(shape,) * parts, in_specs=specs, out_sp...  3.35 us
    pallas_call x1, Pallas kernels, rims(): pl.pallas_call(rims_kernel, out_shape=(shape,) * 4, in_specs=[SMEM, ANY],...  2.13 us
    pallas_call x1, Pallas kernels, unpack_early(): pl.pallas_call(functools.partial(early_unpack_kernel, parts), out_shape=j...  1.08 us
  transfers between devices with their start and end apart: 14, of which 3 were waited for; matrix products, arithmetic and copies ran while one was open for 0% of the time, Pallas kernels for 27%

profile of v1, /device:TPU:5, one launch (start us, length us, event | category | flops | bytes accessed | tf_op | source)
XLA Modules:
  0.0 45.1 jit_solution(6590465455141716627)
XLA Ops:
  0.0 0.0 copy-start.1
  0.0 1.0 %copy-done.1 = bf16[4,4,128,128]{3,2,1,0:T(8,128)(2,1)S(1)} copy-done((bf16[4,4,128,128]{3,2,1,0:T(8,128)(2,1)S(1)}, bf16[4,4,128,128]{3,2,1,0:T(8,128)(2,1)}, u32[]{:S(2)}) %copy-start.1) | copy-done | bytes 524312
  1.0 0.0 copy-start.4
  1.0 0.7 %copy-done.4 = s32[4,4]{1,0:T(4,128)S(1)} copy-done((s32[4,4]{1,0:T(4,128)S(1)}, s32[4,4]{1,0:T(4,128)}, u32[]{:S(2)}) %copy-start.4) | copy-done | bytes 88
  1.7 2.1 %rims.1 = (bf16[2,528,128]{2,1,0:T(8,128)(2,1)S(1)}, bf16[2,528,128]{2,1,0:T(8,128)(2,1)S(1)}, bf16[2,528,128]{2,1,0:T(8,128)(2,1)S(1)}, bf16[2,528,128]{2,1,0:T(8,128)(2,1)S(1)}) custom-call(s32[4,4]{1,0:T(4,128)S(1)} %copy-done.4, bf16[4,512,128]{2,1,0:T(8,128)(2,1)S(1)} %bitcast.2), custom_call_target="tpu_custom_call" | custom-call | tf_op jit(solution)/shard_map/rims/pallas_call | solution.py:65
  3.9 0.1 collective-permute-start.6
  3.9 4.4 %collective-permute-start = (bf16[2,528,128]{2,1,0:T(8,128)(2,1)S(1)}, bf16[2,528,128]{2,1,0:T(8,128)(2,1)S(1)}, u32[]{:S(2)}, u32[]{:S(2)}) collective-permute-start(bf16[2,528,128]{2,1,0:T(8,128)(2,1)S(1)} %get-tuple-element.17), channel_id=1, source_target_pairs={{4,8},{12,16},{20,24},{8,4},{16,12},{24,20},{5,9},{13,17},{21,25},... | collective-permute-start | bytes 811016 | tf_op jit(solution)/shard_map/ppermute | solution.py:415
  8.3 1.3 %collective-permute-start.7 = (bf16[2,528,128]{2,1,0:T(8,128)(2,1)S(1)}, bf16[2,528,128]{2,1,0:T(8,128)(2,1)S(1)}, u32[]{:S(2)}, u32[]{:S(2)}) collective-permute-start(bf16[2,528,128]{2,1,0:T(8,128)(2,1)S(1)} %get-tuple-element.23), channel_id=1, source_target_pairs={{0,1},{2,3},{1,0},{3,2},{4,5},{6,7},{5,4},{7,6},{8,9},{10,11},{9,8... | collective-permute-start | bytes 811016 | tf_op jit(solution)/shard_map/ppermute | solution.py:415
  9.6 3.0 %collective-permute-start.8 = (bf16[2,528,128]{2,1,0:T(8,128)(2,1)S(1)}, bf16[2,528,128]{2,1,0:T(8,128)(2,1)S(1)}, u32[]{:S(2)}, u32[]{:S(2)}) collective-permute-start(bf16[2,528,128]{2,1,0:T(8,128)(2,1)S(1)} %get-tuple-element.24), channel_id=1, source_target_pairs={{1,2},{2,1},{5,6},{6,5},{9,10},{10,9},{13,14},{14,13},{17,18},{18,... | collective-permute-start | bytes 811016 | tf_op jit(solution)/shard_map/ppermute | solution.py:415
  12.6 0.0 copy-start
  12.7 2.8 %copy-done = bf16[4,4,12,128,128]{4,3,2,1,0:T(8,128)(2,1)S(1)} copy-done((bf16[4,4,12,128,128]{4,3,2,1,0:T(8,128)(2,1)S(1)}, bf16[4,4,12,128,128]{4,3,2,1,0:T(8,128)(2,1)}, u32[]{:S(2)}) %copy-start) | copy-done | bytes 6291480
  15.4 0.0 copy-start.2
  15.4 1.0 %copy-done.2 = bf16[4,4,128,128]{3,2,1,0:T(8,128)(2,1)S(1)} copy-done((bf16[4,4,128,128]{3,2,1,0:T(8,128)(2,1)S(1)}, bf16[4,4,128,128]{3,2,1,0:T(8,128)(2,1)}, u32[]{:S(2)}) %copy-start.2) | copy-done | bytes 524312
  16.5 0.0 copy-start.6
  16.5 0.7 %copy-done.6 = s32[4,4,12]{2,1,0:T(4,128)S(1)} copy-done((s32[4,4,12]{2,1,0:T(4,128)S(1)}, s32[4,4,12]{2,1,0:T(4,128)}, u32[]{:S(2)}) %copy-start.6) | copy-done | bytes 792
  17.2 0.0 copy-start.3
  17.2 0.0 copy-start.5
  17.2 7.7 %step_one.1.r = bf16[4,9,128,512]{3,2,1,0:T(8,128)(2,1)S(1)} custom-call(s32[4,4,12]{2,1,0:T(4,128)S(1)} %copy-done.6, bf16[4,4,12,128,128]{4,3,2,1,0:T(8,128)(2,1)S(1)} %copy-done, bf16[4,4,128,128]{3,2,1,0:T(8,128)(2,1)S(1)} %copy-done.2), custom_call_target="tpu_custom_call" | custom-call | flops 805306368 | bytes 6291456 | tf_op jit(solution)/shard_map/step_one/pallas_call | solution.py:111
  24.9 0.0 collective-permute-done.6.row_a
  24.9 0.1 collective-permute-start.9
  25.0 2.5 %collective-permute-start.10 = (bf16[1,528,128]{2,1,0:T(8,128)(2,1)S(1)}, bf16[1,528,128]{2,1,0:T(8,128)(2,1)S(1)}, u32[]{:S(2)}, u32[]{:S(2)}) collective-permute-start(bf16[1,528,128]{2,1,0:T(8,128)(2,1)S(1)} %get-tuple-element.29), channel_id=1, source_target_pairs={{1,2},{2,1},{5,6},{6,5},{9,10},{10,9},{13,14},{14,13},{17,18},{18,... | collective-permute-start | bytes 405512 | tf_op jit(solution)/shard_map/ppermute | solution.py:415
  27.5 0.0 collective-permute-done.row_b
  27.5 0.1 collective-permute-start.1
  27.6 0.0 collective-permute-done.7.col_a
  27.6 3.0 %collective-permute-start.2 = (bf16[1,528,128]{2,1,0:T(8,128)(2,1)S(1)}, bf16[1,528,128]{2,1,0:T(8,128)(2,1)S(1)}, u32[]{:S(2)}, u32[]{:S(2)}) collective-permute-start(bf16[1,528,128]{2,1,0:T(8,128)(2,1)S(1)} %get-tuple-element.31), channel_id=1, source_target_pairs={{1,2},{2,1},{5,6},{6,5},{9,10},{10,9},{13,14},{14,13},{17,18},{18,... | collective-permute-start | bytes 405512 | tf_op jit(solution)/shard_map/ppermute | solution.py:415
  30.7 0.0 collective-permute-done.8.col_b
  30.7 0.0 collective-permute-done.9.corner_aa
  30.7 0.6 %collective-permute-done.10.corner_ab = bf16[1,528,128]{2,1,0:T(8,128)(2,1)S(1)} collective-permute-done((bf16[1,528,128]{2,1,0:T(8,128)(2,1)S(1)}, bf16[1,528,128]{2,1,0:T(8,128)(2,1)S(1)}, u32[]{:S(2)}, u32[]{:S(2)}) %collective-permute-start.10) | collective-permute-done | bytes 135200 | tf_op jit(solution)/shard_map/ppermute | solution.py:415
  31.3 0.0 copy-done.3
  31.3 0.0 copy-done.5
  31.3 2.0 %early_terms.1 = (bf16[17,32,128]{2,1,0:T(8,128)(2,1)S(1)}, bf16[17,32,128]{2,1,0:T(8,128)(2,1)S(1)}, bf16[17,32,128]{2,1,0:T(8,128)(2,1)S(1)}, bf16[17,32,128]{2,1,0:T(8,128)(2,1)S(1)}) custom-call(s32[4,4]{1,0:T(4,128)S(1)} %copy-done.5, bf16[4,9,128,512]{3,2,1,0:T(8,128)(2,1)S(1)} %step_one.1.r, bf16[4,512,128]{2,1,0:T(8,128)(2,1)S(1)} %bitcast.3, ...), custom_call_target="tpu_custom_call" | custom-call | flops 503316480 | bytes 1048576 | tf_op jit(solution)/shard_map/early_terms/pallas_call | solution.py:269
  33.3 0.1 collective-permute-start.11
  33.4 0.7 %collective-permute-start.12 = (bf16[17,32,128]{2,1,0:T(8,128)(2,1)S(1)}, bf16[17,32,128]{2,1,0:T(8,128)(2,1)S(1)}, u32[]{:S(2)}, u32[]{:S(2)}) collective-permute-start(bf16[17,32,128]{2,1,0:T(8,128)(2,1)S(1)} %get-tuple-element.27), channel_id=1, source_target_pairs={{0,2},{1,3},{2,0},{3,1},{4,6},{5,7},{6,4},{7,5},{8,10},{9,11},{10,... | collective-permute-start | bytes 417800 | tf_op jit(solution)/shard_map/ppermute | solution.py:421
  34.1 1.4 %collective-permute-start.13 = (bf16[17,32,128]{2,1,0:T(8,128)(2,1)S(1)}, bf16[17,32,128]{2,1,0:T(8,128)(2,1)S(1)}, u32[]{:S(2)}, u32[]{:S(2)}) collective-permute-start(bf16[17,32,128]{2,1,0:T(8,128)(2,1)S(1)} %get-tuple-element.28), channel_id=1, source_target_pairs={{0,3},{1,2},{2,1},{3,0},{4,7},{5,6},{6,5},{7,4},{8,11},{9,10},{10,... | collective-permute-start | bytes 417800 | tf_op jit(solution)/shard_map/ppermute | solution.py:421
  35.5 0.0 collective-permute-done.1.corner_ba
  35.5 0.0 collective-permute-done.2.corner_bb
  35.5 1.4 %late_terms.1 = (bf16[7,32,128]{2,1,0:T(8,128)(2,1)S(1)}, bf16[7,32,128]{2,1,0:T(8,128)(2,1)S(1)}, bf16[7,32,128]{2,1,0:T(8,128)(2,1)S(1)}, bf16[7,32,128]{2,1,0:T(8,128)(2,1)S(1)}) custom-call(s32[4,4]{1,0:T(4,128)S(1)} %copy-done.5, bf16[4,9,128,512]{3,2,1,0:T(8,128)(2,1)S(1)} %step_one.1.r, bf16[2,528,128]{2,1,0:T(8,128)(2,1)S(1)} %collective-permute-done.row_b, ...), custom_call_target="tpu_custom_call" | custom-call | flops 100663296 | bytes 1048576 | tf_op jit(solution)/shard_map/late_terms/pallas_call | solution.py:269
  36.9 0.1 collective-permute-start.3
  37.0 0.5 %collective-permute-start.4 = (bf16[7,32,128]{2,1,0:T(8,128)(2,1)S(1)}, bf16[7,32,128]{2,1,0:T(8,128)(2,1)S(1)}, u32[]{:S(2)}, u32[]{:S(2)}) collective-permute-start(bf16[7,32,128]{2,1,0:T(8,128)(2,1)S(1)} %get-tuple-element.20), channel_id=1, source_target_pairs={{0,2},{1,3},{2,0},{3,1},{4,6},{5,7},{6,4},{7,5},{8,10},{9,11},{10,... | collective-permute-start | bytes 172040 | tf_op jit(solution)/shard_map/ppermute | solution.py:421
  37.4 0.0 collective-permute-done.11.refs_1_
  37.4 1.7 %collective-permute-start.5 = (bf16[7,32,128]{2,1,0:T(8,128)(2,1)S(1)}, bf16[7,32,128]{2,1,0:T(8,128)(2,1)S(1)}, u32[]{:S(2)}, u32[]{:S(2)}) collective-permute-start(bf16[7,32,128]{2,1,0:T(8,128)(2,1)S(1)} %get-tuple-element.21), channel_id=1, source_target_pairs={{0,3},{1,2},{2,1},{3,0},{4,7},{5,6},{6,5},{7,4},{8,11},{9,10},{10,... | collective-permute-start | bytes 172040 | tf_op jit(solution)/shard_map/ppermute | solution.py:421
  39.1 0.0 collective-permute-done.12.refs_2_
  39.1 3.9 %collective-permute-done.13.refs_3_ = bf16[17,32,128]{2,1,0:T(8,128)(2,1)S(1)} collective-permute-done((bf16[17,32,128]{2,1,0:T(8,128)(2,1)S(1)}, bf16[17,32,128]{2,1,0:T(8,128)(2,1)S(1)}, u32[]{:S(2)}, u32[]{:S(2)}) %collective-permute-start.13) | collective-permute-done | bytes 139296 | tf_op jit(solution)/shard_map/ppermute | solution.py:421
  43.0 1.1 %unpack_early.1.refs_4_ = bf16[4,2,9,2,32,128]{5,4,3,2,1,0:T(8,128)(2,1)} custom-call(bf16[17,32,128]{2,1,0:T(8,128)(2,1)S(1)} %get-tuple-element.25.refs_0_, bf16[17,32,128]{2,1,0:T(8,128)(2,1)S(1)} %collective-permute-done.11.refs_1_, bf16[17,32,128]{2,1,0:T(8,128)(2,1)S(1)} %collective-permute-done.12.refs_2_, ...), custom_call_target="tpu_custom_call" | custom-call | tf_op jit(solution)/shard_map/unpack_early/pallas_call | solution.py:380
  44.1 0.0 collective-permute-done.3.refs_1_
  44.1 0.0 collective-permute-done.4.refs_2_
  44.1 0.2 collective-permute-done.5.refs_3_
  44.3 0.8 %unpack_late.1 = bf16[4,2,9,2,32,128]{5,4,3,2,1,0:T(8,128)(2,1)} custom-call(bf16[7,32,128]{2,1,0:T(8,128)(2,1)S(1)} %get-tuple-element.18.refs_0_, bf16[7,32,128]{2,1,0:T(8,128)(2,1)S(1)} %collective-permute-done.3.refs_1_, bf16[7,32,128]{2,1,0:T(8,128)(2,1)S(1)} %collective-permute-done.4.refs_2_, ...), custom_call_target="tpu_custom_call", output_to_operand_aliasing={{}: (4, {})} | custom-call | tf_op jit(solution)/shard_map/unpack_late/pallas_call | solution.py:397
  (2 shorter events, 0.0 us)
Async XLA Ops:
  0.0 1.0 %copy-start.1 = (bf16[4,4,128,128]{3,2,1,0:T(8,128)(2,1)S(1)}, bf16[4,4,128,128]{3,2,1,0:T(8,128)(2,1)}, u32[]{:S(2)}) copy-start(bf16[4,4,128,128]{3,2,1,0:T(8,128)(2,1)} %prolong.1) | copy-start | bytes 1572868
  1.0 0.7 %copy-start.4 = (s32[4,4]{1,0:T(4,128)S(1)}, s32[4,4]{1,0:T(4,128)}, u32[]{:S(2)}) copy-start(s32[4,4]{1,0:T(4,128)} %agg.5) | copy-start | bytes 196
  3.9 21.0 %collective-permute-start.6 = (bf16[2,528,128]{2,1,0:T(8,128)(2,1)S(1)}, bf16[2,528,128]{2,1,0:T(8,128)(2,1)S(1)}, u32[]{:S(2)}, u32[]{:S(2)}) collective-permute-start(bf16[2,528,128]{2,1,0:T(8,128)(2,1)S(1)} %get-tuple-element.22), channel_id=1, source_target_pairs={{0,4},{8,12},{16,20},{24,28},{4,0},{12,8},{20,16},{28,24},{1,5},{9... | collective-permute-start | bytes 811016 | tf_op jit(solution)/shard_map/ppermute | solution.py:415
  3.9 23.6 %collective-permute-start = (bf16[2,528,128]{2,1,0:T(8,128)(2,1)S(1)}, bf16[2,528,128]{2,1,0:T(8,128)(2,1)S(1)}, u32[]{:S(2)}, u32[]{:S(2)}) collective-permute-start(bf16[2,528,128]{2,1,0:T(8,128)(2,1)S(1)} %get-tuple-element.17), channel_id=1, source_target_pairs={{4,8},{12,16},{20,24},{8,4},{16,12},{24,20},{5,9},{13,17},{21,25},... | collective-permute-start | bytes 811016 | tf_op jit(solution)/shard_map/ppermute | solution.py:415
  8.3 19.3 %collective-permute-start.7 = (bf16[2,528,128]{2,1,0:T(8,128)(2,1)S(1)}, bf16[2,528,128]{2,1,0:T(8,128)(2,1)S(1)}, u32[]{:S(2)}, u32[]{:S(2)}) collective-permute-start(bf16[2,528,128]{2,1,0:T(8,128)(2,1)S(1)} %get-tuple-element.23), channel_id=1, source_target_pairs={{0,1},{2,3},{1,0},{3,2},{4,5},{6,7},{5,4},{7,6},{8,9},{10,11},{9,8... | collective-permute-start | bytes 811016 | tf_op jit(solution)/shard_map/ppermute | solution.py:415
  9.6 21.1 %collective-permute-start.8 = (bf16[2,528,128]{2,1,0:T(8,128)(2,1)S(1)}, bf16[2,528,128]{2,1,0:T(8,128)(2,1)S(1)}, u32[]{:S(2)}, u32[]{:S(2)}) collective-permute-start(bf16[2,528,128]{2,1,0:T(8,128)(2,1)S(1)} %get-tuple-element.24), channel_id=1, source_target_pairs={{1,2},{2,1},{5,6},{6,5},{9,10},{10,9},{13,14},{14,13},{17,18},{18,... | collective-permute-start | bytes 811016 | tf_op jit(solution)/shard_map/ppermute | solution.py:415
  12.6 2.8 %copy-start = (bf16[4,4,12,128,128]{4,3,2,1,0:T(8,128)(2,1)S(1)}, bf16[4,4,12,128,128]{4,3,2,1,0:T(8,128)(2,1)}, u32[]{:S(2)}) copy-start(bf16[4,4,12,128,128]{4,3,2,1,0:T(8,128)(2,1)} %coupling.1) | copy-start | bytes 18874372
  15.4 1.0 %copy-start.2 = (bf16[4,4,128,128]{3,2,1,0:T(8,128)(2,1)S(1)}, bf16[4,4,128,128]{3,2,1,0:T(8,128)(2,1)}, u32[]{:S(2)}) copy-start(bf16[4,4,128,128]{3,2,1,0:T(8,128)(2,1)} %prolong.1) | copy-start | bytes 1572868
  16.5 0.7 %copy-start.6 = (s32[4,4,12]{2,1,0:T(4,128)S(1)}, s32[4,4,12]{2,1,0:T(4,128)}, u32[]{:S(2)}) copy-start(s32[4,4,12]{2,1,0:T(4,128)} %codes.1) | copy-start | bytes 2308
  17.2 14.1 %copy-start.3 = (bf16[4,4,128,128]{3,2,1,0:T(8,128)(2,1)S(1)}, bf16[4,4,128,128]{3,2,1,0:T(8,128)(2,1)}, u32[]{:S(2)}) copy-start(bf16[4,4,128,128]{3,2,1,0:T(8,128)(2,1)} %prolong.1) | copy-start | bytes 1572868
  17.2 14.1 %copy-start.5 = (s32[4,4]{1,0:T(4,128)S(1)}, s32[4,4]{1,0:T(4,128)}, u32[]{:S(2)}) copy-start(s32[4,4]{1,0:T(4,128)} %agg.5) | copy-start | bytes 196
  24.9 5.8 %collective-permute-start.9 = (bf16[1,528,128]{2,1,0:T(8,128)(2,1)S(1)}, bf16[1,528,128]{2,1,0:T(8,128)(2,1)S(1)}, u32[]{:S(2)}, u32[]{:S(2)}) collective-permute-start(bf16[1,528,128]{2,1,0:T(8,128)(2,1)S(1)} %get-tuple-element.30), channel_id=1, source_target_pairs={{0,1},{2,3},{1,0},{3,2},{4,5},{6,7},{5,4},{7,6},{8,9},{10,11},{9,8... | collective-permute-start | bytes 405512 | tf_op jit(solution)/shard_map/ppermute | solution.py:415
  25.0 6.3 %collective-permute-start.10 = (bf16[1,528,128]{2,1,0:T(8,128)(2,1)S(1)}, bf16[1,528,128]{2,1,0:T(8,128)(2,1)S(1)}, u32[]{:S(2)}, u32[]{:S(2)}) collective-permute-start(bf16[1,528,128]{2,1,0:T(8,128)(2,1)S(1)} %get-tuple-element.29), channel_id=1, source_target_pairs={{1,2},{2,1},{5,6},{6,5},{9,10},{10,9},{13,14},{14,13},{17,18},{18,... | collective-permute-start | bytes 405512 | tf_op jit(solution)/shard_map/ppermute | solution.py:415
  27.5 8.0 %collective-permute-start.1 = (bf16[1,528,128]{2,1,0:T(8,128)(2,1)S(1)}, bf16[1,528,128]{2,1,0:T(8,128)(2,1)S(1)}, u32[]{:S(2)}, u32[]{:S(2)}) collective-permute-start(bf16[1,528,128]{2,1,0:T(8,128)(2,1)S(1)} %get-tuple-element.32), channel_id=1, source_target_pairs={{0,1},{2,3},{1,0},{3,2},{4,5},{6,7},{5,4},{7,6},{8,9},{10,11},{9,8... | collective-permute-start | bytes 405512 | tf_op jit(solution)/shard_map/ppermute | solution.py:415
  27.6 7.9 %collective-permute-start.2 = (bf16[1,528,128]{2,1,0:T(8,128)(2,1)S(1)}, bf16[1,528,128]{2,1,0:T(8,128)(2,1)S(1)}, u32[]{:S(2)}, u32[]{:S(2)}) collective-permute-start(bf16[1,528,128]{2,1,0:T(8,128)(2,1)S(1)} %get-tuple-element.31), channel_id=1, source_target_pairs={{1,2},{2,1},{5,6},{6,5},{9,10},{10,9},{13,14},{14,13},{17,18},{18,... | collective-permute-start | bytes 405512 | tf_op jit(solution)/shard_map/ppermute | solution.py:415
  33.3 4.1 %collective-permute-start.11 = (bf16[17,32,128]{2,1,0:T(8,128)(2,1)S(1)}, bf16[17,32,128]{2,1,0:T(8,128)(2,1)S(1)}, u32[]{:S(2)}, u32[]{:S(2)}) collective-permute-start(bf16[17,32,128]{2,1,0:T(8,128)(2,1)S(1)} %get-tuple-element.26), channel_id=1, source_target_pairs={{0,1},{1,0},{2,3},{3,2},{4,5},{5,4},{6,7},{7,6},{8,9},{9,8},{10,11... | collective-permute-start | bytes 417800 | tf_op jit(solution)/shard_map/ppermute | solution.py:421
  33.4 5.7 %collective-permute-start.12 = (bf16[17,32,128]{2,1,0:T(8,128)(2,1)S(1)}, bf16[17,32,128]{2,1,0:T(8,128)(2,1)S(1)}, u32[]{:S(2)}, u32[]{:S(2)}) collective-permute-start(bf16[17,32,128]{2,1,0:T(8,128)(2,1)S(1)} %get-tuple-element.27), channel_id=1, source_target_pairs={{0,2},{1,3},{2,0},{3,1},{4,6},{5,7},{6,4},{7,5},{8,10},{9,11},{10,... | collective-permute-start | bytes 417800 | tf_op jit(solution)/shard_map/ppermute | solution.py:421
  34.1 8.9 %collective-permute-start.13 = (bf16[17,32,128]{2,1,0:T(8,128)(2,1)S(1)}, bf16[17,32,128]{2,1,0:T(8,128)(2,1)S(1)}, u32[]{:S(2)}, u32[]{:S(2)}) collective-permute-start(bf16[17,32,128]{2,1,0:T(8,128)(2,1)S(1)} %get-tuple-element.28), channel_id=1, source_target_pairs={{0,3},{1,2},{2,1},{3,0},{4,7},{5,6},{6,5},{7,4},{8,11},{9,10},{10,... | collective-permute-start | bytes 417800 | tf_op jit(solution)/shard_map/ppermute | solution.py:421
  36.9 7.2 %collective-permute-start.3 = (bf16[7,32,128]{2,1,0:T(8,128)(2,1)S(1)}, bf16[7,32,128]{2,1,0:T(8,128)(2,1)S(1)}, u32[]{:S(2)}, u32[]{:S(2)}) collective-permute-start(bf16[7,32,128]{2,1,0:T(8,128)(2,1)S(1)} %get-tuple-element.19), channel_id=1, source_target_pairs={{0,1},{1,0},{2,3},{3,2},{4,5},{5,4},{6,7},{7,6},{8,9},{9,8},{10,11... | collective-permute-start | bytes 172040 | tf_op jit(solution)/shard_map/ppermute | solution.py:421
  37.0 7.1 %collective-permute-start.4 = (bf16[7,32,128]{2,1,0:T(8,128)(2,1)S(1)}, bf16[7,32,128]{2,1,0:T(8,128)(2,1)S(1)}, u32[]{:S(2)}, u32[]{:S(2)}) collective-permute-start(bf16[7,32,128]{2,1,0:T(8,128)(2,1)S(1)} %get-tuple-element.20), channel_id=1, source_target_pairs={{0,2},{1,3},{2,0},{3,1},{4,6},{5,7},{6,4},{7,5},{8,10},{9,11},{10,... | collective-permute-start | bytes 172040 | tf_op jit(solution)/shard_map/ppermute | solution.py:421
  37.4 6.8 %collective-permute-start.5 = (bf16[7,32,128]{2,1,0:T(8,128)(2,1)S(1)}, bf16[7,32,128]{2,1,0:T(8,128)(2,1)S(1)}, u32[]{:S(2)}, u32[]{:S(2)}) collective-permute-start(bf16[7,32,128]{2,1,0:T(8,128)(2,1)S(1)} %get-tuple-element.21), channel_id=1, source_target_pairs={{0,3},{1,2},{2,1},{3,0},{4,7},{5,6},{6,5},{7,4},{8,11},{9,10},{10,... | collective-permute-start | bytes 172040 | tf_op jit(solution)/shard_map/ppermute | solution.py:421

commit v2 on v1

--- a/solution.py
+++ b/solution.py
@@ -16,8 +16,8 @@
 EARLY = 16
 LATE = 6
 ANY = pl.BlockSpec(memory_space=pl.ANY)
-SMEM = pl.BlockSpec(memory_space=pltpu.SMEM)
 VMEM = pl.BlockSpec(memory_space=pltpu.VMEM)
+HBM = pl.BlockSpec(memory_space=pltpu.HBM)
 BF16 = jnp.bfloat16
 F32 = jnp.float32
 
@@ -30,8 +30,10 @@
     return index + flip - 2 * index * flip
 
 
-def rims_kernel(agg, prolong, row_a, row_b, col_a, col_b, sems):
+def rims_kernel(agg_hbm, prolong, row_a, row_b, col_a, col_b, bits, agg, sems):
     fx, fy = flips()
+    load = pltpu.make_async_copy(agg_hbm, agg, sems.at[16])
+    load.start()
     copies = []
     plans = (
         (row_a, ((1, 0), (1, 1))),
@@ -51,11 +53,15 @@
                     )
                 )
                 copies[-1].start()
+    load.wait()
+    own = {}
+    for k, (u, v) in enumerate(((0, 0), (0, 1), (1, 0), (1, 1))):
+        own[u, v] = lax.rem(agg[2 * turned(u, fx), 2 * turned(v, fy)], 2).astype(F32)
+        bits[k : k + 1, :] = jnp.full((1, BS), own[u, v], F32)
+    bits[4:, :] = jnp.zeros((4, BS), F32)
     for out, quads in plans:
-        for h, (u, v) in enumerate(quads):
-            ur, vr = turned(u, fx), turned(v, fy)
-            bit = lax.rem(agg[2 * ur, 2 * vr], 2).astype(F32)
-            out[h, 0:HEAD, :] = jnp.full((HEAD, BS), bit, F32).astype(BF16)
+        for h, quad in enumerate(quads):
+            out[h, 0:HEAD, :] = jnp.full((HEAD, BS), own[quad], F32).astype(BF16)
     for copy in copies:
         copy.wait()
 
@@ -64,75 +70,133 @@
     shape = jax.ShapeDtypeStruct((2, ROWS, BS), BF16)
     return pl.pallas_call(
         rims_kernel,
-        out_shape=(shape,) * 4,
-        in_specs=[SMEM, ANY],
-        out_specs=(VMEM,) * 4,
-        scratch_shapes=[pltpu.SemaphoreType.DMA((16,))],
+        out_shape=(shape,) * 4 + (jax.ShapeDtypeStruct((8, BS), F32),),
+        in_specs=[HBM, HBM],
+        out_specs=(VMEM,) * 5,
+        scratch_shapes=[pltpu.SMEM((SIDE, SIDE), jnp.int32), pltpu.SemaphoreType.DMA((17,))],
         compiler_params=pltpu.CompilerParams(vmem_limit_bytes=4 << 20),
         name="rims",
     )(agg, prolong_rows)
 
 
-def step_one_kernel(codes, coupling, prolong, out, acc):
-    quad, node = pl.program_id(0), pl.program_id(1)
+NONE = 16 * KA
+
+
+def step_one_kernel(codes_hbm, coupling, prolong_hbm, bits, out, center, blocks, prolong, codes, slot_of, sems):
     fx, fy = flips()
-    ix, iy = node // 2, node % 2
-    x, y = 2 * (quad // 2) + ix, 2 * (quad % 2) + iy
-
-    @pl.when(node == 0)
-    def _():
-        acc[...] = jnp.zeros_like(acc)
-
-    left = prolong[0, 0].T
-    for k in range(0, KA, 2):
-        pair = jnp.concatenate([coupling[0, 0, k], coupling[0, 0, k + 1]], axis=1)
-        both = jnp.dot(left, pair, preferred_element_type=F32)
-        for e in range(2):
-            code = codes[x, y, k + e]
-            off_x = lax.shift_right_logical(code * 13, 6)
-            jx = ix + off_x
-            jy = iy + code - 5 * off_x
-            du, dv = lax.shift_right_logical(jx, 1), lax.shift_right_logical(jy, 1)
-            du = du + fx * (2 - 2 * du)
-            dv = dv + fy * (2 - 2 * dv)
-            at = (du * 3 + dv) * 4 + 2 * (jx & 1) + (jy & 1)
-            acc[at] += both[:, e * BS : (e + 1) * BS]
-
-    @pl.when(node == 3)
-    def _():
-        for t in range(36):
-            out[0, t // 4, :, (t % 4) * BS : (t % 4 + 1) * BS] = acc[t].astype(BF16)
-
-
-def step_one(codes, coupling, prolong):
-    def node_at(q, i):
-        return 2 * (q // 2) + i // 2, 2 * (q % 2) + i % 2
-
+    load_codes = pltpu.make_async_copy(codes_hbm, codes, sems.at[8])
+    load_codes.start()
+    load_prolong = pltpu.make_async_copy(prolong_hbm, prolong, sems.at[9])
+    load_prolong.start()
+
+    def load(quad, m):
+        first = (2 * (quad // 2) + m) * SIDE + 2 * (quad % 2)
+        at = pl.ds(first * KA, 2 * KA)
+        return pltpu.make_async_copy(coupling.at[at], blocks.at[at], sems.at[2 * quad + m])
+
+    for quad in range(4):
+        for m in range(2):
+            load(quad, m).start()
+    blocks[NONE] = jnp.zeros((BS, BS), BF16)
+
+    @pl.loop(0, 16)
+    def _(n):
+        for t in range(25):
+            slot_of[n * 25 + t] = NONE
+
+    load_codes.wait()
+
+    @pl.loop(0, 16)
+    def _(n):
+        for k in range(KA):
+            slot_of[n * 25 + codes[n // SIDE, n % SIDE, k]] = n * KA + k
+
+    load_prolong.wait()
+    zero = jnp.zeros((BS, BS), BF16)
+
+    @pl.loop(0, 4)
+    def _(quad):
+        qx, qy = quad // 2, quad % 2
+        for m in range(2):
+            load(quad, m).wait()
+        left = []
+        for ix in range(2):
+            rows = prolong[2 * qx + ix, pl.ds(pl.multiple_of(qy * 256, 256), 256), :]
+            left.append(rows.T)
+
+        def block(ix, iy, jx, jy):
+            if not (0 <= jy - iy <= 4):
+                return zero
+            n = (2 * qx + ix) * SIDE + 2 * qy + iy
+            return blocks[slot_of[n * 25 + (jx - ix) * 5 + jy - iy]]
+
+        for jx in range(6):
+            for t in range(3):
+                total = None
+                for ix in range(2):
+                    if not (0 <= jx - ix <= 4):
+                        continue
+                    right = jnp.concatenate(
+                        [
+                            jnp.concatenate([block(ix, iy, jx, 2 * t + e) for e in range(2)], axis=1)
+                            for iy in range(2)
+                        ],
+                        axis=0,
+                    )
+                    part = jnp.dot(left[ix], right, preferred_element_type=F32)
+                    total = part if total is None else total + part
+                du, dv = jx // 2, t
+                at = (du + fx * (2 - 2 * du)) * 3 + dv + fy * (2 - 2 * dv)
+                out[quad, at, :, (jx % 2) * 256 : (jx % 2 + 1) * 256] = total.astype(BF16)
+
+    own = [(1, 1), (1, 2), (2, 1), (2, 2)]
+    far = []
+    for u, v in own:
+        ur, vr = turned(u - 1, fx), turned(v - 1, fy)
+        at = pl.ds(pl.multiple_of(vr * 256, 256), 256)
+        far.append(jnp.concatenate([prolong[2 * ur, at, :], prolong[2 * ur + 1, at, :]], axis=0))
+    for i, p in enumerate(own):
+        raw = 2 * turned(p[0] - 1, fx) + turned(p[1] - 1, fy)
+        by_b = [None, None]
+        for j, q in enumerate(own):
+            near = out[raw, (q[0] - p[0] + 1) * 3 + q[1] - p[1] + 1]
+            value = jnp.dot(near, far[j], preferred_element_type=F32)
+            high = bits[j : j + 1, :] * value
+            low = value - high
+            by_b = [low if j == 0 else by_b[0] + low, high if j == 0 else by_b[1] + high]
+        for b in range(2):
+            high = bits[i : i + 1, :] * by_b[b]
+            low = by_b[b] - high
+            if i == 0:
+                center[b] = low
+                center[2 + b] = high
+            else:
+                center[b] += low
+                center[2 + b] += high
+
+
+def step_one(codes, coupling, prolong_rows, bits):
     return pl.pallas_call(
         step_one_kernel,
-        grid=(4, 4),
-        out_shape=jax.ShapeDtypeStruct((4, 9, BS, QUAD), BF16),
-        in_specs=[
-            SMEM,
-            pl.BlockSpec((1, 1, KA, BS, BS), lambda q, i: (*node_at(q, i), 0, 0, 0)),
-            pl.BlockSpec((1, 1, BS, BS), lambda q, i: (*node_at(q, i), 0, 0)),
+        out_shape=(
+            jax.ShapeDtypeStruct((4, 9, BS, QUAD), BF16),
+            jax.ShapeDtypeStruct((4, BS, BS), F32),
+        ),
+        in_specs=[HBM, HBM, HBM, VMEM],
+        out_specs=(VMEM, VMEM),
+        scratch_shapes=[
+            pltpu.VMEM((NONE + 1, BS, BS), BF16),
+            pltpu.VMEM((SIDE, SIDE * BS, BS), BF16),
+            pltpu.SMEM((SIDE, SIDE, KA), jnp.int32),
+            pltpu.SMEM((400,), jnp.int32),
+            pltpu.SemaphoreType.DMA((10,)),
         ],
-        out_specs=pl.BlockSpec((1, 9, BS, QUAD), lambda q, i: (q, 0, 0, 0)),
-        scratch_shapes=[pltpu.VMEM((36, BS, BS), F32)],
         compiler_params=pltpu.CompilerParams(vmem_limit_bytes=16 << 20),
         cost_estimate=pl.CostEstimate(
             flops=2 * 192 * BS**3, bytes_accessed=2 * 192 * BS * BS, transcendentals=0
         ),
         name="step_one",
-    )(codes, coupling, prolong)
-
-
-def own_bits(agg, fx, fy):
-    return {
-        (u + 1, v + 1): lax.rem(agg[2 * turned(u, fx), 2 * turned(v, fy)], 2).astype(F32)
-        for u in range(2)
-        for v in range(2)
-    }
+    )(codes, coupling, prolong_rows, bits)
 
 
 def edge_slots(terms, halves, same_a):
@@ -157,11 +221,13 @@
             out[count + t] = head[t * rows : (t + 1) * rows, :].astype(BF16)
 
 
-def early_kernel(agg, r, prolong, row_a, col_a, col_b, corner_aa, corner_ab, *rest):
+OWN = ((1, 1), (1, 2), (2, 1), (2, 2))
+
+
+def early_kernel(bits, r, center, row_a, col_a, col_b, corner_aa, corner_ab, *rest):
     outs, (slots, head) = rest[:-2], rest[-2:]
     fx, fy = flips()
-    bits = own_bits(agg, fx, fy)
-    split_x = 1.0 - jnp.abs(bits[1, 1] - bits[1, 2])
+    split_x = 1.0 - jnp.abs(bits[0:1, :] - bits[1:2, :])
 
     def far(q):
         u, v = q
@@ -169,89 +235,56 @@
             return {0: corner_ab.at[0], 3: corner_aa.at[0]}.get(v, row_a.at[v - 1])
         return (col_a if v == 3 else col_b).at[u - 1]
 
-    def blocks(q):
-        u, v = q
-        if 1 <= u <= 2 and 1 <= v <= 2:
-            ur, vr = turned(u - 1, fx), turned(v - 1, fy)
-            at = pl.ds(pl.multiple_of(vr * 256, 256), 256)
-            return jnp.concatenate([prolong[2 * ur, at, :], prolong[2 * ur + 1, at, :]], axis=0)
-        return far(q)[HEAD:, :]
-
     def term(p, q):
         raw = 2 * turned(p[0] - 1, fx) + turned(p[1] - 1, fy)
         near = r[raw, (q[0] - p[0] + 1) * 3 + q[1] - p[1] + 1]
-        return jnp.dot(near, blocks(q), preferred_element_type=F32)
+        return jnp.dot(near, far(q)[HEAD:, :], preferred_element_type=F32)
 
     def half(q):
         return far(q)[0:1, :].astype(F32)
 
-    own = [(1, 1), (1, 2), (2, 1), (2, 2)]
-    for i, p in enumerate(own):
-        for j, q in enumerate(own):
-            value = term(p, q)
-            for a in range(2):
-                for b in range(2):
-                    ia = bits[p] if a else 1.0 - bits[p]
-                    ib = bits[q] if b else 1.0 - bits[q]
-                    part = (ia * ib) * value
-                    if i + j == 0:
-                        slots[2 * a + b] = part
-                    else:
-                        slots[2 * a + b] += part
-
+    for t in range(4):
+        slots[t] = center[t]
     rows_a = [(2, 1), (2, 2)], [(3, 1), (3, 2)], split_x
     cols_a = [(1, 2), (2, 2)], [(1, 3), (2, 3)], 1.0 - split_x
     cols_b = [(1, 1), (2, 1)], [(1, 0), (2, 0)], 1.0 - split_x
-    extras = []
     for e, (ps, qs, same_a) in enumerate((rows_a, cols_a, cols_b)):
         terms = [[term(p, q) for q in qs] for p in ps]
         base, extra = edge_slots(terms, [half(q) for q in qs], same_a)
         for v in range(2):
             slots[4 + 2 * e + v] = base[v]
-            if e == 0:
-                slots[12 + v] = extra[v]
-                extras.append(extra[v])
-            elif e == 1:
+            if e == 1:
                 slots[12 + v] += extra[v]
             else:
-                slots[14 + v] = extra[v]
+                slots[12 + e + v] = extra[v]
     slots[10] = term((2, 2), (3, 3))
     slots[11] = term((2, 1), (3, 0))
-    for k, p in enumerate(own):
-        head[k : k + 1, :] = jnp.full((1, BS), bits[p], F32)
+    head[0:8, :] = bits[...]
     for k, q in enumerate(((3, 1), (3, 2), (1, 3), (2, 3), (1, 0), (2, 0), (3, 3), (3, 0))):
         head[4 + k : 5 + k, :] = half(q)
     head[12:, :] = jnp.zeros((head.shape[0] - 12, BS), F32)
     store_pieces(slots, head, outs, EARLY)
 
 
-def late_kernel(agg, r, row_b, corner_ba, corner_bb, *rest):
-    outs, (slots, head, near, sems) = rest[:-4], rest[-4:]
+def late_kernel(bits, r, row_b, corner_ba, corner_bb, *rest):
+    outs, (slots, head) = rest[:-2], rest[-2:]
     fx, fy = flips()
-    copies = []
-    for v in range(2):
-        raw = 2 * fx + turned(v, fy)
-        copies.append(pltpu.make_async_copy(r.at[raw, 0:3], near.at[v], sems.at[v]))
-        copies[-1].start()
-    bits = own_bits(agg, fx, fy)
-    split_x = 1.0 - jnp.abs(bits[1, 1] - bits[1, 2])
+    split_x = 1.0 - jnp.abs(bits[0:1, :] - bits[1:2, :])
 
     def far(v):
         return {0: corner_bb.at[0], 3: corner_ba.at[0]}.get(v, row_b.at[v - 1])
 
     def term(p, v):
-        return jnp.dot(near[p - 1, v - p + 1], far(v)[HEAD:, :], preferred_element_type=F32)
+        near = r[2 * fx + turned(p - 1, fy), v - p + 1]
+        return jnp.dot(near, far(v)[HEAD:, :], preferred_element_type=F32)
 
     def half(v):
         return far(v)[0:1, :].astype(F32)
 
-    for k, p in enumerate([(1, 1), (1, 2), (2, 1), (2, 2)]):
-        head[k : k + 1, :] = jnp.full((1, BS), bits[p], F32)
+    head[0:8, :] = bits[...]
     for k, v in enumerate((1, 2, 3, 0)):
         head[4 + k : 5 + k, :] = half(v)
     head[8:, :] = jnp.zeros((head.shape[0] - 8, BS), F32)
-    for copy in copies:
-        copy.wait()
     terms = [[term(p, v) for v in (1, 2)] for p in (1, 2)]
     base, extra = edge_slots(terms, [half(1), half(2)], split_x)
     for v in range(2):
@@ -262,20 +295,19 @@
     store_pieces(slots, head, outs, LATE)
 
 
-def pieces(kernel, operands, specs, count, parts, extra_scratch, cost, name):
+def pieces(kernel, operands, count, parts, cost, name):
     rows = BS // parts
     heads = -(-HEAD // rows)
     shape = jax.ShapeDtypeStruct((count + heads, rows, BS), BF16)
     return pl.pallas_call(
         kernel,
         out_shape=(shape,) * parts,
-        in_specs=specs,
+        in_specs=[VMEM] * len(operands),
         out_specs=(VMEM,) * parts,
         scratch_shapes=[
             pltpu.VMEM((count, BS, BS), F32),
             pltpu.VMEM((heads * rows, BS), F32),
-        ]
-        + extra_scratch,
+        ],
         compiler_params=pltpu.CompilerParams(vmem_limit_bytes=24 << 20),
         cost_estimate=pl.CostEstimate(flops=cost, bytes_accessed=1 << 20, transcendentals=0),
         name=name,
@@ -424,34 +456,33 @@
 
 def local(coupling, neighbours, prolong, aggregate):
     parts = lax.axis_size("col")
-    prolong_rows = prolong.reshape(SIDE, SIDE * BS, BS)
-    to_row_a, to_row_b, to_col_a, to_col_b = rims(aggregate, prolong_rows)
+    coupling = pltpu.with_memory_space_constraint(coupling.reshape(-1, BS, BS), pltpu.HBM)
+    neighbours = pltpu.with_memory_space_constraint(neighbours, pltpu.HBM)
+    aggregate = pltpu.with_memory_space_constraint(aggregate, pltpu.HBM)
+    prolong_rows = pltpu.with_memory_space_constraint(prolong.reshape(SIDE, SIDE * BS, BS), pltpu.HBM)
+    to_row_a, to_row_b, to_col_a, to_col_b, bits = rims(aggregate, prolong_rows)
     row_a = swap(to_row_a, "row", 0)
     col_a = swap(to_col_a, "col", 0)
     col_b = swap(to_col_b, "col", 1)
     row_b = swap(to_row_b, "row", 1)
-    r = step_one(neighbours, coupling, prolong)
+    r, center = step_one(neighbours, coupling, prolong_rows, bits)
     corner_aa = swap(row_a[1:2], "col", 0)
     corner_ab = swap(row_a[0:1], "col", 1)
     corner_ba = swap(row_b[1:2], "col", 0)
     corner_bb = swap(row_b[0:1], "col", 1)
     early = pieces(
         early_kernel,
-        (aggregate, r, prolong_rows, row_a, col_a, col_b, corner_aa, corner_ab),
-        [SMEM] + [VMEM] * 7,
+        (bits, r, center, row_a, col_a, col_b, corner_aa, corner_ab),
         EARLY,
         parts,
-        [],
-        2 * 30 * BS * BS * QUAD,
+        2 * 14 * BS * BS * QUAD,
         "early_terms",
     )
     late = pieces(
         late_kernel,
-        (aggregate, r, row_b, corner_ba, corner_bb),
-        [SMEM, ANY] + [VMEM] * 3,
+        (bits, r, row_b, corner_ba, corner_bb),
         LATE,
         parts,
-        [pltpu.VMEM((2, 3, BS, QUAD), BF16), pltpu.SemaphoreType.DMA((2,))],
         2 * 6 * BS * BS * QUAD,
         "late_terms",
     )

time: 45.5 us -> 35.3 us (0.78)
  local copies, waits for them, and re-layouts: 6.29 us -> 0.04 us
  Pallas kernels: 15.1 us -> 9.64 us
  waiting for transfers between devices: 4.7 us -> 5.69 us
  starting transfers between devices: 18.9 us -> 19.5 us
    unnamed x14 -> x0, local copies, waits for them, and re-layouts: 6.25 us -> none
    pallas_call x4, Pallas kernels: 13.2 us -> 7.72 us  [the longest x1 5.27 us: step_one(): pl.pallas_call(step_one_kernel, out_shape=(jax.ShapeDtypeStruct((4, 9, BS...]
    ppermute x6, waiting for transfers between devices: 4.07 us -> 4.83 us  [scatter_rows(): lax.ppermute(outs[s], 'col', [(i, i ^ s) for i in range(count)])]
    ppermute x8, starting transfers between devices: 14.5 us -> 15.1 us  [swap(): lax.ppermute(value, axis, [(i, i + 1) for i in first] + [(i + 1, i) for i...]
  transfers between devices with their start and end apart: 14 -> 14, of which waited for: 3 -> 4; matrix products, arithmetic and copies ran while one was open for 0% -> 0% of each run, Pallas kernels for 27% -> 21%
where the time goes in v2:
time: 35.3 us; the launch traced here: 35.1 us
  starting transfers between devices  19.5 us (55%)
  Pallas kernels  9.64 us (27%)
  waiting for transfers between devices  5.69 us (16%)
    ppermute x8, starting transfers between devices, swap(): lax.ppermute(value, axis, [(i, i + 1) for i in first] + [(i + 1, i) for i...  15.1 us
    pallas_call x1, Pallas kernels, step_one(): pl.pallas_call(step_one_kernel, out_shape=(jax.ShapeDtypeStruct((4, 9, BS...  5.27 us
    ppermute x6, waiting for transfers between devices, scatter_rows(): lax.ppermute(outs[s], 'col', [(i, i ^ s) for i in range(count)])  4.83 us
    ppermute x6, starting transfers between devices, scatter_rows(): lax.ppermute(outs[s], 'col', [(i, i ^ s) for i in range(count)])  4.4 us
    pallas_call x1, Pallas kernels, rims(): pl.pallas_call(rims_kernel, out_shape=(shape,) * 4 + (jax.ShapeDtypeStruc...  1.38 us
    pallas_call x1, Pallas kernels, unpack_early(): pl.pallas_call(functools.partial(early_unpack_kernel, parts), out_shape=j...  1.08 us
    pallas_call x2, Pallas kernels, pieces(): pl.pallas_call(kernel, out_shape=(shape,) * parts, in_specs=[VMEM] * len(...  1.08 us
    ppermute x8, waiting for transfers between devices, swap(): lax.ppermute(value, axis, [(i, i + 1) for i in first] + [(i + 1, i) for i...  0.86 us
  transfers between devices with their start and end apart: 14, of which 4 were waited for; matrix products, arithmetic and copies ran while one was open for 0% of the time, Pallas kernels for 21%

profile of v2, /device:TPU:5, one launch (start us, length us, event | category | flops | bytes accessed | tf_op | source)
XLA Modules:
  0.0 35.1 jit_solution(14342324260501570175)
XLA Ops:
  0.0 1.4 %rims.1 = (bf16[2,528,128]{2,1,0:T(8,128)(2,1)S(1)}, bf16[2,528,128]{2,1,0:T(8,128)(2,1)S(1)}, bf16[2,528,128]{2,1,0:T(8,128)(2,1)S(1)}, bf16[2,528,128]{2,1,0:T(8,128)(2,1)S(1)}, f32[8,128]{1,0:T(8,128)S(1)}) custom-call(s32[4,4]{1,0:T(4,128)} %agg_hbm.1, bf16[4,512,128]{2,1,0:T(8,128)(2,1)} %bitcast.4), custom_call_target="tpu_custom_call" | custom-call | tf_op jit(solution)/shard_map/rims/pallas_call | solution.py:71
  1.4 0.1 collective-permute-start.6
  1.5 4.4 %collective-permute-start = (bf16[2,528,128]{2,1,0:T(8,128)(2,1)S(1)}, bf16[2,528,128]{2,1,0:T(8,128)(2,1)S(1)}, u32[]{:S(2)}, u32[]{:S(2)}) collective-permute-start(bf16[2,528,128]{2,1,0:T(8,128)(2,1)S(1)} %get-tuple-element.22), channel_id=1, source_target_pairs={{4,8},{12,16},{20,24},{8,4},{16,12},{24,20},{5,9},{13,17},{21,25},... | collective-permute-start | bytes 811016 | tf_op jit(solution)/shard_map/ppermute | solution.py:447
  5.8 1.3 %collective-permute-start.7 = (bf16[2,528,128]{2,1,0:T(8,128)(2,1)S(1)}, bf16[2,528,128]{2,1,0:T(8,128)(2,1)S(1)}, u32[]{:S(2)}, u32[]{:S(2)}) collective-permute-start(bf16[2,528,128]{2,1,0:T(8,128)(2,1)S(1)} %get-tuple-element.29), channel_id=1, source_target_pairs={{0,1},{2,3},{1,0},{3,2},{4,5},{6,7},{5,4},{7,6},{8,9},{10,11},{9,8... | collective-permute-start | bytes 811016 | tf_op jit(solution)/shard_map/ppermute | solution.py:447
  7.1 3.0 %collective-permute-start.8 = (bf16[2,528,128]{2,1,0:T(8,128)(2,1)S(1)}, bf16[2,528,128]{2,1,0:T(8,128)(2,1)S(1)}, u32[]{:S(2)}, u32[]{:S(2)}) collective-permute-start(bf16[2,528,128]{2,1,0:T(8,128)(2,1)S(1)} %get-tuple-element.30), channel_id=1, source_target_pairs={{1,2},{2,1},{5,6},{6,5},{9,10},{10,9},{13,14},{14,13},{17,18},{18,... | collective-permute-start | bytes 811016 | tf_op jit(solution)/shard_map/ppermute | solution.py:447
  10.2 5.3 %step_one.1 = (bf16[4,9,128,512]{3,2,1,0:T(8,128)(2,1)S(1)}, f32[4,128,128]{2,1,0:T(8,128)S(1)}) custom-call(s32[4,4,12]{2,1,0:T(4,128)} %codes_hbm.1, bf16[192,128,128]{2,1,0:T(8,128)(2,1)} %bitcast.3, bf16[4,512,128]{2,1,0:T(8,128)(2,1)} %bitcast.5, f32[8,128]{1,0:T(8,128)S(1)} %get-tuple-element.20.bits), custom_call_target="tpu_custom_call" | custom-call | flops 805306368 | bytes 6291456 | tf_op jit(solution)/shard_map/step_one/pallas_call | solution.py:179
  15.4 0.0 collective-permute-done.6.row_a
  15.5 0.8 %collective-permute-start.9 = (bf16[1,528,128]{2,1,0:T(8,128)(2,1)S(1)}, bf16[1,528,128]{2,1,0:T(8,128)(2,1)S(1)}, u32[]{:S(2)}, u32[]{:S(2)}) collective-permute-start(bf16[1,528,128]{2,1,0:T(8,128)(2,1)S(1)} %get-tuple-element.36), channel_id=1, source_target_pairs={{0,1},{2,3},{1,0},{3,2},{4,5},{6,7},{5,4},{7,6},{8,9},{10,11},{9,8... | collective-permute-start | bytes 405512 | tf_op jit(solution)/shard_map/ppermute | solution.py:447
  16.2 3.0 %collective-permute-start.10 = (bf16[1,528,128]{2,1,0:T(8,128)(2,1)S(1)}, bf16[1,528,128]{2,1,0:T(8,128)(2,1)S(1)}, u32[]{:S(2)}, u32[]{:S(2)}) collective-permute-start(bf16[1,528,128]{2,1,0:T(8,128)(2,1)S(1)} %get-tuple-element.35), channel_id=1, source_target_pairs={{1,2},{2,1},{5,6},{6,5},{9,10},{10,9},{13,14},{14,13},{17,18},{18,... | collective-permute-start | bytes 405512 | tf_op jit(solution)/shard_map/ppermute | solution.py:447
  19.3 0.0 collective-permute-done.row_b
  19.3 0.1 collective-permute-start.1
  19.4 0.0 collective-permute-done.7.col_a
  19.4 2.5 %collective-permute-start.2 = (bf16[1,528,128]{2,1,0:T(8,128)(2,1)S(1)}, bf16[1,528,128]{2,1,0:T(8,128)(2,1)S(1)}, u32[]{:S(2)}, u32[]{:S(2)}) collective-permute-start(bf16[1,528,128]{2,1,0:T(8,128)(2,1)S(1)} %get-tuple-element.37), channel_id=1, source_target_pairs={{1,2},{2,1},{5,6},{6,5},{9,10},{10,9},{13,14},{14,13},{17,18},{18,... | collective-permute-start | bytes 405512 | tf_op jit(solution)/shard_map/ppermute | solution.py:447
  21.9 0.0 collective-permute-done.8.col_b
  21.9 0.0 collective-permute-done.9.corner_aa
  21.9 0.6 %collective-permute-done.10.corner_ab = bf16[1,528,128]{2,1,0:T(8,128)(2,1)S(1)} collective-permute-done((bf16[1,528,128]{2,1,0:T(8,128)(2,1)S(1)}, bf16[1,528,128]{2,1,0:T(8,128)(2,1)S(1)}, u32[]{:S(2)}, u32[]{:S(2)}) %collective-permute-start.10) | collective-permute-done | bytes 135200 | tf_op jit(solution)/shard_map/ppermute | solution.py:447
  22.6 0.7 %early_terms.1 = (bf16[17,32,128]{2,1,0:T(8,128)(2,1)S(1)}, bf16[17,32,128]{2,1,0:T(8,128)(2,1)S(1)}, bf16[17,32,128]{2,1,0:T(8,128)(2,1)S(1)}, bf16[17,32,128]{2,1,0:T(8,128)(2,1)S(1)}) custom-call(f32[8,128]{1,0:T(8,128)S(1)} %get-tuple-element.20.bits, bf16[4,9,128,512]{3,2,1,0:T(8,128)(2,1)S(1)} %get-tuple-element.21.r, ...), custom_call_target="tpu_custom_call" | custom-call | flops 234881024 | bytes 1048576 | tf_op jit(solution)/shard_map/early_terms/pallas_call | solution.py:302
  23.3 0.1 collective-permute-start.11
  23.3 1.2 %collective-permute-start.12 = (bf16[17,32,128]{2,1,0:T(8,128)(2,1)S(1)}, bf16[17,32,128]{2,1,0:T(8,128)(2,1)S(1)}, u32[]{:S(2)}, u32[]{:S(2)}) collective-permute-start(bf16[17,32,128]{2,1,0:T(8,128)(2,1)S(1)} %get-tuple-element.33), channel_id=1, source_target_pairs={{0,2},{1,3},{2,0},{3,1},{4,6},{5,7},{6,4},{7,5},{8,10},{9,11},{10,... | collective-permute-start | bytes 417800 | tf_op jit(solution)/shard_map/ppermute | solution.py:453
  24.6 0.9 %collective-permute-start.13 = (bf16[17,32,128]{2,1,0:T(8,128)(2,1)S(1)}, bf16[17,32,128]{2,1,0:T(8,128)(2,1)S(1)}, u32[]{:S(2)}, u32[]{:S(2)}) collective-permute-start(bf16[17,32,128]{2,1,0:T(8,128)(2,1)S(1)} %get-tuple-element.34), channel_id=1, source_target_pairs={{0,3},{1,2},{2,1},{3,0},{4,7},{5,6},{6,5},{7,4},{8,11},{9,10},{10,... | collective-permute-start | bytes 417800 | tf_op jit(solution)/shard_map/ppermute | solution.py:453
  25.5 0.0 collective-permute-done.1.corner_ba
  25.5 0.2 collective-permute-done.2.corner_bb
  25.7 0.4 %late_terms.1 = (bf16[7,32,128]{2,1,0:T(8,128)(2,1)S(1)}, bf16[7,32,128]{2,1,0:T(8,128)(2,1)S(1)}, bf16[7,32,128]{2,1,0:T(8,128)(2,1)S(1)}, bf16[7,32,128]{2,1,0:T(8,128)(2,1)S(1)}) custom-call(f32[8,128]{1,0:T(8,128)S(1)} %get-tuple-element.20.bits, bf16[4,9,128,512]{3,2,1,0:T(8,128)(2,1)S(1)} %get-tuple-element.21.r, ...), custom_call_target="tpu_custom_call" | custom-call | flops 100663296 | bytes 1048576 | tf_op jit(solution)/shard_map/late_terms/pallas_call | solution.py:302
  26.1 0.1 collective-permute-start.3
  26.2 0.7 %collective-permute-start.4 = (bf16[7,32,128]{2,1,0:T(8,128)(2,1)S(1)}, bf16[7,32,128]{2,1,0:T(8,128)(2,1)S(1)}, u32[]{:S(2)}, u32[]{:S(2)}) collective-permute-start(bf16[7,32,128]{2,1,0:T(8,128)(2,1)S(1)} %get-tuple-element.25), channel_id=1, source_target_pairs={{0,2},{1,3},{2,0},{3,1},{4,6},{5,7},{6,4},{7,5},{8,10},{9,11},{10,... | collective-permute-start | bytes 172040 | tf_op jit(solution)/shard_map/ppermute | solution.py:453
  26.9 0.0 collective-permute-done.11.refs_1_
  26.9 1.4 %collective-permute-start.5 = (bf16[7,32,128]{2,1,0:T(8,128)(2,1)S(1)}, bf16[7,32,128]{2,1,0:T(8,128)(2,1)S(1)}, u32[]{:S(2)}, u32[]{:S(2)}) collective-permute-start(bf16[7,32,128]{2,1,0:T(8,128)(2,1)S(1)} %get-tuple-element.26), channel_id=1, source_target_pairs={{0,3},{1,2},{2,1},{3,0},{4,7},{5,6},{6,5},{7,4},{8,11},{9,10},{10,... | collective-permute-start | bytes 172040 | tf_op jit(solution)/shard_map/ppermute | solution.py:453
  28.3 0.0 collective-permute-done.12.refs_2_
  28.3 4.6 %collective-permute-done.13.refs_3_ = bf16[17,32,128]{2,1,0:T(8,128)(2,1)S(1)} collective-permute-done((bf16[17,32,128]{2,1,0:T(8,128)(2,1)S(1)}, bf16[17,32,128]{2,1,0:T(8,128)(2,1)S(1)}, u32[]{:S(2)}, u32[]{:S(2)}) %collective-permute-start.13) | collective-permute-done | bytes 139296 | tf_op jit(solution)/shard_map/ppermute | solution.py:453
  33.0 1.1 %unpack_early.1.refs_4_ = bf16[4,2,9,2,32,128]{5,4,3,2,1,0:T(8,128)(2,1)} custom-call(bf16[17,32,128]{2,1,0:T(8,128)(2,1)S(1)} %get-tuple-element.31.refs_0_, bf16[17,32,128]{2,1,0:T(8,128)(2,1)S(1)} %collective-permute-done.11.refs_1_, bf16[17,32,128]{2,1,0:T(8,128)(2,1)S(1)} %collective-permute-done.12.refs_2_, ...), custom_call_target="tpu_custom_call" | custom-call | tf_op jit(solution)/shard_map/unpack_early/pallas_call | solution.py:412
  34.0 0.0 collective-permute-done.3.refs_1_
  34.1 0.0 collective-permute-done.4.refs_2_
  34.1 0.2 collective-permute-done.5.refs_3_
  34.2 0.8 %unpack_late.1 = bf16[4,2,9,2,32,128]{5,4,3,2,1,0:T(8,128)(2,1)} custom-call(bf16[7,32,128]{2,1,0:T(8,128)(2,1)S(1)} %get-tuple-element.23.refs_0_, bf16[7,32,128]{2,1,0:T(8,128)(2,1)S(1)} %collective-permute-done.3.refs_1_, bf16[7,32,128]{2,1,0:T(8,128)(2,1)S(1)} %collective-permute-done.4.refs_2_, ...), custom_call_target="tpu_custom_call", output_to_operand_aliasing={{}: (4, {})} | custom-call | tf_op jit(solution)/shard_map/unpack_late/pallas_call | solution.py:429
  (2 shorter events, 0.0 us)
Async XLA Ops:
  1.4 14.1 %collective-permute-start.6 = (bf16[2,528,128]{2,1,0:T(8,128)(2,1)S(1)}, bf16[2,528,128]{2,1,0:T(8,128)(2,1)S(1)}, u32[]{:S(2)}, u32[]{:S(2)}) collective-permute-start(bf16[2,528,128]{2,1,0:T(8,128)(2,1)S(1)} %get-tuple-element.28), channel_id=1, source_target_pairs={{0,4},{8,12},{16,20},{24,28},{4,0},{12,8},{20,16},{28,24},{1,5},{9... | collective-permute-start | bytes 811016 | tf_op jit(solution)/shard_map/ppermute | solution.py:447
  1.5 17.8 %collective-permute-start = (bf16[2,528,128]{2,1,0:T(8,128)(2,1)S(1)}, bf16[2,528,128]{2,1,0:T(8,128)(2,1)S(1)}, u32[]{:S(2)}, u32[]{:S(2)}) collective-permute-start(bf16[2,528,128]{2,1,0:T(8,128)(2,1)S(1)} %get-tuple-element.22), channel_id=1, source_target_pairs={{4,8},{12,16},{20,24},{8,4},{16,12},{24,20},{5,9},{13,17},{21,25},... | collective-permute-start | bytes 811016 | tf_op jit(solution)/shard_map/ppermute | solution.py:447
  5.8 13.5 %collective-permute-start.7 = (bf16[2,528,128]{2,1,0:T(8,128)(2,1)S(1)}, bf16[2,528,128]{2,1,0:T(8,128)(2,1)S(1)}, u32[]{:S(2)}, u32[]{:S(2)}) collective-permute-start(bf16[2,528,128]{2,1,0:T(8,128)(2,1)S(1)} %get-tuple-element.29), channel_id=1, source_target_pairs={{0,1},{2,3},{1,0},{3,2},{4,5},{6,7},{5,4},{7,6},{8,9},{10,11},{9,8... | collective-permute-start | bytes 811016 | tf_op jit(solution)/shard_map/ppermute | solution.py:447
  7.1 14.8 %collective-permute-start.8 = (bf16[2,528,128]{2,1,0:T(8,128)(2,1)S(1)}, bf16[2,528,128]{2,1,0:T(8,128)(2,1)S(1)}, u32[]{:S(2)}, u32[]{:S(2)}) collective-permute-start(bf16[2,528,128]{2,1,0:T(8,128)(2,1)S(1)} %get-tuple-element.30), channel_id=1, source_target_pairs={{1,2},{2,1},{5,6},{6,5},{9,10},{10,9},{13,14},{14,13},{17,18},{18,... | collective-permute-start | bytes 811016 | tf_op jit(solution)/shard_map/ppermute | solution.py:447
  15.5 6.5 %collective-permute-start.9 = (bf16[1,528,128]{2,1,0:T(8,128)(2,1)S(1)}, bf16[1,528,128]{2,1,0:T(8,128)(2,1)S(1)}, u32[]{:S(2)}, u32[]{:S(2)}) collective-permute-start(bf16[1,528,128]{2,1,0:T(8,128)(2,1)S(1)} %get-tuple-element.36), channel_id=1, source_target_pairs={{0,1},{2,3},{1,0},{3,2},{4,5},{6,7},{5,4},{7,6},{8,9},{10,11},{9,8... | collective-permute-start | bytes 405512 | tf_op jit(solution)/shard_map/ppermute | solution.py:447
  16.2 6.3 %collective-permute-start.10 = (bf16[1,528,128]{2,1,0:T(8,128)(2,1)S(1)}, bf16[1,528,128]{2,1,0:T(8,128)(2,1)S(1)}, u32[]{:S(2)}, u32[]{:S(2)}) collective-permute-start(bf16[1,528,128]{2,1,0:T(8,128)(2,1)S(1)} %get-tuple-element.35), channel_id=1, source_target_pairs={{1,2},{2,1},{5,6},{6,5},{9,10},{10,9},{13,14},{14,13},{17,18},{18,... | collective-permute-start | bytes 405512 | tf_op jit(solution)/shard_map/ppermute | solution.py:447
  19.3 6.2 %collective-permute-start.1 = (bf16[1,528,128]{2,1,0:T(8,128)(2,1)S(1)}, bf16[1,528,128]{2,1,0:T(8,128)(2,1)S(1)}, u32[]{:S(2)}, u32[]{:S(2)}) collective-permute-start(bf16[1,528,128]{2,1,0:T(8,128)(2,1)S(1)} %get-tuple-element.38), channel_id=1, source_target_pairs={{0,1},{2,3},{1,0},{3,2},{4,5},{6,7},{5,4},{7,6},{8,9},{10,11},{9,8... | collective-permute-start | bytes 405512 | tf_op jit(solution)/shard_map/ppermute | solution.py:447
  19.4 6.3 %collective-permute-start.2 = (bf16[1,528,128]{2,1,0:T(8,128)(2,1)S(1)}, bf16[1,528,128]{2,1,0:T(8,128)(2,1)S(1)}, u32[]{:S(2)}, u32[]{:S(2)}) collective-permute-start(bf16[1,528,128]{2,1,0:T(8,128)(2,1)S(1)} %get-tuple-element.37), channel_id=1, source_target_pairs={{1,2},{2,1},{5,6},{6,5},{9,10},{10,9},{13,14},{14,13},{17,18},{18,... | collective-permute-start | bytes 405512 | tf_op jit(solution)/shard_map/ppermute | solution.py:447
  23.3 3.6 %collective-permute-start.11 = (bf16[17,32,128]{2,1,0:T(8,128)(2,1)S(1)}, bf16[17,32,128]{2,1,0:T(8,128)(2,1)S(1)}, u32[]{:S(2)}, u32[]{:S(2)}) collective-permute-start(bf16[17,32,128]{2,1,0:T(8,128)(2,1)S(1)} %get-tuple-element.32), channel_id=1, source_target_pairs={{0,1},{1,0},{2,3},{3,2},{4,5},{5,4},{6,7},{7,6},{8,9},{9,8},{10,11... | collective-permute-start | bytes 417800 | tf_op jit(solution)/shard_map/ppermute | solution.py:453
  23.3 5.0 %collective-permute-start.12 = (bf16[17,32,128]{2,1,0:T(8,128)(2,1)S(1)}, bf16[17,32,128]{2,1,0:T(8,128)(2,1)S(1)}, u32[]{:S(2)}, u32[]{:S(2)}) collective-permute-start(bf16[17,32,128]{2,1,0:T(8,128)(2,1)S(1)} %get-tuple-element.33), channel_id=1, source_target_pairs={{0,2},{1,3},{2,0},{3,1},{4,6},{5,7},{6,4},{7,5},{8,10},{9,11},{10,... | collective-permute-start | bytes 417800 | tf_op jit(solution)/shard_map/ppermute | solution.py:453
  24.6 8.4 %collective-permute-start.13 = (bf16[17,32,128]{2,1,0:T(8,128)(2,1)S(1)}, bf16[17,32,128]{2,1,0:T(8,128)(2,1)S(1)}, u32[]{:S(2)}, u32[]{:S(2)}) collective-permute-start(bf16[17,32,128]{2,1,0:T(8,128)(2,1)S(1)} %get-tuple-element.34), channel_id=1, source_target_pairs={{0,3},{1,2},{2,1},{3,0},{4,7},{5,6},{6,5},{7,4},{8,11},{9,10},{10,... | collective-permute-start | bytes 417800 | tf_op jit(solution)/shard_map/ppermute | solution.py:453
  26.1 7.9 %collective-permute-start.3 = (bf16[7,32,128]{2,1,0:T(8,128)(2,1)S(1)}, bf16[7,32,128]{2,1,0:T(8,128)(2,1)S(1)}, u32[]{:S(2)}, u32[]{:S(2)}) collective-permute-start(bf16[7,32,128]{2,1,0:T(8,128)(2,1)S(1)} %get-tuple-element.24), channel_id=1, source_target_pairs={{0,1},{1,0},{2,3},{3,2},{4,5},{5,4},{6,7},{7,6},{8,9},{9,8},{10,11... | collective-permute-start | bytes 172040 | tf_op jit(solution)/shard_map/ppermute | solution.py:453
  26.2 7.9 %collective-permute-start.4 = (bf16[7,32,128]{2,1,0:T(8,128)(2,1)S(1)}, bf16[7,32,128]{2,1,0:T(8,128)(2,1)S(1)}, u32[]{:S(2)}, u32[]{:S(2)}) collective-permute-start(bf16[7,32,128]{2,1,0:T(8,128)(2,1)S(1)} %get-tuple-element.25), channel_id=1, source_target_pairs={{0,2},{1,3},{2,0},{3,1},{4,6},{5,7},{6,4},{7,5},{8,10},{9,11},{10,... | collective-permute-start | bytes 172040 | tf_op jit(solution)/shard_map/ppermute | solution.py:453
  26.9 7.3 %collective-permute-start.5 = (bf16[7,32,128]{2,1,0:T(8,128)(2,1)S(1)}, bf16[7,32,128]{2,1,0:T(8,128)(2,1)S(1)}, u32[]{:S(2)}, u32[]{:S(2)}) collective-permute-start(bf16[7,32,128]{2,1,0:T(8,128)(2,1)S(1)} %get-tuple-element.26), channel_id=1, source_target_pairs={{0,3},{1,2},{2,1},{3,0},{4,7},{5,6},{6,5},{7,4},{8,11},{9,10},{10,... | collective-permute-start | bytes 172040 | tf_op jit(solution)/shard_map/ppermute | solution.py:453

commit v3 on v2

v3 whole, which is shorter than its diff:
```python
import functools

import jax
import jax.numpy as jnp
from jax import lax
from jax.experimental import pallas as pl
from jax.experimental.pallas import tpu as pltpu
from jax.sharding import PartitionSpec as P

BS = 128
KA = 12
SIDE = 4
QUAD = 4 * BS
HEAD = 16
ROWS = HEAD + QUAD
TALL = BS + HEAD
SLOTS = 20
ANY = pl.BlockSpec(memory_space=pl.ANY)
VMEM = pl.BlockSpec(memory_space=pltpu.VMEM)
HBM = pl.BlockSpec(memory_space=pltpu.HBM)
BF16 = jnp.bfloat16
F32 = jnp.float32


def flips():
    return lax.rem(lax.axis_index("row"), 2), lax.rem(lax.axis_index("col"), 2)


def turned(index, flip):
    return index + flip - 2 * index * flip


def rims_kernel(agg_hbm, prolong, row_a, row_b, col_a, col_b, bits, agg, sems):
    fx, fy = flips()
    load = pltpu.make_async_copy(agg_hbm, agg, sems.at[16])
    load.start()
    copies = []
    plans = (
        (row_a, ((1, 0), (1, 1))),
        (row_b, ((0, 0), (0, 1))),
        (col_a, ((0, 1), (1, 1))),
        (col_b, ((0, 0), (1, 0))),
    )
    for out, quads in plans:
        for h, (u, v) in enumerate(quads):
            ur, vr = turned(u, fx), turned(v, fy)
            for m in range(2):
                copies.append(
                    pltpu.make_async_copy(
                        prolong.at[2 * ur + m, pl.ds(pl.multiple_of(vr * 256, 256), 256), :],
                        out.at[h, HEAD + 256 * m : HEAD + 256 * (m + 1), :],
                        sems.at[len(copies)],
                    )
                )
                copies[-1].start()
    load.wait()
    own = {}
    for k, (u, v) in enumerate(((0, 0), (0, 1), (1, 0), (1, 1))):
        own[u, v] = lax.rem(agg[2 * turned(u, fx), 2 * turned(v, fy)], 2).astype(F32)
        bits[k : k + 1, :] = jnp.full((1, BS), own[u, v], F32)
    bits[4:, :] = jnp.zeros((4, BS), F32)
    for out, quads in plans:
        for h, quad in enumerate(quads):
            out[h, 0:HEAD, :] = jnp.full((HEAD, BS), own[quad], F32).astype(BF16)
    for copy in copies:
        copy.wait()


def rims(agg, prolong_rows):
    shape = jax.ShapeDtypeStruct((2, ROWS, BS), BF16)
    return pl.pallas_call(
        rims_kernel,
        out_shape=(shape,) * 4 + (jax.ShapeDtypeStruct((8, BS), F32),),
        in_specs=[HBM, HBM],
        out_specs=(VMEM,) * 5,
        scratch_shapes=[pltpu.SMEM((SIDE, SIDE), jnp.int32), pltpu.SemaphoreType.DMA((17,))],
        compiler_params=pltpu.CompilerParams(vmem_limit_bytes=4 << 20),
        name="rims",
    )(agg, prolong_rows)


def sums(r, p, quads):
    fx, fy = flips()
    raw = 2 * turned(p[0] - 1, fx) + turned(p[1] - 1, fy)
    blocks = [r[raw, (u - p[0] + 1) * 3 + v - p[1] + 1] for u, v in quads]
    return blocks[0] if len(blocks) == 1 else jnp.concatenate(blocks, axis=1)


OWN = ((1, 1), (1, 2), (2, 1), (2, 2))
NONE = 16 * KA


def step_one_kernel(
    codes_hbm, coupling, prolong_hbm, bits, out, center, to_a, to_b, blocks, prolong, far, codes, slot_of, sems
):
    fx, fy = flips()
    load_codes = pltpu.make_async_copy(codes_hbm, codes, sems.at[8])
    load_codes.start()
    load_prolong = pltpu.make_async_copy(prolong_hbm, prolong, sems.at[9])
    load_prolong.start()

    def load(quad, m):
        first = (2 * (quad // 2) + m) * SIDE + 2 * (quad % 2)
        at = pl.ds(first * KA, 2 * KA)
        return pltpu.make_async_copy(coupling.at[at], blocks.at[at], sems.at[2 * quad + m])

    for quad in range(4):
        for m in range(2):
            load(quad, m).start()
    blocks[NONE] = jnp.zeros((BS, BS), BF16)

    @pl.loop(0, 16)
    def _(n):
        for t in range(25):
            slot_of[n * 25 + t] = NONE

    load_codes.wait()

    @pl.loop(0, 16)
    def _(n):
        for k in range(KA):
            slot_of[n * 25 + codes[n // SIDE, n % SIDE, k]] = n * KA + k

    load_prolong.wait()
    zero = jnp.zeros((BS, BS), BF16)

    @pl.loop(0, 4)
    def _(quad):
        qx, qy = quad // 2, quad % 2
        for m in range(2):
            load(quad, m).wait()
        left = []
        for ix in range(2):
            rows = prolong[2 * qx + ix, pl.ds(pl.multiple_of(qy * 256, 256), 256), :]
            left.append(rows.T)

        def block(ix, iy, jx, jy):
            if not (0 <= jy - iy <= 4):
                return zero
            n = (2 * qx + ix) * SIDE + 2 * qy + iy
            return blocks[slot_of[n * 25 + (jx - ix) * 5 + jy - iy]]

        for jx in range(6):
            for t in range(3):
                total = None
                for ix in range(2):
                    if not (0 <= jx - ix <= 4):
                        continue
                    right = jnp.concatenate(
                        [
                            jnp.concatenate([block(ix, iy, jx, 2 * t + e) for e in range(2)], axis=1)
                            for iy in range(2)
                        ],
                        axis=0,
                    )
                    part = jnp.dot(left[ix], right, preferred_element_type=F32)
                    total = part if total is None else total + part
                du, dv = jx // 2, t
                at = (du + fx * (2 - 2 * du)) * 3 + dv + fy * (2 - 2 * dv)
                out[quad, at, :, (jx % 2) * 256 : (jx % 2 + 1) * 256] = total.astype(BF16)

    for ref, e, j, q in ((to_b, 0, 2, (3, 0)), (to_b, 1, 0, (0, 0)), (to_a, 0, 3, (3, 3)), (to_a, 1, 1, (0, 3))):
        ref[e, 0:BS, :] = sums(out, OWN[j], (q,))
        bit = jnp.broadcast_to(bits[j : j + 1, :], (HEAD, BS)).astype(BF16)
        ref[e, BS:, :] = jnp.concatenate([bit] * 4, axis=1)
    for j, (u, v) in enumerate(OWN):
        ur, vr = turned(u - 1, fx), turned(v - 1, fy)
        at = pl.ds(pl.multiple_of(vr * 256, 256), 256)
        for m in range(2):
            rows = slice(QUAD * j + 256 * m, QUAD * j + 256 * (m + 1))
            part = prolong[2 * ur + m, at, :]
            high = part * bits[j : j + 1, :].astype(BF16)
            far[rows, 0:BS] = part - high
            far[rows, BS:] = high
    for i, p in enumerate(OWN):
        raw = 2 * turned(p[0] - 1, fx) + turned(p[1] - 1, fy)
        near = [out[raw, (q[0] - p[0] + 1) * 3 + q[1] - p[1] + 1] for q in OWN]
        value = jnp.dot(jnp.concatenate(near, axis=1), far[...], preferred_element_type=F32)
        for b in range(2):
            one = value[:, b * BS : (b + 1) * BS]
            high = bits[i : i + 1, :] * one
            low = one - high
            if i == 0:
                center[b] = low
                center[2 + b] = high
            else:
                center[b] += low
                center[2 + b] += high


def step_one(codes, coupling, prolong_rows, bits):
    return pl.pallas_call(
        step_one_kernel,
        out_shape=(
            jax.ShapeDtypeStruct((4, 9, BS, QUAD), BF16),
            jax.ShapeDtypeStruct((4, BS, BS), F32),
            jax.ShapeDtypeStruct((2, TALL, QUAD), BF16),
            jax.ShapeDtypeStruct((2, TALL, QUAD), BF16),
        ),
        in_specs=[HBM, HBM, HBM, VMEM],
        out_specs=(VMEM,) * 4,
        scratch_shapes=[
            pltpu.VMEM((NONE + 1, BS, BS), BF16),
            pltpu.VMEM((SIDE, SIDE * BS, BS), BF16),
            pltpu.VMEM((4 * QUAD, 2 * BS), BF16),
            pltpu.SMEM((SIDE, SIDE, KA), jnp.int32),
            pltpu.SMEM((400,), jnp.int32),
            pltpu.SemaphoreType.DMA((10,)),
        ],
        compiler_params=pltpu.CompilerParams(vmem_limit_bytes=16 << 20),
        cost_estimate=pl.CostEstimate(flops=1 << 33, bytes_accessed=1 << 20, transcendentals=0),
        name="step_one",
    )(codes, coupling, prolong_rows, bits)


def half_of(ref):
    return ref[0:1, :].astype(F32)


def edge_slots(near, far, same_a):
    same_b = 1.0 - jnp.abs(half_of(far[0]) - half_of(far[1]))
    second = far[1][HEAD:, :]
    shared = second * same_b.astype(BF16)
    right = jnp.concatenate(
        [
            jnp.concatenate([far[0][HEAD:, :], jnp.zeros_like(second)], axis=1),
            jnp.concatenate([shared, second - shared], axis=1),
        ],
        axis=0,
    )
    by_p = [jnp.dot(rows, right, preferred_element_type=F32) for rows in near]
    base, extra = [], []
    for v in range(2):
        one, two = (value[:, v * BS : (v + 1) * BS] for value in by_p)
        shared = same_a * two
        base.append(one + shared)
        extra.append(two - shared)
    return base, extra


def inside(axis, count):
    at = lax.axis_index(axis)
    return jnp.where(at == 0, 0.0, jnp.where(at == count - 1, 0.0, 1.0)).astype(F32)


def store_pieces(outs, at, values):
    rows = outs[0].shape[1]
    me = lax.axis_index("col")
    for s, out in enumerate(outs):
        start = pl.multiple_of((me ^ s) * rows, rows)
        for t in range(values.shape[0]):
            out[at + t] = values[t, pl.ds(start, rows), :].astype(BF16)


def store_head(outs, head):
    rows = outs[0].shape[1]
    for out in outs:
        for t in range(out.shape[0] - SLOTS):
            out[SLOTS + t] = head[t * rows : (t + 1) * rows, :].astype(BF16)


def edge_terms(r, bits, edges, same_a, slots, head):
    for e, (far, own, quads, scale) in enumerate(edges):
        base, extra = edge_slots([sums(r, p, quads) for p in own], [far.at[0], far.at[1]], same_a)
        for t in range(2):
            slots[2 * e + t] = base[t] if scale is None else base[t] * scale
            slots[4 + 2 * e + t] = extra[t] if scale is None else extra[t] * scale
            head[2 * e + t : 2 * e + t + 1, :] = half_of(far.at[t])


def near_kernel(counts, bits, r, center, col_a, col_b, *rest):
    outs, (head, slots) = rest[:-2], rest[-2:]
    split_y = jnp.abs(bits[0:1, :] - bits[1:2, :])
    edges = (
        (col_a, ((1, 2), (2, 2)), ((1, 3), (2, 3)), None),
        (col_b, ((1, 1), (2, 1)), ((1, 0), (2, 0)), inside("col", counts[1])),
    )
    head[...] = jnp.zeros_like(head)
    edge_terms(r, bits, edges, split_y, slots, head.at[8:12])
    head[0:4, :] = bits[0:4, :]
    store_pieces(outs, 0, center)
    store_pieces(outs, 8, slots.at[0:4])
    store_pieces(outs, 16, slots.at[4:8])


def far_kernel(counts, bits, r, row_a, row_b, from_a, from_b, head_in, *rest):
    parts = counts[1]
    ins, outs, (slots, head) = rest[:parts], rest[parts : 2 * parts], rest[2 * parts :]
    split_x = 1.0 - jnp.abs(bits[0:1, :] - bits[1:2, :])
    row_in, col_in = inside("row", counts[0]), inside("col", parts)
    edges = (
        (row_a, ((2, 1), (2, 2)), ((3, 1), (3, 2)), None),
        (row_b, ((1, 1), (1, 2)), ((0, 1), (0, 2)), row_in),
    )
    head[...] = head_in[...]
    edge_terms(r, bits, edges, split_x, slots, head.at[4:8])
    corners = (
        (from_a.at[0], row_a.at[1], None),
        (from_b.at[0], row_a.at[0], col_in),
        (from_a.at[1], row_b.at[1], row_in),
        (from_b.at[1], row_b.at[0], row_in * col_in),
    )
    for e, (near, far, scale) in enumerate(corners):
        value = jnp.dot(near[0:BS, :], far[HEAD:, :], preferred_element_type=F32)
        slots[8 + e] = value if scale is None else value * scale
        head[12 + e : 13 + e, :] = near[BS : BS + 1, 0:BS].astype(F32)
    store_pieces(outs, 4, slots.at[0:4])
    store_pieces(outs, 12, slots.at[8:12])
    rows = outs[0].shape[1]
    me = lax.axis_index("col")
    for s in range(parts):
        start = pl.multiple_of((me ^ s) * rows, rows)
        for t in range(4):
            part = slots[4 + t, pl.ds(start, rows), :] + ins[s][16 + t].astype(F32)
            outs[s][16 + t] = part.astype(BF16)
    store_head(outs, head)


def message_shapes(parts):
    rows = BS // parts
    heads = -(-HEAD // rows)
    return jax.ShapeDtypeStruct((SLOTS + heads, rows, BS), BF16), jax.ShapeDtypeStruct((heads * rows, BS), F32)


def near_terms(counts, *operands):
    message, head = message_shapes(counts[1])
    return pl.pallas_call(
        functools.partial(near_kernel, counts),
        out_shape=(message,) * counts[1] + (head,),
        in_specs=[VMEM] * len(operands),
        out_specs=(VMEM,) * (counts[1] + 1),
        scratch_shapes=[pltpu.VMEM((8, BS, BS), F32)],
        compiler_params=pltpu.CompilerParams(vmem_limit_bytes=16 << 20),
        cost_estimate=pl.CostEstimate(flops=1, bytes_accessed=1, transcendentals=0),
        name="near_terms",
    )(*operands)


def far_terms(counts, *operands):
    message, head = message_shapes(counts[1])
    first = len(operands) - counts[1]
    return pl.pallas_call(
        functools.partial(far_kernel, counts),
        out_shape=(message,) * counts[1],
        in_specs=[VMEM] * len(operands),
        out_specs=(VMEM,) * counts[1],
        scratch_shapes=[pltpu.VMEM((12, BS, BS), F32), pltpu.VMEM(head.shape, F32)],
        input_output_aliases={first + s: s for s in range(counts[1])},
        compiler_params=pltpu.CompilerParams(vmem_limit_bytes=16 << 20),
        cost_estimate=pl.CostEstimate(flops=1, bytes_accessed=1, transcendentals=0),
        name="far_terms",
    )(*operands)


def unpack_kernel(parts, steps, fresh, *refs):
    ins = refs[: len(steps)]
    out, buf, sems = refs[-3:]
    me = lax.axis_index("col")
    fx, _ = flips()
    copies = []
    for i, (s, ref) in enumerate(zip(steps, ins)):
        square = me ^ s
        fy = lax.rem(square, 2)
        one = functools.partial(bit_row, ref)
        split_y = jnp.abs(one(0) - one(1))
        split_x = 1.0 - split_y

        def send(places):
            for piece, (owner, code) in places:
                for a in range(2):
                    copies.append(
                        pltpu.make_async_copy(
                            buf.at[i, piece, a], out.at[owner, a, code], sems.at[len(copies)]
                        )
                    )
                    copies[-1].start()

        spread(buf, (i, 0), [ref[t].astype(F32) for t in range(4)])
        send([(0, (square, 4))])
        edges = (
            ((2, 3), split_y, 7 - 6 * fx),
            ((0, 1), split_y, 1 + 6 * fx),
            ((1, 3), split_x, 3 + turn3(2, fy)),
            ((0, 2), split_x, 3 + turn3(0, fy)),
        )
        for e, (ps, used, code) in enumerate(edges):
            at = 2 * e % 4
            spread_edge(
                buf, (i, 1 + e), ref, one, ps, (4 + 2 * e, 5 + 2 * e), (4 + 2 * e, 5 + 2 * e), (16 + at, 17 + at), used
            )
            send([(1 + e, (square, code))])
        high = square ^ 1
        low = square + 2 * fy - 1
        low = jnp.where((low < 0) | (low >= parts), square, low)
        for e, (owner, group, side, b_bit) in enumerate(
            ((high, 6 - 6 * fx, 2, 5), (low, 6 - 6 * fx, 0, 4), (high, 6 * fx, 2, 7), (low, 6 * fx, 0, 6))
        ):
            spread_corner(buf, (i, 5 + e), ref[12 + e].astype(F32), one(12 + e), one(b_bit))
            send([(5 + e, (owner, group + turn3(side, lax.rem(owner, 2))))])
    for copy in copies:
        copy.wait()


def unpack(messages, steps, coarse):
    parts = lax.axis_size("col")
    rows = messages[0].shape[1]
    fresh = coarse is None
    return pl.pallas_call(
        functools.partial(unpack_kernel, parts, steps, fresh),
        out_shape=jax.ShapeDtypeStruct((parts, 2, 9, 2, rows, BS), BF16),
        in_specs=[VMEM] * len(steps) + [ANY] * (not fresh),
        out_specs=ANY,
        scratch_shapes=[
            pltpu.VMEM((len(steps), 9, 2, 2, rows, BS), BF16),
            pltpu.SemaphoreType.DMA((18 * len(steps),)),
        ],
        input_output_aliases={} if fresh else {len(steps): 0},
        compiler_params=pltpu.CompilerParams(vmem_limit_bytes=16 << 20),
        cost_estimate=pl.CostEstimate(flops=1, bytes_accessed=1, transcendentals=0),
        name="unpack",
    )(*messages, *(() if fresh else (coarse,)))


def turn3(index, flip):
    return index + flip * (2 - 2 * index)


def bit_row(ref, k):
    rows = ref.shape[1]
    return ref[SLOTS + k // rows, k % rows : k % rows + 1, :].astype(F32)


def spread(buf, at, center):
    i, piece = at
    for a in range(2):
        for b in range(2):
            buf[i, piece, a, b] = center[2 * a + b].astype(BF16)


def spread_edge(buf, at, ref, one, ps, qs, base, extra, used):
    a_bits = [one(p) for p in ps]
    b_bits = [one(q) for q in qs]
    values = [ref[t].astype(F32) for t in base]
    more = [ref[t].astype(F32) for t in extra]
    center = [None] * 4
    for b in range(2):
        picks = [bit if b else 1.0 - bit for bit in b_bits]
        first = picks[0] * values[0] + picks[1] * values[1]
        second = (used * picks[0]) * more[0] + (used * picks[1]) * more[1]
        for a in range(2):
            ia = [bit if a else 1.0 - bit for bit in a_bits]
            center[2 * a + b] = ia[0] * first + ia[1] * second
    spread(buf, at, center)


def spread_corner(buf, at, value, a_bit, b_bit):
    center = []
    for a in range(2):
        for b in range(2):
            center.append(((a_bit if a else 1.0 - a_bit) * (b_bit if b else 1.0 - b_bit)) * value)
    spread(buf, at, center)


def gate_kernel(first, second, after, first_out, second_out):
    pass


def gate(first, second, after):
    return pl.pallas_call(
        gate_kernel,
        out_shape=tuple(jax.ShapeDtypeStruct(v.shape, v.dtype) for v in (first, second)),
        in_specs=[ANY, ANY, ANY],
        out_specs=(ANY, ANY),
        input_output_aliases={0: 0, 1: 1},
        compiler_params=pltpu.CompilerParams(vmem_limit_bytes=1 << 20),
        cost_estimate=pl.CostEstimate(flops=1 << 33, bytes_accessed=1, transcendentals=0),
        name="gate",
    )(first, second, after)


def other_side(index):
    return index + 1 if index % 2 else index - 1


def row_low(r, c, rows, cols):
    far = other_side(r)
    return (far, c) if 0 <= far < rows else (r, c ^ 1)


def col_low(r, c, rows, cols):
    far = other_side(c)
    return (r, far) if 0 <= far < cols else (r ^ 2, c)


def row_high(r, c, rows, cols):
    return r ^ 1, c


def col_high(r, c, rows, cols):
    return r, c ^ 1


def swap(value, partner):
    rows, cols = lax.axis_size("row"), lax.axis_size("col")
    pairs = []
    for r in range(rows):
        for c in range(cols):
            to_r, to_c = partner(r, c, rows, cols)
            pairs.append((r * cols + c, to_r * cols + to_c))
    return lax.ppermute(value, ("row", "col"), pairs)


def scatter_rows(outs):
    count = len(outs)
    return [outs[0]] + [
        lax.ppermute(outs[s], "col", [(i, i ^ s) for i in range(count)]) for s in range(1, count)
    ]


def local(coupling, neighbours, prolong, aggregate):
    parts = lax.axis_size("col")
    counts = (lax.axis_size("row"), parts)
    coupling = pltpu.with_memory_space_constraint(coupling.reshape(-1, BS, BS), pltpu.HBM)
    neighbours = pltpu.with_memory_space_constraint(neighbours, pltpu.HBM)
    aggregate = pltpu.with_memory_space_constraint(aggregate, pltpu.HBM)
    prolong_rows = pltpu.with_memory_space_constraint(prolong.reshape(SIDE, SIDE * BS, BS), pltpu.HBM)
    to_row_a, to_row_b, to_col_a, to_col_b, bits = rims(aggregate, prolong_rows)
    row_a = swap(to_row_a, row_high)
    row_b = swap(to_row_b, row_low)
    col_a = swap(to_col_a, col_high)
    col_b = swap(to_col_b, col_low)
    r, center, to_a, to_b = step_one(neighbours, coupling, prolong_rows, bits)
    from_b = swap(to_b, col_low)
    from_a = swap(to_a, col_high)
    *outs, head = near_terms(counts, bits, r, center, col_a, col_b)
    row_a, row_b = gate(row_a, row_b, head)
    outs = far_terms(counts, bits, r, row_a, row_b, from_a, from_b, head, *outs)
    outs = scatter_rows(outs)
    coarse = None
    for first, last in ((0, 2), (2, parts - 1), (parts - 1, parts)):
        coarse = unpack(outs[first:last], range(first, last), coarse)
    return coarse[None]


def solution(mesh):
    return jax.shard_map(
        local,
        mesh=mesh,
        in_specs=(
            P("row", "col", None, None, None),
            P("row", "col", None),
            P("row", "col", None, None),
            P("row", "col"),
        ),
        out_specs=P("row", None, None, None, None, "col", None),
        check_vma=False,
    )
```

time: 35.3 us -> 30.6 us (0.87)
  starting transfers between devices: 19.5 us -> 9 us
  waiting for transfers between devices: 5.69 us -> 10.5 us
  Pallas kernels: 9.64 us -> 10.8 us
    ppermute x8 -> x6, starting transfers between devices: 15.1 us -> 6.76 us  [swap(): return lax.ppermute(value, ('row', 'col'), pairs)]
    ppermute x8 -> x6, waiting for transfers between devices: 0.86 us -> 4.57 us  [swap(): return lax.ppermute(value, ('row', 'col'), pairs)]
    ppermute x6 -> x3, starting transfers between devices: 4.4 us -> 2.24 us  [scatter_rows(): lax.ppermute(outs[s], 'col', [(i, i ^ s) for i in range(count)])]
    pallas_call x4 -> x6, Pallas kernels: 2.99 us -> 4.11 us  [the longest x3 2.96 us: unpack(): pl.pallas_call(functools.partial(unpack_kernel, parts, steps, fresh), out...]
    ppermute x6 -> x3, waiting for transfers between devices: 4.83 us -> 5.93 us  [scatter_rows(): lax.ppermute(outs[s], 'col', [(i, i ^ s) for i in range(count)])]
  transfers between devices with their start and end apart: 14 -> 9, of which waited for: 4 -> 4; matrix products, arithmetic and copies ran while one was open for 0% -> 0% of each run, Pallas kernels for 21% -> 26%
where the time goes in v3:
time: 30.6 us; the launch traced here: 30.3 us
  Pallas kernels  10.8 us (35%)
  waiting for transfers between devices  10.5 us (34%)
  starting transfers between devices  9 us (29%)
    ppermute x6, starting transfers between devices, swap(): return lax.ppermute(value, ('row', 'col'), pairs)  6.76 us
    ppermute x3, waiting for transfers between devices, scatter_rows(): lax.ppermute(outs[s], 'col', [(i, i ^ s) for i in range(count)])  5.93 us
    pallas_call x1, Pallas kernels, step_one(): pl.pallas_call(step_one_kernel, out_shape=(jax.ShapeDtypeStruct((4, 9, BS...  5.29 us
    ppermute x6, waiting for transfers between devices, swap(): return lax.ppermute(value, ('row', 'col'), pairs)  4.57 us
    pallas_call x3, Pallas kernels, unpack(): pl.pallas_call(functools.partial(unpack_kernel, parts, steps, fresh), out...  2.96 us
    ppermute x3, starting transfers between devices, scatter_rows(): lax.ppermute(outs[s], 'col', [(i, i ^ s) for i in range(count)])  2.24 us
    pallas_call x1, Pallas kernels, rims(): pl.pallas_call(rims_kernel, out_shape=(shape,) * 4 + (jax.ShapeDtypeStruc...  1.38 us
    pallas_call x1, Pallas kernels, far_terms(): pl.pallas_call(functools.partial(far_kernel, counts), out_shape=(message,...  0.65 us
  transfers between devices with their start and end apart: 9, of which 4 were waited for; matrix products, arithmetic and copies ran while one was open for 0% of the time, Pallas kernels for 26%

profile of v3, /device:TPU:5, one launch (start us, length us, event | category | flops | bytes accessed | tf_op | source)
XLA Modules:
  0.0 30.3 jit_solution(12565734044040134775)
XLA Ops:
  0.0 1.4 %rims.1 = (bf16[2,528,128]{2,1,0:T(8,128)(2,1)S(1)}, bf16[2,528,128]{2,1,0:T(8,128)(2,1)S(1)}, bf16[2,528,128]{2,1,0:T(8,128)(2,1)S(1)}, bf16[2,528,128]{2,1,0:T(8,128)(2,1)S(1)}, f32[8,128]{1,0:T(8,128)S(1)}) custom-call(s32[4,4]{1,0:T(4,128)} %agg_hbm.1, bf16[4,512,128]{2,1,0:T(8,128)(2,1)} %bitcast.3), custom_call_target="tpu_custom_call" | custom-call | tf_op jit(solution)/shard_map/rims/pallas_call | solution.py:71
  1.4 0.1 collective-permute-start
  1.5 2.5 %collective-permute-start.1 = (bf16[2,528,128]{2,1,0:T(8,128)(2,1)S(1)}, bf16[2,528,128]{2,1,0:T(8,128)(2,1)S(1)}, u32[]{:S(2)}, u32[]{:S(2)}) collective-permute-start(bf16[2,528,128]{2,1,0:T(8,128)(2,1)S(1)} %get-tuple-element.28), channel_id=1, source_target_pairs={{0,1},{1,0},{2,3},{3,2},{4,8},{5,9},{6,10},{7,11},{8,4},{9,5},{10,... | collective-permute-start | bytes 811016 | tf_op jit(solution)/shard_map/ppermute | solution.py:510
  3.9 1.2 %collective-permute-start.2 = (bf16[2,528,128]{2,1,0:T(8,128)(2,1)S(1)}, bf16[2,528,128]{2,1,0:T(8,128)(2,1)S(1)}, u32[]{:S(2)}, u32[]{:S(2)}) collective-permute-start(bf16[2,528,128]{2,1,0:T(8,128)(2,1)S(1)} %get-tuple-element.30), channel_id=1, source_target_pairs={{0,1},{1,0},{2,3},{3,2},{4,5},{5,4},{6,7},{7,6},{8,9},{9,8},{10,11... | collective-permute-start | bytes 811016 | tf_op jit(solution)/shard_map/ppermute | solution.py:510
  5.2 1.1 %collective-permute-start.3 = (bf16[2,528,128]{2,1,0:T(8,128)(2,1)S(1)}, bf16[2,528,128]{2,1,0:T(8,128)(2,1)S(1)}, u32[]{:S(2)}, u32[]{:S(2)}) collective-permute-start(bf16[2,528,128]{2,1,0:T(8,128)(2,1)S(1)} %get-tuple-element.31), channel_id=1, source_target_pairs={{0,8},{1,2},{2,1},{3,11},{4,12},{5,6},{6,5},{7,15},{8,0},{9,10},{1... | collective-permute-start | bytes 811016 | tf_op jit(solution)/shard_map/ppermute | solution.py:510
  6.3 5.3 %step_one.1 = (bf16[4,9,128,512]{3,2,1,0:T(8,128)(2,1)S(1)}, f32[4,128,128]{2,1,0:T(8,128)S(1)}, bf16[2,144,512]{2,1,0:T(8,128)(2,1)S(1)}, bf16[2,144,512]{2,1,0:T(8,128)(2,1)S(1)}) custom-call(s32[4,4,12]{2,1,0:T(4,128)} %codes_hbm.1, bf16[192,128,128]{2,1,0:T(8,128)(2,1)} %bitcast.5, bf16[4,512,128]{2,1,0:T(8,128)(2,1)} %bitcast.4, ...), custom_call_target="tpu_custom_call" | custom-call | flops 8589934592 | bytes 1048576 | tf_op jit(solution)/shard_map/step_one/pallas_call | solution.py:192
  11.6 0.5 %collective-permute-start.4 = (bf16[2,144,512]{2,1,0:T(8,128)(2,1)S(1)}, bf16[2,144,512]{2,1,0:T(8,128)(2,1)S(1)}, u32[]{:S(2)}, u32[]{:S(2)}) collective-permute-start(bf16[2,144,512]{2,1,0:T(8,128)(2,1)S(1)} %get-tuple-element.35), channel_id=1, source_target_pairs={{0,1},{1,0},{2,3},{3,2},{4,5},{5,4},{6,7},{7,6},{8,9},{9,8},{10,11... | collective-permute-start | bytes 884744 | tf_op jit(solution)/shard_map/ppermute | solution.py:510
  12.1 0.0 collective-permute-done.2.col_a
  12.1 1.3 %collective-permute-start.5 = (bf16[2,144,512]{2,1,0:T(8,128)(2,1)S(1)}, bf16[2,144,512]{2,1,0:T(8,128)(2,1)S(1)}, u32[]{:S(2)}, u32[]{:S(2)}) collective-permute-start(bf16[2,144,512]{2,1,0:T(8,128)(2,1)S(1)} %get-tuple-element.36), channel_id=1, source_target_pairs={{0,8},{1,2},{2,1},{3,11},{4,12},{5,6},{6,5},{7,15},{8,0},{9,10},{1... | collective-permute-start | bytes 884744 | tf_op jit(solution)/shard_map/ppermute | solution.py:510
  13.5 0.0 collective-permute-done.3.col_b
  13.5 0.5 %near_terms.1 = (bf16[21,32,128]{2,1,0:T(8,128)(2,1)S(1)}, bf16[21,32,128]{2,1,0:T(8,128)(2,1)S(1)}, bf16[21,32,128]{2,1,0:T(8,128)(2,1)S(1)}, bf16[21,32,128]{2,1,0:T(8,128)(2,1)S(1)}, f32[32,128]{1,0:T(8,128)S(1)}) custom-call(f32[8,128]{1,0:T(8,128)S(1)} %get-tuple-element.25.bits, bf16[4,9,128,512]{3,2,1,0:T(8,128)(2,1)S(1)} %get-tuple-element.26.r, ...), custom_call_target="tpu_custom_call" | custom-call | flops 1 | bytes 1 | tf_op jit(solution)/shard_map/near_terms/pallas_call | solution.py:327
  14.0 0.7 %collective-permute-done.first = bf16[2,528,128]{2,1,0:T(8,128)(2,1)S(1)} collective-permute-done((bf16[2,528,128]{2,1,0:T(8,128)(2,1)S(1)}, bf16[2,528,128]{2,1,0:T(8,128)(2,1)S(1)}, u32[]{:S(2)}, u32[]{:S(2)}) %collective-permute-start) | collective-permute-done | bytes 270368 | tf_op jit(solution)/shard_map/ppermute | solution.py:510
  14.6 0.0 collective-permute-done.1.second
  14.6 0.0 collective-permute-done.4.from_a
  14.6 3.9 %collective-permute-done.5.from_b = bf16[2,144,512]{2,1,0:T(8,128)(2,1)S(1)} collective-permute-done((bf16[2,144,512]{2,1,0:T(8,128)(2,1)S(1)}, bf16[2,144,512]{2,1,0:T(8,128)(2,1)S(1)}, u32[]{:S(2)}, u32[]{:S(2)}) %collective-permute-start.5) | collective-permute-done | bytes 294944 | tf_op jit(solution)/shard_map/ppermute | solution.py:510
  18.5 0.7 %far_terms.1 = (bf16[21,32,128]{2,1,0:T(8,128)(2,1)S(1)}, bf16[21,32,128]{2,1,0:T(8,128)(2,1)S(1)}, bf16[21,32,128]{2,1,0:T(8,128)(2,1)S(1)}, bf16[21,32,128]{2,1,0:T(8,128)(2,1)S(1)}) custom-call(f32[8,128]{1,0:T(8,128)S(1)} %get-tuple-element.25.bits, ...), custom_call_target="tpu_custom_call", output_to_operand_aliasing={{0}: (7, {}), {1}: (8, {}), {2}: (9, {}), {3}: (10, {})} | custom-call | flops 1 | bytes 1 | tf_op jit(solution)/shard_map/far_terms/pallas_call | solution.py:342
  19.2 0.5 %collective-permute-start.8 = (bf16[21,32,128]{2,1,0:T(8,128)(2,1)S(1)}, bf16[21,32,128]{2,1,0:T(8,128)(2,1)S(1)}, u32[]{:S(2)}, u32[]{:S(2)}) collective-permute-start(bf16[21,32,128]{2,1,0:T(8,128)(2,1)S(1)} %get-tuple-element.44), channel_id=1, source_target_pairs={{0,1},{1,0},{2,3},{3,2},{4,5},{5,4},{6,7},{7,6},{8,9},{9,8},{10,11... | collective-permute-start | bytes 516104 | tf_op jit(solution)/shard_map/ppermute | solution.py:516
  19.6 0.8 %collective-permute-start.7 = (bf16[21,32,128]{2,1,0:T(8,128)(2,1)S(1)}, bf16[21,32,128]{2,1,0:T(8,128)(2,1)S(1)}, u32[]{:S(2)}, u32[]{:S(2)}) collective-permute-start(bf16[21,32,128]{2,1,0:T(8,128)(2,1)S(1)} %get-tuple-element.42), channel_id=1, source_target_pairs={{0,2},{1,3},{2,0},{3,1},{4,6},{5,7},{6,4},{7,5},{8,10},{9,11},{10,... | collective-permute-start | bytes 516104 | tf_op jit(solution)/shard_map/ppermute | solution.py:516
  20.5 1.0 %collective-permute-start.6 = (bf16[21,32,128]{2,1,0:T(8,128)(2,1)S(1)}, bf16[21,32,128]{2,1,0:T(8,128)(2,1)S(1)}, u32[]{:S(2)}, u32[]{:S(2)}) collective-permute-start(bf16[21,32,128]{2,1,0:T(8,128)(2,1)S(1)} %get-tuple-element.41), channel_id=1, source_target_pairs={{0,3},{1,2},{2,1},{3,0},{4,7},{5,6},{6,5},{7,4},{8,11},{9,10},{10,... | collective-permute-start | bytes 516104 | tf_op jit(solution)/shard_map/ppermute | solution.py:516
  21.4 0.0 collective-permute-done.8.refs_1_
  21.4 1.2 %unpack.3.refs_1_ = bf16[4,2,9,2,32,128]{5,4,3,2,1,0:T(8,128)(2,1)} custom-call(bf16[21,32,128]{2,1,0:T(8,128)(2,1)S(1)} %get-tuple-element.43.refs_0_, bf16[21,32,128]{2,1,0:T(8,128)(2,1)S(1)} %collective-permute-done.8.refs_1_), custom_call_target="tpu_custom_call" | custom-call | flops 1 | bytes 1 | tf_op jit(solution)/shard_map/unpack/pallas_call | solution.py:408
  22.6 2.9 %collective-permute-done.7.refs_0_ = bf16[21,32,128]{2,1,0:T(8,128)(2,1)S(1)} collective-permute-done((bf16[21,32,128]{2,1,0:T(8,128)(2,1)S(1)}, bf16[21,32,128]{2,1,0:T(8,128)(2,1)S(1)}, u32[]{:S(2)}, u32[]{:S(2)}) %collective-permute-start.7) | collective-permute-done | bytes 172064 | tf_op jit(solution)/shard_map/ppermute | solution.py:516
  25.5 0.9 %unpack.4.refs_1_ = bf16[4,2,9,2,32,128]{5,4,3,2,1,0:T(8,128)(2,1)} custom-call(bf16[21,32,128]{2,1,0:T(8,128)(2,1)S(1)} %collective-permute-done.7.refs_0_, bf16[4,2,9,2,32,128]{5,4,3,2,1,0:T(8,128)(2,1)} %unpack.3.refs_1_), custom_call_target="tpu_custom_call", output_to_operand_aliasing={{}: (1, {})} | custom-call | flops 1 | bytes 1 | tf_op jit(solution)/shard_map/unpack/pallas_call | solution.py:408
  26.4 3.0 %collective-permute-done.6.refs_0_ = bf16[21,32,128]{2,1,0:T(8,128)(2,1)S(1)} collective-permute-done((bf16[21,32,128]{2,1,0:T(8,128)(2,1)S(1)}, bf16[21,32,128]{2,1,0:T(8,128)(2,1)S(1)}, u32[]{:S(2)}, u32[]{:S(2)}) %collective-permute-start.6) | collective-permute-done | bytes 172064 | tf_op jit(solution)/shard_map/ppermute | solution.py:516
  29.4 0.9 %unpack.5 = bf16[4,2,9,2,32,128]{5,4,3,2,1,0:T(8,128)(2,1)} custom-call(bf16[21,32,128]{2,1,0:T(8,128)(2,1)S(1)} %collective-permute-done.6.refs_0_, bf16[4,2,9,2,32,128]{5,4,3,2,1,0:T(8,128)(2,1)} %unpack.4.refs_1_), custom_call_target="tpu_custom_call", output_to_operand_aliasing={{}: (1, {})} | custom-call | flops 1 | bytes 1 | tf_op jit(solution)/shard_map/unpack/pallas_call | solution.py:408
  (1 shorter events, 0.0 us)
Async XLA Ops:
  1.4 13.2 %collective-permute-start = (bf16[2,528,128]{2,1,0:T(8,128)(2,1)S(1)}, bf16[2,528,128]{2,1,0:T(8,128)(2,1)S(1)}, u32[]{:S(2)}, u32[]{:S(2)}) collective-permute-start(bf16[2,528,128]{2,1,0:T(8,128)(2,1)S(1)} %get-tuple-element.27), channel_id=1, source_target_pairs={{0,4},{1,5},{2,6},{3,7},{4,0},{5,1},{6,2},{7,3},{8,12},{9,13},{10,... | collective-permute-start | bytes 811016 | tf_op jit(solution)/shard_map/ppermute | solution.py:510
  1.5 13.1 %collective-permute-start.1 = (bf16[2,528,128]{2,1,0:T(8,128)(2,1)S(1)}, bf16[2,528,128]{2,1,0:T(8,128)(2,1)S(1)}, u32[]{:S(2)}, u32[]{:S(2)}) collective-permute-start(bf16[2,528,128]{2,1,0:T(8,128)(2,1)S(1)} %get-tuple-element.28), channel_id=1, source_target_pairs={{0,1},{1,0},{2,3},{3,2},{4,8},{5,9},{6,10},{7,11},{8,4},{9,5},{10,... | collective-permute-start | bytes 811016 | tf_op jit(solution)/shard_map/ppermute | solution.py:510
  3.9 8.2 %collective-permute-start.2 = (bf16[2,528,128]{2,1,0:T(8,128)(2,1)S(1)}, bf16[2,528,128]{2,1,0:T(8,128)(2,1)S(1)}, u32[]{:S(2)}, u32[]{:S(2)}) collective-permute-start(bf16[2,528,128]{2,1,0:T(8,128)(2,1)S(1)} %get-tuple-element.30), channel_id=1, source_target_pairs={{0,1},{1,0},{2,3},{3,2},{4,5},{5,4},{6,7},{7,6},{8,9},{9,8},{10,11... | collective-permute-start | bytes 811016 | tf_op jit(solution)/shard_map/ppermute | solution.py:510
  5.2 8.3 %collective-permute-start.3 = (bf16[2,528,128]{2,1,0:T(8,128)(2,1)S(1)}, bf16[2,528,128]{2,1,0:T(8,128)(2,1)S(1)}, u32[]{:S(2)}, u32[]{:S(2)}) collective-permute-start(bf16[2,528,128]{2,1,0:T(8,128)(2,1)S(1)} %get-tuple-element.31), channel_id=1, source_target_pairs={{0,8},{1,2},{2,1},{3,11},{4,12},{5,6},{6,5},{7,15},{8,0},{9,10},{1... | collective-permute-start | bytes 811016 | tf_op jit(solution)/shard_map/ppermute | solution.py:510
  11.6 3.1 %collective-permute-start.4 = (bf16[2,144,512]{2,1,0:T(8,128)(2,1)S(1)}, bf16[2,144,512]{2,1,0:T(8,128)(2,1)S(1)}, u32[]{:S(2)}, u32[]{:S(2)}) collective-permute-start(bf16[2,144,512]{2,1,0:T(8,128)(2,1)S(1)} %get-tuple-element.35), channel_id=1, source_target_pairs={{0,1},{1,0},{2,3},{3,2},{4,5},{5,4},{6,7},{7,6},{8,9},{9,8},{10,11... | collective-permute-start | bytes 884744 | tf_op jit(solution)/shard_map/ppermute | solution.py:510
  12.1 6.4 %collective-permute-start.5 = (bf16[2,144,512]{2,1,0:T(8,128)(2,1)S(1)}, bf16[2,144,512]{2,1,0:T(8,128)(2,1)S(1)}, u32[]{:S(2)}, u32[]{:S(2)}) collective-permute-start(bf16[2,144,512]{2,1,0:T(8,128)(2,1)S(1)} %get-tuple-element.36), channel_id=1, source_target_pairs={{0,8},{1,2},{2,1},{3,11},{4,12},{5,6},{6,5},{7,15},{8,0},{9,10},{1... | collective-permute-start | bytes 884744 | tf_op jit(solution)/shard_map/ppermute | solution.py:510
  19.2 2.2 %collective-permute-start.8 = (bf16[21,32,128]{2,1,0:T(8,128)(2,1)S(1)}, bf16[21,32,128]{2,1,0:T(8,128)(2,1)S(1)}, u32[]{:S(2)}, u32[]{:S(2)}) collective-permute-start(bf16[21,32,128]{2,1,0:T(8,128)(2,1)S(1)} %get-tuple-element.44), channel_id=1, source_target_pairs={{0,1},{1,0},{2,3},{3,2},{4,5},{5,4},{6,7},{7,6},{8,9},{9,8},{10,11... | collective-permute-start | bytes 516104 | tf_op jit(solution)/shard_map/ppermute | solution.py:516
  19.6 5.8 %collective-permute-start.7 = (bf16[21,32,128]{2,1,0:T(8,128)(2,1)S(1)}, bf16[21,32,128]{2,1,0:T(8,128)(2,1)S(1)}, u32[]{:S(2)}, u32[]{:S(2)}) collective-permute-start(bf16[21,32,128]{2,1,0:T(8,128)(2,1)S(1)} %get-tuple-element.42), channel_id=1, source_target_pairs={{0,2},{1,3},{2,0},{3,1},{4,6},{5,7},{6,4},{7,5},{8,10},{9,11},{10,... | collective-permute-start | bytes 516104 | tf_op jit(solution)/shard_map/ppermute | solution.py:516
  20.5 9.0 %collective-permute-start.6 = (bf16[21,32,128]{2,1,0:T(8,128)(2,1)S(1)}, bf16[21,32,128]{2,1,0:T(8,128)(2,1)S(1)}, u32[]{:S(2)}, u32[]{:S(2)}) collective-permute-start(bf16[21,32,128]{2,1,0:T(8,128)(2,1)S(1)} %get-tuple-element.41), channel_id=1, source_target_pairs={{0,3},{1,2},{2,1},{3,0},{4,7},{5,6},{6,5},{7,4},{8,11},{9,10},{10,... | collective-permute-start | bytes 516104 | tf_op jit(solution)/shard_map/ppermute | solution.py:516

commit v4 on v3

--- a/solution.py
+++ b/solution.py
@@ -13,8 +13,8 @@
 QUAD = 4 * BS
 HEAD = 16
 ROWS = HEAD + QUAD
-TALL = BS + HEAD
-SLOTS = 20
+OWN_SLOTS = 4
+SLOTS = 16
 ANY = pl.BlockSpec(memory_space=pl.ANY)
 VMEM = pl.BlockSpec(memory_space=pltpu.VMEM)
 HBM = pl.BlockSpec(memory_space=pltpu.HBM)
@@ -91,7 +91,7 @@
 
 
 def step_one_kernel(
-    codes_hbm, coupling, prolong_hbm, bits, out, center, to_a, to_b, blocks, prolong, far, codes, slot_of, sems
+    codes_hbm, coupling, prolong_hbm, after, out, to_a, to_b, prolong, blocks, codes, slot_of, sems
 ):
     fx, fy = flips()
     load_codes = pltpu.make_async_copy(codes_hbm, codes, sems.at[8])
@@ -159,50 +159,29 @@
                 at = (du + fx * (2 - 2 * du)) * 3 + dv + fy * (2 - 2 * dv)
                 out[quad, at, :, (jx % 2) * 256 : (jx % 2 + 1) * 256] = total.astype(BF16)
 
-    for ref, e, j, q in ((to_b, 0, 2, (3, 0)), (to_b, 1, 0, (0, 0)), (to_a, 0, 3, (3, 3)), (to_a, 1, 1, (0, 3))):
-        ref[e, 0:BS, :] = sums(out, OWN[j], (q,))
-        bit = jnp.broadcast_to(bits[j : j + 1, :], (HEAD, BS)).astype(BF16)
-        ref[e, BS:, :] = jnp.concatenate([bit] * 4, axis=1)
-    for j, (u, v) in enumerate(OWN):
-        ur, vr = turned(u - 1, fx), turned(v - 1, fy)
-        at = pl.ds(pl.multiple_of(vr * 256, 256), 256)
-        for m in range(2):
-            rows = slice(QUAD * j + 256 * m, QUAD * j + 256 * (m + 1))
-            part = prolong[2 * ur + m, at, :]
-            high = part * bits[j : j + 1, :].astype(BF16)
-            far[rows, 0:BS] = part - high
-            far[rows, BS:] = high
-    for i, p in enumerate(OWN):
-        raw = 2 * turned(p[0] - 1, fx) + turned(p[1] - 1, fy)
-        near = [out[raw, (q[0] - p[0] + 1) * 3 + q[1] - p[1] + 1] for q in OWN]
-        value = jnp.dot(jnp.concatenate(near, axis=1), far[...], preferred_element_type=F32)
-        for b in range(2):
-            one = value[:, b * BS : (b + 1) * BS]
-            high = bits[i : i + 1, :] * one
-            low = one - high
-            if i == 0:
-                center[b] = low
-                center[2 + b] = high
-            else:
-                center[b] += low
-                center[2 + b] += high
-
-
-def step_one(codes, coupling, prolong_rows, bits):
+    for ref, e, p, q in (
+        (to_b, 0, (2, 1), (3, 0)),
+        (to_b, 1, (1, 1), (0, 0)),
+        (to_a, 0, (2, 2), (3, 3)),
+        (to_a, 1, (1, 2), (0, 3)),
+    ):
+        ref[e] = sums(out, p, (q,))
+
+
+def step_one(codes, coupling, prolong_rows, after):
+    corner = jax.ShapeDtypeStruct((2, BS, QUAD), BF16)
     return pl.pallas_call(
         step_one_kernel,
         out_shape=(
             jax.ShapeDtypeStruct((4, 9, BS, QUAD), BF16),
-            jax.ShapeDtypeStruct((4, BS, BS), F32),
-            jax.ShapeDtypeStruct((2, TALL, QUAD), BF16),
-            jax.ShapeDtypeStruct((2, TALL, QUAD), BF16),
+            corner,
+            corner,
+            jax.ShapeDtypeStruct(prolong_rows.shape, BF16),
         ),
-        in_specs=[HBM, HBM, HBM, VMEM],
+        in_specs=[HBM] * 3 + [ANY],
         out_specs=(VMEM,) * 4,
         scratch_shapes=[
             pltpu.VMEM((NONE + 1, BS, BS), BF16),
-            pltpu.VMEM((SIDE, SIDE * BS, BS), BF16),
-            pltpu.VMEM((4 * QUAD, 2 * BS), BF16),
             pltpu.SMEM((SIDE, SIDE, KA), jnp.int32),
             pltpu.SMEM((400,), jnp.int32),
             pltpu.SemaphoreType.DMA((10,)),
@@ -210,7 +189,7 @@
         compiler_params=pltpu.CompilerParams(vmem_limit_bytes=16 << 20),
         cost_estimate=pl.CostEstimate(flops=1 << 33, bytes_accessed=1 << 20, transcendentals=0),
         name="step_one",
-    )(codes, coupling, prolong_rows, bits)
+    )(codes, coupling, prolong_rows, after)
 
 
 def half_of(ref):
@@ -252,48 +231,91 @@
             out[at + t] = values[t, pl.ds(start, rows), :].astype(BF16)
 
 
-def store_head(outs, head):
-    rows = outs[0].shape[1]
-    for out in outs:
-        for t in range(out.shape[0] - SLOTS):
-            out[SLOTS + t] = head[t * rows : (t + 1) * rows, :].astype(BF16)
-
-
-def edge_terms(r, bits, edges, same_a, slots, head):
-    for e, (far, own, quads, scale) in enumerate(edges):
+def near_kernel(parts, bits, r, prolong, after, *rest):
+    outs, (slots, right) = rest[:-2], rest[-2:]
+    fx, fy = flips()
+
+    def by_halves(quads, own, first):
+        for j, (_, parts_of, bit) in enumerate(quads):
+            for m, rows in enumerate(parts_of):
+                step = rows.shape[0]
+                at = QUAD * j + step * m
+                high = rows * bit.astype(BF16)
+                right[at : at + step, 0:BS] = rows - high
+                right[at : at + step, BS:] = high
+        names = [q for q, _, _ in quads]
+        for i, k in enumerate(own):
+            value = jnp.dot(sums(r, OWN[k], names), right[0 : QUAD * len(quads), :], preferred_element_type=F32)
+            for b in range(2):
+                one = value[:, b * BS : (b + 1) * BS]
+                high = bits[k : k + 1, :] * one
+                low = one - high
+                if i == 0:
+                    slots[first + b] = low
+                    slots[first + 2 + b] = high
+                else:
+                    slots[first + b] += low
+                    slots[first + 2 + b] += high
+
+    quads = []
+    for j, (u, v) in enumerate(OWN):
+        ur, vr = turned(u - 1, fx), turned(v - 1, fy)
+        at = pl.ds(pl.multiple_of(vr * 256, 256), 256)
+        quads.append(((u, v), [prolong[2 * ur + m, at, :] for m in range(2)], bits[j : j + 1, :]))
+    by_halves(quads, range(4), 0)
+    rows = BS // parts
+    me = lax.axis_index("col")
+    for s in range(parts):
+        start = pl.multiple_of((me ^ s) * rows, rows)
+        out = outs[s] if s < 2 else outs[s // 2 + 1]
+        for t in range(OWN_SLOTS):
+            value = slots[t, pl.ds(start, rows), :].astype(BF16)
+            if s < 2:
+                out[t] = value
+            else:
+                out[s % 2, t] = value
+
+
+def near_terms(parts, *operands):
+    rows = BS // parts
+    one = jax.ShapeDtypeStruct((OWN_SLOTS, rows, BS), BF16)
+    two = jax.ShapeDtypeStruct((2, OWN_SLOTS, rows, BS), BF16)
+    shapes = (one, one) + (two,) * (parts // 2 - 1)
+    return pl.pallas_call(
+        functools.partial(near_kernel, parts),
+        out_shape=shapes,
+        in_specs=[VMEM] * (len(operands) - 1) + [ANY],
+        out_specs=(VMEM,) * len(shapes),
+        scratch_shapes=[pltpu.VMEM((OWN_SLOTS, BS, BS), F32), pltpu.VMEM((4 * QUAD, 2 * BS), BF16)],
+        compiler_params=pltpu.CompilerParams(vmem_limit_bytes=16 << 20),
+        cost_estimate=pl.CostEstimate(flops=1, bytes_accessed=1, transcendentals=0),
+        name="near_terms",
+    )(*operands)
+
+
+def far_kernel(counts, bits, r, row_a, row_b, col_a, col_b, from_a, from_b, *rest):
+    outs, (slots, head) = rest[:-2], rest[-2:]
+    split_y = jnp.abs(bits[0:1, :] - bits[1:2, :])
+    split_x = 1.0 - split_y
+    row_in, col_in = inside("row", counts[0]), inside("col", counts[1])
+    head[...] = jnp.zeros_like(head)
+    head[0:4, :] = bits[0:4, :]
+    edges = (
+        (row_a, ((2, 1), (2, 2)), ((3, 1), (3, 2)), split_x, None),
+        (row_b, ((1, 1), (1, 2)), ((0, 1), (0, 2)), split_x, row_in),
+        (col_a, ((1, 2), (2, 2)), ((1, 3), (2, 3)), split_y, None),
+        (col_b, ((1, 1), (2, 1)), ((1, 0), (2, 0)), split_y, col_in),
+    )
+    for e, (far, own, quads, same_a, scale) in enumerate(edges):
         base, extra = edge_slots([sums(r, p, quads) for p in own], [far.at[0], far.at[1]], same_a)
         for t in range(2):
             slots[2 * e + t] = base[t] if scale is None else base[t] * scale
-            slots[4 + 2 * e + t] = extra[t] if scale is None else extra[t] * scale
-            head[2 * e + t : 2 * e + t + 1, :] = half_of(far.at[t])
-
-
-def near_kernel(counts, bits, r, center, col_a, col_b, *rest):
-    outs, (head, slots) = rest[:-2], rest[-2:]
-    split_y = jnp.abs(bits[0:1, :] - bits[1:2, :])
-    edges = (
-        (col_a, ((1, 2), (2, 2)), ((1, 3), (2, 3)), None),
-        (col_b, ((1, 1), (2, 1)), ((1, 0), (2, 0)), inside("col", counts[1])),
-    )
-    head[...] = jnp.zeros_like(head)
-    edge_terms(r, bits, edges, split_y, slots, head.at[8:12])
-    head[0:4, :] = bits[0:4, :]
-    store_pieces(outs, 0, center)
-    store_pieces(outs, 8, slots.at[0:4])
-    store_pieces(outs, 16, slots.at[4:8])
-
-
-def far_kernel(counts, bits, r, row_a, row_b, from_a, from_b, head_in, *rest):
-    parts = counts[1]
-    ins, outs, (slots, head) = rest[:parts], rest[parts : 2 * parts], rest[2 * parts :]
-    split_x = 1.0 - jnp.abs(bits[0:1, :] - bits[1:2, :])
-    row_in, col_in = inside("row", counts[0]), inside("col", parts)
-    edges = (
-        (row_a, ((2, 1), (2, 2)), ((3, 1), (3, 2)), None),
-        (row_b, ((1, 1), (1, 2)), ((0, 1), (0, 2)), row_in),
-    )
-    head[...] = head_in[...]
-    edge_terms(r, bits, edges, split_x, slots, head.at[4:8])
+            more = extra[t] if scale is None else extra[t] * scale
+            if e < 2:
+                slots[12 + 2 * e + t] = more
+            else:
+                slots[8 + 2 * e + t] += more
+            head[4 + 2 * e + t : 5 + 2 * e + t, :] = half_of(far.at[t])
     corners = (
         (from_a.at[0], row_a.at[1], None),
         (from_b.at[0], row_a.at[0], col_in),
@@ -301,58 +323,70 @@
         (from_b.at[1], row_b.at[0], row_in * col_in),
     )
     for e, (near, far, scale) in enumerate(corners):
-        value = jnp.dot(near[0:BS, :], far[HEAD:, :], preferred_element_type=F32)
+        value = jnp.dot(near[...], far[HEAD:, :], preferred_element_type=F32)
         slots[8 + e] = value if scale is None else value * scale
-        head[12 + e : 13 + e, :] = near[BS : BS + 1, 0:BS].astype(F32)
-    store_pieces(outs, 4, slots.at[0:4])
-    store_pieces(outs, 12, slots.at[8:12])
+    store_pieces(outs, 0, slots)
     rows = outs[0].shape[1]
-    me = lax.axis_index("col")
-    for s in range(parts):
-        start = pl.multiple_of((me ^ s) * rows, rows)
-        for t in range(4):
-            part = slots[4 + t, pl.ds(start, rows), :] + ins[s][16 + t].astype(F32)
-            outs[s][16 + t] = part.astype(BF16)
-    store_head(outs, head)
-
-
-def message_shapes(parts):
+    for out in outs:
+        for t in range(out.shape[0] - SLOTS):
+            out[SLOTS + t] = head[t * rows : (t + 1) * rows, :].astype(BF16)
+
+
+def far_terms(counts, *operands):
+    parts = counts[1]
     rows = BS // parts
     heads = -(-HEAD // rows)
-    return jax.ShapeDtypeStruct((SLOTS + heads, rows, BS), BF16), jax.ShapeDtypeStruct((heads * rows, BS), F32)
-
-
-def near_terms(counts, *operands):
-    message, head = message_shapes(counts[1])
-    return pl.pallas_call(
-        functools.partial(near_kernel, counts),
-        out_shape=(message,) * counts[1] + (head,),
+    message = jax.ShapeDtypeStruct((SLOTS + heads, rows, BS), BF16)
+    return pl.pallas_call(
+        functools.partial(far_kernel, counts),
+        out_shape=(message,) * parts,
         in_specs=[VMEM] * len(operands),
-        out_specs=(VMEM,) * (counts[1] + 1),
-        scratch_shapes=[pltpu.VMEM((8, BS, BS), F32)],
-        compiler_params=pltpu.CompilerParams(vmem_limit_bytes=16 << 20),
-        cost_estimate=pl.CostEstimate(flops=1, bytes_accessed=1, transcendentals=0),
-        name="near_terms",
-    )(*operands)
-
-
-def far_terms(counts, *operands):
-    message, head = message_shapes(counts[1])
-    first = len(operands) - counts[1]
-    return pl.pallas_call(
-        functools.partial(far_kernel, counts),
-        out_shape=(message,) * counts[1],
-        in_specs=[VMEM] * len(operands),
-        out_specs=(VMEM,) * counts[1],
-        scratch_shapes=[pltpu.VMEM((12, BS, BS), F32), pltpu.VMEM(head.shape, F32)],
-        input_output_aliases={first + s: s for s in range(counts[1])},
+        out_specs=(VMEM,) * parts,
+        scratch_shapes=[pltpu.VMEM((SLOTS, BS, BS), F32), pltpu.VMEM((heads * rows, BS), F32)],
         compiler_params=pltpu.CompilerParams(vmem_limit_bytes=16 << 20),
         cost_estimate=pl.CostEstimate(flops=1, bytes_accessed=1, transcendentals=0),
         name="far_terms",
     )(*operands)
 
 
-def unpack_kernel(parts, steps, fresh, *refs):
+def place_kernel(parts, own, relayed, *rest):
+    direct, (out, sems) = rest[:-3], rest[-2:]
+    me = lax.axis_index("col")
+    pieces = {0: own}
+    for h in range(parts // 2):
+        pieces[2 * h + 1] = relayed.at[h]
+        if h:
+            pieces[2 * h] = direct[h - 1].at[0]
+    copies = []
+    for s in range(parts):
+        square = me ^ s
+        for a in range(2):
+            copies.append(
+                pltpu.make_async_copy(
+                    pieces[s].at[2 * a : 2 * a + 2], out.at[square, a, 4], sems.at[len(copies)]
+                )
+            )
+            copies[-1].start()
+    for copy in copies:
+        copy.wait()
+
+
+def place(own, relayed, direct, coarse):
+    parts = lax.axis_size("col")
+    return pl.pallas_call(
+        functools.partial(place_kernel, parts),
+        out_shape=jax.ShapeDtypeStruct(coarse.shape, BF16),
+        in_specs=[VMEM] * (2 + len(direct)) + [ANY],
+        out_specs=ANY,
+        scratch_shapes=[pltpu.SemaphoreType.DMA((2 * parts,))],
+        input_output_aliases={2 + len(direct): 0},
+        compiler_params=pltpu.CompilerParams(vmem_limit_bytes=4 << 20),
+        cost_estimate=pl.CostEstimate(flops=1, bytes_accessed=1, transcendentals=0),
+        name="place",
+    )(own, relayed, *direct, coarse)
+
+
+def unpack_kernel(parts, steps, *refs):
     ins = refs[: len(steps)]
     out, buf, sems = refs[-3:]
     me = lax.axis_index("col")
@@ -363,40 +397,36 @@
         fy = lax.rem(square, 2)
         one = functools.partial(bit_row, ref)
         split_y = jnp.abs(one(0) - one(1))
+
+        def send(piece, owner, code):
+            for a in range(2):
+                copies.append(
+                    pltpu.make_async_copy(buf.at[i, piece, a], out.at[owner, a, code], sems.at[len(copies)])
+                )
+                copies[-1].start()
+
         split_x = 1.0 - split_y
-
-        def send(places):
-            for piece, (owner, code) in places:
-                for a in range(2):
-                    copies.append(
-                        pltpu.make_async_copy(
-                            buf.at[i, piece, a], out.at[owner, a, code], sems.at[len(copies)]
-                        )
-                    )
-                    copies[-1].start()
-
-        spread(buf, (i, 0), [ref[t].astype(F32) for t in range(4)])
-        send([(0, (square, 4))])
         edges = (
-            ((2, 3), split_y, 7 - 6 * fx),
-            ((0, 1), split_y, 1 + 6 * fx),
-            ((1, 3), split_x, 3 + turn3(2, fy)),
-            ((0, 2), split_x, 3 + turn3(0, fy)),
+            ((2, 3), (12, 13), split_y, 7 - 6 * fx),
+            ((0, 1), (14, 15), split_y, 1 + 6 * fx),
+            ((1, 3), (12, 13), split_x, 3 + turn3(2, fy)),
+            ((0, 2), (14, 15), split_x, 3 + turn3(0, fy)),
         )
-        for e, (ps, used, code) in enumerate(edges):
-            at = 2 * e % 4
-            spread_edge(
-                buf, (i, 1 + e), ref, one, ps, (4 + 2 * e, 5 + 2 * e), (4 + 2 * e, 5 + 2 * e), (16 + at, 17 + at), used
-            )
-            send([(1 + e, (square, code))])
+        for e, (ps, more, used, code) in enumerate(edges):
+            spread_edge(buf, (i, e), ref, one, ps, (4 + 2 * e, 5 + 2 * e), (2 * e, 2 * e + 1), more, used)
+            send(e, square, code)
         high = square ^ 1
         low = square + 2 * fy - 1
         low = jnp.where((low < 0) | (low >= parts), square, low)
-        for e, (owner, group, side, b_bit) in enumerate(
-            ((high, 6 - 6 * fx, 2, 5), (low, 6 - 6 * fx, 0, 4), (high, 6 * fx, 2, 7), (low, 6 * fx, 0, 6))
-        ):
-            spread_corner(buf, (i, 5 + e), ref[12 + e].astype(F32), one(12 + e), one(b_bit))
-            send([(5 + e, (owner, group + turn3(side, lax.rem(owner, 2))))])
+        corners = (
+            (high, 6 - 6 * fx, 2, 9, 5),
+            (low, 6 - 6 * fx, 0, 11, 4),
+            (high, 6 * fx, 2, 8, 7),
+            (low, 6 * fx, 0, 10, 6),
+        )
+        for e, (owner, group, side, a_bit, b_bit) in enumerate(corners):
+            spread_corner(buf, (i, 4 + e), ref[8 + e].astype(F32), one(a_bit), one(b_bit))
+            send(4 + e, owner, group + turn3(side, lax.rem(owner, 2)))
     for copy in copies:
         copy.wait()
 
@@ -406,13 +436,13 @@
     rows = messages[0].shape[1]
     fresh = coarse is None
     return pl.pallas_call(
-        functools.partial(unpack_kernel, parts, steps, fresh),
+        functools.partial(unpack_kernel, parts, steps),
         out_shape=jax.ShapeDtypeStruct((parts, 2, 9, 2, rows, BS), BF16),
         in_specs=[VMEM] * len(steps) + [ANY] * (not fresh),
         out_specs=ANY,
         scratch_shapes=[
-            pltpu.VMEM((len(steps), 9, 2, 2, rows, BS), BF16),
-            pltpu.SemaphoreType.DMA((18 * len(steps),)),
+            pltpu.VMEM((len(steps), 8, 2, 2, rows, BS), BF16),
+            pltpu.SemaphoreType.DMA((16 * len(steps),)),
         ],
         input_output_aliases={} if fresh else {len(steps): 0},
         compiler_params=pltpu.CompilerParams(vmem_limit_bytes=16 << 20),
@@ -461,21 +491,22 @@
     spread(buf, at, center)
 
 
-def gate_kernel(first, second, after, first_out, second_out):
+def gate_kernel(*refs):
     pass
 
 
-def gate(first, second, after):
+def gate(values, after):
+    count = len(values)
     return pl.pallas_call(
         gate_kernel,
-        out_shape=tuple(jax.ShapeDtypeStruct(v.shape, v.dtype) for v in (first, second)),
-        in_specs=[ANY, ANY, ANY],
-        out_specs=(ANY, ANY),
-        input_output_aliases={0: 0, 1: 1},
+        out_shape=tuple(jax.ShapeDtypeStruct(v.shape, v.dtype) for v in values),
+        in_specs=[ANY] * (count + len(after)),
+        out_specs=(ANY,) * count,
+        input_output_aliases={i: i for i in range(count)},
         compiler_params=pltpu.CompilerParams(vmem_limit_bytes=1 << 20),
         cost_estimate=pl.CostEstimate(flops=1 << 33, bytes_accessed=1, transcendentals=0),
         name="gate",
-    )(first, second, after)
+    )(*values, *after)
 
 
 def other_side(index):
@@ -510,11 +541,8 @@
     return lax.ppermute(value, ("row", "col"), pairs)
 
 
-def scatter_rows(outs):
-    count = len(outs)
-    return [outs[0]] + [
-        lax.ppermute(outs[s], "col", [(i, i ^ s) for i in range(count)]) for s in range(1, count)
-    ]
+def xor_swap(value, s):
+    return lax.ppermute(value, "col", [(i, i ^ s) for i in range(lax.axis_size("col"))])
 
 
 def local(coupling, neighbours, prolong, aggregate):
@@ -529,16 +557,20 @@
     row_b = swap(to_row_b, row_low)
     col_a = swap(to_col_a, col_high)
     col_b = swap(to_col_b, col_low)
-    r, center, to_a, to_b = step_one(neighbours, coupling, prolong_rows, bits)
+    r, to_a, to_b, own_blocks = step_one(neighbours, coupling, prolong_rows, bits)
     from_b = swap(to_b, col_low)
     from_a = swap(to_a, col_high)
-    *outs, head = near_terms(counts, bits, r, center, col_a, col_b)
-    row_a, row_b = gate(row_a, row_b, head)
-    outs = far_terms(counts, bits, r, row_a, row_b, from_a, from_b, head, *outs)
-    outs = scatter_rows(outs)
-    coarse = None
-    for first, last in ((0, 2), (2, parts - 1), (parts - 1, parts)):
-        coarse = unpack(outs[first:last], range(first, last), coarse)
+    mine, pair, *cross = near_terms(parts, bits, r, own_blocks, col_a)
+    from_a, *cross = lax.optimization_barrier((from_a, *cross))
+    direct = [xor_swap(value, 2 * h + 2) for h, value in enumerate(cross)]
+    row_a, row_b, col_b, from_b = gate((row_a, row_b, col_b, from_b), (mine,))
+    outs = list(far_terms(counts, bits, r, row_a, row_b, col_a, col_b, from_a, from_b))
+    outs[0], *direct = lax.optimization_barrier((outs[0], *direct))
+    outs = [outs[0]] + [xor_swap(outs[s], s) for s in range(1, parts)]
+    relayed = xor_swap(jnp.stack([pair] + [value[1] for value in direct]), 1)
+    coarse = unpack(outs[:2], range(2), None)
+    coarse = place(mine, relayed, direct, coarse)
+    coarse = unpack(outs[2:], range(2, parts), coarse)
     return coarse[None]
 
 

time: 30.6 us -> 28.7 us (0.938)
  waiting for transfers between devices: 10.5 us -> 9.27 us
  starting transfers between devices: 9 us -> 8.5 us
    ppermute x3 -> x5, waiting for transfers between devices: 5.93 us -> 3.98 us  [xor_swap(): lax.ppermute(value, 'col', [(i, i ^ s) for i in range(lax.axis_size('col'...]
    ppermute x6, starting transfers between devices: 6.76 us -> 5.59 us  [swap(): return lax.ppermute(value, ('row', 'col'), pairs)]
    ppermute x6, waiting for transfers between devices: 4.57 us -> 5.29 us  [swap(): return lax.ppermute(value, ('row', 'col'), pairs)]
    pallas_call x1, Pallas kernels: 5.29 us -> 4.56 us  [step_one(): pl.pallas_call(step_one_kernel, out_shape=(jax.ShapeDtypeStruct((4, 9, BS...]
    ppermute x3 -> x5, starting transfers between devices: 2.24 us -> 2.91 us  [xor_swap(): lax.ppermute(value, 'col', [(i, i ^ s) for i in range(lax.axis_size('col'...]
  transfers between devices with their start and end apart: 9 -> 11, of which waited for: 4 -> 4; matrix products, arithmetic and copies ran while one was open for 0% -> 0% of each run, Pallas kernels for 26% -> 28%
where the time goes in v4:
time: 28.7 us; the launch traced here: 28.5 us
  Pallas kernels  10.6 us (37%)
  waiting for transfers between devices  9.27 us (32%)
  starting transfers between devices  8.5 us (30%)
    ppermute x6, starting transfers between devices, swap(): return lax.ppermute(value, ('row', 'col'), pairs)  5.59 us
    ppermute x6, waiting for transfers between devices, swap(): return lax.ppermute(value, ('row', 'col'), pairs)  5.29 us
    pallas_call x1, Pallas kernels, step_one(): pl.pallas_call(step_one_kernel, out_shape=(jax.ShapeDtypeStruct((4, 9, BS...  4.56 us
    ppermute x5, waiting for transfers between devices, xor_swap(): lax.ppermute(value, 'col', [(i, i ^ s) for i in range(lax.axis_size('col'...  3.98 us
    ppermute x5, starting transfers between devices, xor_swap(): lax.ppermute(value, 'col', [(i, i ^ s) for i in range(lax.axis_size('col'...  2.91 us
    pallas_call x2, Pallas kernels, unpack(): pl.pallas_call(functools.partial(unpack_kernel, parts, steps), out_shape=...  2.23 us
    pallas_call x1, Pallas kernels, rims(): pl.pallas_call(rims_kernel, out_shape=(shape,) * 4 + (jax.ShapeDtypeStruc...  1.38 us
    pallas_call x1, Pallas kernels, far_terms(): pl.pallas_call(functools.partial(far_kernel, counts), out_shape=(message,...  0.95 us
  transfers between devices with their start and end apart: 11, of which 4 were waited for; matrix products, arithmetic and copies ran while one was open for 0% of the time, Pallas kernels for 28%

profile of v4, /device:TPU:5, one launch (start us, length us, event | category | flops | bytes accessed | tf_op | source)
XLA Modules:
  0.0 28.5 jit_solution(11042684308437940199)
XLA Ops:
  0.0 1.4 %rims.1 = (bf16[2,528,128]{2,1,0:T(8,128)(2,1)S(1)}, bf16[2,528,128]{2,1,0:T(8,128)(2,1)S(1)}, bf16[2,528,128]{2,1,0:T(8,128)(2,1)S(1)}, bf16[2,528,128]{2,1,0:T(8,128)(2,1)S(1)}, f32[8,128]{1,0:T(8,128)S(1)}) custom-call(s32[4,4]{1,0:T(4,128)} %agg_hbm.1, bf16[4,512,128]{2,1,0:T(8,128)(2,1)} %bitcast.5), custom_call_target="tpu_custom_call" | custom-call | tf_op jit(solution)/shard_map/rims/pallas_call | solution.py:71
  1.4 0.1 collective-permute-start
  1.5 2.5 %collective-permute-start.1 = (bf16[2,528,128]{2,1,0:T(8,128)(2,1)S(1)}, bf16[2,528,128]{2,1,0:T(8,128)(2,1)S(1)}, u32[]{:S(2)}, u32[]{:S(2)}) collective-permute-start(bf16[2,528,128]{2,1,0:T(8,128)(2,1)S(1)} %get-tuple-element.32), channel_id=1, source_target_pairs={{0,1},{1,0},{2,3},{3,2},{4,8},{5,9},{6,10},{7,11},{8,4},{9,5},{10,... | collective-permute-start | bytes 811016 | tf_op jit(solution)/shard_map/ppermute | solution.py:541
  3.9 2.3 %collective-permute-start.2 = (bf16[2,528,128]{2,1,0:T(8,128)(2,1)S(1)}, bf16[2,528,128]{2,1,0:T(8,128)(2,1)S(1)}, u32[]{:S(2)}, u32[]{:S(2)}) collective-permute-start(bf16[2,528,128]{2,1,0:T(8,128)(2,1)S(1)} %get-tuple-element.33), channel_id=1, source_target_pairs={{0,8},{1,2},{2,1},{3,11},{4,12},{5,6},{6,5},{7,15},{8,0},{9,10},{1... | collective-permute-start | bytes 811016 | tf_op jit(solution)/shard_map/ppermute | solution.py:541
  6.3 0.5 %collective-permute-start.4 = (bf16[2,528,128]{2,1,0:T(8,128)(2,1)S(1)}, bf16[2,528,128]{2,1,0:T(8,128)(2,1)S(1)}, u32[]{:S(2)}, u32[]{:S(2)}) collective-permute-start(bf16[2,528,128]{2,1,0:T(8,128)(2,1)S(1)} %get-tuple-element.36), channel_id=1, source_target_pairs={{0,1},{1,0},{2,3},{3,2},{4,5},{5,4},{6,7},{7,6},{8,9},{9,8},{10,11... | collective-permute-start | bytes 811016 | tf_op jit(solution)/shard_map/ppermute | solution.py:541
  6.7 4.6 %step_one.1 = (bf16[4,9,128,512]{3,2,1,0:T(8,128)(2,1)S(1)}, bf16[2,128,512]{2,1,0:T(8,128)(2,1)S(1)}, bf16[2,128,512]{2,1,0:T(8,128)(2,1)S(1)}, bf16[4,512,128]{2,1,0:T(8,128)(2,1)S(1)}) custom-call(s32[4,4,12]{2,1,0:T(4,128)} %codes_hbm.1, bf16[192,128,128]{2,1,0:T(8,128)(2,1)} %bitcast.7, bf16[4,512,128]{2,1,0:T(8,128)(2,1)} %bitcast.6, ...), custom_call_target="tpu_custom_call" | custom-call | flops 8589934592 | bytes 1048576 | tf_op jit(solution)/shard_map/step_one/pallas_call | solution.py:173
  11.3 0.1 collective-permute-start.5
  11.4 0.0 collective-permute-done.4.after.col_a
  11.4 0.1 collective-permute-start.3
  11.6 0.8 %near_terms.1 = (bf16[4,32,128]{2,1,0:T(8,128)(2,1)S(1)}, bf16[4,32,128]{2,1,0:T(8,128)(2,1)S(1)}, bf16[2,4,32,128]{3,2,1,0:T(8,128)(2,1)S(1)}) custom-call(f32[8,128]{1,0:T(8,128)S(1)} %get-tuple-element.29.after.bits, bf16[4,9,128,512]{3,2,1,0:T(8,128)(2,1)S(1)} %get-tuple-element.30.r, bf16[4,512,128]{2,1,0:T(8,128)(2,1)S(1)} %get-tuple-element.35.prolong, ...), custom_call_target="tpu_custom_call" | custom-call | flops 1 | bytes 1 | tf_op jit(solution)/shard_map/near_terms/pallas_call | solution.py:284
  12.3 0.6 %collective-permute-done.5.from_a = bf16[2,128,512]{2,1,0:T(8,128)(2,1)S(1)} collective-permute-done((bf16[2,128,512]{2,1,0:T(8,128)(2,1)S(1)}, bf16[2,128,512]{2,1,0:T(8,128)(2,1)S(1)}, u32[]{:S(2)}, u32[]{:S(2)}) %collective-permute-start.5) | collective-permute-done | bytes 262176 | tf_op jit(solution)/shard_map/ppermute | solution.py:541
  12.9 0.3 %collective-permute-start.8 = (bf16[2,4,32,128]{3,2,1,0:T(8,128)(2,1)S(1)}, bf16[2,4,32,128]{3,2,1,0:T(8,128)(2,1)S(1)}, u32[]{:S(2)}, u32[]{:S(2)}) collective-permute-start(bf16[2,4,32,128]{3,2,1,0:T(8,128)(2,1)S(1)} %get-tuple-element.49), channel_id=1, source_target_pairs={{0,2},{1,3},{2,0},{3,1},{4,6},{5,7},{6,4},{7,5},{8,10},{9,11},{10,... | collective-permute-start | bytes 196616 | tf_op jit(solution)/shard_map/ppermute | solution.py:545
  13.3 4.7 %collective-permute-done.3.refs_3_ = bf16[2,128,512]{2,1,0:T(8,128)(2,1)S(1)} collective-permute-done((bf16[2,128,512]{2,1,0:T(8,128)(2,1)S(1)}, bf16[2,128,512]{2,1,0:T(8,128)(2,1)S(1)}, u32[]{:S(2)}, u32[]{:S(2)}) %collective-permute-start.3) | collective-permute-done | bytes 262176 | tf_op jit(solution)/shard_map/ppermute | solution.py:541
  18.0 0.0 collective-permute-done.refs_0_
  18.0 0.0 collective-permute-done.1.refs_1_
  18.0 0.0 collective-permute-done.2.refs_2_
  18.0 0.9 %far_terms.1 = (bf16[17,32,128]{2,1,0:T(8,128)(2,1)S(1)}, bf16[17,32,128]{2,1,0:T(8,128)(2,1)S(1)}, bf16[17,32,128]{2,1,0:T(8,128)(2,1)S(1)}, bf16[17,32,128]{2,1,0:T(8,128)(2,1)S(1)}) custom-call(f32[8,128]{1,0:T(8,128)S(1)} %get-tuple-element.29.after.bits, bf16[4,9,128,512]{3,2,1,0:T(8,128)(2,1)S(1)} %get-tuple-element.30.r, ...), custom_call_target="tpu_custom_call" | custom-call | flops 1 | bytes 1 | tf_op jit(solution)/shard_map/far_terms/pallas_call | solution.py:340
  19.0 0.1 collective-permute-start.6
  19.0 1.9 %collective-permute-start.7 = (bf16[17,32,128]{2,1,0:T(8,128)(2,1)S(1)}, bf16[17,32,128]{2,1,0:T(8,128)(2,1)S(1)}, u32[]{:S(2)}, u32[]{:S(2)}) collective-permute-start(bf16[17,32,128]{2,1,0:T(8,128)(2,1)S(1)} %get-tuple-element.46), channel_id=1, source_target_pairs={{0,3},{1,2},{2,1},{3,0},{4,7},{5,6},{6,5},{7,4},{8,11},{9,10},{10,... | collective-permute-start | bytes 417800 | tf_op jit(solution)/shard_map/ppermute | solution.py:545
  21.0 0.0 collective-permute-start.10
  21.0 0.0 collective-permute-done.8.rest_0_
  21.0 0.6 %collective-permute-start.9 = (bf16[2,4,32,128]{3,2,1,0:T(8,128)(2,1)S(1)}, bf16[2,4,32,128]{3,2,1,0:T(8,128)(2,1)S(1)}, u32[]{:S(2)}, u32[]{:S(2)}) collective-permute-start(bf16[2,4,32,128]{3,2,1,0:T(8,128)(2,1)S(1)} %pad_maximum_fusion), channel_id=1, source_target_pairs={{0,1},{1,0},{2,3},{3,2},{4,5},{5,4},{6,7},{7,6},{8,9},{9,8},{10,11... | collective-permute-start | bytes 196616 | tf_op jit(solution)/shard_map/ppermute | solution.py:545
  21.5 0.8 %collective-permute-done.10.refs_1_ = bf16[17,32,128]{2,1,0:T(8,128)(2,1)S(1)} collective-permute-done((bf16[17,32,128]{2,1,0:T(8,128)(2,1)S(1)}, bf16[17,32,128]{2,1,0:T(8,128)(2,1)S(1)}, u32[]{:S(2)}, u32[]{:S(2)}) %collective-permute-start.10) | collective-permute-done | bytes 139296 | tf_op jit(solution)/shard_map/ppermute | solution.py:545
  22.3 1.1 %unpack.2.rest_1_ = bf16[4,2,9,2,32,128]{5,4,3,2,1,0:T(8,128)(2,1)} custom-call(bf16[17,32,128]{2,1,0:T(8,128)(2,1)S(1)} %get-tuple-element.51.refs_0_, bf16[17,32,128]{2,1,0:T(8,128)(2,1)S(1)} %collective-permute-done.10.refs_1_), custom_call_target="tpu_custom_call" | custom-call | flops 1 | bytes 1 | tf_op jit(solution)/shard_map/unpack/pallas_call | solution.py:438
  23.4 0.0 collective-permute-done.9.relayed
  23.4 0.7 %place.1.refs_2_ = bf16[4,2,9,2,32,128]{5,4,3,2,1,0:T(8,128)(2,1)} custom-call(bf16[4,32,128]{2,1,0:T(8,128)(2,1)S(1)} %get-tuple-element.37.refs_4_.own, bf16[2,4,32,128]{3,2,1,0:T(8,128)(2,1)S(1)} %collective-permute-done.9.relayed, bf16[2,4,32,128]{3,2,1,0:T(8,128)(2,1)S(1)} %collective-permute-done.8.rest_0_, ...), custom_call_target="tpu_custom_call", output_to_operand_aliasing={{}: (3, {})} | custom-call | flops 1 | bytes 1 | tf_op jit(solution)/shard_map/place/pallas_call | solution.py:376
  24.2 0.0 collective-permute-done.6.refs_0_
  24.2 3.2 %collective-permute-done.7.refs_1_ = bf16[17,32,128]{2,1,0:T(8,128)(2,1)S(1)} collective-permute-done((bf16[17,32,128]{2,1,0:T(8,128)(2,1)S(1)}, bf16[17,32,128]{2,1,0:T(8,128)(2,1)S(1)}, u32[]{:S(2)}, u32[]{:S(2)}) %collective-permute-start.7) | collective-permute-done | bytes 139296 | tf_op jit(solution)/shard_map/ppermute | solution.py:545
  27.4 1.1 %unpack.3 = bf16[4,2,9,2,32,128]{5,4,3,2,1,0:T(8,128)(2,1)} custom-call(bf16[17,32,128]{2,1,0:T(8,128)(2,1)S(1)} %collective-permute-done.6.refs_0_, bf16[17,32,128]{2,1,0:T(8,128)(2,1)S(1)} %collective-permute-done.7.refs_1_, bf16[4,2,9,2,32,128]{5,4,3,2,1,0:T(8,128)(2,1)} %place.1.refs_2_), custom_call_target="tpu_custom_call", output_to_operand_aliasing={{}: (2, {})} | custom-call | flops 1 | bytes 1 | tf_op jit(solution)/shard_map/unpack/pallas_call | solution.py:438
  (3 shorter events, 0.0 us)
Async XLA Ops:
  1.4 16.6 %collective-permute-start = (bf16[2,528,128]{2,1,0:T(8,128)(2,1)S(1)}, bf16[2,528,128]{2,1,0:T(8,128)(2,1)S(1)}, u32[]{:S(2)}, u32[]{:S(2)}) collective-permute-start(bf16[2,528,128]{2,1,0:T(8,128)(2,1)S(1)} %get-tuple-element.31), channel_id=1, source_target_pairs={{0,4},{1,5},{2,6},{3,7},{4,0},{5,1},{6,2},{7,3},{8,12},{9,13},{10,... | collective-permute-start | bytes 811016 | tf_op jit(solution)/shard_map/ppermute | solution.py:541
  1.5 16.5 %collective-permute-start.1 = (bf16[2,528,128]{2,1,0:T(8,128)(2,1)S(1)}, bf16[2,528,128]{2,1,0:T(8,128)(2,1)S(1)}, u32[]{:S(2)}, u32[]{:S(2)}) collective-permute-start(bf16[2,528,128]{2,1,0:T(8,128)(2,1)S(1)} %get-tuple-element.32), channel_id=1, source_target_pairs={{0,1},{1,0},{2,3},{3,2},{4,8},{5,9},{6,10},{7,11},{8,4},{9,5},{10,... | collective-permute-start | bytes 811016 | tf_op jit(solution)/shard_map/ppermute | solution.py:541
  3.9 14.0 %collective-permute-start.2 = (bf16[2,528,128]{2,1,0:T(8,128)(2,1)S(1)}, bf16[2,528,128]{2,1,0:T(8,128)(2,1)S(1)}, u32[]{:S(2)}, u32[]{:S(2)}) collective-permute-start(bf16[2,528,128]{2,1,0:T(8,128)(2,1)S(1)} %get-tuple-element.33), channel_id=1, source_target_pairs={{0,8},{1,2},{2,1},{3,11},{4,12},{5,6},{6,5},{7,15},{8,0},{9,10},{1... | collective-permute-start | bytes 811016 | tf_op jit(solution)/shard_map/ppermute | solution.py:541
  6.3 5.2 %collective-permute-start.4 = (bf16[2,528,128]{2,1,0:T(8,128)(2,1)S(1)}, bf16[2,528,128]{2,1,0:T(8,128)(2,1)S(1)}, u32[]{:S(2)}, u32[]{:S(2)}) collective-permute-start(bf16[2,528,128]{2,1,0:T(8,128)(2,1)S(1)} %get-tuple-element.36), channel_id=1, source_target_pairs={{0,1},{1,0},{2,3},{3,2},{4,5},{5,4},{6,7},{7,6},{8,9},{9,8},{10,11... | collective-permute-start | bytes 811016 | tf_op jit(solution)/shard_map/ppermute | solution.py:541
  11.3 1.6 %collective-permute-start.5 = (bf16[2,128,512]{2,1,0:T(8,128)(2,1)S(1)}, bf16[2,128,512]{2,1,0:T(8,128)(2,1)S(1)}, u32[]{:S(2)}, u32[]{:S(2)}) collective-permute-start(bf16[2,128,512]{2,1,0:T(8,128)(2,1)S(1)} %get-tuple-element.41), channel_id=1, source_target_pairs={{0,1},{1,0},{2,3},{3,2},{4,5},{5,4},{6,7},{7,6},{8,9},{9,8},{10,11... | collective-permute-start | bytes 786440 | tf_op jit(solution)/shard_map/ppermute | solution.py:541
  11.4 6.6 %collective-permute-start.3 = (bf16[2,128,512]{2,1,0:T(8,128)(2,1)S(1)}, bf16[2,128,512]{2,1,0:T(8,128)(2,1)S(1)}, u32[]{:S(2)}, u32[]{:S(2)}) collective-permute-start(bf16[2,128,512]{2,1,0:T(8,128)(2,1)S(1)} %get-tuple-element.34), channel_id=1, source_target_pairs={{0,8},{1,2},{2,1},{3,11},{4,12},{5,6},{6,5},{7,15},{8,0},{9,10},{1... | collective-permute-start | bytes 786440 | tf_op jit(solution)/shard_map/ppermute | solution.py:541
  12.9 8.0 %collective-permute-start.8 = (bf16[2,4,32,128]{3,2,1,0:T(8,128)(2,1)S(1)}, bf16[2,4,32,128]{3,2,1,0:T(8,128)(2,1)S(1)}, u32[]{:S(2)}, u32[]{:S(2)}) collective-permute-start(bf16[2,4,32,128]{3,2,1,0:T(8,128)(2,1)S(1)} %get-tuple-element.49), channel_id=1, source_target_pairs={{0,2},{1,3},{2,0},{3,1},{4,6},{5,7},{6,4},{7,5},{8,10},{9,11},{10,... | collective-permute-start | bytes 196616 | tf_op jit(solution)/shard_map/ppermute | solution.py:545
  19.0 5.2 %collective-permute-start.6 = (bf16[17,32,128]{2,1,0:T(8,128)(2,1)S(1)}, bf16[17,32,128]{2,1,0:T(8,128)(2,1)S(1)}, u32[]{:S(2)}, u32[]{:S(2)}) collective-permute-start(bf16[17,32,128]{2,1,0:T(8,128)(2,1)S(1)} %get-tuple-element.45), channel_id=1, source_target_pairs={{0,2},{1,3},{2,0},{3,1},{4,6},{5,7},{6,4},{7,5},{8,10},{9,11},{10,... | collective-permute-start | bytes 417800 | tf_op jit(solution)/shard_map/ppermute | solution.py:545
  19.0 8.4 %collective-permute-start.7 = (bf16[17,32,128]{2,1,0:T(8,128)(2,1)S(1)}, bf16[17,32,128]{2,1,0:T(8,128)(2,1)S(1)}, u32[]{:S(2)}, u32[]{:S(2)}) collective-permute-start(bf16[17,32,128]{2,1,0:T(8,128)(2,1)S(1)} %get-tuple-element.46), channel_id=1, source_target_pairs={{0,3},{1,2},{2,1},{3,0},{4,7},{5,6},{6,5},{7,4},{8,11},{9,10},{10,... | collective-permute-start | bytes 417800 | tf_op jit(solution)/shard_map/ppermute | solution.py:545
  21.0 1.4 %collective-permute-start.10 = (bf16[17,32,128]{2,1,0:T(8,128)(2,1)S(1)}, bf16[17,32,128]{2,1,0:T(8,128)(2,1)S(1)}, u32[]{:S(2)}, u32[]{:S(2)}) collective-permute-start(bf16[17,32,128]{2,1,0:T(8,128)(2,1)S(1)} %get-tuple-element.52), channel_id=1, source_target_pairs={{0,1},{1,0},{2,3},{3,2},{4,5},{5,4},{6,7},{7,6},{8,9},{9,8},{10,11... | collective-permute-start | bytes 417800 | tf_op jit(solution)/shard_map/ppermute | solution.py:545
  21.0 2.5 %collective-permute-start.9 = (bf16[2,4,32,128]{3,2,1,0:T(8,128)(2,1)S(1)}, bf16[2,4,32,128]{3,2,1,0:T(8,128)(2,1)S(1)}, u32[]{:S(2)}, u32[]{:S(2)}) collective-permute-start(bf16[2,4,32,128]{3,2,1,0:T(8,128)(2,1)S(1)} %pad_maximum_fusion), channel_id=1, source_target_pairs={{0,1},{1,0},{2,3},{3,2},{4,5},{5,4},{6,7},{7,6},{8,9},{9,8},{10,11... | collective-permute-start | bytes 196616 | tf_op jit(solution)/shard_map/ppermute | solution.py:545

commit v5 on v4

--- a/solution.py
+++ b/solution.py
@@ -11,8 +11,9 @@
 KA = 12
 SIDE = 4
 QUAD = 4 * BS
-HEAD = 16
-ROWS = HEAD + QUAD
+HEAD = 8
+ROWS = 2 * QUAD + HEAD
+BITS = 16
 OWN_SLOTS = 4
 SLOTS = 16
 ANY = pl.BlockSpec(memory_space=pl.ANY)
@@ -48,7 +49,7 @@
                 copies.append(
                     pltpu.make_async_copy(
                         prolong.at[2 * ur + m, pl.ds(pl.multiple_of(vr * 256, 256), 256), :],
-                        out.at[h, HEAD + 256 * m : HEAD + 256 * (m + 1), :],
+                        out.at[QUAD * h + 256 * m : QUAD * h + 256 * (m + 1), :],
                         sems.at[len(copies)],
                     )
                 )
@@ -60,14 +61,14 @@
         bits[k : k + 1, :] = jnp.full((1, BS), own[u, v], F32)
     bits[4:, :] = jnp.zeros((4, BS), F32)
     for out, quads in plans:
-        for h, quad in enumerate(quads):
-            out[h, 0:HEAD, :] = jnp.full((HEAD, BS), own[quad], F32).astype(BF16)
+        at = lax.broadcasted_iota(jnp.int32, (HEAD, BS), 0)
+        out[2 * QUAD :, :] = jnp.where(at == 0, own[quads[0]], own[quads[1]]).astype(BF16)
     for copy in copies:
         copy.wait()
 
 
 def rims(agg, prolong_rows):
-    shape = jax.ShapeDtypeStruct((2, ROWS, BS), BF16)
+    shape = jax.ShapeDtypeStruct((ROWS, BS), BF16)
     return pl.pallas_call(
         rims_kernel,
         out_shape=(shape,) * 4 + (jax.ShapeDtypeStruct((8, BS), F32),),
@@ -104,9 +105,11 @@
         at = pl.ds(first * KA, 2 * KA)
         return pltpu.make_async_copy(coupling.at[at], blocks.at[at], sems.at[2 * quad + m])
 
-    for quad in range(4):
+    def start(quad):
         for m in range(2):
             load(quad, m).start()
+
+    start(0)
     blocks[NONE] = jnp.zeros((BS, BS), BF16)
 
     @pl.loop(0, 16)
@@ -114,6 +117,7 @@
         for t in range(25):
             slot_of[n * 25 + t] = NONE
 
+    start(1)
     load_codes.wait()
 
     @pl.loop(0, 16)
@@ -121,6 +125,7 @@
         for k in range(KA):
             slot_of[n * 25 + codes[n // SIDE, n % SIDE, k]] = n * KA + k
 
+    start(2)
     load_prolong.wait()
     zero = jnp.zeros((BS, BS), BF16)
 
@@ -129,6 +134,11 @@
         qx, qy = quad // 2, quad % 2
         for m in range(2):
             load(quad, m).wait()
+
+        @pl.when(quad == 0)
+        def _():
+            start(3)
+
         left = []
         for ix in range(2):
             rows = prolong[2 * qx + ix, pl.ds(pl.multiple_of(qy * 256, 256), 256), :]
@@ -192,17 +202,21 @@
     )(codes, coupling, prolong_rows, after)
 
 
-def half_of(ref):
-    return ref[0:1, :].astype(F32)
+def half_of(ref, h):
+    return ref[2 * QUAD + h : 2 * QUAD + h + 1, :].astype(F32)
+
+
+def quad_of(ref, h):
+    return ref[QUAD * h : QUAD * (h + 1), :]
 
 
 def edge_slots(near, far, same_a):
-    same_b = 1.0 - jnp.abs(half_of(far[0]) - half_of(far[1]))
-    second = far[1][HEAD:, :]
+    same_b = 1.0 - jnp.abs(half_of(far, 0) - half_of(far, 1))
+    second = quad_of(far, 1)
     shared = second * same_b.astype(BF16)
     right = jnp.concatenate(
         [
-            jnp.concatenate([far[0][HEAD:, :], jnp.zeros_like(second)], axis=1),
+            jnp.concatenate([quad_of(far, 0), jnp.zeros_like(second)], axis=1),
             jnp.concatenate([shared, second - shared], axis=1),
         ],
         axis=0,
@@ -223,12 +237,13 @@
 
 
 def store_pieces(outs, at, values):
-    rows = outs[0].shape[1]
+    rows = BS // len(outs)
     me = lax.axis_index("col")
     for s, out in enumerate(outs):
         start = pl.multiple_of((me ^ s) * rows, rows)
         for t in range(values.shape[0]):
-            out[at + t] = values[t, pl.ds(start, rows), :].astype(BF16)
+            first = (at + t) * rows
+            out[first : first + rows, :] = values[t, pl.ds(start, rows), :].astype(BF16)
 
 
 def near_kernel(parts, bits, r, prolong, after, *rest):
@@ -293,56 +308,77 @@
     )(*operands)
 
 
-def far_kernel(counts, bits, r, row_a, row_b, col_a, col_b, from_a, from_b, *rest):
+def fill_edges(r, edges, slots, head):
+    for e, (far, own, quads, same_a, scale) in enumerate(edges):
+        base, extra = edge_slots([sums(r, p, quads) for p in own], far, same_a)
+        for t in range(2):
+            slots[2 * e + t] = base[t] if scale is None else base[t] * scale
+            slots[4 + 2 * e + t] = extra[t] if scale is None else extra[t] * scale
+            head[2 * e + t : 2 * e + t + 1, :] = half_of(far, t)
+
+
+def mid_kernel(parts, bits, r, col_a, col_b, slots, head):
+    split_y = jnp.abs(bits[0:1, :] - bits[1:2, :])
+    edges = (
+        (col_a, ((1, 2), (2, 2)), ((1, 3), (2, 3)), split_y, None),
+        (col_b, ((1, 1), (2, 1)), ((1, 0), (2, 0)), split_y, inside("col", parts)),
+    )
+    fill_edges(r, edges, slots, head)
+    head[4:8, :] = bits[0:4, :]
+
+
+def mid_terms(parts, *operands):
+    return pl.pallas_call(
+        functools.partial(mid_kernel, parts),
+        out_shape=(jax.ShapeDtypeStruct((8, BS, BS), F32), jax.ShapeDtypeStruct((8, BS), F32)),
+        in_specs=[VMEM] * len(operands),
+        out_specs=(VMEM, VMEM),
+        compiler_params=pltpu.CompilerParams(vmem_limit_bytes=8 << 20),
+        cost_estimate=pl.CostEstimate(flops=1, bytes_accessed=1, transcendentals=0),
+        name="mid_terms",
+    )(*operands)
+
+
+def far_kernel(counts, bits, r, row_a, row_b, from_a, from_b, columns, column_head, *rest):
     outs, (slots, head) = rest[:-2], rest[-2:]
-    split_y = jnp.abs(bits[0:1, :] - bits[1:2, :])
-    split_x = 1.0 - split_y
+    split_x = 1.0 - jnp.abs(bits[0:1, :] - bits[1:2, :])
     row_in, col_in = inside("row", counts[0]), inside("col", counts[1])
     head[...] = jnp.zeros_like(head)
     head[0:4, :] = bits[0:4, :]
+    head[8:12, :] = column_head[0:4, :]
     edges = (
         (row_a, ((2, 1), (2, 2)), ((3, 1), (3, 2)), split_x, None),
         (row_b, ((1, 1), (1, 2)), ((0, 1), (0, 2)), split_x, row_in),
-        (col_a, ((1, 2), (2, 2)), ((1, 3), (2, 3)), split_y, None),
-        (col_b, ((1, 1), (2, 1)), ((1, 0), (2, 0)), split_y, col_in),
     )
-    for e, (far, own, quads, same_a, scale) in enumerate(edges):
-        base, extra = edge_slots([sums(r, p, quads) for p in own], [far.at[0], far.at[1]], same_a)
-        for t in range(2):
-            slots[2 * e + t] = base[t] if scale is None else base[t] * scale
-            more = extra[t] if scale is None else extra[t] * scale
-            if e < 2:
-                slots[12 + 2 * e + t] = more
-            else:
-                slots[8 + 2 * e + t] += more
-            head[4 + 2 * e + t : 5 + 2 * e + t, :] = half_of(far.at[t])
+    fill_edges(r, edges, slots, head.at[4:8])
+    for t in range(4):
+        slots[4 + t] += columns[4 + t]
     corners = (
-        (from_a.at[0], row_a.at[1], None),
-        (from_b.at[0], row_a.at[0], col_in),
-        (from_a.at[1], row_b.at[1], row_in),
-        (from_b.at[1], row_b.at[0], row_in * col_in),
+        (from_a.at[0], quad_of(row_a, 1), None),
+        (from_b.at[0], quad_of(row_a, 0), col_in),
+        (from_a.at[1], quad_of(row_b, 1), row_in),
+        (from_b.at[1], quad_of(row_b, 0), row_in * col_in),
     )
     for e, (near, far, scale) in enumerate(corners):
-        value = jnp.dot(near[...], far[HEAD:, :], preferred_element_type=F32)
+        value = jnp.dot(near[...], far, preferred_element_type=F32)
         slots[8 + e] = value if scale is None else value * scale
-    store_pieces(outs, 0, slots)
-    rows = outs[0].shape[1]
+    store_pieces(outs, 0, slots.at[0:4])
+    store_pieces(outs, 4, columns.at[0:4])
+    store_pieces(outs, 8, slots.at[8:12])
+    store_pieces(outs, 12, slots.at[4:8])
     for out in outs:
-        for t in range(out.shape[0] - SLOTS):
-            out[SLOTS + t] = head[t * rows : (t + 1) * rows, :].astype(BF16)
+        out[out.shape[0] - BITS :, :] = head[...].astype(BF16)
 
 
 def far_terms(counts, *operands):
     parts = counts[1]
-    rows = BS // parts
-    heads = -(-HEAD // rows)
-    message = jax.ShapeDtypeStruct((SLOTS + heads, rows, BS), BF16)
+    message = jax.ShapeDtypeStruct((SLOTS * (BS // parts) + BITS, BS), BF16)
     return pl.pallas_call(
         functools.partial(far_kernel, counts),
         out_shape=(message,) * parts,
         in_specs=[VMEM] * len(operands),
         out_specs=(VMEM,) * parts,
-        scratch_shapes=[pltpu.VMEM((SLOTS, BS, BS), F32), pltpu.VMEM((heads * rows, BS), F32)],
+        scratch_shapes=[pltpu.VMEM((12, BS, BS), F32), pltpu.VMEM((BITS, BS), F32)],
         compiler_params=pltpu.CompilerParams(vmem_limit_bytes=16 << 20),
         cost_estimate=pl.CostEstimate(flops=1, bytes_accessed=1, transcendentals=0),
         name="far_terms",
@@ -399,11 +435,8 @@
         split_y = jnp.abs(one(0) - one(1))
 
         def send(piece, owner, code):
-            for a in range(2):
-                copies.append(
-                    pltpu.make_async_copy(buf.at[i, piece, a], out.at[owner, a, code], sems.at[len(copies)])
-                )
-                copies[-1].start()
+            copies.append(pltpu.make_async_copy(buf.at[i, piece], out.at[owner, :, code], sems.at[len(copies)]))
+            copies[-1].start()
 
         split_x = 1.0 - split_y
         edges = (
@@ -425,7 +458,7 @@
             (low, 6 * fx, 0, 10, 6),
         )
         for e, (owner, group, side, a_bit, b_bit) in enumerate(corners):
-            spread_corner(buf, (i, 4 + e), ref[8 + e].astype(F32), one(a_bit), one(b_bit))
+            spread_corner(buf, (i, 4 + e), slot(ref, 8 + e), one(a_bit), one(b_bit))
             send(4 + e, owner, group + turn3(side, lax.rem(owner, 2)))
     for copy in copies:
         copy.wait()
@@ -433,7 +466,7 @@
 
 def unpack(messages, steps, coarse):
     parts = lax.axis_size("col")
-    rows = messages[0].shape[1]
+    rows = BS // parts
     fresh = coarse is None
     return pl.pallas_call(
         functools.partial(unpack_kernel, parts, steps),
@@ -442,7 +475,7 @@
         out_specs=ANY,
         scratch_shapes=[
             pltpu.VMEM((len(steps), 8, 2, 2, rows, BS), BF16),
-            pltpu.SemaphoreType.DMA((16 * len(steps),)),
+            pltpu.SemaphoreType.DMA((8 * len(steps),)),
         ],
         input_output_aliases={} if fresh else {len(steps): 0},
         compiler_params=pltpu.CompilerParams(vmem_limit_bytes=16 << 20),
@@ -456,8 +489,13 @@
 
 
 def bit_row(ref, k):
-    rows = ref.shape[1]
-    return ref[SLOTS + k // rows, k % rows : k % rows + 1, :].astype(F32)
+    at = ref.shape[0] - BITS + k
+    return ref[at : at + 1, :].astype(F32)
+
+
+def slot(ref, t):
+    rows = (ref.shape[0] - BITS) // SLOTS
+    return ref[t * rows : (t + 1) * rows, :].astype(F32)
 
 
 def spread(buf, at, center):
@@ -470,8 +508,8 @@
 def spread_edge(buf, at, ref, one, ps, qs, base, extra, used):
     a_bits = [one(p) for p in ps]
     b_bits = [one(q) for q in qs]
-    values = [ref[t].astype(F32) for t in base]
-    more = [ref[t].astype(F32) for t in extra]
+    values = [slot(ref, t) for t in base]
+    more = [slot(ref, t) for t in extra]
     center = [None] * 4
     for b in range(2):
         picks = [bit if b else 1.0 - bit for bit in b_bits]
@@ -563,8 +601,9 @@
     mine, pair, *cross = near_terms(parts, bits, r, own_blocks, col_a)
     from_a, *cross = lax.optimization_barrier((from_a, *cross))
     direct = [xor_swap(value, 2 * h + 2) for h, value in enumerate(cross)]
-    row_a, row_b, col_b, from_b = gate((row_a, row_b, col_b, from_b), (mine,))
-    outs = list(far_terms(counts, bits, r, row_a, row_b, col_a, col_b, from_a, from_b))
+    columns, column_head = mid_terms(parts, bits, r, col_a, col_b)
+    row_a, row_b, columns, from_b = gate((row_a, row_b, columns, from_b), (mine,))
+    outs = list(far_terms(counts, bits, r, row_a, row_b, from_a, from_b, columns, column_head))
     outs[0], *direct = lax.optimization_barrier((outs[0], *direct))
     outs = [outs[0]] + [xor_swap(outs[s], s) for s in range(1, parts)]
     relayed = xor_swap(jnp.stack([pair] + [value[1] for value in direct]), 1)

time: 28.7 us -> 28 us (0.976)
  waiting for transfers between devices: 9.27 us -> 7.89 us
  starting transfers between devices: 8.5 us -> 9.33 us
    ppermute x6, waiting for transfers between devices: 5.29 us -> 3.58 us  [swap(): return lax.ppermute(value, ('row', 'col'), pairs)]
    ppermute x6, starting transfers between devices: 5.59 us -> 6.74 us  [swap(): return lax.ppermute(value, ('row', 'col'), pairs)]
    pallas_call x0 -> x1, Pallas kernels: none -> 0.46 us  [mid_terms(): pl.pallas_call(functools.partial(mid_kernel, parts), out_shape=(jax.Shape...]
    ppermute x5, starting transfers between devices: 2.91 us -> 2.58 us  [xor_swap(): lax.ppermute(value, 'col', [(i, i ^ s) for i in range(lax.axis_size('col'...]
    ppermute x5, waiting for transfers between devices: 3.98 us -> 4.31 us  [xor_swap(): lax.ppermute(value, 'col', [(i, i ^ s) for i in range(lax.axis_size('col'...]
    pallas_call x1, Pallas kernels: 0.95 us -> 0.63 us  [far_terms(): pl.pallas_call(functools.partial(far_kernel, counts), out_shape=(message,...]
    pallas_call x2, Pallas kernels: 2.23 us -> 1.94 us  [unpack(): pl.pallas_call(functools.partial(unpack_kernel, parts, steps), out_shape=...]
  transfers between devices with their start and end apart: 11 -> 11, of which waited for: 4 -> 4; matrix products, arithmetic and copies ran while one was open for 0% -> 0% of each run, Pallas kernels for 28% -> 29%
where the time goes in v5:
time: 28 us; the launch traced here: 27.8 us
  Pallas kernels  10.5 us (38%)
  starting transfers between devices  9.33 us (33%)
  waiting for transfers between devices  7.89 us (28%)
    ppermute x6, starting transfers between devices, swap(): return lax.ppermute(value, ('row', 'col'), pairs)  6.74 us
    pallas_call x1, Pallas kernels, step_one(): pl.pallas_call(step_one_kernel, out_shape=(jax.ShapeDtypeStruct((4, 9, BS...  4.57 us
    ppermute x5, waiting for transfers between devices, xor_swap(): lax.ppermute(value, 'col', [(i, i ^ s) for i in range(lax.axis_size('col'...  4.31 us
    ppermute x6, waiting for transfers between devices, swap(): return lax.ppermute(value, ('row', 'col'), pairs)  3.58 us
    ppermute x5, starting transfers between devices, xor_swap(): lax.ppermute(value, 'col', [(i, i ^ s) for i in range(lax.axis_size('col'...  2.58 us
    pallas_call x2, Pallas kernels, unpack(): pl.pallas_call(functools.partial(unpack_kernel, parts, steps), out_shape=...  1.94 us
    pallas_call x1, Pallas kernels, rims(): pl.pallas_call(rims_kernel, out_shape=(shape,) * 4 + (jax.ShapeDtypeStruc...  1.38 us
    pallas_call x1, Pallas kernels, near_terms(): pl.pallas_call(functools.partial(near_kernel, parts), out_shape=shapes, i...  0.76 us
  transfers between devices with their start and end apart: 11, of which 4 were waited for; matrix products, arithmetic and copies ran while one was open for 0% of the time, Pallas kernels for 29%

profile of v5, /device:TPU:5, one launch (start us, length us, event | category | flops | bytes accessed | tf_op | source)
XLA Modules:
  0.0 27.8 jit_solution(18179075825143677362)
XLA Ops:
  0.0 1.4 %rims.1 = (bf16[1032,128]{1,0:T(8,128)(2,1)S(1)}, bf16[1032,128]{1,0:T(8,128)(2,1)S(1)}, bf16[1032,128]{1,0:T(8,128)(2,1)S(1)}, bf16[1032,128]{1,0:T(8,128)(2,1)S(1)}, f32[8,128]{1,0:T(8,128)S(1)}) custom-call(s32[4,4]{1,0:T(4,128)} %agg_hbm.1, bf16[4,512,128]{2,1,0:T(8,128)(2,1)} %bitcast.5), custom_call_target="tpu_custom_call" | custom-call | tf_op jit(solution)/shard_map/rims/pallas_call | solution.py:72
  1.4 0.1 collective-permute-start
  1.5 2.5 %collective-permute-start.1 = (bf16[1032,128]{1,0:T(8,128)(2,1)S(1)}, bf16[1032,128]{1,0:T(8,128)(2,1)S(1)}, u32[]{:S(2)}, u32[]{:S(2)}) collective-permute-start(bf16[1032,128]{1,0:T(8,128)(2,1)S(1)} %get-tuple-element.34), channel_id=1, source_target_pairs={{0,1},{1,0},{2,3},{3,2},{4,8},{5,9},{6,10},{7,11},{8,4},{9,5},{10,... | collective-permute-start | bytes 792584 | tf_op jit(solution)/shard_map/ppermute | solution.py:579
  3.9 1.2 %collective-permute-start.2 = (bf16[1032,128]{1,0:T(8,128)(2,1)S(1)}, bf16[1032,128]{1,0:T(8,128)(2,1)S(1)}, u32[]{:S(2)}, u32[]{:S(2)}) collective-permute-start(bf16[1032,128]{1,0:T(8,128)(2,1)S(1)} %get-tuple-element.35), channel_id=1, source_target_pairs={{0,1},{1,0},{2,3},{3,2},{4,5},{5,4},{6,7},{7,6},{8,9},{9,8},{10,11... | collective-permute-start | bytes 792584 | tf_op jit(solution)/shard_map/ppermute | solution.py:579
  5.2 1.1 %collective-permute-start.3 = (bf16[1032,128]{1,0:T(8,128)(2,1)S(1)}, bf16[1032,128]{1,0:T(8,128)(2,1)S(1)}, u32[]{:S(2)}, u32[]{:S(2)}) collective-permute-start(bf16[1032,128]{1,0:T(8,128)(2,1)S(1)} %get-tuple-element.36), channel_id=1, source_target_pairs={{0,8},{1,2},{2,1},{3,11},{4,12},{5,6},{6,5},{7,15},{8,0},{9,10},{1... | collective-permute-start | bytes 792584 | tf_op jit(solution)/shard_map/ppermute | solution.py:579
  6.3 4.6 %step_one.1 = (bf16[4,9,128,512]{3,2,1,0:T(8,128)(2,1)S(1)}, bf16[2,128,512]{2,1,0:T(8,128)(2,1)S(1)}, bf16[2,128,512]{2,1,0:T(8,128)(2,1)S(1)}, bf16[4,512,128]{2,1,0:T(8,128)(2,1)S(1)}) custom-call(s32[4,4,12]{2,1,0:T(4,128)} %codes_hbm.1, bf16[192,128,128]{2,1,0:T(8,128)(2,1)} %bitcast.7, bf16[4,512,128]{2,1,0:T(8,128)(2,1)} %bitcast.6, ...), custom_call_target="tpu_custom_call" | custom-call | flops 8589934592 | bytes 1048576 | tf_op jit(solution)/shard_map/step_one/pallas_call | solution.py:183
  10.8 0.5 %collective-permute-start.5 = (bf16[2,128,512]{2,1,0:T(8,128)(2,1)S(1)}, bf16[2,128,512]{2,1,0:T(8,128)(2,1)S(1)}, u32[]{:S(2)}, u32[]{:S(2)}) collective-permute-start(bf16[2,128,512]{2,1,0:T(8,128)(2,1)S(1)} %get-tuple-element.43), channel_id=1, source_target_pairs={{0,1},{1,0},{2,3},{3,2},{4,5},{5,4},{6,7},{7,6},{8,9},{9,8},{10,11... | collective-permute-start | bytes 786440 | tf_op jit(solution)/shard_map/ppermute | solution.py:579
  11.4 0.0 collective-permute-done.2.col_a.after
  11.4 1.3 %collective-permute-start.4 = (bf16[2,128,512]{2,1,0:T(8,128)(2,1)S(1)}, bf16[2,128,512]{2,1,0:T(8,128)(2,1)S(1)}, u32[]{:S(2)}, u32[]{:S(2)}) collective-permute-start(bf16[2,128,512]{2,1,0:T(8,128)(2,1)S(1)} %get-tuple-element.38), channel_id=1, source_target_pairs={{0,8},{1,2},{2,1},{3,11},{4,12},{5,6},{6,5},{7,15},{8,0},{9,10},{1... | collective-permute-start | bytes 786440 | tf_op jit(solution)/shard_map/ppermute | solution.py:579
  12.7 0.8 %near_terms.1 = (bf16[4,32,128]{2,1,0:T(8,128)(2,1)S(1)}, bf16[4,32,128]{2,1,0:T(8,128)(2,1)S(1)}, bf16[2,4,32,128]{3,2,1,0:T(8,128)(2,1)S(1)}) custom-call(f32[8,128]{1,0:T(8,128)S(1)} %get-tuple-element.31.after.bits, bf16[4,9,128,512]{3,2,1,0:T(8,128)(2,1)S(1)} %get-tuple-element.32.r, bf16[4,512,128]{2,1,0:T(8,128)(2,1)S(1)} %get-tuple-element.39.prolong, ...), custom_call_target="tpu_custom_call" | custom-call | flops 1 | bytes 1 | tf_op jit(solution)/shard_map/near_terms/pallas_call | solution.py:299
  13.5 0.0 collective-permute-done.5.from_a
  13.5 0.4 %collective-permute-start.8 = (bf16[2,4,32,128]{3,2,1,0:T(8,128)(2,1)S(1)}, bf16[2,4,32,128]{3,2,1,0:T(8,128)(2,1)S(1)}, u32[]{:S(2)}, u32[]{:S(2)}) collective-permute-start(bf16[2,4,32,128]{3,2,1,0:T(8,128)(2,1)S(1)} %get-tuple-element.53), channel_id=1, source_target_pairs={{0,2},{1,3},{2,0},{3,1},{4,6},{5,7},{6,4},{7,5},{8,10},{9,11},{10,... | collective-permute-start | bytes 196616 | tf_op jit(solution)/shard_map/ppermute | solution.py:583
  13.9 0.0 collective-permute-done.3.col_b
  13.9 0.5 %mid_terms.1 = (f32[8,128,128]{2,1,0:T(8,128)S(1)}, f32[8,128]{1,0:T(8,128)S(1)}) custom-call(f32[8,128]{1,0:T(8,128)S(1)} %get-tuple-element.31.after.bits, bf16[4,9,128,512]{3,2,1,0:T(8,128)(2,1)S(1)} %get-tuple-element.32.r, bf16[1032,128]{1,0:T(8,128)(2,1)S(1)} %collective-permute-done.2.col_a.after, bf16[1032,128]{1,0:T(8,128)(2,1)S(1)} %collective-permute-done.3.col_b), custom_call_target="tpu_custom_call" | custom-call | flops 1 | bytes 1 | tf_op jit(solution)/shard_map/mid_terms/pallas_call | solution.py:331
  14.3 3.6 %collective-permute-done.4.refs_3_ = bf16[2,128,512]{2,1,0:T(8,128)(2,1)S(1)} collective-permute-done((bf16[2,128,512]{2,1,0:T(8,128)(2,1)S(1)}, bf16[2,128,512]{2,1,0:T(8,128)(2,1)S(1)}, u32[]{:S(2)}, u32[]{:S(2)}) %collective-permute-start.4) | collective-permute-done | bytes 262176 | tf_op jit(solution)/shard_map/ppermute | solution.py:579
  17.9 0.0 collective-permute-done.refs_0_
  17.9 0.0 collective-permute-done.1.refs_1_
  17.9 0.6 %far_terms.1 = (bf16[528,128]{1,0:T(8,128)(2,1)S(1)}, bf16[528,128]{1,0:T(8,128)(2,1)S(1)}, bf16[528,128]{1,0:T(8,128)(2,1)S(1)}, bf16[528,128]{1,0:T(8,128)(2,1)S(1)}) custom-call(f32[8,128]{1,0:T(8,128)S(1)} %get-tuple-element.31.after.bits, bf16[4,9,128,512]{3,2,1,0:T(8,128)(2,1)S(1)} %get-tuple-element.32.r, ...), custom_call_target="tpu_custom_call" | custom-call | flops 1 | bytes 1 | tf_op jit(solution)/shard_map/far_terms/pallas_call | solution.py:376
  18.5 0.1 collective-permute-start.6
  18.6 1.5 %collective-permute-start.7 = (bf16[528,128]{1,0:T(8,128)(2,1)S(1)}, bf16[528,128]{1,0:T(8,128)(2,1)S(1)}, u32[]{:S(2)}, u32[]{:S(2)}) collective-permute-start(bf16[528,128]{1,0:T(8,128)(2,1)S(1)} %get-tuple-element.50), channel_id=1, source_target_pairs={{0,3},{1,2},{2,1},{3,0},{4,7},{5,6},{6,5},{7,4},{8,11},{9,10},{10,... | collective-permute-start | bytes 405512 | tf_op jit(solution)/shard_map/ppermute | solution.py:583
  20.2 0.3 collective-permute-start.10
  20.5 0.0 collective-permute-done.8.rest_0_
  20.5 0.3 %collective-permute-start.9 = (bf16[2,4,32,128]{3,2,1,0:T(8,128)(2,1)S(1)}, bf16[2,4,32,128]{3,2,1,0:T(8,128)(2,1)S(1)}, u32[]{:S(2)}, u32[]{:S(2)}) collective-permute-start(bf16[2,4,32,128]{3,2,1,0:T(8,128)(2,1)S(1)} %pad_maximum_fusion), channel_id=1, source_target_pairs={{0,1},{1,0},{2,3},{3,2},{4,5},{5,4},{6,7},{7,6},{8,9},{9,8},{10,11... | collective-permute-start | bytes 196616 | tf_op jit(solution)/shard_map/ppermute | solution.py:583
  20.8 0.8 %collective-permute-done.10.refs_1_ = bf16[528,128]{1,0:T(8,128)(2,1)S(1)} collective-permute-done((bf16[528,128]{1,0:T(8,128)(2,1)S(1)}, bf16[528,128]{1,0:T(8,128)(2,1)S(1)}, u32[]{:S(2)}, u32[]{:S(2)}) %collective-permute-start.10) | collective-permute-done | bytes 135200 | tf_op jit(solution)/shard_map/ppermute | solution.py:583
  21.5 1.0 %unpack.2.rest_1_ = bf16[4,2,9,2,32,128]{5,4,3,2,1,0:T(8,128)(2,1)} custom-call(bf16[528,128]{1,0:T(8,128)(2,1)S(1)} %get-tuple-element.55.refs_0_, bf16[528,128]{1,0:T(8,128)(2,1)S(1)} %collective-permute-done.10.refs_1_), custom_call_target="tpu_custom_call" | custom-call | flops 1 | bytes 1 | tf_op jit(solution)/shard_map/unpack/pallas_call | solution.py:471
  22.5 0.0 collective-permute-done.9.relayed
  22.5 0.7 %place.1.refs_2_ = bf16[4,2,9,2,32,128]{5,4,3,2,1,0:T(8,128)(2,1)} custom-call(bf16[4,32,128]{2,1,0:T(8,128)(2,1)S(1)} %get-tuple-element.40.refs_4_.own, bf16[2,4,32,128]{3,2,1,0:T(8,128)(2,1)S(1)} %collective-permute-done.9.relayed, bf16[2,4,32,128]{3,2,1,0:T(8,128)(2,1)S(1)} %collective-permute-done.8.rest_0_, ...), custom_call_target="tpu_custom_call", output_to_operand_aliasing={{}: (3, {})} | custom-call | flops 1 | bytes 1 | tf_op jit(solution)/shard_map/place/pallas_call | solution.py:412
  23.3 0.6 %collective-permute-done.6.refs_0_ = bf16[528,128]{1,0:T(8,128)(2,1)S(1)} collective-permute-done((bf16[528,128]{1,0:T(8,128)(2,1)S(1)}, bf16[528,128]{1,0:T(8,128)(2,1)S(1)}, u32[]{:S(2)}, u32[]{:S(2)}) %collective-permute-start.6) | collective-permute-done | bytes 135200 | tf_op jit(solution)/shard_map/ppermute | solution.py:583
  23.9 2.9 %collective-permute-done.7.refs_1_ = bf16[528,128]{1,0:T(8,128)(2,1)S(1)} collective-permute-done((bf16[528,128]{1,0:T(8,128)(2,1)S(1)}, bf16[528,128]{1,0:T(8,128)(2,1)S(1)}, u32[]{:S(2)}, u32[]{:S(2)}) %collective-permute-start.7) | collective-permute-done | bytes 135200 | tf_op jit(solution)/shard_map/ppermute | solution.py:583
  26.8 1.0 %unpack.3 = bf16[4,2,9,2,32,128]{5,4,3,2,1,0:T(8,128)(2,1)} custom-call(bf16[528,128]{1,0:T(8,128)(2,1)S(1)} %collective-permute-done.6.refs_0_, bf16[528,128]{1,0:T(8,128)(2,1)S(1)} %collective-permute-done.7.refs_1_, bf16[4,2,9,2,32,128]{5,4,3,2,1,0:T(8,128)(2,1)} %place.1.refs_2_), custom_call_target="tpu_custom_call", output_to_operand_aliasing={{}: (2, {})} | custom-call | flops 1 | bytes 1 | tf_op jit(solution)/shard_map/unpack/pallas_call | solution.py:471
  (3 shorter events, 0.0 us)
Async XLA Ops:
  1.4 16.5 %collective-permute-start = (bf16[1032,128]{1,0:T(8,128)(2,1)S(1)}, bf16[1032,128]{1,0:T(8,128)(2,1)S(1)}, u32[]{:S(2)}, u32[]{:S(2)}) collective-permute-start(bf16[1032,128]{1,0:T(8,128)(2,1)S(1)} %get-tuple-element.33), channel_id=1, source_target_pairs={{0,4},{1,5},{2,6},{3,7},{4,0},{5,1},{6,2},{7,3},{8,12},{9,13},{10,... | collective-permute-start | bytes 792584 | tf_op jit(solution)/shard_map/ppermute | solution.py:579
  1.5 16.4 %collective-permute-start.1 = (bf16[1032,128]{1,0:T(8,128)(2,1)S(1)}, bf16[1032,128]{1,0:T(8,128)(2,1)S(1)}, u32[]{:S(2)}, u32[]{:S(2)}) collective-permute-start(bf16[1032,128]{1,0:T(8,128)(2,1)S(1)} %get-tuple-element.34), channel_id=1, source_target_pairs={{0,1},{1,0},{2,3},{3,2},{4,8},{5,9},{6,10},{7,11},{8,4},{9,5},{10,... | collective-permute-start | bytes 792584 | tf_op jit(solution)/shard_map/ppermute | solution.py:579
  3.9 7.5 %collective-permute-start.2 = (bf16[1032,128]{1,0:T(8,128)(2,1)S(1)}, bf16[1032,128]{1,0:T(8,128)(2,1)S(1)}, u32[]{:S(2)}, u32[]{:S(2)}) collective-permute-start(bf16[1032,128]{1,0:T(8,128)(2,1)S(1)} %get-tuple-element.35), channel_id=1, source_target_pairs={{0,1},{1,0},{2,3},{3,2},{4,5},{5,4},{6,7},{7,6},{8,9},{9,8},{10,11... | collective-permute-start | bytes 792584 | tf_op jit(solution)/shard_map/ppermute | solution.py:579
  5.2 8.7 %collective-permute-start.3 = (bf16[1032,128]{1,0:T(8,128)(2,1)S(1)}, bf16[1032,128]{1,0:T(8,128)(2,1)S(1)}, u32[]{:S(2)}, u32[]{:S(2)}) collective-permute-start(bf16[1032,128]{1,0:T(8,128)(2,1)S(1)} %get-tuple-element.36), channel_id=1, source_target_pairs={{0,8},{1,2},{2,1},{3,11},{4,12},{5,6},{6,5},{7,15},{8,0},{9,10},{1... | collective-permute-start | bytes 792584 | tf_op jit(solution)/shard_map/ppermute | solution.py:579
  10.8 2.6 %collective-permute-start.5 = (bf16[2,128,512]{2,1,0:T(8,128)(2,1)S(1)}, bf16[2,128,512]{2,1,0:T(8,128)(2,1)S(1)}, u32[]{:S(2)}, u32[]{:S(2)}) collective-permute-start(bf16[2,128,512]{2,1,0:T(8,128)(2,1)S(1)} %get-tuple-element.43), channel_id=1, source_target_pairs={{0,1},{1,0},{2,3},{3,2},{4,5},{5,4},{6,7},{7,6},{8,9},{9,8},{10,11... | collective-permute-start | bytes 786440 | tf_op jit(solution)/shard_map/ppermute | solution.py:579
  11.4 6.5 %collective-permute-start.4 = (bf16[2,128,512]{2,1,0:T(8,128)(2,1)S(1)}, bf16[2,128,512]{2,1,0:T(8,128)(2,1)S(1)}, u32[]{:S(2)}, u32[]{:S(2)}) collective-permute-start(bf16[2,128,512]{2,1,0:T(8,128)(2,1)S(1)} %get-tuple-element.38), channel_id=1, source_target_pairs={{0,8},{1,2},{2,1},{3,11},{4,12},{5,6},{6,5},{7,15},{8,0},{9,10},{1... | collective-permute-start | bytes 786440 | tf_op jit(solution)/shard_map/ppermute | solution.py:579
  13.5 7.0 %collective-permute-start.8 = (bf16[2,4,32,128]{3,2,1,0:T(8,128)(2,1)S(1)}, bf16[2,4,32,128]{3,2,1,0:T(8,128)(2,1)S(1)}, u32[]{:S(2)}, u32[]{:S(2)}) collective-permute-start(bf16[2,4,32,128]{3,2,1,0:T(8,128)(2,1)S(1)} %get-tuple-element.53), channel_id=1, source_target_pairs={{0,2},{1,3},{2,0},{3,1},{4,6},{5,7},{6,4},{7,5},{8,10},{9,11},{10,... | collective-permute-start | bytes 196616 | tf_op jit(solution)/shard_map/ppermute | solution.py:583
  18.5 5.3 %collective-permute-start.6 = (bf16[528,128]{1,0:T(8,128)(2,1)S(1)}, bf16[528,128]{1,0:T(8,128)(2,1)S(1)}, u32[]{:S(2)}, u32[]{:S(2)}) collective-permute-start(bf16[528,128]{1,0:T(8,128)(2,1)S(1)} %get-tuple-element.49), channel_id=1, source_target_pairs={{0,2},{1,3},{2,0},{3,1},{4,6},{5,7},{6,4},{7,5},{8,10},{9,11},{10,... | collective-permute-start | bytes 405512 | tf_op jit(solution)/shard_map/ppermute | solution.py:583
  18.6 8.2 %collective-permute-start.7 = (bf16[528,128]{1,0:T(8,128)(2,1)S(1)}, bf16[528,128]{1,0:T(8,128)(2,1)S(1)}, u32[]{:S(2)}, u32[]{:S(2)}) collective-permute-start(bf16[528,128]{1,0:T(8,128)(2,1)S(1)} %get-tuple-element.50), channel_id=1, source_target_pairs={{0,3},{1,2},{2,1},{3,0},{4,7},{5,6},{6,5},{7,4},{8,11},{9,10},{10,... | collective-permute-start | bytes 405512 | tf_op jit(solution)/shard_map/ppermute | solution.py:583
  20.2 1.4 %collective-permute-start.10 = (bf16[528,128]{1,0:T(8,128)(2,1)S(1)}, bf16[528,128]{1,0:T(8,128)(2,1)S(1)}, u32[]{:S(2)}, u32[]{:S(2)}) collective-permute-start(bf16[528,128]{1,0:T(8,128)(2,1)S(1)} %get-tuple-element.56), channel_id=1, source_target_pairs={{0,1},{1,0},{2,3},{3,2},{4,5},{5,4},{6,7},{7,6},{8,9},{9,8},{10,11... | collective-permute-start | bytes 405512 | tf_op jit(solution)/shard_map/ppermute | solution.py:583
  20.5 2.0 %collective-permute-start.9 = (bf16[2,4,32,128]{3,2,1,0:T(8,128)(2,1)S(1)}, bf16[2,4,32,128]{3,2,1,0:T(8,128)(2,1)S(1)}, u32[]{:S(2)}, u32[]{:S(2)}) collective-permute-start(bf16[2,4,32,128]{3,2,1,0:T(8,128)(2,1)S(1)} %pad_maximum_fusion), channel_id=1, source_target_pairs={{0,1},{1,0},{2,3},{3,2},{4,5},{5,4},{6,7},{7,6},{8,9},{9,8},{10,11... | collective-permute-start | bytes 196616 | tf_op jit(solution)/shard_map/ppermute | solution.py:583

commit v6 on v5

--- a/solution.py
+++ b/solution.py
@@ -14,8 +14,8 @@
 HEAD = 8
 ROWS = 2 * QUAD + HEAD
 BITS = 16
-OWN_SLOTS = 4
-SLOTS = 16
+OWN_SLOTS = 6
+SLOTS = 14
 ANY = pl.BlockSpec(memory_space=pl.ANY)
 VMEM = pl.BlockSpec(memory_space=pltpu.VMEM)
 HBM = pl.BlockSpec(memory_space=pltpu.HBM)
@@ -246,8 +246,8 @@
             out[first : first + rows, :] = values[t, pl.ds(start, rows), :].astype(BF16)
 
 
-def near_kernel(parts, bits, r, prolong, after, *rest):
-    outs, (slots, right) = rest[:-2], rest[-2:]
+def near_kernel(parts, bits, r, prolong, col_a, *rest):
+    outs, (extra_a, slots, right) = rest[:-3], rest[-3:]
     fx, fy = flips()
 
     def by_halves(quads, own, first):
@@ -278,6 +278,11 @@
         at = pl.ds(pl.multiple_of(vr * 256, 256), 256)
         quads.append(((u, v), [prolong[2 * ur + m, at, :] for m in range(2)], bits[j : j + 1, :]))
     by_halves(quads, range(4), 0)
+    near = [sums(r, p, ((1, 3), (2, 3))) for p in ((1, 2), (2, 2))]
+    base, extra = edge_slots(near, col_a, jnp.abs(bits[0:1, :] - bits[1:2, :]))
+    for t in range(2):
+        slots[4 + t] = base[t]
+        extra_a[t] = extra[t]
     rows = BS // parts
     me = lax.axis_index("col")
     for s in range(parts):
@@ -295,11 +300,11 @@
     rows = BS // parts
     one = jax.ShapeDtypeStruct((OWN_SLOTS, rows, BS), BF16)
     two = jax.ShapeDtypeStruct((2, OWN_SLOTS, rows, BS), BF16)
-    shapes = (one, one) + (two,) * (parts // 2 - 1)
+    shapes = (one, one) + (two,) * (parts // 2 - 1) + (jax.ShapeDtypeStruct((2, BS, BS), F32),)
     return pl.pallas_call(
         functools.partial(near_kernel, parts),
         out_shape=shapes,
-        in_specs=[VMEM] * (len(operands) - 1) + [ANY],
+        in_specs=[VMEM] * len(operands),
         out_specs=(VMEM,) * len(shapes),
         scratch_shapes=[pltpu.VMEM((OWN_SLOTS, BS, BS), F32), pltpu.VMEM((4 * QUAD, 2 * BS), BF16)],
         compiler_params=pltpu.CompilerParams(vmem_limit_bytes=16 << 20),
@@ -317,20 +322,22 @@
             head[2 * e + t : 2 * e + t + 1, :] = half_of(far, t)
 
 
-def mid_kernel(parts, bits, r, col_a, col_b, slots, head):
-    split_y = jnp.abs(bits[0:1, :] - bits[1:2, :])
-    edges = (
-        (col_a, ((1, 2), (2, 2)), ((1, 3), (2, 3)), split_y, None),
-        (col_b, ((1, 1), (2, 1)), ((1, 0), (2, 0)), split_y, inside("col", parts)),
-    )
-    fill_edges(r, edges, slots, head)
+def mid_kernel(parts, bits, r, col_a, col_b, columns, head):
+    near = [sums(r, p, ((1, 0), (2, 0))) for p in ((1, 1), (2, 1))]
+    base, extra = edge_slots(near, col_b, jnp.abs(bits[0:1, :] - bits[1:2, :]))
+    scale = inside("col", parts)
+    for t in range(2):
+        columns[t] = base[t] * scale
+        columns[2 + t] = extra[t] * scale
+        head[t : t + 1, :] = half_of(col_a, t)
+        head[2 + t : 3 + t, :] = half_of(col_b, t)
     head[4:8, :] = bits[0:4, :]
 
 
 def mid_terms(parts, *operands):
     return pl.pallas_call(
         functools.partial(mid_kernel, parts),
-        out_shape=(jax.ShapeDtypeStruct((8, BS, BS), F32), jax.ShapeDtypeStruct((8, BS), F32)),
+        out_shape=(jax.ShapeDtypeStruct((4, BS, BS), F32), jax.ShapeDtypeStruct((8, BS), F32)),
         in_specs=[VMEM] * len(operands),
         out_specs=(VMEM, VMEM),
         compiler_params=pltpu.CompilerParams(vmem_limit_bytes=8 << 20),
@@ -339,7 +346,7 @@
     )(*operands)
 
 
-def far_kernel(counts, bits, r, row_a, row_b, from_a, from_b, columns, column_head, *rest):
+def far_kernel(counts, bits, r, row_a, row_b, from_a, from_b, columns, column_head, extra_a, *rest):
     outs, (slots, head) = rest[:-2], rest[-2:]
     split_x = 1.0 - jnp.abs(bits[0:1, :] - bits[1:2, :])
     row_in, col_in = inside("row", counts[0]), inside("col", counts[1])
@@ -351,8 +358,9 @@
         (row_b, ((1, 1), (1, 2)), ((0, 1), (0, 2)), split_x, row_in),
     )
     fill_edges(r, edges, slots, head.at[4:8])
-    for t in range(4):
-        slots[4 + t] += columns[4 + t]
+    for t in range(2):
+        slots[4 + t] += extra_a[t]
+        slots[6 + t] += columns[2 + t]
     corners = (
         (from_a.at[0], quad_of(row_a, 1), None),
         (from_b.at[0], quad_of(row_a, 0), col_in),
@@ -363,9 +371,9 @@
         value = jnp.dot(near[...], far, preferred_element_type=F32)
         slots[8 + e] = value if scale is None else value * scale
     store_pieces(outs, 0, slots.at[0:4])
-    store_pieces(outs, 4, columns.at[0:4])
-    store_pieces(outs, 8, slots.at[8:12])
-    store_pieces(outs, 12, slots.at[4:8])
+    store_pieces(outs, 4, columns.at[0:2])
+    store_pieces(outs, 6, slots.at[8:12])
+    store_pieces(outs, 10, slots.at[4:8])
     for out in outs:
         out[out.shape[0] - BITS :, :] = head[...].astype(BF16)
 
@@ -385,45 +393,8 @@
     )(*operands)
 
 
-def place_kernel(parts, own, relayed, *rest):
-    direct, (out, sems) = rest[:-3], rest[-2:]
-    me = lax.axis_index("col")
-    pieces = {0: own}
-    for h in range(parts // 2):
-        pieces[2 * h + 1] = relayed.at[h]
-        if h:
-            pieces[2 * h] = direct[h - 1].at[0]
-    copies = []
-    for s in range(parts):
-        square = me ^ s
-        for a in range(2):
-            copies.append(
-                pltpu.make_async_copy(
-                    pieces[s].at[2 * a : 2 * a + 2], out.at[square, a, 4], sems.at[len(copies)]
-                )
-            )
-            copies[-1].start()
-    for copy in copies:
-        copy.wait()
-
-
-def place(own, relayed, direct, coarse):
-    parts = lax.axis_size("col")
-    return pl.pallas_call(
-        functools.partial(place_kernel, parts),
-        out_shape=jax.ShapeDtypeStruct(coarse.shape, BF16),
-        in_specs=[VMEM] * (2 + len(direct)) + [ANY],
-        out_specs=ANY,
-        scratch_shapes=[pltpu.SemaphoreType.DMA((2 * parts,))],
-        input_output_aliases={2 + len(direct): 0},
-        compiler_params=pltpu.CompilerParams(vmem_limit_bytes=4 << 20),
-        cost_estimate=pl.CostEstimate(flops=1, bytes_accessed=1, transcendentals=0),
-        name="place",
-    )(own, relayed, *direct, coarse)
-
-
 def unpack_kernel(parts, steps, *refs):
-    ins = refs[: len(steps)]
+    ins, owns = refs[: len(steps)], refs[len(steps) : 2 * len(steps)]
     out, buf, sems = refs[-3:]
     me = lax.axis_index("col")
     fx, _ = flips()
@@ -431,6 +402,12 @@
     for i, (s, ref) in enumerate(zip(steps, ins)):
         square = me ^ s
         fy = lax.rem(square, 2)
+        own = owns[i] if s == 0 else owns[i].at[s // 2 if s % 2 else 0]
+        for a in range(2):
+            copies.append(
+                pltpu.make_async_copy(own.at[2 * a : 2 * a + 2], out.at[square, a, 4], sems.at[len(copies)])
+            )
+            copies[-1].start()
         one = functools.partial(bit_row, ref)
         split_y = jnp.abs(one(0) - one(1))
 
@@ -440,13 +417,15 @@
 
         split_x = 1.0 - split_y
         edges = (
-            ((2, 3), (12, 13), split_y, 7 - 6 * fx),
-            ((0, 1), (14, 15), split_y, 1 + 6 * fx),
-            ((1, 3), (12, 13), split_x, 3 + turn3(2, fy)),
-            ((0, 2), (14, 15), split_x, 3 + turn3(0, fy)),
+            ((2, 3), (0, 1), (10, 11), split_y, 7 - 6 * fx),
+            ((0, 1), (2, 3), (12, 13), split_y, 1 + 6 * fx),
+            ((1, 3), None, (10, 11), split_x, 3 + turn3(2, fy)),
+            ((0, 2), (4, 5), (12, 13), split_x, 3 + turn3(0, fy)),
         )
-        for e, (ps, more, used, code) in enumerate(edges):
-            spread_edge(buf, (i, e), ref, one, ps, (4 + 2 * e, 5 + 2 * e), (2 * e, 2 * e + 1), more, used)
+        for e, (ps, base, more, used, code) in enumerate(edges):
+            values = [slot(ref, t) for t in base] if base else [own[4 + t].astype(F32) for t in range(2)]
+            second = [slot(ref, t) for t in more]
+            spread_edge(buf, (i, e), one, ps, (4 + 2 * e, 5 + 2 * e), values, second, used)
             send(e, square, code)
         high = square ^ 1
         low = square + 2 * fy - 1
@@ -458,30 +437,30 @@
             (low, 6 * fx, 0, 10, 6),
         )
         for e, (owner, group, side, a_bit, b_bit) in enumerate(corners):
-            spread_corner(buf, (i, 4 + e), slot(ref, 8 + e), one(a_bit), one(b_bit))
+            spread_corner(buf, (i, 4 + e), slot(ref, 6 + e), one(a_bit), one(b_bit))
             send(4 + e, owner, group + turn3(side, lax.rem(owner, 2)))
     for copy in copies:
         copy.wait()
 
 
-def unpack(messages, steps, coarse):
+def unpack(messages, owns, steps, coarse):
     parts = lax.axis_size("col")
     rows = BS // parts
     fresh = coarse is None
     return pl.pallas_call(
         functools.partial(unpack_kernel, parts, steps),
         out_shape=jax.ShapeDtypeStruct((parts, 2, 9, 2, rows, BS), BF16),
-        in_specs=[VMEM] * len(steps) + [ANY] * (not fresh),
+        in_specs=[VMEM] * (2 * len(steps)) + [ANY] * (not fresh),
         out_specs=ANY,
         scratch_shapes=[
             pltpu.VMEM((len(steps), 8, 2, 2, rows, BS), BF16),
-            pltpu.SemaphoreType.DMA((8 * len(steps),)),
+            pltpu.SemaphoreType.DMA((10 * len(steps),)),
         ],
-        input_output_aliases={} if fresh else {len(steps): 0},
+        input_output_aliases={} if fresh else {2 * len(steps): 0},
         compiler_params=pltpu.CompilerParams(vmem_limit_bytes=16 << 20),
         cost_estimate=pl.CostEstimate(flops=1, bytes_accessed=1, transcendentals=0),
         name="unpack",
-    )(*messages, *(() if fresh else (coarse,)))
+    )(*messages, *owns, *(() if fresh else (coarse,)))
 
 
 def turn3(index, flip):
@@ -505,11 +484,9 @@
             buf[i, piece, a, b] = center[2 * a + b].astype(BF16)
 
 
-def spread_edge(buf, at, ref, one, ps, qs, base, extra, used):
+def spread_edge(buf, at, one, ps, qs, values, more, used):
     a_bits = [one(p) for p in ps]
     b_bits = [one(q) for q in qs]
-    values = [slot(ref, t) for t in base]
-    more = [slot(ref, t) for t in extra]
     center = [None] * 4
     for b in range(2):
         picks = [bit if b else 1.0 - bit for bit in b_bits]
@@ -598,18 +575,20 @@
     r, to_a, to_b, own_blocks = step_one(neighbours, coupling, prolong_rows, bits)
     from_b = swap(to_b, col_low)
     from_a = swap(to_a, col_high)
-    mine, pair, *cross = near_terms(parts, bits, r, own_blocks, col_a)
+    mine, pair, *cross, extra_a = near_terms(parts, bits, r, own_blocks, col_a)
     from_a, *cross = lax.optimization_barrier((from_a, *cross))
     direct = [xor_swap(value, 2 * h + 2) for h, value in enumerate(cross)]
     columns, column_head = mid_terms(parts, bits, r, col_a, col_b)
     row_a, row_b, columns, from_b = gate((row_a, row_b, columns, from_b), (mine,))
-    outs = list(far_terms(counts, bits, r, row_a, row_b, from_a, from_b, columns, column_head))
+    outs = list(far_terms(counts, bits, r, row_a, row_b, from_a, from_b, columns, column_head, extra_a))
     outs[0], *direct = lax.optimization_barrier((outs[0], *direct))
     outs = [outs[0]] + [xor_swap(outs[s], s) for s in range(1, parts)]
     relayed = xor_swap(jnp.stack([pair] + [value[1] for value in direct]), 1)
-    coarse = unpack(outs[:2], range(2), None)
-    coarse = place(mine, relayed, direct, coarse)
-    coarse = unpack(outs[2:], range(2, parts), coarse)
+    owns = [mine, relayed]
+    for value in direct:
+        owns += [value, relayed]
+    coarse = unpack(outs[:2], owns[:2], range(2), None)
+    coarse = unpack(outs[2:], owns[2:], range(2, parts), coarse)
     return coarse[None]
 
 

time: 28 us -> 27.7 us (0.989)
  Pallas kernels: 10.5 us -> 9.88 us
  waiting for transfers between devices: 7.89 us -> 8.4 us
    pallas_call x1 -> x0, Pallas kernels: 0.73 us -> none  [place(): pl.pallas_call(functools.partial(place_kernel, parts), out_shape=jax.Shap...]
    ppermute x5, waiting for transfers between devices: 4.31 us -> 4.62 us  [xor_swap(): lax.ppermute(value, 'col', [(i, i ^ s) for i in range(lax.axis_size('col'...]
  transfers between devices with their start and end apart: 11 -> 11, of which waited for: 4 -> 5; matrix products, arithmetic and copies ran while one was open for 0% -> 0% of each run, Pallas kernels for 29% -> 27%
where the time goes in v6:
time: 27.7 us; the launch traced here: 27.4 us
  Pallas kernels  9.88 us (36%)
  starting transfers between devices  9.05 us (33%)
  waiting for transfers between devices  8.4 us (30%)
    ppermute x6, starting transfers between devices, swap(): return lax.ppermute(value, ('row', 'col'), pairs)  6.74 us
    ppermute x5, waiting for transfers between devices, xor_swap(): lax.ppermute(value, 'col', [(i, i ^ s) for i in range(lax.axis_size('col'...  4.62 us
    pallas_call x1, Pallas kernels, step_one(): pl.pallas_call(step_one_kernel, out_shape=(jax.ShapeDtypeStruct((4, 9, BS...  4.56 us
    ppermute x6, waiting for transfers between devices, swap(): return lax.ppermute(value, ('row', 'col'), pairs)  3.78 us
    ppermute x5, starting transfers between devices, xor_swap(): lax.ppermute(value, 'col', [(i, i ^ s) for i in range(lax.axis_size('col'...  2.32 us
    pallas_call x2, Pallas kernels, unpack(): pl.pallas_call(functools.partial(unpack_kernel, parts, steps), out_shape=...  2.02 us
    pallas_call x1, Pallas kernels, rims(): pl.pallas_call(rims_kernel, out_shape=(shape,) * 4 + (jax.ShapeDtypeStruc...  1.38 us
    pallas_call x1, Pallas kernels, near_terms(): pl.pallas_call(functools.partial(near_kernel, parts), out_shape=shapes, i...  0.98 us
  transfers between devices with their start and end apart: 11, of which 5 were waited for; matrix products, arithmetic and copies ran while one was open for 0% of the time, Pallas kernels for 27%

profile of v6, /device:TPU:5, one launch (start us, length us, event | category | flops | bytes accessed | tf_op | source)
XLA Modules:
  0.0 27.4 jit_solution(1882032052958664764)
XLA Ops:
  0.0 1.4 %rims.1 = (bf16[1032,128]{1,0:T(8,128)(2,1)S(1)}, bf16[1032,128]{1,0:T(8,128)(2,1)S(1)}, bf16[1032,128]{1,0:T(8,128)(2,1)S(1)}, bf16[1032,128]{1,0:T(8,128)(2,1)S(1)}, f32[8,128]{1,0:T(8,128)S(1)}) custom-call(s32[4,4]{1,0:T(4,128)} %agg_hbm.1, bf16[4,512,128]{2,1,0:T(8,128)(2,1)} %bitcast.5), custom_call_target="tpu_custom_call" | custom-call | tf_op jit(solution)/shard_map/rims/pallas_call | solution.py:72
  1.4 0.1 collective-permute-start
  1.5 2.5 %collective-permute-start.1 = (bf16[1032,128]{1,0:T(8,128)(2,1)S(1)}, bf16[1032,128]{1,0:T(8,128)(2,1)S(1)}, u32[]{:S(2)}, u32[]{:S(2)}) collective-permute-start(bf16[1032,128]{1,0:T(8,128)(2,1)S(1)} %get-tuple-element.35), channel_id=1, source_target_pairs={{0,1},{1,0},{2,3},{3,2},{4,8},{5,9},{6,10},{7,11},{8,4},{9,5},{10,... | collective-permute-start | bytes 792584 | tf_op jit(solution)/shard_map/ppermute | solution.py:556
  3.9 1.2 %collective-permute-start.2 = (bf16[1032,128]{1,0:T(8,128)(2,1)S(1)}, bf16[1032,128]{1,0:T(8,128)(2,1)S(1)}, u32[]{:S(2)}, u32[]{:S(2)}) collective-permute-start(bf16[1032,128]{1,0:T(8,128)(2,1)S(1)} %get-tuple-element.36), channel_id=1, source_target_pairs={{0,1},{1,0},{2,3},{3,2},{4,5},{5,4},{6,7},{7,6},{8,9},{9,8},{10,11... | collective-permute-start | bytes 792584 | tf_op jit(solution)/shard_map/ppermute | solution.py:556
  5.2 1.1 %collective-permute-start.3 = (bf16[1032,128]{1,0:T(8,128)(2,1)S(1)}, bf16[1032,128]{1,0:T(8,128)(2,1)S(1)}, u32[]{:S(2)}, u32[]{:S(2)}) collective-permute-start(bf16[1032,128]{1,0:T(8,128)(2,1)S(1)} %get-tuple-element.37), channel_id=1, source_target_pairs={{0,8},{1,2},{2,1},{3,11},{4,12},{5,6},{6,5},{7,15},{8,0},{9,10},{1... | collective-permute-start | bytes 792584 | tf_op jit(solution)/shard_map/ppermute | solution.py:556
  6.3 4.6 %step_one.1 = (bf16[4,9,128,512]{3,2,1,0:T(8,128)(2,1)S(1)}, bf16[2,128,512]{2,1,0:T(8,128)(2,1)S(1)}, bf16[2,128,512]{2,1,0:T(8,128)(2,1)S(1)}, bf16[4,512,128]{2,1,0:T(8,128)(2,1)S(1)}) custom-call(s32[4,4,12]{2,1,0:T(4,128)} %codes_hbm.1, bf16[192,128,128]{2,1,0:T(8,128)(2,1)} %bitcast.7, bf16[4,512,128]{2,1,0:T(8,128)(2,1)} %bitcast.6, ...), custom_call_target="tpu_custom_call" | custom-call | flops 8589934592 | bytes 1048576 | tf_op jit(solution)/shard_map/step_one/pallas_call | solution.py:183
  10.8 0.5 %collective-permute-start.5 = (bf16[2,128,512]{2,1,0:T(8,128)(2,1)S(1)}, bf16[2,128,512]{2,1,0:T(8,128)(2,1)S(1)}, u32[]{:S(2)}, u32[]{:S(2)}) collective-permute-start(bf16[2,128,512]{2,1,0:T(8,128)(2,1)S(1)} %get-tuple-element.44), channel_id=1, source_target_pairs={{0,1},{1,0},{2,3},{3,2},{4,5},{5,4},{6,7},{7,6},{8,9},{9,8},{10,11... | collective-permute-start | bytes 786440 | tf_op jit(solution)/shard_map/ppermute | solution.py:556
  11.4 0.0 collective-permute-done.2.col_a
  11.4 1.3 %collective-permute-start.4 = (bf16[2,128,512]{2,1,0:T(8,128)(2,1)S(1)}, bf16[2,128,512]{2,1,0:T(8,128)(2,1)S(1)}, u32[]{:S(2)}, u32[]{:S(2)}) collective-permute-start(bf16[2,128,512]{2,1,0:T(8,128)(2,1)S(1)} %get-tuple-element.39), channel_id=1, source_target_pairs={{0,8},{1,2},{2,1},{3,11},{4,12},{5,6},{6,5},{7,15},{8,0},{9,10},{1... | collective-permute-start | bytes 786440 | tf_op jit(solution)/shard_map/ppermute | solution.py:556
  12.7 1.0 %near_terms.1 = (bf16[6,32,128]{2,1,0:T(8,128)(2,1)S(1)}, bf16[6,32,128]{2,1,0:T(8,128)(2,1)S(1)}, bf16[2,6,32,128]{3,2,1,0:T(8,128)(2,1)S(1)}, f32[2,128,128]{2,1,0:T(8,128)S(1)}) custom-call(f32[8,128]{1,0:T(8,128)S(1)} %get-tuple-element.32.after.bits, bf16[4,9,128,512]{3,2,1,0:T(8,128)(2,1)S(1)} %get-tuple-element.33.r, ...), custom_call_target="tpu_custom_call" | custom-call | flops 1 | bytes 1 | tf_op jit(solution)/shard_map/near_terms/pallas_call | solution.py:304
  13.7 0.0 collective-permute-done.5.from_a
  13.7 0.3 %collective-permute-start.8 = (bf16[2,6,32,128]{3,2,1,0:T(8,128)(2,1)S(1)}, bf16[2,6,32,128]{3,2,1,0:T(8,128)(2,1)S(1)}, u32[]{:S(2)}, u32[]{:S(2)}) collective-permute-start(bf16[2,6,32,128]{3,2,1,0:T(8,128)(2,1)S(1)} %get-tuple-element.54), channel_id=1, source_target_pairs={{0,2},{1,3},{2,0},{3,1},{4,6},{5,7},{6,4},{7,5},{8,10},{9,11},{10,... | collective-permute-start | bytes 294920 | tf_op jit(solution)/shard_map/ppermute | solution.py:560
  14.0 0.0 collective-permute-done.3.col_b
  14.0 0.3 %mid_terms.1 = (f32[4,128,128]{2,1,0:T(8,128)S(1)}, f32[8,128]{1,0:T(8,128)S(1)}) custom-call(f32[8,128]{1,0:T(8,128)S(1)} %get-tuple-element.32.after.bits, bf16[4,9,128,512]{3,2,1,0:T(8,128)(2,1)S(1)} %get-tuple-element.33.r, bf16[1032,128]{1,0:T(8,128)(2,1)S(1)} %collective-permute-done.2.col_a, bf16[1032,128]{1,0:T(8,128)(2,1)S(1)} %collective-permute-done.3.col_b), custom_call_target="tpu_custom_call" | custom-call | flops 1 | bytes 1 | tf_op jit(solution)/shard_map/mid_terms/pallas_call | solution.py:338
  14.3 3.8 %collective-permute-done.4.refs_3_ = bf16[2,128,512]{2,1,0:T(8,128)(2,1)S(1)} collective-permute-done((bf16[2,128,512]{2,1,0:T(8,128)(2,1)S(1)}, bf16[2,128,512]{2,1,0:T(8,128)(2,1)S(1)}, u32[]{:S(2)}, u32[]{:S(2)}) %collective-permute-start.4) | collective-permute-done | bytes 262176 | tf_op jit(solution)/shard_map/ppermute | solution.py:556
  18.1 0.0 collective-permute-done.refs_0_
  18.1 0.0 collective-permute-done.1.refs_1_
  18.1 0.6 %far_terms.1 = (bf16[464,128]{1,0:T(8,128)(2,1)S(1)}, bf16[464,128]{1,0:T(8,128)(2,1)S(1)}, bf16[464,128]{1,0:T(8,128)(2,1)S(1)}, bf16[464,128]{1,0:T(8,128)(2,1)S(1)}) custom-call(f32[8,128]{1,0:T(8,128)S(1)} %get-tuple-element.32.after.bits, bf16[4,9,128,512]{3,2,1,0:T(8,128)(2,1)S(1)} %get-tuple-element.33.r, ...), custom_call_target="tpu_custom_call" | custom-call | flops 1 | bytes 1 | tf_op jit(solution)/shard_map/far_terms/pallas_call | solution.py:384
  18.8 0.1 collective-permute-start.6
  18.8 1.4 %collective-permute-start.7 = (bf16[464,128]{1,0:T(8,128)(2,1)S(1)}, bf16[464,128]{1,0:T(8,128)(2,1)S(1)}, u32[]{:S(2)}, u32[]{:S(2)}) collective-permute-start(bf16[464,128]{1,0:T(8,128)(2,1)S(1)} %get-tuple-element.52), channel_id=1, source_target_pairs={{0,3},{1,2},{2,1},{3,0},{4,7},{5,6},{6,5},{7,4},{8,11},{9,10},{10,... | collective-permute-start | bytes 356360 | tf_op jit(solution)/shard_map/ppermute | solution.py:560
  20.2 0.5 %collective-permute-start.10 = (bf16[464,128]{1,0:T(8,128)(2,1)S(1)}, bf16[464,128]{1,0:T(8,128)(2,1)S(1)}, u32[]{:S(2)}, u32[]{:S(2)}) collective-permute-start(bf16[464,128]{1,0:T(8,128)(2,1)S(1)} %get-tuple-element.58), channel_id=1, source_target_pairs={{0,1},{1,0},{2,3},{3,2},{4,5},{5,4},{6,7},{7,6},{8,9},{9,8},{10,11... | collective-permute-start | bytes 356360 | tf_op jit(solution)/shard_map/ppermute | solution.py:560
  20.7 0.0 collective-permute-done.8.refs_2_
  20.7 0.1 collective-permute-start.9
  20.8 0.9 %collective-permute-done.10.refs_1_ = bf16[464,128]{1,0:T(8,128)(2,1)S(1)} collective-permute-done((bf16[464,128]{1,0:T(8,128)(2,1)S(1)}, bf16[464,128]{1,0:T(8,128)(2,1)S(1)}, u32[]{:S(2)}, u32[]{:S(2)}) %collective-permute-start.10) | collective-permute-done | bytes 118816 | tf_op jit(solution)/shard_map/ppermute | solution.py:560
  21.7 0.4 %collective-permute-done.9.refs_3_ = bf16[2,6,32,128]{3,2,1,0:T(8,128)(2,1)S(1)} collective-permute-done((bf16[2,6,32,128]{3,2,1,0:T(8,128)(2,1)S(1)}, bf16[2,6,32,128]{3,2,1,0:T(8,128)(2,1)S(1)}, u32[]{:S(2)}, u32[]{:S(2)}) %collective-permute-start.9) | collective-permute-done | bytes 98336 | tf_op jit(solution)/shard_map/ppermute | solution.py:560
  22.1 1.0 %unpack.2.refs_4_ = bf16[4,2,9,2,32,128]{5,4,3,2,1,0:T(8,128)(2,1)} custom-call(bf16[464,128]{1,0:T(8,128)(2,1)S(1)} %get-tuple-element.57.refs_0_, bf16[464,128]{1,0:T(8,128)(2,1)S(1)} %collective-permute-done.10.refs_1_, bf16[6,32,128]{2,1,0:T(8,128)(2,1)S(1)} %get-tuple-element.41.refs_4_.refs_2_, bf16[2,6,32,128]{3,2,1,0:T(8,128)(2,1)S(1)} %collective-permute-done.9.refs_3_), custom_call_target="tpu_custom_call" | custom-call | flops 1 | bytes 1 | tf_op jit(solution)/shard_map/unpack/pallas_call | solution.py:450
  23.1 0.8 %collective-permute-done.6.refs_0_ = bf16[464,128]{1,0:T(8,128)(2,1)S(1)} collective-permute-done((bf16[464,128]{1,0:T(8,128)(2,1)S(1)}, bf16[464,128]{1,0:T(8,128)(2,1)S(1)}, u32[]{:S(2)}, u32[]{:S(2)}) %collective-permute-start.6) | collective-permute-done | bytes 118816 | tf_op jit(solution)/shard_map/ppermute | solution.py:560
  23.9 2.5 %collective-permute-done.7.refs_1_ = bf16[464,128]{1,0:T(8,128)(2,1)S(1)} collective-permute-done((bf16[464,128]{1,0:T(8,128)(2,1)S(1)}, bf16[464,128]{1,0:T(8,128)(2,1)S(1)}, u32[]{:S(2)}, u32[]{:S(2)}) %collective-permute-start.7) | collective-permute-done | bytes 118816 | tf_op jit(solution)/shard_map/ppermute | solution.py:560
  26.4 1.0 %unpack.3 = bf16[4,2,9,2,32,128]{5,4,3,2,1,0:T(8,128)(2,1)} custom-call(bf16[464,128]{1,0:T(8,128)(2,1)S(1)} %collective-permute-done.6.refs_0_, bf16[464,128]{1,0:T(8,128)(2,1)S(1)} %collective-permute-done.7.refs_1_, bf16[2,6,32,128]{3,2,1,0:T(8,128)(2,1)S(1)} %collective-permute-done.8.refs_2_, ...), custom_call_target="tpu_custom_call", output_to_operand_aliasing={{}: (4, {})} | custom-call | flops 1 | bytes 1 | tf_op jit(solution)/shard_map/unpack/pallas_call | solution.py:450
  (3 shorter events, 0.0 us)
Async XLA Ops:
  1.4 16.7 %collective-permute-start = (bf16[1032,128]{1,0:T(8,128)(2,1)S(1)}, bf16[1032,128]{1,0:T(8,128)(2,1)S(1)}, u32[]{:S(2)}, u32[]{:S(2)}) collective-permute-start(bf16[1032,128]{1,0:T(8,128)(2,1)S(1)} %get-tuple-element.34), channel_id=1, source_target_pairs={{0,4},{1,5},{2,6},{3,7},{4,0},{5,1},{6,2},{7,3},{8,12},{9,13},{10,... | collective-permute-start | bytes 792584 | tf_op jit(solution)/shard_map/ppermute | solution.py:556
  1.5 16.6 %collective-permute-start.1 = (bf16[1032,128]{1,0:T(8,128)(2,1)S(1)}, bf16[1032,128]{1,0:T(8,128)(2,1)S(1)}, u32[]{:S(2)}, u32[]{:S(2)}) collective-permute-start(bf16[1032,128]{1,0:T(8,128)(2,1)S(1)} %get-tuple-element.35), channel_id=1, source_target_pairs={{0,1},{1,0},{2,3},{3,2},{4,8},{5,9},{6,10},{7,11},{8,4},{9,5},{10,... | collective-permute-start | bytes 792584 | tf_op jit(solution)/shard_map/ppermute | solution.py:556
  3.9 7.4 %collective-permute-start.2 = (bf16[1032,128]{1,0:T(8,128)(2,1)S(1)}, bf16[1032,128]{1,0:T(8,128)(2,1)S(1)}, u32[]{:S(2)}, u32[]{:S(2)}) collective-permute-start(bf16[1032,128]{1,0:T(8,128)(2,1)S(1)} %get-tuple-element.36), channel_id=1, source_target_pairs={{0,1},{1,0},{2,3},{3,2},{4,5},{5,4},{6,7},{7,6},{8,9},{9,8},{10,11... | collective-permute-start | bytes 792584 | tf_op jit(solution)/shard_map/ppermute | solution.py:556
  5.2 8.9 %collective-permute-start.3 = (bf16[1032,128]{1,0:T(8,128)(2,1)S(1)}, bf16[1032,128]{1,0:T(8,128)(2,1)S(1)}, u32[]{:S(2)}, u32[]{:S(2)}) collective-permute-start(bf16[1032,128]{1,0:T(8,128)(2,1)S(1)} %get-tuple-element.37), channel_id=1, source_target_pairs={{0,8},{1,2},{2,1},{3,11},{4,12},{5,6},{6,5},{7,15},{8,0},{9,10},{1... | collective-permute-start | bytes 792584 | tf_op jit(solution)/shard_map/ppermute | solution.py:556
  10.8 2.9 %collective-permute-start.5 = (bf16[2,128,512]{2,1,0:T(8,128)(2,1)S(1)}, bf16[2,128,512]{2,1,0:T(8,128)(2,1)S(1)}, u32[]{:S(2)}, u32[]{:S(2)}) collective-permute-start(bf16[2,128,512]{2,1,0:T(8,128)(2,1)S(1)} %get-tuple-element.44), channel_id=1, source_target_pairs={{0,1},{1,0},{2,3},{3,2},{4,5},{5,4},{6,7},{7,6},{8,9},{9,8},{10,11... | collective-permute-start | bytes 786440 | tf_op jit(solution)/shard_map/ppermute | solution.py:556
  11.4 6.7 %collective-permute-start.4 = (bf16[2,128,512]{2,1,0:T(8,128)(2,1)S(1)}, bf16[2,128,512]{2,1,0:T(8,128)(2,1)S(1)}, u32[]{:S(2)}, u32[]{:S(2)}) collective-permute-start(bf16[2,128,512]{2,1,0:T(8,128)(2,1)S(1)} %get-tuple-element.39), channel_id=1, source_target_pairs={{0,8},{1,2},{2,1},{3,11},{4,12},{5,6},{6,5},{7,15},{8,0},{9,10},{1... | collective-permute-start | bytes 786440 | tf_op jit(solution)/shard_map/ppermute | solution.py:556
  13.7 7.0 %collective-permute-start.8 = (bf16[2,6,32,128]{3,2,1,0:T(8,128)(2,1)S(1)}, bf16[2,6,32,128]{3,2,1,0:T(8,128)(2,1)S(1)}, u32[]{:S(2)}, u32[]{:S(2)}) collective-permute-start(bf16[2,6,32,128]{3,2,1,0:T(8,128)(2,1)S(1)} %get-tuple-element.54), channel_id=1, source_target_pairs={{0,2},{1,3},{2,0},{3,1},{4,6},{5,7},{6,4},{7,5},{8,10},{9,11},{10,... | collective-permute-start | bytes 294920 | tf_op jit(solution)/shard_map/ppermute | solution.py:560
  18.8 5.1 %collective-permute-start.6 = (bf16[464,128]{1,0:T(8,128)(2,1)S(1)}, bf16[464,128]{1,0:T(8,128)(2,1)S(1)}, u32[]{:S(2)}, u32[]{:S(2)}) collective-permute-start(bf16[464,128]{1,0:T(8,128)(2,1)S(1)} %get-tuple-element.51), channel_id=1, source_target_pairs={{0,2},{1,3},{2,0},{3,1},{4,6},{5,7},{6,4},{7,5},{8,10},{9,11},{10,... | collective-permute-start | bytes 356360 | tf_op jit(solution)/shard_map/ppermute | solution.py:560
  18.8 7.6 %collective-permute-start.7 = (bf16[464,128]{1,0:T(8,128)(2,1)S(1)}, bf16[464,128]{1,0:T(8,128)(2,1)S(1)}, u32[]{:S(2)}, u32[]{:S(2)}) collective-permute-start(bf16[464,128]{1,0:T(8,128)(2,1)S(1)} %get-tuple-element.52), channel_id=1, source_target_pairs={{0,3},{1,2},{2,1},{3,0},{4,7},{5,6},{6,5},{7,4},{8,11},{9,10},{10,... | collective-permute-start | bytes 356360 | tf_op jit(solution)/shard_map/ppermute | solution.py:560
  20.2 1.5 %collective-permute-start.10 = (bf16[464,128]{1,0:T(8,128)(2,1)S(1)}, bf16[464,128]{1,0:T(8,128)(2,1)S(1)}, u32[]{:S(2)}, u32[]{:S(2)}) collective-permute-start(bf16[464,128]{1,0:T(8,128)(2,1)S(1)} %get-tuple-element.58), channel_id=1, source_target_pairs={{0,1},{1,0},{2,3},{3,2},{4,5},{5,4},{6,7},{7,6},{8,9},{9,8},{10,11... | collective-permute-start | bytes 356360 | tf_op jit(solution)/shard_map/ppermute | solution.py:560
  20.7 1.4 %collective-permute-start.9 = (bf16[2,6,32,128]{3,2,1,0:T(8,128)(2,1)S(1)}, bf16[2,6,32,128]{3,2,1,0:T(8,128)(2,1)S(1)}, u32[]{:S(2)}, u32[]{:S(2)}) collective-permute-start(bf16[2,6,32,128]{3,2,1,0:T(8,128)(2,1)S(1)} %pad_maximum_fusion), channel_id=1, source_target_pairs={{0,1},{1,0},{2,3},{3,2},{4,5},{5,4},{6,7},{7,6},{8,9},{9,8},{10,11... | collective-permute-start | bytes 294920 | tf_op jit(solution)/shard_map/ppermute | solution.py:560

commit v7 on v6

--- a/solution.py
+++ b/solution.py
@@ -535,7 +535,11 @@
 
 def col_low(r, c, rows, cols):
     far = other_side(c)
-    return (r, far) if 0 <= far < cols else (r ^ 2, c)
+    if 0 <= far < cols:
+        return r, far
+    if r % 2:
+        return (r - 2 if r >= 2 else r - 1), c
+    return (r + 2 if r + 2 < rows else r + 1), c
 
 
 def row_high(r, c, rows, cols):

time: 27.7 us -> 27.3 us (0.986)
  starting transfers between devices: 9.05 us -> 8.06 us
  waiting for transfers between devices: 8.4 us -> 9 us
    ppermute x6, starting transfers between devices: 6.74 us -> 5.63 us  [swap(): return lax.ppermute(value, ('row', 'col'), pairs)]
    ppermute x6, waiting for transfers between devices: 3.78 us -> 4.7 us  [swap(): return lax.ppermute(value, ('row', 'col'), pairs)]
    ppermute x5, waiting for transfers between devices: 4.62 us -> 4.3 us  [xor_swap(): lax.ppermute(value, 'col', [(i, i ^ s) for i in range(lax.axis_size('col'...]
  transfers between devices with their start and end apart: 11 -> 11, of which waited for: 5 -> 5; matrix products, arithmetic and copies ran while one was open for 0% -> 0% of each run, Pallas kernels for 27% -> 28%
where the time goes in v7:
time: 27.3 us; the launch traced here: 27.1 us
  Pallas kernels  9.88 us (36%)
  waiting for transfers between devices  9 us (33%)
  starting transfers between devices  8.06 us (30%)
    ppermute x6, starting transfers between devices, swap(): return lax.ppermute(value, ('row', 'col'), pairs)  5.63 us
    ppermute x6, waiting for transfers between devices, swap(): return lax.ppermute(value, ('row', 'col'), pairs)  4.7 us
    pallas_call x1, Pallas kernels, step_one(): pl.pallas_call(step_one_kernel, out_shape=(jax.ShapeDtypeStruct((4, 9, BS...  4.56 us
    ppermute x5, waiting for transfers between devices, xor_swap(): lax.ppermute(value, 'col', [(i, i ^ s) for i in range(lax.axis_size('col'...  4.3 us
    ppermute x5, starting transfers between devices, xor_swap(): lax.ppermute(value, 'col', [(i, i ^ s) for i in range(lax.axis_size('col'...  2.43 us
    pallas_call x2, Pallas kernels, unpack(): pl.pallas_call(functools.partial(unpack_kernel, parts, steps), out_shape=...  2.02 us
    pallas_call x1, Pallas kernels, rims(): pl.pallas_call(rims_kernel, out_shape=(shape,) * 4 + (jax.ShapeDtypeStruc...  1.38 us
    pallas_call x1, Pallas kernels, near_terms(): pl.pallas_call(functools.partial(near_kernel, parts), out_shape=shapes, i...  0.98 us
  transfers between devices with their start and end apart: 11, of which 5 were waited for; matrix products, arithmetic and copies ran while one was open for 0% of the time, Pallas kernels for 28%

profile of v7, /device:TPU:5, one launch (start us, length us, event | category | flops | bytes accessed | tf_op | source)
XLA Modules:
  0.0 27.1 jit_solution(6304657458395490972)
XLA Ops:
  0.0 1.4 %rims.1 = (bf16[1032,128]{1,0:T(8,128)(2,1)S(1)}, bf16[1032,128]{1,0:T(8,128)(2,1)S(1)}, bf16[1032,128]{1,0:T(8,128)(2,1)S(1)}, bf16[1032,128]{1,0:T(8,128)(2,1)S(1)}, f32[8,128]{1,0:T(8,128)S(1)}) custom-call(s32[4,4]{1,0:T(4,128)} %agg_hbm.1, bf16[4,512,128]{2,1,0:T(8,128)(2,1)} %bitcast.5), custom_call_target="tpu_custom_call" | custom-call | tf_op jit(solution)/shard_map/rims/pallas_call | solution.py:72
  1.4 0.1 collective-permute-start
  1.5 2.5 %collective-permute-start.1 = (bf16[1032,128]{1,0:T(8,128)(2,1)S(1)}, bf16[1032,128]{1,0:T(8,128)(2,1)S(1)}, u32[]{:S(2)}, u32[]{:S(2)}) collective-permute-start(bf16[1032,128]{1,0:T(8,128)(2,1)S(1)} %get-tuple-element.35), channel_id=1, source_target_pairs={{0,1},{1,0},{2,3},{3,2},{4,8},{5,9},{6,10},{7,11},{8,4},{9,5},{10,... | collective-permute-start | bytes 792584 | tf_op jit(solution)/shard_map/ppermute | solution.py:560
  3.9 1.2 %collective-permute-start.2 = (bf16[1032,128]{1,0:T(8,128)(2,1)S(1)}, bf16[1032,128]{1,0:T(8,128)(2,1)S(1)}, u32[]{:S(2)}, u32[]{:S(2)}) collective-permute-start(bf16[1032,128]{1,0:T(8,128)(2,1)S(1)} %get-tuple-element.36), channel_id=1, source_target_pairs={{0,1},{1,0},{2,3},{3,2},{4,5},{5,4},{6,7},{7,6},{8,9},{9,8},{10,11... | collective-permute-start | bytes 792584 | tf_op jit(solution)/shard_map/ppermute | solution.py:560
  5.2 1.1 %collective-permute-start.3 = (bf16[1032,128]{1,0:T(8,128)(2,1)S(1)}, bf16[1032,128]{1,0:T(8,128)(2,1)S(1)}, u32[]{:S(2)}, u32[]{:S(2)}) collective-permute-start(bf16[1032,128]{1,0:T(8,128)(2,1)S(1)} %get-tuple-element.37), channel_id=1, source_target_pairs={{0,8},{1,2},{2,1},{3,11},{4,0},{5,6},{6,5},{7,3},{8,16},{9,10},{10... | collective-permute-start | bytes 792584 | tf_op jit(solution)/shard_map/ppermute | solution.py:560
  6.3 4.6 %step_one.1 = (bf16[4,9,128,512]{3,2,1,0:T(8,128)(2,1)S(1)}, bf16[2,128,512]{2,1,0:T(8,128)(2,1)S(1)}, bf16[2,128,512]{2,1,0:T(8,128)(2,1)S(1)}, bf16[4,512,128]{2,1,0:T(8,128)(2,1)S(1)}) custom-call(s32[4,4,12]{2,1,0:T(4,128)} %codes_hbm.1, bf16[192,128,128]{2,1,0:T(8,128)(2,1)} %bitcast.7, bf16[4,512,128]{2,1,0:T(8,128)(2,1)} %bitcast.6, ...), custom_call_target="tpu_custom_call" | custom-call | flops 8589934592 | bytes 1048576 | tf_op jit(solution)/shard_map/step_one/pallas_call | solution.py:183
  10.8 0.1 collective-permute-start.5
  10.9 0.0 collective-permute-done.2.col_a
  10.9 0.7 %collective-permute-start.4 = (bf16[2,128,512]{2,1,0:T(8,128)(2,1)S(1)}, bf16[2,128,512]{2,1,0:T(8,128)(2,1)S(1)}, u32[]{:S(2)}, u32[]{:S(2)}) collective-permute-start(bf16[2,128,512]{2,1,0:T(8,128)(2,1)S(1)} %get-tuple-element.39), channel_id=1, source_target_pairs={{0,8},{1,2},{2,1},{3,11},{4,0},{5,6},{6,5},{7,3},{8,16},{9,10},{10... | collective-permute-start | bytes 786440 | tf_op jit(solution)/shard_map/ppermute | solution.py:560
  11.6 1.0 %near_terms.1 = (bf16[6,32,128]{2,1,0:T(8,128)(2,1)S(1)}, bf16[6,32,128]{2,1,0:T(8,128)(2,1)S(1)}, bf16[2,6,32,128]{3,2,1,0:T(8,128)(2,1)S(1)}, f32[2,128,128]{2,1,0:T(8,128)S(1)}) custom-call(f32[8,128]{1,0:T(8,128)S(1)} %get-tuple-element.32.after.bits, bf16[4,9,128,512]{3,2,1,0:T(8,128)(2,1)S(1)} %get-tuple-element.33.r, ...), custom_call_target="tpu_custom_call" | custom-call | flops 1 | bytes 1 | tf_op jit(solution)/shard_map/near_terms/pallas_call | solution.py:304
  12.6 0.0 collective-permute-done.5.from_a
  12.6 0.2 collective-permute-start.8
  12.8 0.0 collective-permute-done.3.col_b
  12.8 0.3 %mid_terms.1 = (f32[4,128,128]{2,1,0:T(8,128)S(1)}, f32[8,128]{1,0:T(8,128)S(1)}) custom-call(f32[8,128]{1,0:T(8,128)S(1)} %get-tuple-element.32.after.bits, bf16[4,9,128,512]{3,2,1,0:T(8,128)(2,1)S(1)} %get-tuple-element.33.r, bf16[1032,128]{1,0:T(8,128)(2,1)S(1)} %collective-permute-done.2.col_a, bf16[1032,128]{1,0:T(8,128)(2,1)S(1)} %collective-permute-done.3.col_b), custom_call_target="tpu_custom_call" | custom-call | flops 1 | bytes 1 | tf_op jit(solution)/shard_map/mid_terms/pallas_call | solution.py:338
  13.1 4.7 %collective-permute-done.4.refs_3_ = bf16[2,128,512]{2,1,0:T(8,128)(2,1)S(1)} collective-permute-done((bf16[2,128,512]{2,1,0:T(8,128)(2,1)S(1)}, bf16[2,128,512]{2,1,0:T(8,128)(2,1)S(1)}, u32[]{:S(2)}, u32[]{:S(2)}) %collective-permute-start.4) | collective-permute-done | bytes 262176 | tf_op jit(solution)/shard_map/ppermute | solution.py:560
  17.8 0.0 collective-permute-done.refs_0_
  17.8 0.0 collective-permute-done.1.refs_1_
  17.8 0.6 %far_terms.1 = (bf16[464,128]{1,0:T(8,128)(2,1)S(1)}, bf16[464,128]{1,0:T(8,128)(2,1)S(1)}, bf16[464,128]{1,0:T(8,128)(2,1)S(1)}, bf16[464,128]{1,0:T(8,128)(2,1)S(1)}) custom-call(f32[8,128]{1,0:T(8,128)S(1)} %get-tuple-element.32.after.bits, bf16[4,9,128,512]{3,2,1,0:T(8,128)(2,1)S(1)} %get-tuple-element.33.r, ...), custom_call_target="tpu_custom_call" | custom-call | flops 1 | bytes 1 | tf_op jit(solution)/shard_map/far_terms/pallas_call | solution.py:384
  18.5 0.1 collective-permute-start.6
  18.6 1.6 %collective-permute-start.7 = (bf16[464,128]{1,0:T(8,128)(2,1)S(1)}, bf16[464,128]{1,0:T(8,128)(2,1)S(1)}, u32[]{:S(2)}, u32[]{:S(2)}) collective-permute-start(bf16[464,128]{1,0:T(8,128)(2,1)S(1)} %get-tuple-element.52), channel_id=1, source_target_pairs={{0,3},{1,2},{2,1},{3,0},{4,7},{5,6},{6,5},{7,4},{8,11},{9,10},{10,... | collective-permute-start | bytes 356360 | tf_op jit(solution)/shard_map/ppermute | solution.py:564
  20.1 0.3 collective-permute-start.10
  20.4 0.0 collective-permute-done.8.refs_2_
  20.4 0.3 %collective-permute-start.9 = (bf16[2,6,32,128]{3,2,1,0:T(8,128)(2,1)S(1)}, bf16[2,6,32,128]{3,2,1,0:T(8,128)(2,1)S(1)}, u32[]{:S(2)}, u32[]{:S(2)}) collective-permute-start(bf16[2,6,32,128]{3,2,1,0:T(8,128)(2,1)S(1)} %pad_maximum_fusion), channel_id=1, source_target_pairs={{0,1},{1,0},{2,3},{3,2},{4,5},{5,4},{6,7},{7,6},{8,9},{9,8},{10,11... | collective-permute-start | bytes 294920 | tf_op jit(solution)/shard_map/ppermute | solution.py:564
  20.7 0.7 %collective-permute-done.10.refs_1_ = bf16[464,128]{1,0:T(8,128)(2,1)S(1)} collective-permute-done((bf16[464,128]{1,0:T(8,128)(2,1)S(1)}, bf16[464,128]{1,0:T(8,128)(2,1)S(1)}, u32[]{:S(2)}, u32[]{:S(2)}) %collective-permute-start.10) | collective-permute-done | bytes 118816 | tf_op jit(solution)/shard_map/ppermute | solution.py:564
  21.5 0.3 %collective-permute-done.9.refs_3_ = bf16[2,6,32,128]{3,2,1,0:T(8,128)(2,1)S(1)} collective-permute-done((bf16[2,6,32,128]{3,2,1,0:T(8,128)(2,1)S(1)}, bf16[2,6,32,128]{3,2,1,0:T(8,128)(2,1)S(1)}, u32[]{:S(2)}, u32[]{:S(2)}) %collective-permute-start.9) | collective-permute-done | bytes 98336 | tf_op jit(solution)/shard_map/ppermute | solution.py:564
  21.8 1.0 %unpack.2.refs_4_ = bf16[4,2,9,2,32,128]{5,4,3,2,1,0:T(8,128)(2,1)} custom-call(bf16[464,128]{1,0:T(8,128)(2,1)S(1)} %get-tuple-element.57.refs_0_, bf16[464,128]{1,0:T(8,128)(2,1)S(1)} %collective-permute-done.10.refs_1_, bf16[6,32,128]{2,1,0:T(8,128)(2,1)S(1)} %get-tuple-element.41.refs_4_.refs_2_, bf16[2,6,32,128]{3,2,1,0:T(8,128)(2,1)S(1)} %collective-permute-done.9.refs_3_), custom_call_target="tpu_custom_call" | custom-call | flops 1 | bytes 1 | tf_op jit(solution)/shard_map/unpack/pallas_call | solution.py:450
  22.8 0.6 %collective-permute-done.6.refs_0_ = bf16[464,128]{1,0:T(8,128)(2,1)S(1)} collective-permute-done((bf16[464,128]{1,0:T(8,128)(2,1)S(1)}, bf16[464,128]{1,0:T(8,128)(2,1)S(1)}, u32[]{:S(2)}, u32[]{:S(2)}) %collective-permute-start.6) | collective-permute-done | bytes 118816 | tf_op jit(solution)/shard_map/ppermute | solution.py:564
  23.5 2.6 %collective-permute-done.7.refs_1_ = bf16[464,128]{1,0:T(8,128)(2,1)S(1)} collective-permute-done((bf16[464,128]{1,0:T(8,128)(2,1)S(1)}, bf16[464,128]{1,0:T(8,128)(2,1)S(1)}, u32[]{:S(2)}, u32[]{:S(2)}) %collective-permute-start.7) | collective-permute-done | bytes 118816 | tf_op jit(solution)/shard_map/ppermute | solution.py:564
  26.0 1.0 %unpack.3 = bf16[4,2,9,2,32,128]{5,4,3,2,1,0:T(8,128)(2,1)} custom-call(bf16[464,128]{1,0:T(8,128)(2,1)S(1)} %collective-permute-done.6.refs_0_, bf16[464,128]{1,0:T(8,128)(2,1)S(1)} %collective-permute-done.7.refs_1_, bf16[2,6,32,128]{3,2,1,0:T(8,128)(2,1)S(1)} %collective-permute-done.8.refs_2_, ...), custom_call_target="tpu_custom_call", output_to_operand_aliasing={{}: (4, {})} | custom-call | flops 1 | bytes 1 | tf_op jit(solution)/shard_map/unpack/pallas_call | solution.py:450
  (3 shorter events, 0.0 us)
Async XLA Ops:
  1.4 16.4 %collective-permute-start = (bf16[1032,128]{1,0:T(8,128)(2,1)S(1)}, bf16[1032,128]{1,0:T(8,128)(2,1)S(1)}, u32[]{:S(2)}, u32[]{:S(2)}) collective-permute-start(bf16[1032,128]{1,0:T(8,128)(2,1)S(1)} %get-tuple-element.34), channel_id=1, source_target_pairs={{0,4},{1,5},{2,6},{3,7},{4,0},{5,1},{6,2},{7,3},{8,12},{9,13},{10,... | collective-permute-start | bytes 792584 | tf_op jit(solution)/shard_map/ppermute | solution.py:560
  1.5 16.4 %collective-permute-start.1 = (bf16[1032,128]{1,0:T(8,128)(2,1)S(1)}, bf16[1032,128]{1,0:T(8,128)(2,1)S(1)}, u32[]{:S(2)}, u32[]{:S(2)}) collective-permute-start(bf16[1032,128]{1,0:T(8,128)(2,1)S(1)} %get-tuple-element.35), channel_id=1, source_target_pairs={{0,1},{1,0},{2,3},{3,2},{4,8},{5,9},{6,10},{7,11},{8,4},{9,5},{10,... | collective-permute-start | bytes 792584 | tf_op jit(solution)/shard_map/ppermute | solution.py:560
  3.9 7.0 %collective-permute-start.2 = (bf16[1032,128]{1,0:T(8,128)(2,1)S(1)}, bf16[1032,128]{1,0:T(8,128)(2,1)S(1)}, u32[]{:S(2)}, u32[]{:S(2)}) collective-permute-start(bf16[1032,128]{1,0:T(8,128)(2,1)S(1)} %get-tuple-element.36), channel_id=1, source_target_pairs={{0,1},{1,0},{2,3},{3,2},{4,5},{5,4},{6,7},{7,6},{8,9},{9,8},{10,11... | collective-permute-start | bytes 792584 | tf_op jit(solution)/shard_map/ppermute | solution.py:560
  5.2 7.7 %collective-permute-start.3 = (bf16[1032,128]{1,0:T(8,128)(2,1)S(1)}, bf16[1032,128]{1,0:T(8,128)(2,1)S(1)}, u32[]{:S(2)}, u32[]{:S(2)}) collective-permute-start(bf16[1032,128]{1,0:T(8,128)(2,1)S(1)} %get-tuple-element.37), channel_id=1, source_target_pairs={{0,8},{1,2},{2,1},{3,11},{4,0},{5,6},{6,5},{7,3},{8,16},{9,10},{10... | collective-permute-start | bytes 792584 | tf_op jit(solution)/shard_map/ppermute | solution.py:560
  10.8 1.8 %collective-permute-start.5 = (bf16[2,128,512]{2,1,0:T(8,128)(2,1)S(1)}, bf16[2,128,512]{2,1,0:T(8,128)(2,1)S(1)}, u32[]{:S(2)}, u32[]{:S(2)}) collective-permute-start(bf16[2,128,512]{2,1,0:T(8,128)(2,1)S(1)} %get-tuple-element.44), channel_id=1, source_target_pairs={{0,1},{1,0},{2,3},{3,2},{4,5},{5,4},{6,7},{7,6},{8,9},{9,8},{10,11... | collective-permute-start | bytes 786440 | tf_op jit(solution)/shard_map/ppermute | solution.py:560
  10.9 6.9 %collective-permute-start.4 = (bf16[2,128,512]{2,1,0:T(8,128)(2,1)S(1)}, bf16[2,128,512]{2,1,0:T(8,128)(2,1)S(1)}, u32[]{:S(2)}, u32[]{:S(2)}) collective-permute-start(bf16[2,128,512]{2,1,0:T(8,128)(2,1)S(1)} %get-tuple-element.39), channel_id=1, source_target_pairs={{0,8},{1,2},{2,1},{3,11},{4,0},{5,6},{6,5},{7,3},{8,16},{9,10},{10... | collective-permute-start | bytes 786440 | tf_op jit(solution)/shard_map/ppermute | solution.py:560
  12.6 7.8 %collective-permute-start.8 = (bf16[2,6,32,128]{3,2,1,0:T(8,128)(2,1)S(1)}, bf16[2,6,32,128]{3,2,1,0:T(8,128)(2,1)S(1)}, u32[]{:S(2)}, u32[]{:S(2)}) collective-permute-start(bf16[2,6,32,128]{3,2,1,0:T(8,128)(2,1)S(1)} %get-tuple-element.54), channel_id=1, source_target_pairs={{0,2},{1,3},{2,0},{3,1},{4,6},{5,7},{6,4},{7,5},{8,10},{9,11},{10,... | collective-permute-start | bytes 294920 | tf_op jit(solution)/shard_map/ppermute | solution.py:564
  18.5 5.0 %collective-permute-start.6 = (bf16[464,128]{1,0:T(8,128)(2,1)S(1)}, bf16[464,128]{1,0:T(8,128)(2,1)S(1)}, u32[]{:S(2)}, u32[]{:S(2)}) collective-permute-start(bf16[464,128]{1,0:T(8,128)(2,1)S(1)} %get-tuple-element.51), channel_id=1, source_target_pairs={{0,2},{1,3},{2,0},{3,1},{4,6},{5,7},{6,4},{7,5},{8,10},{9,11},{10,... | collective-permute-start | bytes 356360 | tf_op jit(solution)/shard_map/ppermute | solution.py:564
  18.6 7.5 %collective-permute-start.7 = (bf16[464,128]{1,0:T(8,128)(2,1)S(1)}, bf16[464,128]{1,0:T(8,128)(2,1)S(1)}, u32[]{:S(2)}, u32[]{:S(2)}) collective-permute-start(bf16[464,128]{1,0:T(8,128)(2,1)S(1)} %get-tuple-element.52), channel_id=1, source_target_pairs={{0,3},{1,2},{2,1},{3,0},{4,7},{5,6},{6,5},{7,4},{8,11},{9,10},{10,... | collective-permute-start | bytes 356360 | tf_op jit(solution)/shard_map/ppermute | solution.py:564
  20.1 1.3 %collective-permute-start.10 = (bf16[464,128]{1,0:T(8,128)(2,1)S(1)}, bf16[464,128]{1,0:T(8,128)(2,1)S(1)}, u32[]{:S(2)}, u32[]{:S(2)}) collective-permute-start(bf16[464,128]{1,0:T(8,128)(2,1)S(1)} %get-tuple-element.58), channel_id=1, source_target_pairs={{0,1},{1,0},{2,3},{3,2},{4,5},{5,4},{6,7},{7,6},{8,9},{9,8},{10,11... | collective-permute-start | bytes 356360 | tf_op jit(solution)/shard_map/ppermute | solution.py:564
  20.4 1.4 %collective-permute-start.9 = (bf16[2,6,32,128]{3,2,1,0:T(8,128)(2,1)S(1)}, bf16[2,6,32,128]{3,2,1,0:T(8,128)(2,1)S(1)}, u32[]{:S(2)}, u32[]{:S(2)}) collective-permute-start(bf16[2,6,32,128]{3,2,1,0:T(8,128)(2,1)S(1)} %pad_maximum_fusion), channel_id=1, source_target_pairs={{0,1},{1,0},{2,3},{3,2},{4,5},{5,4},{6,7},{7,6},{8,9},{9,8},{10,11... | collective-permute-start | bytes 294920 | tf_op jit(solution)/shard_map/ppermute | solution.py:564

commit v8 on v7

--- a/solution.py
+++ b/solution.py
@@ -14,8 +14,8 @@
 HEAD = 8
 ROWS = 2 * QUAD + HEAD
 BITS = 16
-OWN_SLOTS = 6
-SLOTS = 14
+OWN_SLOTS = 8
+SLOTS = 12
 ANY = pl.BlockSpec(memory_space=pl.ANY)
 VMEM = pl.BlockSpec(memory_space=pltpu.VMEM)
 HBM = pl.BlockSpec(memory_space=pltpu.HBM)
@@ -246,8 +246,8 @@
             out[first : first + rows, :] = values[t, pl.ds(start, rows), :].astype(BF16)
 
 
-def near_kernel(parts, bits, r, prolong, col_a, *rest):
-    outs, (extra_a, slots, right) = rest[:-3], rest[-3:]
+def near_kernel(parts, bits, r, prolong, col_a, col_b, *rest):
+    outs, (columns, column_head, slots, right) = rest[:-4], rest[-4:]
     fx, fy = flips()
 
     def by_halves(quads, own, first):
@@ -278,11 +278,15 @@
         at = pl.ds(pl.multiple_of(vr * 256, 256), 256)
         quads.append(((u, v), [prolong[2 * ur + m, at, :] for m in range(2)], bits[j : j + 1, :]))
     by_halves(quads, range(4), 0)
-    near = [sums(r, p, ((1, 3), (2, 3))) for p in ((1, 2), (2, 2))]
-    base, extra = edge_slots(near, col_a, jnp.abs(bits[0:1, :] - bits[1:2, :]))
-    for t in range(2):
-        slots[4 + t] = base[t]
-        extra_a[t] = extra[t]
+    split_y = jnp.abs(bits[0:1, :] - bits[1:2, :])
+    for e, (far, own, side, scale) in enumerate(((col_a, 2, 3, None), (col_b, 1, 0, inside("col", parts)))):
+        near = [sums(r, (u, own), ((1, side), (2, side))) for u in (1, 2)]
+        base, extra = edge_slots(near, far, split_y)
+        for t in range(2):
+            slots[4 + 2 * e + t] = base[t] if scale is None else base[t] * scale
+            columns[2 * e + t] = extra[t] if scale is None else extra[t] * scale
+            column_head[2 * e + t : 2 * e + t + 1, :] = half_of(far, t)
+    column_head[4:8, :] = bits[0:4, :]
     rows = BS // parts
     me = lax.axis_index("col")
     for s in range(parts):
@@ -300,7 +304,8 @@
     rows = BS // parts
     one = jax.ShapeDtypeStruct((OWN_SLOTS, rows, BS), BF16)
     two = jax.ShapeDtypeStruct((2, OWN_SLOTS, rows, BS), BF16)
-    shapes = (one, one) + (two,) * (parts // 2 - 1) + (jax.ShapeDtypeStruct((2, BS, BS), F32),)
+    shapes = (one, one) + (two,) * (parts // 2 - 1)
+    shapes += (jax.ShapeDtypeStruct((4, BS, BS), F32), jax.ShapeDtypeStruct((8, BS), F32))
     return pl.pallas_call(
         functools.partial(near_kernel, parts),
         out_shape=shapes,
@@ -322,31 +327,7 @@
             head[2 * e + t : 2 * e + t + 1, :] = half_of(far, t)
 
 
-def mid_kernel(parts, bits, r, col_a, col_b, columns, head):
-    near = [sums(r, p, ((1, 0), (2, 0))) for p in ((1, 1), (2, 1))]
-    base, extra = edge_slots(near, col_b, jnp.abs(bits[0:1, :] - bits[1:2, :]))
-    scale = inside("col", parts)
-    for t in range(2):
-        columns[t] = base[t] * scale
-        columns[2 + t] = extra[t] * scale
-        head[t : t + 1, :] = half_of(col_a, t)
-        head[2 + t : 3 + t, :] = half_of(col_b, t)
-    head[4:8, :] = bits[0:4, :]
-
-
-def mid_terms(parts, *operands):
-    return pl.pallas_call(
-        functools.partial(mid_kernel, parts),
-        out_shape=(jax.ShapeDtypeStruct((4, BS, BS), F32), jax.ShapeDtypeStruct((8, BS), F32)),
-        in_specs=[VMEM] * len(operands),
-        out_specs=(VMEM, VMEM),
-        compiler_params=pltpu.CompilerParams(vmem_limit_bytes=8 << 20),
-        cost_estimate=pl.CostEstimate(flops=1, bytes_accessed=1, transcendentals=0),
-        name="mid_terms",
-    )(*operands)
-
-
-def far_kernel(counts, bits, r, row_a, row_b, from_a, from_b, columns, column_head, extra_a, *rest):
+def far_kernel(counts, bits, r, row_a, row_b, from_a, from_b, columns, column_head, *rest):
     outs, (slots, head) = rest[:-2], rest[-2:]
     split_x = 1.0 - jnp.abs(bits[0:1, :] - bits[1:2, :])
     row_in, col_in = inside("row", counts[0]), inside("col", counts[1])
@@ -358,9 +339,8 @@
         (row_b, ((1, 1), (1, 2)), ((0, 1), (0, 2)), split_x, row_in),
     )
     fill_edges(r, edges, slots, head.at[4:8])
-    for t in range(2):
-        slots[4 + t] += extra_a[t]
-        slots[6 + t] += columns[2 + t]
+    for t in range(4):
+        slots[4 + t] += columns[t]
     corners = (
         (from_a.at[0], quad_of(row_a, 1), None),
         (from_b.at[0], quad_of(row_a, 0), col_in),
@@ -371,9 +351,8 @@
         value = jnp.dot(near[...], far, preferred_element_type=F32)
         slots[8 + e] = value if scale is None else value * scale
     store_pieces(outs, 0, slots.at[0:4])
-    store_pieces(outs, 4, columns.at[0:2])
-    store_pieces(outs, 6, slots.at[8:12])
-    store_pieces(outs, 10, slots.at[4:8])
+    store_pieces(outs, 4, slots.at[8:12])
+    store_pieces(outs, 8, slots.at[4:8])
     for out in outs:
         out[out.shape[0] - BITS :, :] = head[...].astype(BF16)
 
@@ -402,7 +381,7 @@
     for i, (s, ref) in enumerate(zip(steps, ins)):
         square = me ^ s
         fy = lax.rem(square, 2)
-        own = owns[i] if s == 0 else owns[i].at[s // 2 if s % 2 else 0]
+        own = owns[i] if s < 2 else owns[i].at[s // 2 - 1 if s % 2 else 0]
         for a in range(2):
             copies.append(
                 pltpu.make_async_copy(own.at[2 * a : 2 * a + 2], out.at[square, a, 4], sems.at[len(copies)])
@@ -417,13 +396,16 @@
 
         split_x = 1.0 - split_y
         edges = (
-            ((2, 3), (0, 1), (10, 11), split_y, 7 - 6 * fx),
-            ((0, 1), (2, 3), (12, 13), split_y, 1 + 6 * fx),
-            ((1, 3), None, (10, 11), split_x, 3 + turn3(2, fy)),
-            ((0, 2), (4, 5), (12, 13), split_x, 3 + turn3(0, fy)),
+            ((2, 3), (8, 9), split_y, 7 - 6 * fx),
+            ((0, 1), (10, 11), split_y, 1 + 6 * fx),
+            ((1, 3), (8, 9), split_x, 3 + turn3(2, fy)),
+            ((0, 2), (10, 11), split_x, 3 + turn3(0, fy)),
         )
-        for e, (ps, base, more, used, code) in enumerate(edges):
-            values = [slot(ref, t) for t in base] if base else [own[4 + t].astype(F32) for t in range(2)]
+        for e, (ps, more, used, code) in enumerate(edges):
+            if e < 2:
+                values = [slot(ref, 2 * e + t) for t in range(2)]
+            else:
+                values = [own[2 * e + t].astype(F32) for t in range(2)]
             second = [slot(ref, t) for t in more]
             spread_edge(buf, (i, e), one, ps, (4 + 2 * e, 5 + 2 * e), values, second, used)
             send(e, square, code)
@@ -437,7 +419,7 @@
             (low, 6 * fx, 0, 10, 6),
         )
         for e, (owner, group, side, a_bit, b_bit) in enumerate(corners):
-            spread_corner(buf, (i, 4 + e), slot(ref, 6 + e), one(a_bit), one(b_bit))
+            spread_corner(buf, (i, 4 + e), slot(ref, 4 + e), one(a_bit), one(b_bit))
             send(4 + e, owner, group + turn3(side, lax.rem(owner, 2)))
     for copy in copies:
         copy.wait()
@@ -579,16 +561,15 @@
     r, to_a, to_b, own_blocks = step_one(neighbours, coupling, prolong_rows, bits)
     from_b = swap(to_b, col_low)
     from_a = swap(to_a, col_high)
-    mine, pair, *cross, extra_a = near_terms(parts, bits, r, own_blocks, col_a)
-    from_a, *cross = lax.optimization_barrier((from_a, *cross))
+    mine, pair, *cross, columns, column_head = near_terms(parts, bits, r, own_blocks, col_a, col_b)
     direct = [xor_swap(value, 2 * h + 2) for h, value in enumerate(cross)]
-    columns, column_head = mid_terms(parts, bits, r, col_a, col_b)
     row_a, row_b, columns, from_b = gate((row_a, row_b, columns, from_b), (mine,))
-    outs = list(far_terms(counts, bits, r, row_a, row_b, from_a, from_b, columns, column_head, extra_a))
-    outs[0], *direct = lax.optimization_barrier((outs[0], *direct))
+    outs = list(far_terms(counts, bits, r, row_a, row_b, from_a, from_b, columns, column_head))
+    outs[0], pair, *direct = lax.optimization_barrier((outs[0], pair, *direct))
     outs = [outs[0]] + [xor_swap(outs[s], s) for s in range(1, parts)]
-    relayed = xor_swap(jnp.stack([pair] + [value[1] for value in direct]), 1)
-    owns = [mine, relayed]
+    pair = xor_swap(pair, 1)
+    relayed = xor_swap(jnp.concatenate([value[1:2] for value in direct]), 1)
+    owns = [mine, pair]
     for value in direct:
         owns += [value, relayed]
     coarse = unpack(outs[:2], owns[:2], range(2), None)

time: 27.3 us -> 27 us (0.989)
  waiting for transfers between devices: 9 us -> 7.28 us
  starting transfers between devices: 8.06 us -> 9.54 us
    ppermute x5 -> x6, starting transfers between devices: 2.43 us -> 3.97 us  [xor_swap(): lax.ppermute(value, 'col', [(i, i ^ s) for i in range(lax.axis_size('col'...]
    ppermute x5 -> x6, waiting for transfers between devices: 4.3 us -> 3.18 us  [xor_swap(): lax.ppermute(value, 'col', [(i, i ^ s) for i in range(lax.axis_size('col'...]
    ppermute x6, waiting for transfers between devices: 4.7 us -> 4.1 us  [swap(): return lax.ppermute(value, ('row', 'col'), pairs)]
    pallas_call x1 -> x0, Pallas kernels: 0.31 us -> none  [mid_terms(): pl.pallas_call(functools.partial(mid_kernel, parts), out_shape=(jax.Shape...]
  transfers between devices with their start and end apart: 11 -> 12, of which waited for: 5 -> 3; matrix products, arithmetic and copies ran while one was open for 0% -> 0% of each run, Pallas kernels for 28% -> 28%
where the time goes in v8:
time: 27 us; the launch traced here: 26.7 us
  Pallas kernels  9.81 us (36%)
  starting transfers between devices  9.54 us (35%)
  waiting for transfers between devices  7.28 us (27%)
    ppermute x6, starting transfers between devices, swap(): return lax.ppermute(value, ('row', 'col'), pairs)  5.57 us
    pallas_call x1, Pallas kernels, step_one(): pl.pallas_call(step_one_kernel, out_shape=(jax.ShapeDtypeStruct((4, 9, BS...  4.56 us
    ppermute x6, waiting for transfers between devices, swap(): return lax.ppermute(value, ('row', 'col'), pairs)  4.1 us
    ppermute x6, starting transfers between devices, xor_swap(): lax.ppermute(value, 'col', [(i, i ^ s) for i in range(lax.axis_size('col'...  3.97 us
    ppermute x6, waiting for transfers between devices, xor_swap(): lax.ppermute(value, 'col', [(i, i ^ s) for i in range(lax.axis_size('col'...  3.18 us
    pallas_call x2, Pallas kernels, unpack(): pl.pallas_call(functools.partial(unpack_kernel, parts, steps), out_shape=...  2.06 us
    pallas_call x1, Pallas kernels, rims(): pl.pallas_call(rims_kernel, out_shape=(shape,) * 4 + (jax.ShapeDtypeStruc...  1.38 us
    pallas_call x1, Pallas kernels, near_terms(): pl.pallas_call(functools.partial(near_kernel, parts), out_shape=shapes, i...  1.18 us
  transfers between devices with their start and end apart: 12, of which 3 were waited for; matrix products, arithmetic and copies ran while one was open for 0% of the time, Pallas kernels for 28%

profile of v8, /device:TPU:5, one launch (start us, length us, event | category | flops | bytes accessed | tf_op | source)
XLA Modules:
  0.0 26.7 jit_solution(15713496736086584674)
XLA Ops:
  0.0 1.4 %rims.1 = (bf16[1032,128]{1,0:T(8,128)(2,1)S(1)}, bf16[1032,128]{1,0:T(8,128)(2,1)S(1)}, bf16[1032,128]{1,0:T(8,128)(2,1)S(1)}, bf16[1032,128]{1,0:T(8,128)(2,1)S(1)}, f32[8,128]{1,0:T(8,128)S(1)}) custom-call(s32[4,4]{1,0:T(4,128)} %agg_hbm.1, bf16[4,512,128]{2,1,0:T(8,128)(2,1)} %bitcast.3), custom_call_target="tpu_custom_call" | custom-call | tf_op jit(solution)/shard_map/rims/pallas_call | solution.py:72
  1.4 0.1 collective-permute-start
  1.5 2.5 %collective-permute-start.1 = (bf16[1032,128]{1,0:T(8,128)(2,1)S(1)}, bf16[1032,128]{1,0:T(8,128)(2,1)S(1)}, u32[]{:S(2)}, u32[]{:S(2)}) collective-permute-start(bf16[1032,128]{1,0:T(8,128)(2,1)S(1)} %get-tuple-element.33), channel_id=1, source_target_pairs={{0,1},{1,0},{2,3},{3,2},{4,8},{5,9},{6,10},{7,11},{8,4},{9,5},{10,... | collective-permute-start | bytes 792584 | tf_op jit(solution)/shard_map/ppermute | solution.py:542
  3.9 1.2 %collective-permute-start.2 = (bf16[1032,128]{1,0:T(8,128)(2,1)S(1)}, bf16[1032,128]{1,0:T(8,128)(2,1)S(1)}, u32[]{:S(2)}, u32[]{:S(2)}) collective-permute-start(bf16[1032,128]{1,0:T(8,128)(2,1)S(1)} %get-tuple-element.35), channel_id=1, source_target_pairs={{0,1},{1,0},{2,3},{3,2},{4,5},{5,4},{6,7},{7,6},{8,9},{9,8},{10,11... | collective-permute-start | bytes 792584 | tf_op jit(solution)/shard_map/ppermute | solution.py:542
  5.2 1.1 %collective-permute-start.3 = (bf16[1032,128]{1,0:T(8,128)(2,1)S(1)}, bf16[1032,128]{1,0:T(8,128)(2,1)S(1)}, u32[]{:S(2)}, u32[]{:S(2)}) collective-permute-start(bf16[1032,128]{1,0:T(8,128)(2,1)S(1)} %get-tuple-element.36), channel_id=1, source_target_pairs={{0,8},{1,2},{2,1},{3,11},{4,0},{5,6},{6,5},{7,3},{8,16},{9,10},{10... | collective-permute-start | bytes 792584 | tf_op jit(solution)/shard_map/ppermute | solution.py:542
  6.3 4.6 %step_one.1 = (bf16[4,9,128,512]{3,2,1,0:T(8,128)(2,1)S(1)}, bf16[2,128,512]{2,1,0:T(8,128)(2,1)S(1)}, bf16[2,128,512]{2,1,0:T(8,128)(2,1)S(1)}, bf16[4,512,128]{2,1,0:T(8,128)(2,1)S(1)}) custom-call(s32[4,4,12]{2,1,0:T(4,128)} %codes_hbm.1, bf16[192,128,128]{2,1,0:T(8,128)(2,1)} %bitcast.5, bf16[4,512,128]{2,1,0:T(8,128)(2,1)} %bitcast.4, ...), custom_call_target="tpu_custom_call" | custom-call | flops 8589934592 | bytes 1048576 | tf_op jit(solution)/shard_map/step_one/pallas_call | solution.py:183
  10.8 0.7 %collective-permute-start.4 = (bf16[2,128,512]{2,1,0:T(8,128)(2,1)S(1)}, bf16[2,128,512]{2,1,0:T(8,128)(2,1)S(1)}, u32[]{:S(2)}, u32[]{:S(2)}) collective-permute-start(bf16[2,128,512]{2,1,0:T(8,128)(2,1)S(1)} %get-tuple-element.38), channel_id=1, source_target_pairs={{0,8},{1,2},{2,1},{3,11},{4,0},{5,6},{6,5},{7,3},{8,16},{9,10},{10... | collective-permute-start | bytes 786440 | tf_op jit(solution)/shard_map/ppermute | solution.py:542
  11.5 0.0 collective-permute-done.2.col_a
  11.5 0.0 collective-permute-start.5
  11.5 0.0 collective-permute-done.3.col_b
  11.5 1.2 %near_terms.1 = (bf16[8,32,128]{2,1,0:T(8,128)(2,1)S(1)}, bf16[8,32,128]{2,1,0:T(8,128)(2,1)S(1)}, bf16[2,8,32,128]{3,2,1,0:T(8,128)(2,1)S(1)}, f32[4,128,128]{2,1,0:T(8,128)S(1)}, f32[8,128]{1,0:T(8,128)S(1)}) custom-call(f32[8,128]{1,0:T(8,128)S(1)} %get-tuple-element.30.after.bits, bf16[4,9,128,512]{3,2,1,0:T(8,128)(2,1)S(1)} %get-tuple-element.31.r, ...), custom_call_target="tpu_custom_call" | custom-call | flops 1 | bytes 1 | tf_op jit(solution)/shard_map/near_terms/pallas_call | solution.py:309
  12.7 1.3 %collective-permute-start.8 = (bf16[2,8,32,128]{3,2,1,0:T(8,128)(2,1)S(1)}, bf16[2,8,32,128]{3,2,1,0:T(8,128)(2,1)S(1)}, u32[]{:S(2)}, u32[]{:S(2)}) collective-permute-start(bf16[2,8,32,128]{3,2,1,0:T(8,128)(2,1)S(1)} %get-tuple-element.50), channel_id=1, source_target_pairs={{0,2},{1,3},{2,0},{3,1},{4,6},{5,7},{6,4},{7,5},{8,10},{9,11},{10,... | collective-permute-start | bytes 393224 | tf_op jit(solution)/shard_map/ppermute | solution.py:546
  14.0 4.1 %collective-permute-done.4.refs_3_ = bf16[2,128,512]{2,1,0:T(8,128)(2,1)S(1)} collective-permute-done((bf16[2,128,512]{2,1,0:T(8,128)(2,1)S(1)}, bf16[2,128,512]{2,1,0:T(8,128)(2,1)S(1)}, u32[]{:S(2)}, u32[]{:S(2)}) %collective-permute-start.4) | collective-permute-done | bytes 262176 | tf_op jit(solution)/shard_map/ppermute | solution.py:542
  18.1 0.0 collective-permute-done.refs_0_
  18.1 0.0 collective-permute-done.1.refs_1_
  18.1 0.0 collective-permute-done.5.from_a
  18.1 0.6 %far_terms.1 = (bf16[400,128]{1,0:T(8,128)(2,1)S(1)}, bf16[400,128]{1,0:T(8,128)(2,1)S(1)}, bf16[400,128]{1,0:T(8,128)(2,1)S(1)}, bf16[400,128]{1,0:T(8,128)(2,1)S(1)}) custom-call(f32[8,128]{1,0:T(8,128)S(1)} %get-tuple-element.30.after.bits, bf16[4,9,128,512]{3,2,1,0:T(8,128)(2,1)S(1)} %get-tuple-element.31.r, ...), custom_call_target="tpu_custom_call" | custom-call | flops 1 | bytes 1 | tf_op jit(solution)/shard_map/far_terms/pallas_call | solution.py:363
  18.7 0.1 collective-permute-start.10
  18.8 0.1 collective-permute-start.6
  18.9 2.0 %collective-permute-start.7 = (bf16[400,128]{1,0:T(8,128)(2,1)S(1)}, bf16[400,128]{1,0:T(8,128)(2,1)S(1)}, u32[]{:S(2)}, u32[]{:S(2)}) collective-permute-start(bf16[400,128]{1,0:T(8,128)(2,1)S(1)} %get-tuple-element.47), channel_id=1, source_target_pairs={{0,3},{1,2},{2,1},{3,0},{4,7},{5,6},{6,5},{7,4},{8,11},{9,10},{10,... | collective-permute-start | bytes 307208 | tf_op jit(solution)/shard_map/ppermute | solution.py:546
  20.9 0.0 collective-permute-done.8.refs_2_
  21.0 0.0 collective-permute-start.11
  21.0 0.5 %collective-permute-start.9 = (bf16[1,8,32,128]{3,2,1,0:T(8,128)(2,1)S(1)}, bf16[1,8,32,128]{3,2,1,0:T(8,128)(2,1)S(1)}, u32[]{:S(2)}, u32[]{:S(2)}) collective-permute-start(bf16[1,8,32,128]{3,2,1,0:T(8,128)(2,1)S(1)} %slice.3), channel_id=1, source_target_pairs={{0,1},{1,0},{2,3},{3,2},{4,5},{5,4},{6,7},{7,6},{8,9},{9,8},{10,11... | collective-permute-start | bytes 196616 | tf_op jit(solution)/shard_map/ppermute | solution.py:546
  21.5 0.0 collective-permute-done.10.refs_1_
  21.5 0.7 %collective-permute-done.11.refs_3_ = bf16[8,32,128]{2,1,0:T(8,128)(2,1)S(1)} collective-permute-done((bf16[8,32,128]{2,1,0:T(8,128)(2,1)S(1)}, bf16[8,32,128]{2,1,0:T(8,128)(2,1)S(1)}, u32[]{:S(2)}, u32[]{:S(2)}) %collective-permute-start.11) | collective-permute-done | bytes 65568 | tf_op jit(solution)/shard_map/ppermute | solution.py:546
  22.2 1.0 %unpack.2.refs_4_ = bf16[4,2,9,2,32,128]{5,4,3,2,1,0:T(8,128)(2,1)} custom-call(bf16[400,128]{1,0:T(8,128)(2,1)S(1)} %get-tuple-element.52.refs_0_, bf16[400,128]{1,0:T(8,128)(2,1)S(1)} %collective-permute-done.10.refs_1_, bf16[8,32,128]{2,1,0:T(8,128)(2,1)S(1)} %get-tuple-element.39.refs_4_.refs_2_, bf16[8,32,128]{2,1,0:T(8,128)(2,1)S(1)} %collective-permute-done.11.refs_3_), custom_call_target="tpu_custom_call" | custom-call | flops 1 | bytes 1 | tf_op jit(solution)/shard_map/unpack/pallas_call | solution.py:432
  23.2 0.0 collective-permute-done.6.refs_0_
  23.3 2.4 %collective-permute-done.7.refs_1_ = bf16[400,128]{1,0:T(8,128)(2,1)S(1)} collective-permute-done((bf16[400,128]{1,0:T(8,128)(2,1)S(1)}, bf16[400,128]{1,0:T(8,128)(2,1)S(1)}, u32[]{:S(2)}, u32[]{:S(2)}) %collective-permute-start.7) | collective-permute-done | bytes 102432 | tf_op jit(solution)/shard_map/ppermute | solution.py:546
  25.7 0.0 collective-permute-done.9.refs_3_
  25.7 1.0 %unpack.3 = bf16[4,2,9,2,32,128]{5,4,3,2,1,0:T(8,128)(2,1)} custom-call(bf16[400,128]{1,0:T(8,128)(2,1)S(1)} %collective-permute-done.6.refs_0_, bf16[400,128]{1,0:T(8,128)(2,1)S(1)} %collective-permute-done.7.refs_1_, bf16[2,8,32,128]{3,2,1,0:T(8,128)(2,1)S(1)} %collective-permute-done.8.refs_2_, ...), custom_call_target="tpu_custom_call", output_to_operand_aliasing={{}: (4, {})} | custom-call | flops 1 | bytes 1 | tf_op jit(solution)/shard_map/unpack/pallas_call | solution.py:432
  (2 shorter events, 0.0 us)
Async XLA Ops:
  1.4 16.7 %collective-permute-start = (bf16[1032,128]{1,0:T(8,128)(2,1)S(1)}, bf16[1032,128]{1,0:T(8,128)(2,1)S(1)}, u32[]{:S(2)}, u32[]{:S(2)}) collective-permute-start(bf16[1032,128]{1,0:T(8,128)(2,1)S(1)} %get-tuple-element.32), channel_id=1, source_target_pairs={{0,4},{1,5},{2,6},{3,7},{4,0},{5,1},{6,2},{7,3},{8,12},{9,13},{10,... | collective-permute-start | bytes 792584 | tf_op jit(solution)/shard_map/ppermute | solution.py:542
  1.5 16.6 %collective-permute-start.1 = (bf16[1032,128]{1,0:T(8,128)(2,1)S(1)}, bf16[1032,128]{1,0:T(8,128)(2,1)S(1)}, u32[]{:S(2)}, u32[]{:S(2)}) collective-permute-start(bf16[1032,128]{1,0:T(8,128)(2,1)S(1)} %get-tuple-element.33), channel_id=1, source_target_pairs={{0,1},{1,0},{2,3},{3,2},{4,8},{5,9},{6,10},{7,11},{8,4},{9,5},{10,... | collective-permute-start | bytes 792584 | tf_op jit(solution)/shard_map/ppermute | solution.py:542
  3.9 7.6 %collective-permute-start.2 = (bf16[1032,128]{1,0:T(8,128)(2,1)S(1)}, bf16[1032,128]{1,0:T(8,128)(2,1)S(1)}, u32[]{:S(2)}, u32[]{:S(2)}) collective-permute-start(bf16[1032,128]{1,0:T(8,128)(2,1)S(1)} %get-tuple-element.35), channel_id=1, source_target_pairs={{0,1},{1,0},{2,3},{3,2},{4,5},{5,4},{6,7},{7,6},{8,9},{9,8},{10,11... | collective-permute-start | bytes 792584 | tf_op jit(solution)/shard_map/ppermute | solution.py:542
  5.2 6.4 %collective-permute-start.3 = (bf16[1032,128]{1,0:T(8,128)(2,1)S(1)}, bf16[1032,128]{1,0:T(8,128)(2,1)S(1)}, u32[]{:S(2)}, u32[]{:S(2)}) collective-permute-start(bf16[1032,128]{1,0:T(8,128)(2,1)S(1)} %get-tuple-element.36), channel_id=1, source_target_pairs={{0,8},{1,2},{2,1},{3,11},{4,0},{5,6},{6,5},{7,3},{8,16},{9,10},{10... | collective-permute-start | bytes 792584 | tf_op jit(solution)/shard_map/ppermute | solution.py:542
  10.8 7.3 %collective-permute-start.4 = (bf16[2,128,512]{2,1,0:T(8,128)(2,1)S(1)}, bf16[2,128,512]{2,1,0:T(8,128)(2,1)S(1)}, u32[]{:S(2)}, u32[]{:S(2)}) collective-permute-start(bf16[2,128,512]{2,1,0:T(8,128)(2,1)S(1)} %get-tuple-element.38), channel_id=1, source_target_pairs={{0,8},{1,2},{2,1},{3,11},{4,0},{5,6},{6,5},{7,3},{8,16},{9,10},{10... | collective-permute-start | bytes 786440 | tf_op jit(solution)/shard_map/ppermute | solution.py:542
  11.5 6.6 %collective-permute-start.5 = (bf16[2,128,512]{2,1,0:T(8,128)(2,1)S(1)}, bf16[2,128,512]{2,1,0:T(8,128)(2,1)S(1)}, u32[]{:S(2)}, u32[]{:S(2)}) collective-permute-start(bf16[2,128,512]{2,1,0:T(8,128)(2,1)S(1)} %get-tuple-element.42), channel_id=1, source_target_pairs={{0,1},{1,0},{2,3},{3,2},{4,5},{5,4},{6,7},{7,6},{8,9},{9,8},{10,11... | collective-permute-start | bytes 786440 | tf_op jit(solution)/shard_map/ppermute | solution.py:542
  12.7 8.2 %collective-permute-start.8 = (bf16[2,8,32,128]{3,2,1,0:T(8,128)(2,1)S(1)}, bf16[2,8,32,128]{3,2,1,0:T(8,128)(2,1)S(1)}, u32[]{:S(2)}, u32[]{:S(2)}) collective-permute-start(bf16[2,8,32,128]{3,2,1,0:T(8,128)(2,1)S(1)} %get-tuple-element.50), channel_id=1, source_target_pairs={{0,2},{1,3},{2,0},{3,1},{4,6},{5,7},{6,4},{7,5},{8,10},{9,11},{10,... | collective-permute-start | bytes 393224 | tf_op jit(solution)/shard_map/ppermute | solution.py:546
  18.7 2.7 %collective-permute-start.10 = (bf16[400,128]{1,0:T(8,128)(2,1)S(1)}, bf16[400,128]{1,0:T(8,128)(2,1)S(1)}, u32[]{:S(2)}, u32[]{:S(2)}) collective-permute-start(bf16[400,128]{1,0:T(8,128)(2,1)S(1)} %get-tuple-element.53), channel_id=1, source_target_pairs={{0,1},{1,0},{2,3},{3,2},{4,5},{5,4},{6,7},{7,6},{8,9},{9,8},{10,11... | collective-permute-start | bytes 307208 | tf_op jit(solution)/shard_map/ppermute | solution.py:546
  18.8 4.4 %collective-permute-start.6 = (bf16[400,128]{1,0:T(8,128)(2,1)S(1)}, bf16[400,128]{1,0:T(8,128)(2,1)S(1)}, u32[]{:S(2)}, u32[]{:S(2)}) collective-permute-start(bf16[400,128]{1,0:T(8,128)(2,1)S(1)} %get-tuple-element.46), channel_id=1, source_target_pairs={{0,2},{1,3},{2,0},{3,1},{4,6},{5,7},{6,4},{7,5},{8,10},{9,11},{10,... | collective-permute-start | bytes 307208 | tf_op jit(solution)/shard_map/ppermute | solution.py:546
  18.9 6.8 %collective-permute-start.7 = (bf16[400,128]{1,0:T(8,128)(2,1)S(1)}, bf16[400,128]{1,0:T(8,128)(2,1)S(1)}, u32[]{:S(2)}, u32[]{:S(2)}) collective-permute-start(bf16[400,128]{1,0:T(8,128)(2,1)S(1)} %get-tuple-element.47), channel_id=1, source_target_pairs={{0,3},{1,2},{2,1},{3,0},{4,7},{5,6},{6,5},{7,4},{8,11},{9,10},{10,... | collective-permute-start | bytes 307208 | tf_op jit(solution)/shard_map/ppermute | solution.py:546
  21.0 1.3 %collective-permute-start.11 = (bf16[8,32,128]{2,1,0:T(8,128)(2,1)S(1)}, bf16[8,32,128]{2,1,0:T(8,128)(2,1)S(1)}, u32[]{:S(2)}, u32[]{:S(2)}) collective-permute-start(bf16[8,32,128]{2,1,0:T(8,128)(2,1)S(1)} %get-tuple-element.54), channel_id=1, source_target_pairs={{0,1},{1,0},{2,3},{3,2},{4,5},{5,4},{6,7},{7,6},{8,9},{9,8},{10,11... | collective-permute-start | bytes 196616 | tf_op jit(solution)/shard_map/ppermute | solution.py:546
  21.0 4.7 %collective-permute-start.9 = (bf16[1,8,32,128]{3,2,1,0:T(8,128)(2,1)S(1)}, bf16[1,8,32,128]{3,2,1,0:T(8,128)(2,1)S(1)}, u32[]{:S(2)}, u32[]{:S(2)}) collective-permute-start(bf16[1,8,32,128]{3,2,1,0:T(8,128)(2,1)S(1)} %slice.3), channel_id=1, source_target_pairs={{0,1},{1,0},{2,3},{3,2},{4,5},{5,4},{6,7},{7,6},{8,9},{9,8},{10,11... | collective-permute-start | bytes 196616 | tf_op jit(solution)/shard_map/ppermute | solution.py:546

commit v9 on v8

--- a/solution.py
+++ b/solution.py
@@ -572,8 +572,9 @@
     owns = [mine, pair]
     for value in direct:
         owns += [value, relayed]
-    coarse = unpack(outs[:2], owns[:2], range(2), None)
-    coarse = unpack(outs[2:], owns[2:], range(2, parts), coarse)
+    coarse = None
+    for first, last in ((0, 2), (2, parts - 1), (parts - 1, parts)):
+        coarse = unpack(outs[first:last], owns[first:last], range(first, last), coarse)
     return coarse[None]
 
 

time: 27 us -> 26.7 us (0.989)
  waiting for transfers between devices: 7.28 us -> 6.43 us
  Pallas kernels: 9.81 us -> 10.4 us
    ppermute x6, waiting for transfers between devices: 3.18 us -> 2.34 us  [xor_swap(): lax.ppermute(value, 'col', [(i, i ^ s) for i in range(lax.axis_size('col'...]
    pallas_call x2 -> x3, Pallas kernels: 2.06 us -> 2.68 us  [unpack(): pl.pallas_call(functools.partial(unpack_kernel, parts, steps), out_shape=...]
  transfers between devices with their start and end apart: 12 -> 12, of which waited for: 3 -> 3; matrix products, arithmetic and copies ran while one was open for 0% -> 0% of each run, Pallas kernels for 28% -> 31%
where the time goes in v9:
time: 26.7 us; the launch traced here: 26.5 us
  Pallas kernels  10.4 us (39%)
  starting transfers between devices  9.54 us (36%)
  waiting for transfers between devices  6.43 us (24%)
    ppermute x6, starting transfers between devices, swap(): return lax.ppermute(value, ('row', 'col'), pairs)  5.57 us
    pallas_call x1, Pallas kernels, step_one(): pl.pallas_call(step_one_kernel, out_shape=(jax.ShapeDtypeStruct((4, 9, BS...  4.56 us
    ppermute x6, waiting for transfers between devices, swap(): return lax.ppermute(value, ('row', 'col'), pairs)  4.09 us
    ppermute x6, starting transfers between devices, xor_swap(): lax.ppermute(value, 'col', [(i, i ^ s) for i in range(lax.axis_size('col'...  3.97 us
    pallas_call x3, Pallas kernels, unpack(): pl.pallas_call(functools.partial(unpack_kernel, parts, steps), out_shape=...  2.68 us
    ppermute x6, waiting for transfers between devices, xor_swap(): lax.ppermute(value, 'col', [(i, i ^ s) for i in range(lax.axis_size('col'...  2.34 us
    pallas_call x1, Pallas kernels, rims(): pl.pallas_call(rims_kernel, out_shape=(shape,) * 4 + (jax.ShapeDtypeStruc...  1.38 us
    pallas_call x1, Pallas kernels, near_terms(): pl.pallas_call(functools.partial(near_kernel, parts), out_shape=shapes, i...  1.18 us
  transfers between devices with their start and end apart: 12, of which 3 were waited for; matrix products, arithmetic and copies ran while one was open for 0% of the time, Pallas kernels for 31%

profile of v9, /device:TPU:5, one launch (start us, length us, event | category | flops | bytes accessed | tf_op | source)
XLA Modules:
  0.0 26.5 jit_solution(13291291256961297101)
XLA Ops:
  0.0 1.4 %rims.1 = (bf16[1032,128]{1,0:T(8,128)(2,1)S(1)}, bf16[1032,128]{1,0:T(8,128)(2,1)S(1)}, bf16[1032,128]{1,0:T(8,128)(2,1)S(1)}, bf16[1032,128]{1,0:T(8,128)(2,1)S(1)}, f32[8,128]{1,0:T(8,128)S(1)}) custom-call(s32[4,4]{1,0:T(4,128)} %agg_hbm.1, bf16[4,512,128]{2,1,0:T(8,128)(2,1)} %bitcast.3), custom_call_target="tpu_custom_call" | custom-call | tf_op jit(solution)/shard_map/rims/pallas_call | solution.py:72
  1.4 0.1 collective-permute-start
  1.5 2.5 %collective-permute-start.1 = (bf16[1032,128]{1,0:T(8,128)(2,1)S(1)}, bf16[1032,128]{1,0:T(8,128)(2,1)S(1)}, u32[]{:S(2)}, u32[]{:S(2)}) collective-permute-start(bf16[1032,128]{1,0:T(8,128)(2,1)S(1)} %get-tuple-element.33), channel_id=1, source_target_pairs={{0,1},{1,0},{2,3},{3,2},{4,8},{5,9},{6,10},{7,11},{8,4},{9,5},{10,... | collective-permute-start | bytes 792584 | tf_op jit(solution)/shard_map/ppermute | solution.py:542
  3.9 1.2 %collective-permute-start.2 = (bf16[1032,128]{1,0:T(8,128)(2,1)S(1)}, bf16[1032,128]{1,0:T(8,128)(2,1)S(1)}, u32[]{:S(2)}, u32[]{:S(2)}) collective-permute-start(bf16[1032,128]{1,0:T(8,128)(2,1)S(1)} %get-tuple-element.35), channel_id=1, source_target_pairs={{0,1},{1,0},{2,3},{3,2},{4,5},{5,4},{6,7},{7,6},{8,9},{9,8},{10,11... | collective-permute-start | bytes 792584 | tf_op jit(solution)/shard_map/ppermute | solution.py:542
  5.2 1.1 %collective-permute-start.3 = (bf16[1032,128]{1,0:T(8,128)(2,1)S(1)}, bf16[1032,128]{1,0:T(8,128)(2,1)S(1)}, u32[]{:S(2)}, u32[]{:S(2)}) collective-permute-start(bf16[1032,128]{1,0:T(8,128)(2,1)S(1)} %get-tuple-element.36), channel_id=1, source_target_pairs={{0,8},{1,2},{2,1},{3,11},{4,0},{5,6},{6,5},{7,3},{8,16},{9,10},{10... | collective-permute-start | bytes 792584 | tf_op jit(solution)/shard_map/ppermute | solution.py:542
  6.3 4.6 %step_one.1 = (bf16[4,9,128,512]{3,2,1,0:T(8,128)(2,1)S(1)}, bf16[2,128,512]{2,1,0:T(8,128)(2,1)S(1)}, bf16[2,128,512]{2,1,0:T(8,128)(2,1)S(1)}, bf16[4,512,128]{2,1,0:T(8,128)(2,1)S(1)}) custom-call(s32[4,4,12]{2,1,0:T(4,128)} %codes_hbm.1, bf16[192,128,128]{2,1,0:T(8,128)(2,1)} %bitcast.5, bf16[4,512,128]{2,1,0:T(8,128)(2,1)} %bitcast.4, ...), custom_call_target="tpu_custom_call" | custom-call | flops 8589934592 | bytes 1048576 | tf_op jit(solution)/shard_map/step_one/pallas_call | solution.py:183
  10.8 0.7 %collective-permute-start.4 = (bf16[2,128,512]{2,1,0:T(8,128)(2,1)S(1)}, bf16[2,128,512]{2,1,0:T(8,128)(2,1)S(1)}, u32[]{:S(2)}, u32[]{:S(2)}) collective-permute-start(bf16[2,128,512]{2,1,0:T(8,128)(2,1)S(1)} %get-tuple-element.38), channel_id=1, source_target_pairs={{0,8},{1,2},{2,1},{3,11},{4,0},{5,6},{6,5},{7,3},{8,16},{9,10},{10... | collective-permute-start | bytes 786440 | tf_op jit(solution)/shard_map/ppermute | solution.py:542
  11.5 0.0 collective-permute-done.2.col_a
  11.5 0.0 collective-permute-start.5
  11.5 0.0 collective-permute-done.3.col_b
  11.5 1.2 %near_terms.1 = (bf16[8,32,128]{2,1,0:T(8,128)(2,1)S(1)}, bf16[8,32,128]{2,1,0:T(8,128)(2,1)S(1)}, bf16[2,8,32,128]{3,2,1,0:T(8,128)(2,1)S(1)}, f32[4,128,128]{2,1,0:T(8,128)S(1)}, f32[8,128]{1,0:T(8,128)S(1)}) custom-call(f32[8,128]{1,0:T(8,128)S(1)} %get-tuple-element.30.after.bits, bf16[4,9,128,512]{3,2,1,0:T(8,128)(2,1)S(1)} %get-tuple-element.31.r, ...), custom_call_target="tpu_custom_call" | custom-call | flops 1 | bytes 1 | tf_op jit(solution)/shard_map/near_terms/pallas_call | solution.py:309
  12.7 1.3 %collective-permute-start.7 = (bf16[2,8,32,128]{3,2,1,0:T(8,128)(2,1)S(1)}, bf16[2,8,32,128]{3,2,1,0:T(8,128)(2,1)S(1)}, u32[]{:S(2)}, u32[]{:S(2)}) collective-permute-start(bf16[2,8,32,128]{3,2,1,0:T(8,128)(2,1)S(1)} %get-tuple-element.49), channel_id=1, source_target_pairs={{0,2},{1,3},{2,0},{3,1},{4,6},{5,7},{6,4},{7,5},{8,10},{9,11},{10,... | collective-permute-start | bytes 393224 | tf_op jit(solution)/shard_map/ppermute | solution.py:546
  14.0 4.1 %collective-permute-done.4.refs_3_ = bf16[2,128,512]{2,1,0:T(8,128)(2,1)S(1)} collective-permute-done((bf16[2,128,512]{2,1,0:T(8,128)(2,1)S(1)}, bf16[2,128,512]{2,1,0:T(8,128)(2,1)S(1)}, u32[]{:S(2)}, u32[]{:S(2)}) %collective-permute-start.4) | collective-permute-done | bytes 262176 | tf_op jit(solution)/shard_map/ppermute | solution.py:542
  18.1 0.0 collective-permute-done.refs_0_
  18.1 0.0 collective-permute-done.1.refs_1_
  18.1 0.0 collective-permute-done.5.from_a
  18.1 0.6 %far_terms.1 = (bf16[400,128]{1,0:T(8,128)(2,1)S(1)}, bf16[400,128]{1,0:T(8,128)(2,1)S(1)}, bf16[400,128]{1,0:T(8,128)(2,1)S(1)}, bf16[400,128]{1,0:T(8,128)(2,1)S(1)}) custom-call(f32[8,128]{1,0:T(8,128)S(1)} %get-tuple-element.30.after.bits, bf16[4,9,128,512]{3,2,1,0:T(8,128)(2,1)S(1)} %get-tuple-element.31.r, ...), custom_call_target="tpu_custom_call" | custom-call | flops 1 | bytes 1 | tf_op jit(solution)/shard_map/far_terms/pallas_call | solution.py:363
  18.7 0.1 collective-permute-start.10
  18.8 0.1 collective-permute-start.9
  18.9 2.0 %collective-permute-start.6 = (bf16[400,128]{1,0:T(8,128)(2,1)S(1)}, bf16[400,128]{1,0:T(8,128)(2,1)S(1)}, u32[]{:S(2)}, u32[]{:S(2)}) collective-permute-start(bf16[400,128]{1,0:T(8,128)(2,1)S(1)} %get-tuple-element.46), channel_id=1, source_target_pairs={{0,3},{1,2},{2,1},{3,0},{4,7},{5,6},{6,5},{7,4},{8,11},{9,10},{10,... | collective-permute-start | bytes 307208 | tf_op jit(solution)/shard_map/ppermute | solution.py:546
  20.9 0.0 collective-permute-done.7.refs_1_
  20.9 0.0 collective-permute-start.11
  21.0 0.5 %collective-permute-start.8 = (bf16[1,8,32,128]{3,2,1,0:T(8,128)(2,1)S(1)}, bf16[1,8,32,128]{3,2,1,0:T(8,128)(2,1)S(1)}, u32[]{:S(2)}, u32[]{:S(2)}) collective-permute-start(bf16[1,8,32,128]{3,2,1,0:T(8,128)(2,1)S(1)} %slice.3), channel_id=1, source_target_pairs={{0,1},{1,0},{2,3},{3,2},{4,5},{5,4},{6,7},{7,6},{8,9},{9,8},{10,11... | collective-permute-start | bytes 196616 | tf_op jit(solution)/shard_map/ppermute | solution.py:546
  21.5 0.0 collective-permute-done.10.refs_1_
  21.5 0.7 %collective-permute-done.11.refs_3_ = bf16[8,32,128]{2,1,0:T(8,128)(2,1)S(1)} collective-permute-done((bf16[8,32,128]{2,1,0:T(8,128)(2,1)S(1)}, bf16[8,32,128]{2,1,0:T(8,128)(2,1)S(1)}, u32[]{:S(2)}, u32[]{:S(2)}) %collective-permute-start.11) | collective-permute-done | bytes 65568 | tf_op jit(solution)/shard_map/ppermute | solution.py:546
  22.2 1.0 %unpack.3.refs_2_ = bf16[4,2,9,2,32,128]{5,4,3,2,1,0:T(8,128)(2,1)} custom-call(bf16[400,128]{1,0:T(8,128)(2,1)S(1)} %get-tuple-element.52.refs_0_, bf16[400,128]{1,0:T(8,128)(2,1)S(1)} %collective-permute-done.10.refs_1_, bf16[8,32,128]{2,1,0:T(8,128)(2,1)S(1)} %get-tuple-element.39.refs_4_.refs_2_, bf16[8,32,128]{2,1,0:T(8,128)(2,1)S(1)} %collective-permute-done.11.refs_3_), custom_call_target="tpu_custom_call" | custom-call | flops 1 | bytes 1 | tf_op jit(solution)/shard_map/unpack/pallas_call | solution.py:432
  23.2 0.0 collective-permute-done.9.refs_0_
  23.2 0.8 %unpack.4.refs_2_ = bf16[4,2,9,2,32,128]{5,4,3,2,1,0:T(8,128)(2,1)} custom-call(bf16[400,128]{1,0:T(8,128)(2,1)S(1)} %collective-permute-done.9.refs_0_, bf16[2,8,32,128]{3,2,1,0:T(8,128)(2,1)S(1)} %collective-permute-done.7.refs_1_, bf16[4,2,9,2,32,128]{5,4,3,2,1,0:T(8,128)(2,1)} %unpack.3.refs_2_), custom_call_target="tpu_custom_call", output_to_operand_aliasing={{}: (2, {})} | custom-call | flops 1 | bytes 1 | tf_op jit(solution)/shard_map/unpack/pallas_call | solution.py:432
  24.1 1.6 %collective-permute-done.6.refs_0_ = bf16[400,128]{1,0:T(8,128)(2,1)S(1)} collective-permute-done((bf16[400,128]{1,0:T(8,128)(2,1)S(1)}, bf16[400,128]{1,0:T(8,128)(2,1)S(1)}, u32[]{:S(2)}, u32[]{:S(2)}) %collective-permute-start.6) | collective-permute-done | bytes 102432 | tf_op jit(solution)/shard_map/ppermute | solution.py:546
  25.7 0.0 collective-permute-done.8.refs_1_
  25.7 0.8 %unpack.5 = bf16[4,2,9,2,32,128]{5,4,3,2,1,0:T(8,128)(2,1)} custom-call(bf16[400,128]{1,0:T(8,128)(2,1)S(1)} %collective-permute-done.6.refs_0_, bf16[1,8,32,128]{3,2,1,0:T(8,128)(2,1)S(1)} %collective-permute-done.8.refs_1_, bf16[4,2,9,2,32,128]{5,4,3,2,1,0:T(8,128)(2,1)} %unpack.4.refs_2_), custom_call_target="tpu_custom_call", output_to_operand_aliasing={{}: (2, {})} | custom-call | flops 1 | bytes 1 | tf_op jit(solution)/shard_map/unpack/pallas_call | solution.py:432
  (2 shorter events, 0.0 us)
Async XLA Ops:
  1.4 16.7 %collective-permute-start = (bf16[1032,128]{1,0:T(8,128)(2,1)S(1)}, bf16[1032,128]{1,0:T(8,128)(2,1)S(1)}, u32[]{:S(2)}, u32[]{:S(2)}) collective-permute-start(bf16[1032,128]{1,0:T(8,128)(2,1)S(1)} %get-tuple-element.32), channel_id=1, source_target_pairs={{0,4},{1,5},{2,6},{3,7},{4,0},{5,1},{6,2},{7,3},{8,12},{9,13},{10,... | collective-permute-start | bytes 792584 | tf_op jit(solution)/shard_map/ppermute | solution.py:542
  1.5 16.6 %collective-permute-start.1 = (bf16[1032,128]{1,0:T(8,128)(2,1)S(1)}, bf16[1032,128]{1,0:T(8,128)(2,1)S(1)}, u32[]{:S(2)}, u32[]{:S(2)}) collective-permute-start(bf16[1032,128]{1,0:T(8,128)(2,1)S(1)} %get-tuple-element.33), channel_id=1, source_target_pairs={{0,1},{1,0},{2,3},{3,2},{4,8},{5,9},{6,10},{7,11},{8,4},{9,5},{10,... | collective-permute-start | bytes 792584 | tf_op jit(solution)/shard_map/ppermute | solution.py:542
  3.9 7.6 %collective-permute-start.2 = (bf16[1032,128]{1,0:T(8,128)(2,1)S(1)}, bf16[1032,128]{1,0:T(8,128)(2,1)S(1)}, u32[]{:S(2)}, u32[]{:S(2)}) collective-permute-start(bf16[1032,128]{1,0:T(8,128)(2,1)S(1)} %get-tuple-element.35), channel_id=1, source_target_pairs={{0,1},{1,0},{2,3},{3,2},{4,5},{5,4},{6,7},{7,6},{8,9},{9,8},{10,11... | collective-permute-start | bytes 792584 | tf_op jit(solution)/shard_map/ppermute | solution.py:542
  5.2 6.4 %collective-permute-start.3 = (bf16[1032,128]{1,0:T(8,128)(2,1)S(1)}, bf16[1032,128]{1,0:T(8,128)(2,1)S(1)}, u32[]{:S(2)}, u32[]{:S(2)}) collective-permute-start(bf16[1032,128]{1,0:T(8,128)(2,1)S(1)} %get-tuple-element.36), channel_id=1, source_target_pairs={{0,8},{1,2},{2,1},{3,11},{4,0},{5,6},{6,5},{7,3},{8,16},{9,10},{10... | collective-permute-start | bytes 792584 | tf_op jit(solution)/shard_map/ppermute | solution.py:542
  10.8 7.3 %collective-permute-start.4 = (bf16[2,128,512]{2,1,0:T(8,128)(2,1)S(1)}, bf16[2,128,512]{2,1,0:T(8,128)(2,1)S(1)}, u32[]{:S(2)}, u32[]{:S(2)}) collective-permute-start(bf16[2,128,512]{2,1,0:T(8,128)(2,1)S(1)} %get-tuple-element.38), channel_id=1, source_target_pairs={{0,8},{1,2},{2,1},{3,11},{4,0},{5,6},{6,5},{7,3},{8,16},{9,10},{10... | collective-permute-start | bytes 786440 | tf_op jit(solution)/shard_map/ppermute | solution.py:542
  11.5 6.6 %collective-permute-start.5 = (bf16[2,128,512]{2,1,0:T(8,128)(2,1)S(1)}, bf16[2,128,512]{2,1,0:T(8,128)(2,1)S(1)}, u32[]{:S(2)}, u32[]{:S(2)}) collective-permute-start(bf16[2,128,512]{2,1,0:T(8,128)(2,1)S(1)} %get-tuple-element.42), channel_id=1, source_target_pairs={{0,1},{1,0},{2,3},{3,2},{4,5},{5,4},{6,7},{7,6},{8,9},{9,8},{10,11... | collective-permute-start | bytes 786440 | tf_op jit(solution)/shard_map/ppermute | solution.py:542
  12.7 8.2 %collective-permute-start.7 = (bf16[2,8,32,128]{3,2,1,0:T(8,128)(2,1)S(1)}, bf16[2,8,32,128]{3,2,1,0:T(8,128)(2,1)S(1)}, u32[]{:S(2)}, u32[]{:S(2)}) collective-permute-start(bf16[2,8,32,128]{3,2,1,0:T(8,128)(2,1)S(1)} %get-tuple-element.49), channel_id=1, source_target_pairs={{0,2},{1,3},{2,0},{3,1},{4,6},{5,7},{6,4},{7,5},{8,10},{9,11},{10,... | collective-permute-start | bytes 393224 | tf_op jit(solution)/shard_map/ppermute | solution.py:546
  18.7 2.7 %collective-permute-start.10 = (bf16[400,128]{1,0:T(8,128)(2,1)S(1)}, bf16[400,128]{1,0:T(8,128)(2,1)S(1)}, u32[]{:S(2)}, u32[]{:S(2)}) collective-permute-start(bf16[400,128]{1,0:T(8,128)(2,1)S(1)} %get-tuple-element.53), channel_id=1, source_target_pairs={{0,1},{1,0},{2,3},{3,2},{4,5},{5,4},{6,7},{7,6},{8,9},{9,8},{10,11... | collective-permute-start | bytes 307208 | tf_op jit(solution)/shard_map/ppermute | solution.py:546
  18.8 4.4 %collective-permute-start.9 = (bf16[400,128]{1,0:T(8,128)(2,1)S(1)}, bf16[400,128]{1,0:T(8,128)(2,1)S(1)}, u32[]{:S(2)}, u32[]{:S(2)}) collective-permute-start(bf16[400,128]{1,0:T(8,128)(2,1)S(1)} %get-tuple-element.51), channel_id=1, source_target_pairs={{0,2},{1,3},{2,0},{3,1},{4,6},{5,7},{6,4},{7,5},{8,10},{9,11},{10,... | collective-permute-start | bytes 307208 | tf_op jit(solution)/shard_map/ppermute | solution.py:546
  18.9 6.8 %collective-permute-start.6 = (bf16[400,128]{1,0:T(8,128)(2,1)S(1)}, bf16[400,128]{1,0:T(8,128)(2,1)S(1)}, u32[]{:S(2)}, u32[]{:S(2)}) collective-permute-start(bf16[400,128]{1,0:T(8,128)(2,1)S(1)} %get-tuple-element.46), channel_id=1, source_target_pairs={{0,3},{1,2},{2,1},{3,0},{4,7},{5,6},{6,5},{7,4},{8,11},{9,10},{10,... | collective-permute-start | bytes 307208 | tf_op jit(solution)/shard_map/ppermute | solution.py:546
  20.9 1.3 %collective-permute-start.11 = (bf16[8,32,128]{2,1,0:T(8,128)(2,1)S(1)}, bf16[8,32,128]{2,1,0:T(8,128)(2,1)S(1)}, u32[]{:S(2)}, u32[]{:S(2)}) collective-permute-start(bf16[8,32,128]{2,1,0:T(8,128)(2,1)S(1)} %get-tuple-element.54), channel_id=1, source_target_pairs={{0,1},{1,0},{2,3},{3,2},{4,5},{5,4},{6,7},{7,6},{8,9},{9,8},{10,11... | collective-permute-start | bytes 196616 | tf_op jit(solution)/shard_map/ppermute | solution.py:546
  21.0 4.7 %collective-permute-start.8 = (bf16[1,8,32,128]{3,2,1,0:T(8,128)(2,1)S(1)}, bf16[1,8,32,128]{3,2,1,0:T(8,128)(2,1)S(1)}, u32[]{:S(2)}, u32[]{:S(2)}) collective-permute-start(bf16[1,8,32,128]{3,2,1,0:T(8,128)(2,1)S(1)} %slice.3), channel_id=1, source_target_pairs={{0,1},{1,0},{2,3},{3,2},{4,5},{5,4},{6,7},{7,6},{8,9},{9,8},{10,11... | collective-permute-start | bytes 196616 | tf_op jit(solution)/shard_map/ppermute | solution.py:546

commit v10 on v9

--- a/solution.py
+++ b/solution.py
@@ -31,16 +31,14 @@
     return index + flip - 2 * index * flip
 
 
-def rims_kernel(agg_hbm, prolong, row_a, row_b, col_a, col_b, bits, agg, sems):
+def rims_kernel(agg_hbm, prolong, row_a, row_b, bits, agg, sems):
     fx, fy = flips()
-    load = pltpu.make_async_copy(agg_hbm, agg, sems.at[16])
+    load = pltpu.make_async_copy(agg_hbm, agg, sems.at[8])
     load.start()
     copies = []
     plans = (
         (row_a, ((1, 0), (1, 1))),
         (row_b, ((0, 0), (0, 1))),
-        (col_a, ((0, 1), (1, 1))),
-        (col_b, ((0, 0), (1, 0))),
     )
     for out, quads in plans:
         for h, (u, v) in enumerate(quads):
@@ -71,13 +69,34 @@
     shape = jax.ShapeDtypeStruct((ROWS, BS), BF16)
     return pl.pallas_call(
         rims_kernel,
-        out_shape=(shape,) * 4 + (jax.ShapeDtypeStruct((8, BS), F32),),
+        out_shape=(shape,) * 2 + (jax.ShapeDtypeStruct((8, BS), F32),),
         in_specs=[HBM, HBM],
-        out_specs=(VMEM,) * 5,
-        scratch_shapes=[pltpu.SMEM((SIDE, SIDE), jnp.int32), pltpu.SemaphoreType.DMA((17,))],
+        out_specs=(VMEM,) * 3,
+        scratch_shapes=[pltpu.SMEM((SIDE, SIDE), jnp.int32), pltpu.SemaphoreType.DMA((9,))],
         compiler_params=pltpu.CompilerParams(vmem_limit_bytes=4 << 20),
         name="rims",
     )(agg, prolong_rows)
+
+
+def column_rims_kernel(row_a, row_b, bits, col_a, col_b):
+    at = lax.broadcasted_iota(jnp.int32, (HEAD, BS), 0)
+    for v, out in ((1, col_a), (0, col_b)):
+        for h, rows in enumerate((row_b, row_a)):
+            out[QUAD * h : QUAD * (h + 1), :] = rows[QUAD * v : QUAD * (v + 1), :]
+        out[2 * QUAD :, :] = jnp.where(at == 0, bits[v : v + 1, :], bits[2 + v : 3 + v, :]).astype(BF16)
+
+
+def column_rims(row_a, row_b, bits):
+    shape = jax.ShapeDtypeStruct((ROWS, BS), BF16)
+    return pl.pallas_call(
+        column_rims_kernel,
+        out_shape=(shape,) * 2,
+        in_specs=[VMEM] * 3,
+        out_specs=(VMEM,) * 2,
+        compiler_params=pltpu.CompilerParams(vmem_limit_bytes=4 << 20),
+        cost_estimate=pl.CostEstimate(flops=1, bytes_accessed=1, transcendentals=0),
+        name="column_rims",
+    )(row_a, row_b, bits)
 
 
 def sums(r, p, quads):
@@ -553,12 +572,13 @@
     neighbours = pltpu.with_memory_space_constraint(neighbours, pltpu.HBM)
     aggregate = pltpu.with_memory_space_constraint(aggregate, pltpu.HBM)
     prolong_rows = pltpu.with_memory_space_constraint(prolong.reshape(SIDE, SIDE * BS, BS), pltpu.HBM)
-    to_row_a, to_row_b, to_col_a, to_col_b, bits = rims(aggregate, prolong_rows)
+    to_row_a, to_row_b, bits = rims(aggregate, prolong_rows)
+    to_col_a, to_col_b = column_rims(to_row_a, to_row_b, bits)
     row_a = swap(to_row_a, row_high)
     row_b = swap(to_row_b, row_low)
     col_a = swap(to_col_a, col_high)
     col_b = swap(to_col_b, col_low)
-    r, to_a, to_b, own_blocks = step_one(neighbours, coupling, prolong_rows, bits)
+    r, to_a, to_b, own_blocks = step_one(neighbours, coupling, prolong_rows, to_col_b)
     from_b = swap(to_b, col_low)
     from_a = swap(to_a, col_high)
     mine, pair, *cross, columns, column_head = near_terms(parts, bits, r, own_blocks, col_a, col_b)

time: 26.7 us -> 26.7 us (level)
    pallas_call x1 -> x2, Pallas kernels: 1.38 us -> 1.17 us  [the longest x1 1.14 us: rims(): pl.pallas_call(rims_kernel, out_shape=(shape,) * 2 + (jax.ShapeDtypeStruc...]
where the time goes in v10:
time: 26.7 us; the launch traced here: 26.4 us
  Pallas kernels  10.2 us (38%)
  starting transfers between devices  9.67 us (36%)
  waiting for transfers between devices  6.45 us (24%)
    ppermute x6, starting transfers between devices, swap(): return lax.ppermute(value, ('row', 'col'), pairs)  5.64 us
    pallas_call x1, Pallas kernels, step_one(): pl.pallas_call(step_one_kernel, out_shape=(jax.ShapeDtypeStruct((4, 9, BS...  4.56 us
    ppermute x6, waiting for transfers between devices, swap(): return lax.ppermute(value, ('row', 'col'), pairs)  4.11 us
    ppermute x6, starting transfers between devices, xor_swap(): lax.ppermute(value, 'col', [(i, i ^ s) for i in range(lax.axis_size('col'...  4.03 us
    pallas_call x3, Pallas kernels, unpack(): pl.pallas_call(functools.partial(unpack_kernel, parts, steps), out_shape=...  2.68 us
    ppermute x6, waiting for transfers between devices, xor_swap(): lax.ppermute(value, 'col', [(i, i ^ s) for i in range(lax.axis_size('col'...  2.34 us
    pallas_call x1, Pallas kernels, near_terms(): pl.pallas_call(functools.partial(near_kernel, parts), out_shape=shapes, i...  1.17 us
    pallas_call x1, Pallas kernels, rims(): pl.pallas_call(rims_kernel, out_shape=(shape,) * 2 + (jax.ShapeDtypeStruc...  1.14 us
  transfers between devices with their start and end apart: 12, of which 3 were waited for; matrix products, arithmetic and copies ran while one was open for 0% of the time, Pallas kernels for 31%

profile of v10, /device:TPU:5, one launch (start us, length us, event | category | flops | bytes accessed | tf_op | source)
XLA Modules:
  0.0 26.4 jit_solution(9112926107144861489)
XLA Ops:
  0.0 1.1 %rims.1 = (bf16[1032,128]{1,0:T(8,128)(2,1)S(1)}, bf16[1032,128]{1,0:T(8,128)(2,1)S(1)}, f32[8,128]{1,0:T(8,128)S(1)}) custom-call(s32[4,4]{1,0:T(4,128)} %agg_hbm.1, bf16[4,512,128]{2,1,0:T(8,128)(2,1)} %bitcast.3), custom_call_target="tpu_custom_call" | custom-call | tf_op jit(solution)/shard_map/rims/pallas_call | solution.py:70
  1.1 0.1 collective-permute-start
  1.2 2.5 %collective-permute-start.1 = (bf16[1032,128]{1,0:T(8,128)(2,1)S(1)}, bf16[1032,128]{1,0:T(8,128)(2,1)S(1)}, u32[]{:S(2)}, u32[]{:S(2)}) collective-permute-start(bf16[1032,128]{1,0:T(8,128)(2,1)S(1)} %get-tuple-element.32.row_b), channel_id=1, source_target_pairs={{0,1},{1,0},{2,3},{3,2},{4,8},{5,9},{6,10},{7,11},{8,4},{9,5},{10,... | collective-permute-start | bytes 792584 | tf_op jit(solution)/shard_map/ppermute | solution.py:561
  3.7 1.3 %collective-permute-start.2 = (bf16[1032,128]{1,0:T(8,128)(2,1)S(1)}, bf16[1032,128]{1,0:T(8,128)(2,1)S(1)}, u32[]{:S(2)}, u32[]{:S(2)}) collective-permute-start(bf16[1032,128]{1,0:T(8,128)(2,1)S(1)} %get-tuple-element.36), channel_id=1, source_target_pairs={{0,1},{1,0},{2,3},{3,2},{4,5},{5,4},{6,7},{7,6},{8,9},{9,8},{10,11... | collective-permute-start | bytes 792584 | tf_op jit(solution)/shard_map/ppermute | solution.py:561
  5.0 1.2 %collective-permute-start.3 = (bf16[1032,128]{1,0:T(8,128)(2,1)S(1)}, bf16[1032,128]{1,0:T(8,128)(2,1)S(1)}, u32[]{:S(2)}, u32[]{:S(2)}) collective-permute-start(bf16[1032,128]{1,0:T(8,128)(2,1)S(1)} %get-tuple-element.33.after), channel_id=1, source_target_pairs={{0,8},{1,2},{2,1},{3,11},{4,0},{5,6},{6,5},{7,3},{8,16},{9,10},{10... | collective-permute-start | bytes 792584 | tf_op jit(solution)/shard_map/ppermute | solution.py:561
  6.2 4.6 %step_one.1 = (bf16[4,9,128,512]{3,2,1,0:T(8,128)(2,1)S(1)}, bf16[2,128,512]{2,1,0:T(8,128)(2,1)S(1)}, bf16[2,128,512]{2,1,0:T(8,128)(2,1)S(1)}, bf16[4,512,128]{2,1,0:T(8,128)(2,1)S(1)}) custom-call(s32[4,4,12]{2,1,0:T(4,128)} %codes_hbm.1, bf16[192,128,128]{2,1,0:T(8,128)(2,1)} %bitcast.5, bf16[4,512,128]{2,1,0:T(8,128)(2,1)} %bitcast.4, ...), custom_call_target="tpu_custom_call" | custom-call | flops 8589934592 | bytes 1048576 | tf_op jit(solution)/shard_map/step_one/pallas_call | solution.py:202
  10.8 0.6 %collective-permute-start.4 = (bf16[2,128,512]{2,1,0:T(8,128)(2,1)S(1)}, bf16[2,128,512]{2,1,0:T(8,128)(2,1)S(1)}, u32[]{:S(2)}, u32[]{:S(2)}) collective-permute-start(bf16[2,128,512]{2,1,0:T(8,128)(2,1)S(1)} %get-tuple-element.38), channel_id=1, source_target_pairs={{0,8},{1,2},{2,1},{3,11},{4,0},{5,6},{6,5},{7,3},{8,16},{9,10},{10... | collective-permute-start | bytes 786440 | tf_op jit(solution)/shard_map/ppermute | solution.py:561
  11.4 0.0 collective-permute-done.2.col_a
  11.4 0.0 collective-permute-start.5
  11.4 0.0 collective-permute-done.3.col_b
  11.4 1.2 %near_terms.1 = (bf16[8,32,128]{2,1,0:T(8,128)(2,1)S(1)}, bf16[8,32,128]{2,1,0:T(8,128)(2,1)S(1)}, bf16[2,8,32,128]{3,2,1,0:T(8,128)(2,1)S(1)}, f32[4,128,128]{2,1,0:T(8,128)S(1)}, f32[8,128]{1,0:T(8,128)S(1)}) custom-call(f32[8,128]{1,0:T(8,128)S(1)} %get-tuple-element.30.bits, bf16[4,9,128,512]{3,2,1,0:T(8,128)(2,1)S(1)} %get-tuple-element.34.r, ...), custom_call_target="tpu_custom_call" | custom-call | flops 1 | bytes 1 | tf_op jit(solution)/shard_map/near_terms/pallas_call | solution.py:328
  12.6 1.3 %collective-permute-start.7 = (bf16[2,8,32,128]{3,2,1,0:T(8,128)(2,1)S(1)}, bf16[2,8,32,128]{3,2,1,0:T(8,128)(2,1)S(1)}, u32[]{:S(2)}, u32[]{:S(2)}) collective-permute-start(bf16[2,8,32,128]{3,2,1,0:T(8,128)(2,1)S(1)} %get-tuple-element.49), channel_id=1, source_target_pairs={{0,2},{1,3},{2,0},{3,1},{4,6},{5,7},{6,4},{7,5},{8,10},{9,11},{10,... | collective-permute-start | bytes 393224 | tf_op jit(solution)/shard_map/ppermute | solution.py:565
  13.9 4.1 %collective-permute-done.4.refs_3_ = bf16[2,128,512]{2,1,0:T(8,128)(2,1)S(1)} collective-permute-done((bf16[2,128,512]{2,1,0:T(8,128)(2,1)S(1)}, bf16[2,128,512]{2,1,0:T(8,128)(2,1)S(1)}, u32[]{:S(2)}, u32[]{:S(2)}) %collective-permute-start.4) | collective-permute-done | bytes 262176 | tf_op jit(solution)/shard_map/ppermute | solution.py:561
  18.0 0.0 collective-permute-done.refs_0_
  18.0 0.0 collective-permute-done.1.refs_1_
  18.0 0.0 collective-permute-done.5.from_a
  18.0 0.6 %far_terms.1 = (bf16[400,128]{1,0:T(8,128)(2,1)S(1)}, bf16[400,128]{1,0:T(8,128)(2,1)S(1)}, bf16[400,128]{1,0:T(8,128)(2,1)S(1)}, bf16[400,128]{1,0:T(8,128)(2,1)S(1)}) custom-call(f32[8,128]{1,0:T(8,128)S(1)} %get-tuple-element.30.bits, bf16[4,9,128,512]{3,2,1,0:T(8,128)(2,1)S(1)} %get-tuple-element.34.r, bf16[1032,128]{1,0:T(8,128)(2,1)S(1)} %get-tuple-element.40.row_a, ...), custom_call_target="tpu_custom_call" | custom-call | flops 1 | bytes 1 | tf_op jit(solution)/shard_map/far_terms/pallas_call | solution.py:382
  18.7 0.1 collective-permute-start.10
  18.7 0.1 collective-permute-start.9
  18.8 2.0 %collective-permute-start.6 = (bf16[400,128]{1,0:T(8,128)(2,1)S(1)}, bf16[400,128]{1,0:T(8,128)(2,1)S(1)}, u32[]{:S(2)}, u32[]{:S(2)}) collective-permute-start(bf16[400,128]{1,0:T(8,128)(2,1)S(1)} %get-tuple-element.46), channel_id=1, source_target_pairs={{0,3},{1,2},{2,1},{3,0},{4,7},{5,6},{6,5},{7,4},{8,11},{9,10},{10,... | collective-permute-start | bytes 307208 | tf_op jit(solution)/shard_map/ppermute | solution.py:565
  20.9 0.0 collective-permute-done.7.refs_1_
  20.9 0.0 collective-permute-start.11
  20.9 0.5 %collective-permute-start.8 = (bf16[1,8,32,128]{3,2,1,0:T(8,128)(2,1)S(1)}, bf16[1,8,32,128]{3,2,1,0:T(8,128)(2,1)S(1)}, u32[]{:S(2)}, u32[]{:S(2)}) collective-permute-start(bf16[1,8,32,128]{3,2,1,0:T(8,128)(2,1)S(1)} %slice.3), channel_id=1, source_target_pairs={{0,1},{1,0},{2,3},{3,2},{4,5},{5,4},{6,7},{7,6},{8,9},{9,8},{10,11... | collective-permute-start | bytes 196616 | tf_op jit(solution)/shard_map/ppermute | solution.py:565
  21.4 0.0 collective-permute-done.10.refs_1_
  21.4 0.7 %collective-permute-done.11.refs_3_ = bf16[8,32,128]{2,1,0:T(8,128)(2,1)S(1)} collective-permute-done((bf16[8,32,128]{2,1,0:T(8,128)(2,1)S(1)}, bf16[8,32,128]{2,1,0:T(8,128)(2,1)S(1)}, u32[]{:S(2)}, u32[]{:S(2)}) %collective-permute-start.11) | collective-permute-done | bytes 65568 | tf_op jit(solution)/shard_map/ppermute | solution.py:565
  22.1 1.0 %unpack.3.refs_2_ = bf16[4,2,9,2,32,128]{5,4,3,2,1,0:T(8,128)(2,1)} custom-call(bf16[400,128]{1,0:T(8,128)(2,1)S(1)} %get-tuple-element.52.refs_0_, bf16[400,128]{1,0:T(8,128)(2,1)S(1)} %collective-permute-done.10.refs_1_, bf16[8,32,128]{2,1,0:T(8,128)(2,1)S(1)} %get-tuple-element.39.refs_4_.refs_2_, bf16[8,32,128]{2,1,0:T(8,128)(2,1)S(1)} %collective-permute-done.11.refs_3_), custom_call_target="tpu_custom_call" | custom-call | flops 1 | bytes 1 | tf_op jit(solution)/shard_map/unpack/pallas_call | solution.py:451
  23.2 0.0 collective-permute-done.9.refs_0_
  23.2 0.8 %unpack.4.refs_2_ = bf16[4,2,9,2,32,128]{5,4,3,2,1,0:T(8,128)(2,1)} custom-call(bf16[400,128]{1,0:T(8,128)(2,1)S(1)} %collective-permute-done.9.refs_0_, bf16[2,8,32,128]{3,2,1,0:T(8,128)(2,1)S(1)} %collective-permute-done.7.refs_1_, bf16[4,2,9,2,32,128]{5,4,3,2,1,0:T(8,128)(2,1)} %unpack.3.refs_2_), custom_call_target="tpu_custom_call", output_to_operand_aliasing={{}: (2, {})} | custom-call | flops 1 | bytes 1 | tf_op jit(solution)/shard_map/unpack/pallas_call | solution.py:451
  24.0 1.6 %collective-permute-done.6.refs_0_ = bf16[400,128]{1,0:T(8,128)(2,1)S(1)} collective-permute-done((bf16[400,128]{1,0:T(8,128)(2,1)S(1)}, bf16[400,128]{1,0:T(8,128)(2,1)S(1)}, u32[]{:S(2)}, u32[]{:S(2)}) %collective-permute-start.6) | collective-permute-done | bytes 102432 | tf_op jit(solution)/shard_map/ppermute | solution.py:565
  25.6 0.0 collective-permute-done.8.refs_1_
  25.6 0.8 %unpack.5 = bf16[4,2,9,2,32,128]{5,4,3,2,1,0:T(8,128)(2,1)} custom-call(bf16[400,128]{1,0:T(8,128)(2,1)S(1)} %collective-permute-done.6.refs_0_, bf16[1,8,32,128]{3,2,1,0:T(8,128)(2,1)S(1)} %collective-permute-done.8.refs_1_, bf16[4,2,9,2,32,128]{5,4,3,2,1,0:T(8,128)(2,1)} %unpack.4.refs_2_), custom_call_target="tpu_custom_call", output_to_operand_aliasing={{}: (2, {})} | custom-call | flops 1 | bytes 1 | tf_op jit(solution)/shard_map/unpack/pallas_call | solution.py:451
  (3 shorter events, 0.0 us)
Async XLA Ops:
  1.1 16.9 %collective-permute-start = (bf16[1032,128]{1,0:T(8,128)(2,1)S(1)}, bf16[1032,128]{1,0:T(8,128)(2,1)S(1)}, u32[]{:S(2)}, u32[]{:S(2)}) collective-permute-start(bf16[1032,128]{1,0:T(8,128)(2,1)S(1)} %get-tuple-element.31.row_a), channel_id=1, source_target_pairs={{0,4},{1,5},{2,6},{3,7},{4,0},{5,1},{6,2},{7,3},{8,12},{9,13},{10,... | collective-permute-start | bytes 792584 | tf_op jit(solution)/shard_map/ppermute | solution.py:561
  1.2 16.8 %collective-permute-start.1 = (bf16[1032,128]{1,0:T(8,128)(2,1)S(1)}, bf16[1032,128]{1,0:T(8,128)(2,1)S(1)}, u32[]{:S(2)}, u32[]{:S(2)}) collective-permute-start(bf16[1032,128]{1,0:T(8,128)(2,1)S(1)} %get-tuple-element.32.row_b), channel_id=1, source_target_pairs={{0,1},{1,0},{2,3},{3,2},{4,8},{5,9},{6,10},{7,11},{8,4},{9,5},{10,... | collective-permute-start | bytes 792584 | tf_op jit(solution)/shard_map/ppermute | solution.py:561
  3.7 7.7 %collective-permute-start.2 = (bf16[1032,128]{1,0:T(8,128)(2,1)S(1)}, bf16[1032,128]{1,0:T(8,128)(2,1)S(1)}, u32[]{:S(2)}, u32[]{:S(2)}) collective-permute-start(bf16[1032,128]{1,0:T(8,128)(2,1)S(1)} %get-tuple-element.36), channel_id=1, source_target_pairs={{0,1},{1,0},{2,3},{3,2},{4,5},{5,4},{6,7},{7,6},{8,9},{9,8},{10,11... | collective-permute-start | bytes 792584 | tf_op jit(solution)/shard_map/ppermute | solution.py:561
  5.0 6.4 %collective-permute-start.3 = (bf16[1032,128]{1,0:T(8,128)(2,1)S(1)}, bf16[1032,128]{1,0:T(8,128)(2,1)S(1)}, u32[]{:S(2)}, u32[]{:S(2)}) collective-permute-start(bf16[1032,128]{1,0:T(8,128)(2,1)S(1)} %get-tuple-element.33.after), channel_id=1, source_target_pairs={{0,8},{1,2},{2,1},{3,11},{4,0},{5,6},{6,5},{7,3},{8,16},{9,10},{10... | collective-permute-start | bytes 792584 | tf_op jit(solution)/shard_map/ppermute | solution.py:561
  10.8 7.3 %collective-permute-start.4 = (bf16[2,128,512]{2,1,0:T(8,128)(2,1)S(1)}, bf16[2,128,512]{2,1,0:T(8,128)(2,1)S(1)}, u32[]{:S(2)}, u32[]{:S(2)}) collective-permute-start(bf16[2,128,512]{2,1,0:T(8,128)(2,1)S(1)} %get-tuple-element.38), channel_id=1, source_target_pairs={{0,8},{1,2},{2,1},{3,11},{4,0},{5,6},{6,5},{7,3},{8,16},{9,10},{10... | collective-permute-start | bytes 786440 | tf_op jit(solution)/shard_map/ppermute | solution.py:561
  11.4 6.6 %collective-permute-start.5 = (bf16[2,128,512]{2,1,0:T(8,128)(2,1)S(1)}, bf16[2,128,512]{2,1,0:T(8,128)(2,1)S(1)}, u32[]{:S(2)}, u32[]{:S(2)}) collective-permute-start(bf16[2,128,512]{2,1,0:T(8,128)(2,1)S(1)} %get-tuple-element.42), channel_id=1, source_target_pairs={{0,1},{1,0},{2,3},{3,2},{4,5},{5,4},{6,7},{7,6},{8,9},{9,8},{10,11... | collective-permute-start | bytes 786440 | tf_op jit(solution)/shard_map/ppermute | solution.py:561
  12.6 8.3 %collective-permute-start.7 = (bf16[2,8,32,128]{3,2,1,0:T(8,128)(2,1)S(1)}, bf16[2,8,32,128]{3,2,1,0:T(8,128)(2,1)S(1)}, u32[]{:S(2)}, u32[]{:S(2)}) collective-permute-start(bf16[2,8,32,128]{3,2,1,0:T(8,128)(2,1)S(1)} %get-tuple-element.49), channel_id=1, source_target_pairs={{0,2},{1,3},{2,0},{3,1},{4,6},{5,7},{6,4},{7,5},{8,10},{9,11},{10,... | collective-permute-start | bytes 393224 | tf_op jit(solution)/shard_map/ppermute | solution.py:565
  18.7 2.7 %collective-permute-start.10 = (bf16[400,128]{1,0:T(8,128)(2,1)S(1)}, bf16[400,128]{1,0:T(8,128)(2,1)S(1)}, u32[]{:S(2)}, u32[]{:S(2)}) collective-permute-start(bf16[400,128]{1,0:T(8,128)(2,1)S(1)} %get-tuple-element.53), channel_id=1, source_target_pairs={{0,1},{1,0},{2,3},{3,2},{4,5},{5,4},{6,7},{7,6},{8,9},{9,8},{10,11... | collective-permute-start | bytes 307208 | tf_op jit(solution)/shard_map/ppermute | solution.py:565
  18.7 4.4 %collective-permute-start.9 = (bf16[400,128]{1,0:T(8,128)(2,1)S(1)}, bf16[400,128]{1,0:T(8,128)(2,1)S(1)}, u32[]{:S(2)}, u32[]{:S(2)}) collective-permute-start(bf16[400,128]{1,0:T(8,128)(2,1)S(1)} %get-tuple-element.51), channel_id=1, source_target_pairs={{0,2},{1,3},{2,0},{3,1},{4,6},{5,7},{6,4},{7,5},{8,10},{9,11},{10,... | collective-permute-start | bytes 307208 | tf_op jit(solution)/shard_map/ppermute | solution.py:565
  18.8 6.8 %collective-permute-start.6 = (bf16[400,128]{1,0:T(8,128)(2,1)S(1)}, bf16[400,128]{1,0:T(8,128)(2,1)S(1)}, u32[]{:S(2)}, u32[]{:S(2)}) collective-permute-start(bf16[400,128]{1,0:T(8,128)(2,1)S(1)} %get-tuple-element.46), channel_id=1, source_target_pairs={{0,3},{1,2},{2,1},{3,0},{4,7},{5,6},{6,5},{7,4},{8,11},{9,10},{10,... | collective-permute-start | bytes 307208 | tf_op jit(solution)/shard_map/ppermute | solution.py:565
  20.9 1.3 %collective-permute-start.11 = (bf16[8,32,128]{2,1,0:T(8,128)(2,1)S(1)}, bf16[8,32,128]{2,1,0:T(8,128)(2,1)S(1)}, u32[]{:S(2)}, u32[]{:S(2)}) collective-permute-start(bf16[8,32,128]{2,1,0:T(8,128)(2,1)S(1)} %get-tuple-element.54), channel_id=1, source_target_pairs={{0,1},{1,0},{2,3},{3,2},{4,5},{5,4},{6,7},{7,6},{8,9},{9,8},{10,11... | collective-permute-start | bytes 196616 | tf_op jit(solution)/shard_map/ppermute | solution.py:565
  20.9 4.7 %collective-permute-start.8 = (bf16[1,8,32,128]{3,2,1,0:T(8,128)(2,1)S(1)}, bf16[1,8,32,128]{3,2,1,0:T(8,128)(2,1)S(1)}, u32[]{:S(2)}, u32[]{:S(2)}) collective-permute-start(bf16[1,8,32,128]{3,2,1,0:T(8,128)(2,1)S(1)} %slice.3), channel_id=1, source_target_pairs={{0,1},{1,0},{2,3},{3,2},{4,5},{5,4},{6,7},{7,6},{8,9},{9,8},{10,11... | collective-permute-start | bytes 196616 | tf_op jit(solution)/shard_map/ppermute | solution.py:565

commit v11 on v10

--- a/solution.py
+++ b/solution.py
@@ -593,8 +593,8 @@
     for value in direct:
         owns += [value, relayed]
     coarse = None
-    for first, last in ((0, 2), (2, parts - 1), (parts - 1, parts)):
-        coarse = unpack(outs[first:last], owns[first:last], range(first, last), coarse)
+    for steps in (range(0, parts, 2), range(1, parts, 2)):
+        coarse = unpack([outs[t] for t in steps], [owns[t] for t in steps], steps, coarse)
     return coarse[None]
 
 

time: 26.7 us -> 25.8 us (0.966)
  Pallas kernels: 10.2 us -> 9.59 us
    pallas_call x3 -> x2, Pallas kernels: 2.68 us -> 2.06 us  [unpack(): pl.pallas_call(functools.partial(unpack_kernel, parts, steps), out_shape=...]
  transfers between devices with their start and end apart: 12 -> 12, of which waited for: 3 -> 3; matrix products, arithmetic and copies ran while one was open for 0% -> 0% of each run, Pallas kernels for 31% -> 29%
where the time goes in v11:
time: 25.8 us; the launch traced here: 25.4 us
  Pallas kernels  9.59 us (37%)
  starting transfers between devices  9.46 us (37%)
  waiting for transfers between devices  6.3 us (24%)
    ppermute x6, starting transfers between devices, swap(): return lax.ppermute(value, ('row', 'col'), pairs)  5.64 us
    pallas_call x1, Pallas kernels, step_one(): pl.pallas_call(step_one_kernel, out_shape=(jax.ShapeDtypeStruct((4, 9, BS...  4.56 us
    ppermute x6, waiting for transfers between devices, swap(): return lax.ppermute(value, ('row', 'col'), pairs)  4.11 us
    ppermute x6, starting transfers between devices, xor_swap(): lax.ppermute(value, 'col', [(i, i ^ s) for i in range(lax.axis_size('col'...  3.82 us
    ppermute x6, waiting for transfers between devices, xor_swap(): lax.ppermute(value, 'col', [(i, i ^ s) for i in range(lax.axis_size('col'...  2.19 us
    pallas_call x2, Pallas kernels, unpack(): pl.pallas_call(functools.partial(unpack_kernel, parts, steps), out_shape=...  2.06 us
    pallas_call x1, Pallas kernels, near_terms(): pl.pallas_call(functools.partial(near_kernel, parts), out_shape=shapes, i...  1.17 us
    pallas_call x1, Pallas kernels, rims(): pl.pallas_call(rims_kernel, out_shape=(shape,) * 2 + (jax.ShapeDtypeStruc...  1.14 us
  transfers between devices with their start and end apart: 12, of which 3 were waited for; matrix products, arithmetic and copies ran while one was open for 0% of the time, Pallas kernels for 29%

profile of v11, /device:TPU:5, one launch (start us, length us, event | category | flops | bytes accessed | tf_op | source)
XLA Modules:
  0.0 25.4 jit_solution(14660920922738596455)
XLA Ops:
  0.0 1.1 %rims.1 = (bf16[1032,128]{1,0:T(8,128)(2,1)S(1)}, bf16[1032,128]{1,0:T(8,128)(2,1)S(1)}, f32[8,128]{1,0:T(8,128)S(1)}) custom-call(s32[4,4]{1,0:T(4,128)} %agg_hbm.1, bf16[4,512,128]{2,1,0:T(8,128)(2,1)} %bitcast.3), custom_call_target="tpu_custom_call" | custom-call | tf_op jit(solution)/shard_map/rims/pallas_call | solution.py:70
  1.1 0.1 collective-permute-start
  1.2 2.5 %collective-permute-start.1 = (bf16[1032,128]{1,0:T(8,128)(2,1)S(1)}, bf16[1032,128]{1,0:T(8,128)(2,1)S(1)}, u32[]{:S(2)}, u32[]{:S(2)}) collective-permute-start(bf16[1032,128]{1,0:T(8,128)(2,1)S(1)} %get-tuple-element.32.row_b), channel_id=1, source_target_pairs={{0,1},{1,0},{2,3},{3,2},{4,8},{5,9},{6,10},{7,11},{8,4},{9,5},{10,... | collective-permute-start | bytes 792584 | tf_op jit(solution)/shard_map/ppermute | solution.py:561
  3.7 1.3 %collective-permute-start.2 = (bf16[1032,128]{1,0:T(8,128)(2,1)S(1)}, bf16[1032,128]{1,0:T(8,128)(2,1)S(1)}, u32[]{:S(2)}, u32[]{:S(2)}) collective-permute-start(bf16[1032,128]{1,0:T(8,128)(2,1)S(1)} %get-tuple-element.36), channel_id=1, source_target_pairs={{0,1},{1,0},{2,3},{3,2},{4,5},{5,4},{6,7},{7,6},{8,9},{9,8},{10,11... | collective-permute-start | bytes 792584 | tf_op jit(solution)/shard_map/ppermute | solution.py:561
  5.0 1.2 %collective-permute-start.3 = (bf16[1032,128]{1,0:T(8,128)(2,1)S(1)}, bf16[1032,128]{1,0:T(8,128)(2,1)S(1)}, u32[]{:S(2)}, u32[]{:S(2)}) collective-permute-start(bf16[1032,128]{1,0:T(8,128)(2,1)S(1)} %get-tuple-element.33.after), channel_id=1, source_target_pairs={{0,8},{1,2},{2,1},{3,11},{4,0},{5,6},{6,5},{7,3},{8,16},{9,10},{10... | collective-permute-start | bytes 792584 | tf_op jit(solution)/shard_map/ppermute | solution.py:561
  6.2 4.6 %step_one.1 = (bf16[4,9,128,512]{3,2,1,0:T(8,128)(2,1)S(1)}, bf16[2,128,512]{2,1,0:T(8,128)(2,1)S(1)}, bf16[2,128,512]{2,1,0:T(8,128)(2,1)S(1)}, bf16[4,512,128]{2,1,0:T(8,128)(2,1)S(1)}) custom-call(s32[4,4,12]{2,1,0:T(4,128)} %codes_hbm.1, bf16[192,128,128]{2,1,0:T(8,128)(2,1)} %bitcast.5, bf16[4,512,128]{2,1,0:T(8,128)(2,1)} %bitcast.4, ...), custom_call_target="tpu_custom_call" | custom-call | flops 8589934592 | bytes 1048576 | tf_op jit(solution)/shard_map/step_one/pallas_call | solution.py:202
  10.8 0.6 %collective-permute-start.4 = (bf16[2,128,512]{2,1,0:T(8,128)(2,1)S(1)}, bf16[2,128,512]{2,1,0:T(8,128)(2,1)S(1)}, u32[]{:S(2)}, u32[]{:S(2)}) collective-permute-start(bf16[2,128,512]{2,1,0:T(8,128)(2,1)S(1)} %get-tuple-element.38), channel_id=1, source_target_pairs={{0,8},{1,2},{2,1},{3,11},{4,0},{5,6},{6,5},{7,3},{8,16},{9,10},{10... | collective-permute-start | bytes 786440 | tf_op jit(solution)/shard_map/ppermute | solution.py:561
  11.4 0.0 collective-permute-done.2.col_a
  11.4 0.0 collective-permute-start.5
  11.4 0.0 collective-permute-done.3.col_b
  11.4 1.2 %near_terms.1 = (bf16[8,32,128]{2,1,0:T(8,128)(2,1)S(1)}, bf16[8,32,128]{2,1,0:T(8,128)(2,1)S(1)}, bf16[2,8,32,128]{3,2,1,0:T(8,128)(2,1)S(1)}, f32[4,128,128]{2,1,0:T(8,128)S(1)}, f32[8,128]{1,0:T(8,128)S(1)}) custom-call(f32[8,128]{1,0:T(8,128)S(1)} %get-tuple-element.30.bits, bf16[4,9,128,512]{3,2,1,0:T(8,128)(2,1)S(1)} %get-tuple-element.34.r, ...), custom_call_target="tpu_custom_call" | custom-call | flops 1 | bytes 1 | tf_op jit(solution)/shard_map/near_terms/pallas_call | solution.py:328
  12.6 1.3 %collective-permute-start.8 = (bf16[2,8,32,128]{3,2,1,0:T(8,128)(2,1)S(1)}, bf16[2,8,32,128]{3,2,1,0:T(8,128)(2,1)S(1)}, u32[]{:S(2)}, u32[]{:S(2)}) collective-permute-start(bf16[2,8,32,128]{3,2,1,0:T(8,128)(2,1)S(1)} %get-tuple-element.50), channel_id=1, source_target_pairs={{0,2},{1,3},{2,0},{3,1},{4,6},{5,7},{6,4},{7,5},{8,10},{9,11},{10,... | collective-permute-start | bytes 393224 | tf_op jit(solution)/shard_map/ppermute | solution.py:565
  13.9 4.1 %collective-permute-done.4.refs_3_ = bf16[2,128,512]{2,1,0:T(8,128)(2,1)S(1)} collective-permute-done((bf16[2,128,512]{2,1,0:T(8,128)(2,1)S(1)}, bf16[2,128,512]{2,1,0:T(8,128)(2,1)S(1)}, u32[]{:S(2)}, u32[]{:S(2)}) %collective-permute-start.4) | collective-permute-done | bytes 262176 | tf_op jit(solution)/shard_map/ppermute | solution.py:561
  18.0 0.0 collective-permute-done.refs_0_
  18.0 0.0 collective-permute-done.1.refs_1_
  18.0 0.0 collective-permute-done.5.from_a
  18.0 0.6 %far_terms.1 = (bf16[400,128]{1,0:T(8,128)(2,1)S(1)}, bf16[400,128]{1,0:T(8,128)(2,1)S(1)}, bf16[400,128]{1,0:T(8,128)(2,1)S(1)}, bf16[400,128]{1,0:T(8,128)(2,1)S(1)}) custom-call(f32[8,128]{1,0:T(8,128)S(1)} %get-tuple-element.30.bits, bf16[4,9,128,512]{3,2,1,0:T(8,128)(2,1)S(1)} %get-tuple-element.34.r, bf16[1032,128]{1,0:T(8,128)(2,1)S(1)} %get-tuple-element.40.row_a, ...), custom_call_target="tpu_custom_call" | custom-call | flops 1 | bytes 1 | tf_op jit(solution)/shard_map/far_terms/pallas_call | solution.py:382
  18.7 0.1 collective-permute-start.11
  18.7 0.2 collective-permute-start.6
  19.0 1.6 %collective-permute-start.7 = (bf16[400,128]{1,0:T(8,128)(2,1)S(1)}, bf16[400,128]{1,0:T(8,128)(2,1)S(1)}, u32[]{:S(2)}, u32[]{:S(2)}) collective-permute-start(bf16[400,128]{1,0:T(8,128)(2,1)S(1)} %get-tuple-element.47), channel_id=1, source_target_pairs={{0,3},{1,2},{2,1},{3,0},{4,7},{5,6},{6,5},{7,4},{8,11},{9,10},{10,... | collective-permute-start | bytes 307208 | tf_op jit(solution)/shard_map/ppermute | solution.py:565
  20.6 0.0 collective-permute-done.8.refs_3_
  20.6 0.1 collective-permute-start.10
  20.7 0.5 %collective-permute-start.9 = (bf16[8,32,128]{2,1,0:T(8,128)(2,1)S(1)}, bf16[8,32,128]{2,1,0:T(8,128)(2,1)S(1)}, u32[]{:S(2)}, u32[]{:S(2)}) collective-permute-start(bf16[8,32,128]{2,1,0:T(8,128)(2,1)S(1)} %get-tuple-element.51), channel_id=1, source_target_pairs={{0,1},{1,0},{2,3},{3,2},{4,5},{5,4},{6,7},{7,6},{8,9},{9,8},{10,11... | collective-permute-start | bytes 196616 | tf_op jit(solution)/shard_map/ppermute | solution.py:565
  21.2 1.4 %collective-permute-done.11.refs_1_ = bf16[400,128]{1,0:T(8,128)(2,1)S(1)} collective-permute-done((bf16[400,128]{1,0:T(8,128)(2,1)S(1)}, bf16[400,128]{1,0:T(8,128)(2,1)S(1)}, u32[]{:S(2)}, u32[]{:S(2)}) %collective-permute-start.11) | collective-permute-done | bytes 102432 | tf_op jit(solution)/shard_map/ppermute | solution.py:565
  22.6 1.0 %unpack.2.refs_4_ = bf16[4,2,9,2,32,128]{5,4,3,2,1,0:T(8,128)(2,1)} custom-call(bf16[400,128]{1,0:T(8,128)(2,1)S(1)} %get-tuple-element.53.refs_0_, bf16[400,128]{1,0:T(8,128)(2,1)S(1)} %collective-permute-done.11.refs_1_, bf16[8,32,128]{2,1,0:T(8,128)(2,1)S(1)} %get-tuple-element.39.refs_4_.refs_2_, bf16[2,8,32,128]{3,2,1,0:T(8,128)(2,1)S(1)} %collective-permute-done.8.refs_3_), custom_call_target="tpu_custom_call" | custom-call | flops 1 | bytes 1 | tf_op jit(solution)/shard_map/unpack/pallas_call | solution.py:451
  23.6 0.0 collective-permute-done.6.refs_0_
  23.6 0.8 %collective-permute-done.7.refs_1_ = bf16[400,128]{1,0:T(8,128)(2,1)S(1)} collective-permute-done((bf16[400,128]{1,0:T(8,128)(2,1)S(1)}, bf16[400,128]{1,0:T(8,128)(2,1)S(1)}, u32[]{:S(2)}, u32[]{:S(2)}) %collective-permute-start.7) | collective-permute-done | bytes 102432 | tf_op jit(solution)/shard_map/ppermute | solution.py:565
  24.4 0.0 collective-permute-done.10.refs_3_
  24.4 0.0 collective-permute-done.9.refs_2_
  24.4 1.0 %unpack.3 = bf16[4,2,9,2,32,128]{5,4,3,2,1,0:T(8,128)(2,1)} custom-call(bf16[400,128]{1,0:T(8,128)(2,1)S(1)} %collective-permute-done.6.refs_0_, bf16[400,128]{1,0:T(8,128)(2,1)S(1)} %collective-permute-done.7.refs_1_, bf16[8,32,128]{2,1,0:T(8,128)(2,1)S(1)} %collective-permute-done.9.refs_2_, ...), custom_call_target="tpu_custom_call", output_to_operand_aliasing={{}: (4, {})} | custom-call | flops 1 | bytes 1 | tf_op jit(solution)/shard_map/unpack/pallas_call | solution.py:451
  (3 shorter events, 0.0 us)
Async XLA Ops:
  1.1 16.9 %collective-permute-start = (bf16[1032,128]{1,0:T(8,128)(2,1)S(1)}, bf16[1032,128]{1,0:T(8,128)(2,1)S(1)}, u32[]{:S(2)}, u32[]{:S(2)}) collective-permute-start(bf16[1032,128]{1,0:T(8,128)(2,1)S(1)} %get-tuple-element.31.row_a), channel_id=1, source_target_pairs={{0,4},{1,5},{2,6},{3,7},{4,0},{5,1},{6,2},{7,3},{8,12},{9,13},{10,... | collective-permute-start | bytes 792584 | tf_op jit(solution)/shard_map/ppermute | solution.py:561
  1.2 16.8 %collective-permute-start.1 = (bf16[1032,128]{1,0:T(8,128)(2,1)S(1)}, bf16[1032,128]{1,0:T(8,128)(2,1)S(1)}, u32[]{:S(2)}, u32[]{:S(2)}) collective-permute-start(bf16[1032,128]{1,0:T(8,128)(2,1)S(1)} %get-tuple-element.32.row_b), channel_id=1, source_target_pairs={{0,1},{1,0},{2,3},{3,2},{4,8},{5,9},{6,10},{7,11},{8,4},{9,5},{10,... | collective-permute-start | bytes 792584 | tf_op jit(solution)/shard_map/ppermute | solution.py:561
  3.7 7.7 %collective-permute-start.2 = (bf16[1032,128]{1,0:T(8,128)(2,1)S(1)}, bf16[1032,128]{1,0:T(8,128)(2,1)S(1)}, u32[]{:S(2)}, u32[]{:S(2)}) collective-permute-start(bf16[1032,128]{1,0:T(8,128)(2,1)S(1)} %get-tuple-element.36), channel_id=1, source_target_pairs={{0,1},{1,0},{2,3},{3,2},{4,5},{5,4},{6,7},{7,6},{8,9},{9,8},{10,11... | collective-permute-start | bytes 792584 | tf_op jit(solution)/shard_map/ppermute | solution.py:561
  5.0 6.4 %collective-permute-start.3 = (bf16[1032,128]{1,0:T(8,128)(2,1)S(1)}, bf16[1032,128]{1,0:T(8,128)(2,1)S(1)}, u32[]{:S(2)}, u32[]{:S(2)}) collective-permute-start(bf16[1032,128]{1,0:T(8,128)(2,1)S(1)} %get-tuple-element.33.after), channel_id=1, source_target_pairs={{0,8},{1,2},{2,1},{3,11},{4,0},{5,6},{6,5},{7,3},{8,16},{9,10},{10... | collective-permute-start | bytes 792584 | tf_op jit(solution)/shard_map/ppermute | solution.py:561
  10.8 7.3 %collective-permute-start.4 = (bf16[2,128,512]{2,1,0:T(8,128)(2,1)S(1)}, bf16[2,128,512]{2,1,0:T(8,128)(2,1)S(1)}, u32[]{:S(2)}, u32[]{:S(2)}) collective-permute-start(bf16[2,128,512]{2,1,0:T(8,128)(2,1)S(1)} %get-tuple-element.38), channel_id=1, source_target_pairs={{0,8},{1,2},{2,1},{3,11},{4,0},{5,6},{6,5},{7,3},{8,16},{9,10},{10... | collective-permute-start | bytes 786440 | tf_op jit(solution)/shard_map/ppermute | solution.py:561
  11.4 6.6 %collective-permute-start.5 = (bf16[2,128,512]{2,1,0:T(8,128)(2,1)S(1)}, bf16[2,128,512]{2,1,0:T(8,128)(2,1)S(1)}, u32[]{:S(2)}, u32[]{:S(2)}) collective-permute-start(bf16[2,128,512]{2,1,0:T(8,128)(2,1)S(1)} %get-tuple-element.42), channel_id=1, source_target_pairs={{0,1},{1,0},{2,3},{3,2},{4,5},{5,4},{6,7},{7,6},{8,9},{9,8},{10,11... | collective-permute-start | bytes 786440 | tf_op jit(solution)/shard_map/ppermute | solution.py:561
  12.6 8.0 %collective-permute-start.8 = (bf16[2,8,32,128]{3,2,1,0:T(8,128)(2,1)S(1)}, bf16[2,8,32,128]{3,2,1,0:T(8,128)(2,1)S(1)}, u32[]{:S(2)}, u32[]{:S(2)}) collective-permute-start(bf16[2,8,32,128]{3,2,1,0:T(8,128)(2,1)S(1)} %get-tuple-element.50), channel_id=1, source_target_pairs={{0,2},{1,3},{2,0},{3,1},{4,6},{5,7},{6,4},{7,5},{8,10},{9,11},{10,... | collective-permute-start | bytes 393224 | tf_op jit(solution)/shard_map/ppermute | solution.py:565
  18.7 3.9 %collective-permute-start.11 = (bf16[400,128]{1,0:T(8,128)(2,1)S(1)}, bf16[400,128]{1,0:T(8,128)(2,1)S(1)}, u32[]{:S(2)}, u32[]{:S(2)}) collective-permute-start(bf16[400,128]{1,0:T(8,128)(2,1)S(1)} %get-tuple-element.54), channel_id=1, source_target_pairs={{0,2},{1,3},{2,0},{3,1},{4,6},{5,7},{6,4},{7,5},{8,10},{9,11},{10,... | collective-permute-start | bytes 307208 | tf_op jit(solution)/shard_map/ppermute | solution.py:565
  18.7 4.8 %collective-permute-start.6 = (bf16[400,128]{1,0:T(8,128)(2,1)S(1)}, bf16[400,128]{1,0:T(8,128)(2,1)S(1)}, u32[]{:S(2)}, u32[]{:S(2)}) collective-permute-start(bf16[400,128]{1,0:T(8,128)(2,1)S(1)} %get-tuple-element.46), channel_id=1, source_target_pairs={{0,1},{1,0},{2,3},{3,2},{4,5},{5,4},{6,7},{7,6},{8,9},{9,8},{10,11... | collective-permute-start | bytes 307208 | tf_op jit(solution)/shard_map/ppermute | solution.py:565
  19.0 5.4 %collective-permute-start.7 = (bf16[400,128]{1,0:T(8,128)(2,1)S(1)}, bf16[400,128]{1,0:T(8,128)(2,1)S(1)}, u32[]{:S(2)}, u32[]{:S(2)}) collective-permute-start(bf16[400,128]{1,0:T(8,128)(2,1)S(1)} %get-tuple-element.47), channel_id=1, source_target_pairs={{0,3},{1,2},{2,1},{3,0},{4,7},{5,6},{6,5},{7,4},{8,11},{9,10},{10,... | collective-permute-start | bytes 307208 | tf_op jit(solution)/shard_map/ppermute | solution.py:565
  20.6 3.8 %collective-permute-start.10 = (bf16[1,8,32,128]{3,2,1,0:T(8,128)(2,1)S(1)}, bf16[1,8,32,128]{3,2,1,0:T(8,128)(2,1)S(1)}, u32[]{:S(2)}, u32[]{:S(2)}) collective-permute-start(bf16[1,8,32,128]{3,2,1,0:T(8,128)(2,1)S(1)} %slice.3), channel_id=1, source_target_pairs={{0,1},{1,0},{2,3},{3,2},{4,5},{5,4},{6,7},{7,6},{8,9},{9,8},{10,11... | collective-permute-start | bytes 196616 | tf_op jit(solution)/shard_map/ppermute | solution.py:565
  20.7 3.7 %collective-permute-start.9 = (bf16[8,32,128]{2,1,0:T(8,128)(2,1)S(1)}, bf16[8,32,128]{2,1,0:T(8,128)(2,1)S(1)}, u32[]{:S(2)}, u32[]{:S(2)}) collective-permute-start(bf16[8,32,128]{2,1,0:T(8,128)(2,1)S(1)} %get-tuple-element.51), channel_id=1, source_target_pairs={{0,1},{1,0},{2,3},{3,2},{4,5},{5,4},{6,7},{7,6},{8,9},{9,8},{10,11... | collective-permute-start | bytes 196616 | tf_op jit(solution)/shard_map/ppermute | solution.py:565

commit v12 on v11

--- a/solution.py
+++ b/solution.py
@@ -593,7 +593,7 @@
     for value in direct:
         owns += [value, relayed]
     coarse = None
-    for steps in (range(0, parts, 2), range(1, parts, 2)):
+    for steps in (range(0, parts, 2), range(parts - 1, 0, -2)):
         coarse = unpack([outs[t] for t in steps], [owns[t] for t in steps], steps, coarse)
     return coarse[None]
 

time: 25.8 us -> 25.8 us (level)
  the two profiles are of different devices: /device:TPU:5 before, /device:TPU:20 now
where the time goes in v12:
time: 25.8 us; the launch traced here: 25.6 us
  starting transfers between devices  10.6 us (41%)
  Pallas kernels  9.58 us (37%)
  waiting for transfers between devices  5.27 us (20%)
    ppermute x6, starting transfers between devices, swap(): return lax.ppermute(value, ('row', 'col'), pairs)  5.47 us
    ppermute x6, starting transfers between devices, xor_swap(): lax.ppermute(value, 'col', [(i, i ^ s) for i in range(lax.axis_size('col'...  5.18 us
    pallas_call x1, Pallas kernels, step_one(): pl.pallas_call(step_one_kernel, out_shape=(jax.ShapeDtypeStruct((4, 9, BS...  4.56 us
    ppermute x6, waiting for transfers between devices, xor_swap(): lax.ppermute(value, 'col', [(i, i ^ s) for i in range(lax.axis_size('col'...  2.92 us
    ppermute x6, waiting for transfers between devices, swap(): return lax.ppermute(value, ('row', 'col'), pairs)  2.35 us
    pallas_call x2, Pallas kernels, unpack(): pl.pallas_call(functools.partial(unpack_kernel, parts, steps), out_shape=...  2.06 us
    pallas_call x1, Pallas kernels, near_terms(): pl.pallas_call(functools.partial(near_kernel, parts), out_shape=shapes, i...  1.16 us
    pallas_call x1, Pallas kernels, rims(): pl.pallas_call(rims_kernel, out_shape=(shape,) * 2 + (jax.ShapeDtypeStruc...  1.14 us
  transfers between devices with their start and end apart: 12, of which 3 were waited for; matrix products, arithmetic and copies ran while one was open for 0% of the time, Pallas kernels for 29%

profile of v12, /device:TPU:20, one launch (start us, length us, event | category | flops | bytes accessed | tf_op | source)
XLA Modules:
  0.0 25.6 jit_solution(1143687473275357564)
XLA Ops:
  0.0 1.1 %rims.1 = (bf16[1032,128]{1,0:T(8,128)(2,1)S(1)}, bf16[1032,128]{1,0:T(8,128)(2,1)S(1)}, f32[8,128]{1,0:T(8,128)S(1)}) custom-call(s32[4,4]{1,0:T(4,128)} %agg_hbm.1, bf16[4,512,128]{2,1,0:T(8,128)(2,1)} %bitcast.3), custom_call_target="tpu_custom_call" | custom-call | tf_op jit(solution)/shard_map/rims/pallas_call | solution.py:70
  1.1 0.6 %collective-permute-start = (bf16[1032,128]{1,0:T(8,128)(2,1)S(1)}, bf16[1032,128]{1,0:T(8,128)(2,1)S(1)}, u32[]{:S(2)}, u32[]{:S(2)}) collective-permute-start(bf16[1032,128]{1,0:T(8,128)(2,1)S(1)} %get-tuple-element.31.row_a), channel_id=1, source_target_pairs={{0,4},{1,5},{2,6},{3,7},{4,0},{5,1},{6,2},{7,3},{8,12},{9,13},{10,... | collective-permute-start | bytes 792584 | tf_op jit(solution)/shard_map/ppermute | solution.py:561
  1.7 2.5 %collective-permute-start.1 = (bf16[1032,128]{1,0:T(8,128)(2,1)S(1)}, bf16[1032,128]{1,0:T(8,128)(2,1)S(1)}, u32[]{:S(2)}, u32[]{:S(2)}) collective-permute-start(bf16[1032,128]{1,0:T(8,128)(2,1)S(1)} %get-tuple-element.32.row_b), channel_id=1, source_target_pairs={{0,1},{1,0},{2,3},{3,2},{4,8},{5,9},{6,10},{7,11},{8,4},{9,5},{10,... | collective-permute-start | bytes 792584 | tf_op jit(solution)/shard_map/ppermute | solution.py:561
  4.3 0.1 collective-permute-start.2
  4.4 0.5 %collective-permute-start.3 = (bf16[1032,128]{1,0:T(8,128)(2,1)S(1)}, bf16[1032,128]{1,0:T(8,128)(2,1)S(1)}, u32[]{:S(2)}, u32[]{:S(2)}) collective-permute-start(bf16[1032,128]{1,0:T(8,128)(2,1)S(1)} %get-tuple-element.33.after), channel_id=1, source_target_pairs={{0,8},{1,2},{2,1},{3,11},{4,0},{5,6},{6,5},{7,3},{8,16},{9,10},{10... | collective-permute-start | bytes 792584 | tf_op jit(solution)/shard_map/ppermute | solution.py:561
  4.9 4.6 %step_one.1 = (bf16[4,9,128,512]{3,2,1,0:T(8,128)(2,1)S(1)}, bf16[2,128,512]{2,1,0:T(8,128)(2,1)S(1)}, bf16[2,128,512]{2,1,0:T(8,128)(2,1)S(1)}, bf16[4,512,128]{2,1,0:T(8,128)(2,1)S(1)}) custom-call(s32[4,4,12]{2,1,0:T(4,128)} %codes_hbm.1, bf16[192,128,128]{2,1,0:T(8,128)(2,1)} %bitcast.5, bf16[4,512,128]{2,1,0:T(8,128)(2,1)} %bitcast.4, ...), custom_call_target="tpu_custom_call" | custom-call | flops 8589934592 | bytes 1048576 | tf_op jit(solution)/shard_map/step_one/pallas_call | solution.py:202
  9.4 0.5 %collective-permute-start.4 = (bf16[2,128,512]{2,1,0:T(8,128)(2,1)S(1)}, bf16[2,128,512]{2,1,0:T(8,128)(2,1)S(1)}, u32[]{:S(2)}, u32[]{:S(2)}) collective-permute-start(bf16[2,128,512]{2,1,0:T(8,128)(2,1)S(1)} %get-tuple-element.38), channel_id=1, source_target_pairs={{0,8},{1,2},{2,1},{3,11},{4,0},{5,6},{6,5},{7,3},{8,16},{9,10},{10... | collective-permute-start | bytes 786440 | tf_op jit(solution)/shard_map/ppermute | solution.py:561
  9.9 0.0 collective-permute-done.2.col_a
  9.9 1.3 %collective-permute-start.5 = (bf16[2,128,512]{2,1,0:T(8,128)(2,1)S(1)}, bf16[2,128,512]{2,1,0:T(8,128)(2,1)S(1)}, u32[]{:S(2)}, u32[]{:S(2)}) collective-permute-start(bf16[2,128,512]{2,1,0:T(8,128)(2,1)S(1)} %get-tuple-element.42), channel_id=1, source_target_pairs={{0,1},{1,0},{2,3},{3,2},{4,5},{5,4},{6,7},{7,6},{8,9},{9,8},{10,11... | collective-permute-start | bytes 786440 | tf_op jit(solution)/shard_map/ppermute | solution.py:561
  11.2 0.0 collective-permute-done.3.col_b
  11.2 1.2 %near_terms.1 = (bf16[8,32,128]{2,1,0:T(8,128)(2,1)S(1)}, bf16[8,32,128]{2,1,0:T(8,128)(2,1)S(1)}, bf16[2,8,32,128]{3,2,1,0:T(8,128)(2,1)S(1)}, f32[4,128,128]{2,1,0:T(8,128)S(1)}, f32[8,128]{1,0:T(8,128)S(1)}) custom-call(f32[8,128]{1,0:T(8,128)S(1)} %get-tuple-element.30.bits, bf16[4,9,128,512]{3,2,1,0:T(8,128)(2,1)S(1)} %get-tuple-element.34.r, ...), custom_call_target="tpu_custom_call" | custom-call | flops 1 | bytes 1 | tf_op jit(solution)/shard_map/near_terms/pallas_call | solution.py:328
  12.4 1.1 %collective-permute-start.8 = (bf16[2,8,32,128]{3,2,1,0:T(8,128)(2,1)S(1)}, bf16[2,8,32,128]{3,2,1,0:T(8,128)(2,1)S(1)}, u32[]{:S(2)}, u32[]{:S(2)}) collective-permute-start(bf16[2,8,32,128]{3,2,1,0:T(8,128)(2,1)S(1)} %get-tuple-element.50), channel_id=1, source_target_pairs={{0,2},{1,3},{2,0},{3,1},{4,6},{5,7},{6,4},{7,5},{8,10},{9,11},{10,... | collective-permute-start | bytes 393224 | tf_op jit(solution)/shard_map/ppermute | solution.py:565
  13.5 2.3 %collective-permute-done.4.refs_3_ = bf16[2,128,512]{2,1,0:T(8,128)(2,1)S(1)} collective-permute-done((bf16[2,128,512]{2,1,0:T(8,128)(2,1)S(1)}, bf16[2,128,512]{2,1,0:T(8,128)(2,1)S(1)}, u32[]{:S(2)}, u32[]{:S(2)}) %collective-permute-start.4) | collective-permute-done | bytes 262176 | tf_op jit(solution)/shard_map/ppermute | solution.py:561
  15.9 0.0 collective-permute-done.refs_0_
  15.9 0.0 collective-permute-done.1.refs_1_
  15.9 0.0 collective-permute-done.5.from_a
  15.9 0.6 %far_terms.1 = (bf16[400,128]{1,0:T(8,128)(2,1)S(1)}, bf16[400,128]{1,0:T(8,128)(2,1)S(1)}, bf16[400,128]{1,0:T(8,128)(2,1)S(1)}, bf16[400,128]{1,0:T(8,128)(2,1)S(1)}) custom-call(f32[8,128]{1,0:T(8,128)S(1)} %get-tuple-element.30.bits, bf16[4,9,128,512]{3,2,1,0:T(8,128)(2,1)S(1)} %get-tuple-element.34.r, bf16[1032,128]{1,0:T(8,128)(2,1)S(1)} %get-tuple-element.40.row_a, ...), custom_call_target="tpu_custom_call" | custom-call | flops 1 | bytes 1 | tf_op jit(solution)/shard_map/far_terms/pallas_call | solution.py:382
  16.5 1.8 %collective-permute-start.11 = (bf16[400,128]{1,0:T(8,128)(2,1)S(1)}, bf16[400,128]{1,0:T(8,128)(2,1)S(1)}, u32[]{:S(2)}, u32[]{:S(2)}) collective-permute-start(bf16[400,128]{1,0:T(8,128)(2,1)S(1)} %get-tuple-element.54), channel_id=1, source_target_pairs={{0,2},{1,3},{2,0},{3,1},{4,6},{5,7},{6,4},{7,5},{8,10},{9,11},{10,... | collective-permute-start | bytes 307208 | tf_op jit(solution)/shard_map/ppermute | solution.py:565
  18.3 1.6 %collective-permute-start.6 = (bf16[400,128]{1,0:T(8,128)(2,1)S(1)}, bf16[400,128]{1,0:T(8,128)(2,1)S(1)}, u32[]{:S(2)}, u32[]{:S(2)}) collective-permute-start(bf16[400,128]{1,0:T(8,128)(2,1)S(1)} %get-tuple-element.46), channel_id=1, source_target_pairs={{0,3},{1,2},{2,1},{3,0},{4,7},{5,6},{6,5},{7,4},{8,11},{9,10},{10,... | collective-permute-start | bytes 307208 | tf_op jit(solution)/shard_map/ppermute | solution.py:565
  19.9 0.0 collective-permute-start.7
  19.9 0.0 collective-permute-done.8.refs_3_
  19.9 0.6 %collective-permute-start.9 = (bf16[1,8,32,128]{3,2,1,0:T(8,128)(2,1)S(1)}, bf16[1,8,32,128]{3,2,1,0:T(8,128)(2,1)S(1)}, u32[]{:S(2)}, u32[]{:S(2)}) collective-permute-start(bf16[1,8,32,128]{3,2,1,0:T(8,128)(2,1)S(1)} %slice.3), channel_id=1, source_target_pairs={{0,1},{1,0},{2,3},{3,2},{4,5},{5,4},{6,7},{7,6},{8,9},{9,8},{10,11... | collective-permute-start | bytes 196616 | tf_op jit(solution)/shard_map/ppermute | solution.py:565
  20.5 0.1 collective-permute-start.10
  20.6 0.9 %collective-permute-done.11.refs_1_ = bf16[400,128]{1,0:T(8,128)(2,1)S(1)} collective-permute-done((bf16[400,128]{1,0:T(8,128)(2,1)S(1)}, bf16[400,128]{1,0:T(8,128)(2,1)S(1)}, u32[]{:S(2)}, u32[]{:S(2)}) %collective-permute-start.11) | collective-permute-done | bytes 102432 | tf_op jit(solution)/shard_map/ppermute | solution.py:565
  21.5 1.0 %unpack.2.refs_4_ = bf16[4,2,9,2,32,128]{5,4,3,2,1,0:T(8,128)(2,1)} custom-call(bf16[400,128]{1,0:T(8,128)(2,1)S(1)} %get-tuple-element.53.refs_0_, bf16[400,128]{1,0:T(8,128)(2,1)S(1)} %collective-permute-done.11.refs_1_, bf16[8,32,128]{2,1,0:T(8,128)(2,1)S(1)} %get-tuple-element.39.refs_4_.refs_2_, bf16[2,8,32,128]{3,2,1,0:T(8,128)(2,1)S(1)} %collective-permute-done.8.refs_3_), custom_call_target="tpu_custom_call" | custom-call | flops 1 | bytes 1 | tf_op jit(solution)/shard_map/unpack/pallas_call | solution.py:451
  22.5 2.0 %collective-permute-done.6.refs_0_ = bf16[400,128]{1,0:T(8,128)(2,1)S(1)} collective-permute-done((bf16[400,128]{1,0:T(8,128)(2,1)S(1)}, bf16[400,128]{1,0:T(8,128)(2,1)S(1)}, u32[]{:S(2)}, u32[]{:S(2)}) %collective-permute-start.6) | collective-permute-done | bytes 102432 | tf_op jit(solution)/shard_map/ppermute | solution.py:565
  24.5 0.0 collective-permute-done.7.refs_1_
  24.5 0.0 collective-permute-done.9.refs_2_
  24.5 0.0 collective-permute-done.10.refs_3_
  24.5 1.0 %unpack.3 = bf16[4,2,9,2,32,128]{5,4,3,2,1,0:T(8,128)(2,1)} custom-call(bf16[400,128]{1,0:T(8,128)(2,1)S(1)} %collective-permute-done.6.refs_0_, bf16[400,128]{1,0:T(8,128)(2,1)S(1)} %collective-permute-done.7.refs_1_, bf16[1,8,32,128]{3,2,1,0:T(8,128)(2,1)S(1)} %collective-permute-done.9.refs_2_, ...), custom_call_target="tpu_custom_call", output_to_operand_aliasing={{}: (4, {})} | custom-call | flops 1 | bytes 1 | tf_op jit(solution)/shard_map/unpack/pallas_call | solution.py:451
  (3 shorter events, 0.0 us)
Async XLA Ops:
  1.1 14.7 %collective-permute-start = (bf16[1032,128]{1,0:T(8,128)(2,1)S(1)}, bf16[1032,128]{1,0:T(8,128)(2,1)S(1)}, u32[]{:S(2)}, u32[]{:S(2)}) collective-permute-start(bf16[1032,128]{1,0:T(8,128)(2,1)S(1)} %get-tuple-element.31.row_a), channel_id=1, source_target_pairs={{0,4},{1,5},{2,6},{3,7},{4,0},{5,1},{6,2},{7,3},{8,12},{9,13},{10,... | collective-permute-start | bytes 792584 | tf_op jit(solution)/shard_map/ppermute | solution.py:561
  1.7 14.2 %collective-permute-start.1 = (bf16[1032,128]{1,0:T(8,128)(2,1)S(1)}, bf16[1032,128]{1,0:T(8,128)(2,1)S(1)}, u32[]{:S(2)}, u32[]{:S(2)}) collective-permute-start(bf16[1032,128]{1,0:T(8,128)(2,1)S(1)} %get-tuple-element.32.row_b), channel_id=1, source_target_pairs={{0,1},{1,0},{2,3},{3,2},{4,8},{5,9},{6,10},{7,11},{8,4},{9,5},{10,... | collective-permute-start | bytes 792584 | tf_op jit(solution)/shard_map/ppermute | solution.py:561
  4.3 5.7 %collective-permute-start.2 = (bf16[1032,128]{1,0:T(8,128)(2,1)S(1)}, bf16[1032,128]{1,0:T(8,128)(2,1)S(1)}, u32[]{:S(2)}, u32[]{:S(2)}) collective-permute-start(bf16[1032,128]{1,0:T(8,128)(2,1)S(1)} %get-tuple-element.36), channel_id=1, source_target_pairs={{0,1},{1,0},{2,3},{3,2},{4,5},{5,4},{6,7},{7,6},{8,9},{9,8},{10,11... | collective-permute-start | bytes 792584 | tf_op jit(solution)/shard_map/ppermute | solution.py:561
  4.4 6.9 %collective-permute-start.3 = (bf16[1032,128]{1,0:T(8,128)(2,1)S(1)}, bf16[1032,128]{1,0:T(8,128)(2,1)S(1)}, u32[]{:S(2)}, u32[]{:S(2)}) collective-permute-start(bf16[1032,128]{1,0:T(8,128)(2,1)S(1)} %get-tuple-element.33.after), channel_id=1, source_target_pairs={{0,8},{1,2},{2,1},{3,11},{4,0},{5,6},{6,5},{7,3},{8,16},{9,10},{10... | collective-permute-start | bytes 792584 | tf_op jit(solution)/shard_map/ppermute | solution.py:561
  9.4 6.4 %collective-permute-start.4 = (bf16[2,128,512]{2,1,0:T(8,128)(2,1)S(1)}, bf16[2,128,512]{2,1,0:T(8,128)(2,1)S(1)}, u32[]{:S(2)}, u32[]{:S(2)}) collective-permute-start(bf16[2,128,512]{2,1,0:T(8,128)(2,1)S(1)} %get-tuple-element.38), channel_id=1, source_target_pairs={{0,8},{1,2},{2,1},{3,11},{4,0},{5,6},{6,5},{7,3},{8,16},{9,10},{10... | collective-permute-start | bytes 786440 | tf_op jit(solution)/shard_map/ppermute | solution.py:561
  9.9 5.9 %collective-permute-start.5 = (bf16[2,128,512]{2,1,0:T(8,128)(2,1)S(1)}, bf16[2,128,512]{2,1,0:T(8,128)(2,1)S(1)}, u32[]{:S(2)}, u32[]{:S(2)}) collective-permute-start(bf16[2,128,512]{2,1,0:T(8,128)(2,1)S(1)} %get-tuple-element.42), channel_id=1, source_target_pairs={{0,1},{1,0},{2,3},{3,2},{4,5},{5,4},{6,7},{7,6},{8,9},{9,8},{10,11... | collective-permute-start | bytes 786440 | tf_op jit(solution)/shard_map/ppermute | solution.py:561
  12.4 7.5 %collective-permute-start.8 = (bf16[2,8,32,128]{3,2,1,0:T(8,128)(2,1)S(1)}, bf16[2,8,32,128]{3,2,1,0:T(8,128)(2,1)S(1)}, u32[]{:S(2)}, u32[]{:S(2)}) collective-permute-start(bf16[2,8,32,128]{3,2,1,0:T(8,128)(2,1)S(1)} %get-tuple-element.50), channel_id=1, source_target_pairs={{0,2},{1,3},{2,0},{3,1},{4,6},{5,7},{6,4},{7,5},{8,10},{9,11},{10,... | collective-permute-start | bytes 393224 | tf_op jit(solution)/shard_map/ppermute | solution.py:565
  16.5 5.0 %collective-permute-start.11 = (bf16[400,128]{1,0:T(8,128)(2,1)S(1)}, bf16[400,128]{1,0:T(8,128)(2,1)S(1)}, u32[]{:S(2)}, u32[]{:S(2)}) collective-permute-start(bf16[400,128]{1,0:T(8,128)(2,1)S(1)} %get-tuple-element.54), channel_id=1, source_target_pairs={{0,2},{1,3},{2,0},{3,1},{4,6},{5,7},{6,4},{7,5},{8,10},{9,11},{10,... | collective-permute-start | bytes 307208 | tf_op jit(solution)/shard_map/ppermute | solution.py:565
  18.3 6.2 %collective-permute-start.6 = (bf16[400,128]{1,0:T(8,128)(2,1)S(1)}, bf16[400,128]{1,0:T(8,128)(2,1)S(1)}, u32[]{:S(2)}, u32[]{:S(2)}) collective-permute-start(bf16[400,128]{1,0:T(8,128)(2,1)S(1)} %get-tuple-element.46), channel_id=1, source_target_pairs={{0,3},{1,2},{2,1},{3,0},{4,7},{5,6},{6,5},{7,4},{8,11},{9,10},{10,... | collective-permute-start | bytes 307208 | tf_op jit(solution)/shard_map/ppermute | solution.py:565
  19.9 4.6 %collective-permute-start.7 = (bf16[400,128]{1,0:T(8,128)(2,1)S(1)}, bf16[400,128]{1,0:T(8,128)(2,1)S(1)}, u32[]{:S(2)}, u32[]{:S(2)}) collective-permute-start(bf16[400,128]{1,0:T(8,128)(2,1)S(1)} %get-tuple-element.47), channel_id=1, source_target_pairs={{0,1},{1,0},{2,3},{3,2},{4,5},{5,4},{6,7},{7,6},{8,9},{9,8},{10,11... | collective-permute-start | bytes 307208 | tf_op jit(solution)/shard_map/ppermute | solution.py:565
  19.9 4.6 %collective-permute-start.9 = (bf16[1,8,32,128]{3,2,1,0:T(8,128)(2,1)S(1)}, bf16[1,8,32,128]{3,2,1,0:T(8,128)(2,1)S(1)}, u32[]{:S(2)}, u32[]{:S(2)}) collective-permute-start(bf16[1,8,32,128]{3,2,1,0:T(8,128)(2,1)S(1)} %slice.3), channel_id=1, source_target_pairs={{0,1},{1,0},{2,3},{3,2},{4,5},{5,4},{6,7},{7,6},{8,9},{9,8},{10,11... | collective-permute-start | bytes 196616 | tf_op jit(solution)/shard_map/ppermute | solution.py:565
  20.5 4.0 %collective-permute-start.10 = (bf16[8,32,128]{2,1,0:T(8,128)(2,1)S(1)}, bf16[8,32,128]{2,1,0:T(8,128)(2,1)S(1)}, u32[]{:S(2)}, u32[]{:S(2)}) collective-permute-start(bf16[8,32,128]{2,1,0:T(8,128)(2,1)S(1)} %get-tuple-element.52), channel_id=1, source_target_pairs={{0,1},{1,0},{2,3},{3,2},{4,5},{5,4},{6,7},{7,6},{8,9},{9,8},{10,11... | collective-permute-start | bytes 196616 | tf_op jit(solution)/shard_map/ppermute | solution.py:565
